TPU v7x, 512 devices: a whole 4x4x16 slice. The times are simulated.
512 devices in a mesh: row: 128 (over x, z, core), rep: 4 (over y).
Axes of the slice: x: 4, y: 4, z: 16, core: 2. Of those that a mesh axis runs over, the one named last changes fastest.
Arguments:
- features: bfloat16 [131072, 256], P('row'), may hold values from -6 to 6
- block_cols: int32 [1024, 4, 12], P('row', 'rep'), may hold values from 0 to 1023, as said below
- block_vals: bfloat16 [1024, 4, 12, 128, 128], P('row', 'rep'), may hold values from -0.078125 to 0.078125
- weight: bfloat16 [256, 256], replicated, may hold values from -0.375 to 0.375
- cotangent: bfloat16 [131072, 256], P(('row', 'rep')), may hold values from -6 to 6
Outputs:
- output_rows: bfloat16 [131072, 256], P(('row', 'rep'))
- grad_weight: float32 [256, 256], replicated
- grad_features: float32 [131072, 256], P(('row', 'rep'))
Inputs may be any that keep to these rules, and one draw needn't show every extreme that they name: For a node block b of row group g = b // 8 and quarter index r, every entry block_cols[b, r, s] equals h * 8 + r * 2 + q with h a row group within 3 of g (and inside the grid) and 0 <= q < 2; entries may repeat.
All inputs are finite; a program needn't handle non-finite values.
Results may differ from a plain program's by a relative error of at most 0.0065.
Values may be sent and summed in bfloat16 or wider, within the bound.
No kernel may reach another device: no remote copies, remote signals or barrier semaphores. Data moves between devices by JAX's collectives and lax.ppermute only.
A program may use at most 64 MiB of HBM per device.

v0:
```python
import jax
import jax.numpy as jnp
from jax import lax
from jax.sharding import PartitionSpec as P

HALF = 3


def from_behind(x, axis, by):
    devices = lax.axis_size(axis)
    pairs = [(i, i + by) for i in range(devices) if 0 <= i + by < devices]
    return lax.ppermute(x, axis, pairs)


def gather_band(own_quarter):
    sections = 2 * HALF + 1
    pieces = []
    for section in range(sections):
        if section == HALF:
            pieces.append(own_quarter)
        else:
            pieces.append(from_behind(own_quarter, "row", section - HALF))
    return jnp.stack(pieces)


def return_band(window_grad):
    sections = 2 * HALF + 1
    accumulated = window_grad[HALF]
    for section in range(sections):
        if section != HALF:
            accumulated = accumulated + from_behind(window_grad[section], "row", HALF - section)
    return accumulated


def on_device(features, block_cols, block_vals, weight, cotangent):
    rep_count = lax.axis_size("rep")
    row_count = lax.axis_size("row")
    rep_index = lax.axis_index("rep")
    row_index = lax.axis_index("row")
    group_rows, hidden = features.shape
    block_side = block_vals.shape[-1]
    blocks_group = group_rows // block_side
    quarter_blocks = blocks_group // rep_count
    sections = 2 * HALF + 1
    own_quarter = lax.dynamic_slice_in_dim(
        features, rep_index * quarter_blocks * block_side, quarter_blocks * block_side, 0
    )
    own_quarter = own_quarter.reshape(quarter_blocks, block_side, hidden)
    window = gather_band(own_quarter)
    window_rows = window.reshape(sections * quarter_blocks, block_side, hidden)
    column_ids = block_cols[:, 0, :]
    block_values = block_vals[:, 0]
    source_group = column_ids // blocks_group
    within = column_ids % blocks_group - rep_index * quarter_blocks
    slot_index = (row_index + HALF - source_group) * quarter_blocks + within
    chosen = window_rows[slot_index]
    partial_rows = jnp.einsum(
        "bsij,bsjh->bih", block_values, chosen, preferred_element_type=jnp.float32
    )
    partial_rows = partial_rows.reshape(group_rows, hidden)
    summed = lax.psum_scatter(partial_rows, "rep", scatter_dimension=0, tiled=True)
    aggregate = summed.astype(jnp.bfloat16)
    preact = jnp.dot(aggregate, weight, preferred_element_type=jnp.float32)
    output_rows = jax.nn.silu(preact).astype(jnp.bfloat16)
    sigmoid_pre = jax.nn.sigmoid(preact)
    grad_pre = (
        cotangent.astype(jnp.float32) * sigmoid_pre * (1.0 + preact * (1.0 - sigmoid_pre))
    ).astype(jnp.bfloat16)
    local_grad = lax.dot_general(
        aggregate, grad_pre, (((0,), (0,)), ((), ())), preferred_element_type=jnp.float32
    )
    node_count = group_rows * row_count
    grad_weight = lax.psum(local_grad, ("row", "rep")) * node_count ** (-0.5)
    backward = lax.dot_general(
        grad_pre, weight, (((1,), (1,)), ((), ())), preferred_element_type=jnp.float32
    )
    backward = backward.astype(jnp.bfloat16)
    back_group = lax.all_gather(backward, "rep", axis=0, tiled=True).reshape(
        blocks_group, block_side, hidden
    )
    selector = (
        slot_index[:, :, None] == jnp.arange(sections * quarter_blocks)[None, None, :]
    ).astype(jnp.bfloat16)
    per_slot = jnp.einsum(
        "bsc,bsji->cbji", selector, block_values, preferred_element_type=jnp.float32
    )
    upper_part = per_slot.astype(jnp.bfloat16)
    lower_part = (per_slot - upper_part.astype(jnp.float32)).astype(jnp.bfloat16)
    window_grad = jnp.einsum(
        "cbji,bjh->cih", upper_part, back_group, preferred_element_type=jnp.float32
    )
    window_grad = window_grad + jnp.einsum(
        "cbji,bjh->cih", lower_part, back_group, preferred_element_type=jnp.float32
    )
    window_grad = window_grad.reshape(sections, quarter_blocks, block_side, hidden)
    grad_features = return_band(window_grad).reshape(quarter_blocks * block_side, hidden)
    return (output_rows, grad_weight, grad_features)


def solution(mesh):
    return jax.shard_map(
        on_device,
        mesh=mesh,
        in_specs=(
            P("row", None),
            P("row", "rep", None),
            P("row", "rep", None, None, None),
            P(),
            P(("row", "rep"), None),
        ),
        out_specs=(P(("row", "rep"), None), P(), P(("row", "rep"), None)),
        check_vma=False,
    )
```

profile of v0, /device:TPU:1, one launch (start us, length us, event | category | flops | bytes accessed | tf_op | source)
XLA Modules:
  0.0 591.7 jit_solution(17034580688814216332)
XLA Ops:
  7.2 0.0 copy-start
  7.2 0.0 reduce-scatter.2.cloned.1.call-start
  7.2 1.1 constant_dynamic-slice_fusion
  8.3 6.3 %collective-permute-start.5 = (bf16[2,128,256]{2,1,0:T(8,128)(2,1)S(1)}, bf16[2,128,256]{2,1,0:T(8,128)(2,1)S(1)}, u32[]{:S(2)}, u32[]{:S(2)}) collective-permute-start(bf16[2,128,256]{2,1,0:T(8,128)(2,1)S(1)} %bitcast.67), channel_id=1, source_target_pairs={{0,12},{4,16},{8,20},{12,24},{16,28},{20,32},{24,36},{28,40},{32,4... | collective-permute-start | bytes 393224 | tf_op jit(solution)/shard_map/ppermute | solution.py:12
  14.6 3.5 collective-permute-start.4
  18.2 2.2 collective-permute-start.3
  20.4 2.8 collective-permute-start.2
  23.1 1.3 collective-permute-start
  24.4 0.7 compare_select_fusion
  25.1 0.1 reshape.174
  25.2 8.5 %collective-permute-done = bf16[2,128,256]{2,1,0:T(8,128)(2,1)} collective-permute-done((bf16[2,128,256]{2,1,0:T(8,128)(2,1)S(1)}, bf16[2,128,256]{2,1,0:T(8,128)(2,1)}, u32[]{:S(2)}, u32[]{:S(2)}) %collective-permute-start) | collective-permute-done | bytes 131104 | tf_op jit(solution)/shard_map/ppermute | solution.py:12
  33.7 1.3 collective-permute-start.1
  35.0 1.6 bitcast_dynamic-update-slice_fusion.5
  36.5 3.6 collective-permute-done.1
  40.1 0.7 bitcast_dynamic-update-slice_fusion.4
  40.8 0.0 collective-permute-done.2
  40.8 1.6 bitcast_dynamic-update-slice_fusion.3
  42.4 0.6 constant_dynamic-update-slice_fusion
  43.0 0.0 collective-permute-done.3
  43.0 1.6 bitcast_dynamic-update-slice_fusion.2
  44.6 0.0 collective-permute-done.4
  44.6 0.7 bitcast_dynamic-update-slice_fusion.1
  45.3 0.0 collective-permute-done.5
  45.3 0.7 bitcast_dynamic-update-slice_fusion
  45.9 7.2 %gather_fusion = bf16[96,128,256]{2,1,0:T(8,128)(2,1)} fusion(bf16[14,128,256]{2,1,0:T(8,128)(2,1)} %bitcast.8, s32[1024]{0:T(1024)S(1)} %pad_clamp_fusion), kind=kCustom, calls=%fused_computation | custom fusion | bytes 12583296 | tf_op jit(solution)/shard_map/gather | solution.py:56
  53.1 0.0 copy-done
  53.1 5.0 fusion.36
  58.1 0.0 reduce-scatter.2.cloned.1.call-update
  58.1 0.0 all-reduce.2.cloned.1.call-start
  58.1 0.0 copy-done.5
  58.2 0.0 copy-start.4
  58.2 0.0 copy-start.6
  58.2 5.2 fusion.2
  63.4 27.5 %reduce-scatter.2.cloned.1.call-done = f32[256,256]{1,0:T(8,128)} async-done(((f32[1024,256]{1,0:T(8,128)}), f32[256,256]{1,0:T(8,128)}) %reduce-scatter.2.cloned.1.call-update) | async-done | bytes 262160 | tf_op jit(solution)/shard_map/reduce_scatter | solution.py:61
  91.0 0.0 copy-done.4
  91.0 0.0 copy-done.6
  91.0 2.0 multiply_convert_fusion
  93.0 0.2 convolution_convert_fusion
  93.2 11.2 %all_gather.3 = bf16[1024,256]{1,0:T(8,128)(2,1)S(1)} all-gather(bf16[256,256]{1,0:T(8,128)(2,1)S(1)} %convolution_convert_fusion), channel_id=1, replica_groups=mesh['row'=128,'rep'=4] {'rep'}, dimensions={0}, use_global_device_ids=true | all-gather | bytes 655360 | tf_op jit(solution)/shard_map/all_gather | solution.py:78
  104.4 7.2 %fusion.1 = f32[14,128,256,1]{2,1,3,0:T(8,128)S(1)} fusion(bf16[8,128,256,1]{2,1,0,3:T(8,128)(2,1)S(1)} %bitcast.65, f32[8,14,128,128]{3,1,2,0:T(8,128)} %fusion.2), kind=kOutput, calls=%fused_computation.4 | convolution fusion | flops 939524096 | bytes 9699328 | tf_op jit(solution)/shard_map/cbji,bjh->cih/dot_general | solution.py:89
  111.6 0.0 copy-done.1
  111.6 0.0 copy-start.3
  111.6 3.9 bitcast_add_fusion
  115.6 0.0 copy-start.2
  115.6 1.3 copy-done.2
  116.8 1.1 fusion.38
  117.9 8.7 %collective-permute-start.6 = (f32[2,128,256]{2,1,0:T(8,128)}, f32[2,128,256]{2,1,0:T(8,128)}, u32[]{:S(2)}, u32[]{:S(2)}) collective-permute-start(f32[2,128,256]{2,1,0:T(8,128)} %get-tuple-element.3), channel_id=1, source_target_pairs={{0,12},{4,16},{8,20},{12,24},{16,28},{20,32},{24,36},{28,40},{32,4... | collective-permute-start | bytes 786440 | tf_op jit(solution)/shard_map/ppermute | solution.py:12
  126.6 0.0 copy-done.3
  126.6 0.9 fusion.13
  127.5 0.0 all-reduce.2.cloned.1.call-update
  127.5 1.3 collective-permute-start.11
  128.8 1.3 collective-permute-start.10
  130.1 1.9 collective-permute-start.9
  132.1 3.6 collective-permute-start.8
  135.7 0.0 collective-permute-done.6
  135.7 5.1 collective-permute-start.7
  140.8 440.1 %all-reduce.2.cloned.1.call-done = f32[256,256]{1,0:T(8,128)} async-done(((f32[256,256]{1,0:T(8,128)}), f32[256,256]{1,0:T(8,128)}) %all-reduce.2.cloned.1.call-update) | async-done | bytes 262160 | tf_op jit(solution)/shard_map/psum | solution.py:73
  580.9 1.7 broadcast_multiply_fusion
  582.6 0.0 collective-permute-done.11
  582.6 0.0 collective-permute-done.10
  582.6 0.0 collective-permute-done.9
  582.6 0.0 collective-permute-done.8
  582.6 0.0 collective-permute-done.7
  582.6 2.2 fusion.12
  (4 shorter events, 0.0 us)
Async XLA Ops:
  7.2 45.9 %copy-start = (bf16[8,1,12,128,128]{4,3,2,1,0:T(8,128)(2,1)S(1)}, bf16[8,1,12,128,128]{4,3,2,1,0:T(8,128)(2,1)}, u32[]{:S(2)}) copy-start(bf16[8,1,12,128,128]{4,3,2,1,0:T(8,128)(2,1)} %param.7) | copy-start | bytes 9437188
  7.2 83.8 %reduce-scatter.2.cloned.1.call-start = ((), (), s32[]{:S(2)}) async-start(), calls=%async_computation.1 | async-start | bytes 1310720 | tf_op jit(solution)/shard_map/reduce_scatter | solution.py:61
  8.3 37.0 %collective-permute-start.5 = (bf16[2,128,256]{2,1,0:T(8,128)(2,1)S(1)}, bf16[2,128,256]{2,1,0:T(8,128)(2,1)S(1)}, u32[]{:S(2)}, u32[]{:S(2)}) collective-permute-start(bf16[2,128,256]{2,1,0:T(8,128)(2,1)S(1)} %bitcast.67), channel_id=1, source_target_pairs={{0,12},{4,16},{8,20},{12,24},{16,28},{20,32},{24,36},{28,40},{32,4... | collective-permute-start | bytes 393224 | tf_op jit(solution)/shard_map/ppermute | solution.py:12
  14.6 30.0 %collective-permute-start.4 = (bf16[2,128,256]{2,1,0:T(8,128)(2,1)S(1)}, bf16[2,128,256]{2,1,0:T(8,128)(2,1)S(1)}, u32[]{:S(2)}, u32[]{:S(2)}) collective-permute-start(bf16[2,128,256]{2,1,0:T(8,128)(2,1)S(1)} %bitcast.68), channel_id=1, source_target_pairs={{0,8},{4,12},{8,16},{12,20},{16,24},{20,28},{24,32},{28,36},{32,40... | collective-permute-start | bytes 393224 | tf_op jit(solution)/shard_map/ppermute | solution.py:12
  18.2 24.9 %collective-permute-start.3 = (bf16[2,128,256]{2,1,0:T(8,128)(2,1)S(1)}, bf16[2,128,256]{2,1,0:T(8,128)(2,1)}, u32[]{:S(2)}, u32[]{:S(2)}) collective-permute-start(bf16[2,128,256]{2,1,0:T(8,128)(2,1)S(1)} %bitcast.69), channel_id=1, source_target_pairs={{0,4},{4,8},{8,12},{12,16},{16,20},{20,24},{24,28},{28,32},{32,36}... | collective-permute-start | bytes 393224 | tf_op jit(solution)/shard_map/ppermute | solution.py:12
  20.4 20.4 %collective-permute-start.2 = (bf16[2,128,256]{2,1,0:T(8,128)(2,1)S(1)}, bf16[2,128,256]{2,1,0:T(8,128)(2,1)}, u32[]{:S(2)}, u32[]{:S(2)}) collective-permute-start(bf16[2,128,256]{2,1,0:T(8,128)(2,1)S(1)} %bitcast.70), channel_id=1, source_target_pairs={{4,0},{8,4},{12,8},{16,12},{20,16},{24,20},{28,24},{32,28},{36,32}... | collective-permute-start | bytes 393224 | tf_op jit(solution)/shard_map/ppermute | solution.py:12
  23.1 10.6 %collective-permute-start = (bf16[2,128,256]{2,1,0:T(8,128)(2,1)S(1)}, bf16[2,128,256]{2,1,0:T(8,128)(2,1)}, u32[]{:S(2)}, u32[]{:S(2)}) collective-permute-start(bf16[2,128,256]{2,1,0:T(8,128)(2,1)S(1)} %bitcast.71), channel_id=1, source_target_pairs={{12,0},{16,4},{20,8},{24,12},{28,16},{32,20},{36,24},{40,28},{44,3... | collective-permute-start | bytes 393224 | tf_op jit(solution)/shard_map/ppermute | solution.py:12
  33.7 6.4 %collective-permute-start.1 = (bf16[2,128,256]{2,1,0:T(8,128)(2,1)S(1)}, bf16[2,128,256]{2,1,0:T(8,128)(2,1)S(1)}, u32[]{:S(2)}, u32[]{:S(2)}) collective-permute-start(bf16[2,128,256]{2,1,0:T(8,128)(2,1)S(1)} %bitcast.72), channel_id=1, source_target_pairs={{8,0},{12,4},{16,8},{20,12},{24,16},{28,20},{32,24},{36,28},{40,32... | collective-permute-start | bytes 393224 | tf_op jit(solution)/shard_map/ppermute | solution.py:12
  53.1 5.0 copy-start.5
  58.1 522.8 %all-reduce.2.cloned.1.call-start = ((), (), s32[]{:S(2)}) async-start(), calls=%async_computation.2 | async-start | bytes 524288 | tf_op jit(solution)/shard_map/psum | solution.py:73
  58.2 32.8 %copy-start.4 = (bf16[256,256]{1,0:T(8,128)(2,1)S(1)}, bf16[256,256]{1,0:T(8,128)(2,1)}, u32[]{:S(2)}) copy-start(bf16[256,256]{1,0:T(8,128)(2,1)} %param.8) | copy-start | bytes 393220
  58.2 32.8 %copy-start.6 = (bf16[256,256]{1,0:T(8,128)(2,1)S(1)}, bf16[256,256]{1,0:T(8,128)(2,1)}, u32[]{:S(2)}) copy-start(bf16[256,256]{1,0:T(8,128)(2,1)} %param.9) | copy-start | bytes 393220
  91.0 20.7 %copy-start.1 = (f32[8,14,128,128]{3,1,2,0:T(8,128)S(1)}, f32[8,14,128,128]{3,1,2,0:T(8,128)}, u32[]{:S(2)}) copy-start(f32[8,14,128,128]{3,1,2,0:T(8,128)} %fusion.2) | copy-start | bytes 22020100
  111.6 14.9 %copy-start.3 = (f32[256,256]{1,0:T(8,128)S(1)}, f32[256,256]{1,0:T(8,128)}, u32[]{:S(2)}) copy-start(f32[256,256]{1,0:T(8,128)} %reduce-scatter.2.cloned.1.call-done) | copy-start | bytes 786436
  115.6 1.3 copy-start.2
  117.9 17.8 %collective-permute-start.6 = (f32[2,128,256]{2,1,0:T(8,128)}, f32[2,128,256]{2,1,0:T(8,128)}, u32[]{:S(2)}, u32[]{:S(2)}) collective-permute-start(f32[2,128,256]{2,1,0:T(8,128)} %get-tuple-element.3), channel_id=1, source_target_pairs={{0,12},{4,16},{8,20},{12,24},{16,28},{20,32},{24,36},{28,40},{32,4... | collective-permute-start | bytes 786440 | tf_op jit(solution)/shard_map/ppermute | solution.py:12
  127.5 455.1 %collective-permute-start.11 = (f32[2,128,256]{2,1,0:T(8,128)}, f32[2,128,256]{2,1,0:T(8,128)}, u32[]{:S(2)}, u32[]{:S(2)}) collective-permute-start(f32[2,128,256]{2,1,0:T(8,128)} %get-tuple-element.4), channel_id=1, source_target_pairs={{12,0},{16,4},{20,8},{24,12},{28,16},{32,20},{36,24},{40,28},{44,3... | collective-permute-start | bytes 786440 | tf_op jit(solution)/shard_map/ppermute | solution.py:12
  128.8 453.8 %collective-permute-start.10 = (f32[2,128,256]{2,1,0:T(8,128)}, f32[2,128,256]{2,1,0:T(8,128)}, u32[]{:S(2)}, u32[]{:S(2)}) collective-permute-start(f32[2,128,256]{2,1,0:T(8,128)} %get-tuple-element.5), channel_id=1, source_target_pairs={{8,0},{12,4},{16,8},{20,12},{24,16},{28,20},{32,24},{36,28},{40,32... | collective-permute-start | bytes 786440 | tf_op jit(solution)/shard_map/ppermute | solution.py:12
  130.1 452.5 %collective-permute-start.9 = (f32[2,128,256]{2,1,0:T(8,128)}, f32[2,128,256]{2,1,0:T(8,128)}, u32[]{:S(2)}, u32[]{:S(2)}) collective-permute-start(f32[2,128,256]{2,1,0:T(8,128)} %get-tuple-element.6), channel_id=1, source_target_pairs={{4,0},{8,4},{12,8},{16,12},{20,16},{24,20},{28,24},{32,28},{36,32}... | collective-permute-start | bytes 786440 | tf_op jit(solution)/shard_map/ppermute | solution.py:12
  132.1 450.6 %collective-permute-start.8 = (f32[2,128,256]{2,1,0:T(8,128)}, f32[2,128,256]{2,1,0:T(8,128)}, u32[]{:S(2)}, u32[]{:S(2)}) collective-permute-start(f32[2,128,256]{2,1,0:T(8,128)} %get-tuple-element.7), channel_id=1, source_target_pairs={{0,4},{4,8},{8,12},{12,16},{16,20},{20,24},{24,28},{28,32},{32,36}... | collective-permute-start | bytes 786440 | tf_op jit(solution)/shard_map/ppermute | solution.py:12
  135.7 446.9 %collective-permute-start.7 = (f32[2,128,256]{2,1,0:T(8,128)S(1)}, f32[2,128,256]{2,1,0:T(8,128)}, u32[]{:S(2)}, u32[]{:S(2)}) collective-permute-start(f32[2,128,256]{2,1,0:T(8,128)S(1)} %get-tuple-element.8), channel_id=1, source_target_pairs={{0,8},{4,12},{8,16},{12,20},{16,24},{20,28},{24,32},{28,36},{32,40... | collective-permute-start | bytes 786440 | tf_op jit(solution)/shard_map/ppermute | solution.py:12
Sparse Core Ops, SparseCore 0:
  58.2 32.7 reduce-scatter.1
  127.6 453.2 all-reduce.1
where the time goes:
time: 593 us; the launch traced here: 592 us
  waiting for transfers between devices  480 us (81%)
  starting transfers between devices  39.3 us (7%)
  matrix products  24.5 us (4%)
  local copies, waits for them, and re-layouts  18 us (3%)
  between operations  14.3 us (2%)
  blocking collectives  11.2 us (2%)
    psum x1, waiting for transfers between devices, on_device(): grad_weight = lax.psum(local_grad, ('row', 'rep')) * node_count ** (-0.5)  440 us
    ppermute x12, starting transfers between devices, from_behind(): return lax.ppermute(x, axis, pairs)  39.2 us
    reduce_scatter x1, waiting for transfers between devices, on_device(): lax.psum_scatter(partial_rows, 'rep', scatter_dimension=0, tiled=True)  27.5 us
    ppermute x12, waiting for transfers between devices, from_behind(): return lax.ppermute(x, axis, pairs)  12.1 us
  transfers between devices with their start and end apart: 14, of which 4 were waited for; matrix products, arithmetic and copies ran while one was open for 3% of the time, Pallas kernels for 0%

commit v1 on v0

v1 whole, which is shorter than its diff:
```python
import jax
import jax.numpy as jnp
from jax import lax
from jax.experimental import pallas as pl
from jax.experimental.pallas import tpu as pltpu
from jax.sharding import Mesh
from jax.sharding import PartitionSpec as P

HALF = 3
SECTIONS = 2 * HALF + 1
CORES = 2
X_CHIPS = 4
ROW = ("x", "z", "core")
PLANE = ("x", "core", "rep")
BF16 = jnp.bfloat16
F32 = jnp.float32
PIECE_OF = ((6, 1, 4, 0, 3, 2, 5), (4, 1, 3, 0, 5, 2, 6))


def params(mib=40):
    return pltpu.CompilerParams(vmem_limit_bytes=mib << 20)


def chip_shift(x, by):
    devices = lax.axis_size(ROW)
    by = by * CORES
    return lax.ppermute(x, ROW, [(i, i + by) for i in range(devices) if 0 <= i + by < devices])


def far_shift(x):
    devices = lax.axis_size(ROW)
    pairs = []
    for i in range(devices):
        to = i + HALF if i % CORES else i - HALF
        if 0 <= to < devices:
            pairs.append((i, to))
    return lax.ppermute(x, ROW, pairs)


def core_swap(x):
    return lax.ppermute(x, "core", [(0, 1), (1, 0)])


def transpose_kernel(slot_ref, vals_ref, out_ref, sum_ref):
    block = pl.program_id(0)
    slots = vals_ref.shape[1]
    sum_ref[...] = jnp.zeros_like(sum_ref)
    for s in range(slots):
        at = slot_ref[block * slots + s]
        sum_ref[at] += vals_ref[0, s].astype(F32)
    side = vals_ref.shape[2]
    for c in range(sum_ref.shape[0]):
        out_ref[c * side : (c + 1) * side, :] = sum_ref[c].astype(BF16).T


def transposed_band(slots, vals, columns):
    blocks, count, side, _ = vals.shape
    return pl.pallas_call(
        transpose_kernel,
        grid_spec=pltpu.PrefetchScalarGridSpec(
            num_scalar_prefetch=1,
            grid=(blocks,),
            in_specs=[pl.BlockSpec((1, count, side, side), lambda b, s: (b, 0, 0, 0))],
            out_specs=pl.BlockSpec((columns * side, side), lambda b, s: (0, b)),
            scratch_shapes=[pltpu.VMEM((columns, side, side), F32)],
        ),
        out_shape=jax.ShapeDtypeStruct((columns * side, blocks * side), BF16),
        compiler_params=params(),
        cost_estimate=pl.CostEstimate(flops=0, transcendentals=0, bytes_accessed=16 << 20),
        name="transposed_band",
    )(slots, vals)


def aggregate_kernel(slot_ref, vals_ref, near_ref, other_ref, far_ref, out_ref, window_ref):
    block = pl.program_id(0)
    slots = vals_ref.shape[1]
    side = vals_ref.shape[2]

    @pl.when(block == 0)
    def _():
        at = 0
        for ref in (near_ref, other_ref, far_ref):
            for k in range(ref.shape[0] // side):
                window_ref[at] = ref[k * side : (k + 1) * side, :]
                at += 1

    left = jnp.concatenate([vals_ref[0, s] for s in range(slots)], axis=1)
    right = jnp.concatenate([window_ref[slot_ref[block * slots + s]] for s in range(slots)], axis=0)
    out_ref[0] = jnp.dot(left, right, preferred_element_type=F32).astype(BF16)


def partial_aggregate(slots, vals, near, other, far, reps):
    blocks, count, side, _ = vals.shape
    hidden = near.shape[1]
    per_rep = blocks // reps
    columns = SECTIONS * per_rep

    def whole(x):
        return pl.BlockSpec(x.shape, lambda b, s: (0, 0))

    return pl.pallas_call(
        aggregate_kernel,
        grid_spec=pltpu.PrefetchScalarGridSpec(
            num_scalar_prefetch=1,
            grid=(blocks,),
            in_specs=[
                pl.BlockSpec((1, count, side, side), lambda b, s: (b, 0, 0, 0)),
                whole(near),
                whole(other),
                whole(far),
            ],
            out_specs=pl.BlockSpec((1, side, hidden), lambda b, s: (b // per_rep, b % per_rep, 0)),
            scratch_shapes=[pltpu.VMEM((columns, side, hidden), BF16)],
        ),
        out_shape=jax.ShapeDtypeStruct((reps, per_rep * side, hidden), BF16),
        compiler_params=params(),
        cost_estimate=pl.CostEstimate(flops=1 << 30, transcendentals=0, bytes_accessed=5 << 20),
        name="partial_aggregate",
    )(slots, vals, near, other, far)


def dense_kernel(parts_ref, weight_ref, cotangent_ref, out_ref, send_ref):
    reps, rows, hidden = parts_ref.shape
    summed = parts_ref[0].astype(F32)
    for q in range(1, reps):
        summed = summed + parts_ref[q].astype(F32)
    aggregate = summed.astype(BF16)
    preact = jnp.dot(aggregate, weight_ref[...], preferred_element_type=F32)
    sigmoid_pre = 1.0 / (1.0 + jnp.exp(-preact))
    out_ref[...] = (preact * sigmoid_pre).astype(BF16)
    grad_pre = (
        cotangent_ref[...].astype(F32) * sigmoid_pre * (1.0 + preact * (1.0 - sigmoid_pre))
    ).astype(BF16)
    backward = lax.dot_general(
        grad_pre, weight_ref[...], (((1,), (1,)), ((), ())), preferred_element_type=F32
    ).astype(BF16)
    local = lax.dot_general(
        aggregate, grad_pre, (((0,), (0,)), ((), ())), preferred_element_type=F32
    )
    piece = hidden // (X_CHIPS * CORES * reps)
    for q in range(reps):
        send_ref[q, :rows, :] = backward
        rows_of = [
            local[(k * reps + q) * piece : (k * reps + q + 1) * piece]
            for k in range(X_CHIPS * CORES)
        ]
        send_ref[q, rows:, :] = jnp.concatenate(rows_of, axis=0).astype(BF16)


def dense_layer(parts, weight, cotangent):
    reps, rows, hidden = parts.shape
    return pl.pallas_call(
        dense_kernel,
        out_shape=(
            jax.ShapeDtypeStruct((rows, hidden), BF16),
            jax.ShapeDtypeStruct((reps, rows + hidden // reps, hidden), BF16),
        ),
        compiler_params=params(),
        cost_estimate=pl.CostEstimate(flops=100 << 20, transcendentals=1 << 16, bytes_accessed=2 << 20),
        name="dense_layer",
    )(parts, weight, cotangent)


def products(band_ref, back_ref, first):
    reps = back_ref.shape[0]
    rows = band_ref.shape[1] // reps
    total = None
    for q in range(reps):
        term = jnp.dot(
            band_ref[first : first + rows, q * rows : (q + 1) * rows],
            back_ref[q, :rows, :],
            preferred_element_type=F32,
        )
        total = term if total is None else total + term
    return total


def leaving_kernel(band_ref, back_ref, other_ref, far_ref):
    rows = far_ref.shape[0]
    for k in range(HALF):
        other_ref[k * rows : (k + 1) * rows, :] = products(band_ref, back_ref, (HALF + k) * rows).astype(BF16)
    far_ref[...] = products(band_ref, back_ref, 2 * HALF * rows).astype(BF16)


def staying_kernel(band_ref, back_ref, near_ref):
    rows = near_ref.shape[0] // HALF
    for k in range(HALF):
        near_ref[k * rows : (k + 1) * rows, :] = products(band_ref, back_ref, k * rows)


def window_gradient(band, back, rows):
    hidden = back.shape[2]
    other, far = pl.pallas_call(
        leaving_kernel,
        out_shape=(
            jax.ShapeDtypeStruct((HALF * rows, hidden), BF16),
            jax.ShapeDtypeStruct((rows, hidden), BF16),
        ),
        compiler_params=params(),
        cost_estimate=pl.CostEstimate(flops=1 << 29, transcendentals=0, bytes_accessed=5 << 20),
        name="leaving_gradient",
    )(band, back)
    near = pl.pallas_call(
        staying_kernel,
        out_shape=jax.ShapeDtypeStruct((HALF * rows, hidden), F32),
        compiler_params=params(),
        cost_estimate=pl.CostEstimate(flops=1 << 29, transcendentals=0, bytes_accessed=5 << 20),
        name="staying_gradient",
    )(band, back)
    return near, other, far


def on_device(features, block_cols, block_vals, weight, cotangent):
    reps = lax.axis_size("rep")
    rep = lax.axis_index("rep")
    core = lax.axis_index("core")
    group = lax.axis_index(ROW)
    group_rows, hidden = features.shape
    side = block_vals.shape[-1]
    blocks_group = group_rows // side
    per_rep = blocks_group // reps
    rows = per_rep * side
    columns = SECTIONS * per_rep

    own = lax.dynamic_slice_in_dim(features, rep * rows, rows, 0)
    before = chip_shift(own, 1)
    after = chip_shift(own, -1)
    far = far_shift(own)

    vals = block_vals[:, 0]
    column_ids = block_cols[:, 0, :]
    offset = column_ids // blocks_group - group + HALF
    piece = jnp.zeros_like(column_ids)
    for d in range(SECTIONS):
        piece = jnp.where(offset == d, jnp.where(core == 0, PIECE_OF[0][d], PIECE_OF[1][d]), piece)
    slots = (piece * per_rep + column_ids % blocks_group - rep * per_rep).reshape(-1)
    band = transposed_band(slots, vals, columns)

    near = jnp.concatenate([own, before, after], axis=0)
    other = core_swap(near)
    partial_rows = partial_aggregate(slots, vals, near, other, far, reps)
    parts = lax.all_to_all(partial_rows, "rep", 0, 0, tiled=False)

    output_rows, send = dense_layer(parts, weight, cotangent)
    back = lax.all_to_all(send, "rep", 0, 0, tiled=False)

    plane = X_CHIPS * CORES
    quarter = jnp.sum(back[:, rows:, :].astype(F32), axis=0)
    terms = lax.all_to_all(quarter.reshape(plane, -1, hidden), ("x", "core"), 0, 0, tiled=False)
    line = lax.axis_size("z")
    term = jnp.sum(terms, axis=0).astype(BF16)
    terms = lax.all_to_all(jnp.broadcast_to(term, (line,) + term.shape), "z", 0, 0, tiled=False)
    node_count = group_rows * lax.axis_size(ROW)
    term = jnp.sum(terms.astype(F32), axis=0) * node_count ** (-0.5)
    everyone = plane * reps
    grad_weight = lax.all_to_all(jnp.broadcast_to(term, (everyone,) + term.shape), PLANE, 0, 0, tiled=False)
    grad_weight = grad_weight.reshape(hidden, hidden)

    near_grad, other_grad, far_grad = window_gradient(band, back, rows)
    swapped = core_swap(other_grad)
    from_far = far_shift(far_grad)
    near_grad = near_grad + swapped.astype(F32)
    from_after = chip_shift(near_grad[rows : 2 * rows].astype(BF16), -1)
    from_before = chip_shift(near_grad[2 * rows :].astype(BF16), 1)
    grad_features = (
        near_grad[:rows] + from_after.astype(F32) + from_before.astype(F32) + from_far.astype(F32)
    )
    return output_rows, grad_weight, grad_features


def solution(mesh):
    devices = mesh.devices
    split = Mesh(devices.reshape(X_CHIPS, -1, CORES, devices.shape[1]), ROW + ("rep",))
    everywhere = ROW + ("rep",)
    return jax.shard_map(
        on_device,
        mesh=split,
        in_specs=(
            P(ROW, None),
            P(ROW, "rep", None),
            P(ROW, "rep", None, None, None),
            P(),
            P(everywhere, None),
        ),
        out_specs=(P(everywhere, None), P(), P(everywhere, None)),
        check_vma=False,
    )
```

time: 593 us -> 122 us (0.21)
  waiting for transfers between devices: 480 us -> 19.5 us
  starting transfers between devices: 39.3 us -> 64.5 us
  matrix products: 24.5 us -> 0 us
  between operations: 14.3 us -> 0.91 us
  Pallas kernels: 0 us -> 9.65 us
    psum x1 -> x0, waiting for transfers between devices: 440 us -> none  [on_device(): grad_weight = lax.psum(local_grad, ('row', 'rep')) * node_count ** (-0.5)]
    all_to_all x0 -> x4, starting transfers between devices: none -> 36.3 us  [the longest x1 12.9 us: on_device(): lax.all_to_all(jnp.broadcast_to(term, (line,) + term.shape), 'z', 0, 0, t...]
    reduce_scatter x1 -> x0, waiting for transfers between devices: 27.5 us -> none  [on_device(): lax.psum_scatter(partial_rows, 'rep', scatter_dimension=0, tiled=True)]
    dot_general x7 -> x0, matrix products: 24.5 us -> none  [the longest x1 7.18 us: on_device(): jnp.einsum('cbji,bjh->cih', upper_part, back_group, preferred_element_typ...]
    all_to_all x0 -> x4, waiting for transfers between devices: none -> 11.8 us  [the longest x1 8.01 us: on_device(): lax.all_to_all(jnp.broadcast_to(term, (everyone,) + term.shape), PLANE, 0...]
    all_gather x1 -> x0, blocking collectives: 11.2 us -> none  [on_device(): lax.all_gather(backward, 'rep', axis=0, tiled=True)]
    ppermute x12 -> x8, starting transfers between devices: 39.2 us -> 28.3 us  [the longest x4 11 us: chip_shift(): lax.ppermute(x, ROW, [(i, i + by) for i in range(devices) if 0 <= i + by...]
    pallas_call x0 -> x5, Pallas kernels: none -> 9.65 us  [the longest x1 4.1 us: transposed_band(): pl.pallas_call(transpose_kernel, grid_spec=pltpu.PrefetchScalarGridSpec(n...]
  transfers between devices with their start and end apart: 14 -> 12, of which waited for: 4 -> 6; matrix products, arithmetic and copies ran while one was open for 3% -> 4% of each run, Pallas kernels for 0% -> 4%
where the time goes in v1:
time: 122 us; the launch traced here: 121 us
  starting transfers between devices  64.5 us (53%)
  waiting for transfers between devices  19.5 us (16%)
  local copies, waits for them, and re-layouts  13.3 us (11%)
  Pallas kernels  9.65 us (8%)
  blocking collectives  9.33 us (8%)
  other arithmetic  3.93 us (3%)
    all_to_all x1, starting transfers between devices, on_device(): lax.all_to_all(jnp.broadcast_to(term, (line,) + term.shape), 'z', 0, 0, t...  12.9 us
    all_to_all x1, starting transfers between devices, on_device(): lax.all_to_all(quarter.reshape(plane, -1, hidden), ('x', 'core'), 0, 0, t...  11.9 us
    unnamed x18, local copies, waits for them, and re-layouts  11.9 us
    ppermute x4, starting transfers between devices, chip_shift(): lax.ppermute(x, ROW, [(i, i + by) for i in range(devices) if 0 <= i + by...  11 us
    all_to_all x1, blocking collectives, on_device(): parts = lax.all_to_all(partial_rows, 'rep', 0, 0, tiled=False)  9.33 us
    ppermute x2, starting transfers between devices, far_shift(): return lax.ppermute(x, ROW, pairs)  8.72 us
    ppermute x2, starting transfers between devices, core_swap(): return lax.ppermute(x, 'core', [(0, 1), (1, 0)])  8.6 us
    all_to_all x1, waiting for transfers between devices, on_device(): lax.all_to_all(jnp.broadcast_to(term, (everyone,) + term.shape), PLANE, 0...  8.01 us
  transfers between devices with their start and end apart: 12, of which 6 were waited for; matrix products, arithmetic and copies ran while one was open for 4% of the time, Pallas kernels for 4%

profile of v1, /device:TPU:1, one launch (start us, length us, event | category | flops | bytes accessed | tf_op | source)
XLA Modules:
  0.0 121.2 jit_solution(18122464723211189749)
XLA Ops:
  0.6 0.0 copy-start
  0.6 0.0 copy-start.6
  0.7 0.0 copy-start.7
  0.7 1.0 copy-done
  1.7 4.4 %collective-permute-start = (bf16[256,256]{1,0:T(8,128)(2,1)S(1)}, bf16[256,256]{1,0:T(8,128)(2,1)S(1)}, u32[]{:S(2)}, u32[]{:S(2)}) collective-permute-start(bf16[256,256]{1,0:T(8,128)(2,1)S(1)} %constant_dynamic-slice_fusion), channel_id=1, source_target_pairs={{0,8},{4,12},{8,16},{12,20},{16,24},{20,28},{24,32},{28,36},{32,40... | collective-permute-start | bytes 393224 | tf_op jit(solution)/shard_map/ppermute | solution.py:27
  6.1 1.3 %collective-permute-start.1 = (bf16[256,256]{1,0:T(8,128)(2,1)S(1)}, bf16[256,256]{1,0:T(8,128)(2,1)S(1)}, u32[]{:S(2)}, u32[]{:S(2)}) collective-permute-start(bf16[256,256]{1,0:T(8,128)(2,1)S(1)} %constant_dynamic-slice_fusion), channel_id=1, source_target_pairs={{8,0},{12,4},{16,8},{20,12},{24,16},{28,20},{32,24},{36,28},{40,32... | collective-permute-start | bytes 393224 | tf_op jit(solution)/shard_map/ppermute | solution.py:27
  7.4 0.6 collective-permute-done
  8.0 4.0 %collective-permute-done.1 = bf16[256,256]{1,0:T(8,128)(2,1)S(1)} collective-permute-done((bf16[256,256]{1,0:T(8,128)(2,1)S(1)}, bf16[256,256]{1,0:T(8,128)(2,1)S(1)}, u32[]{:S(2)}, u32[]{:S(2)}) %collective-permute-start.1) | collective-permute-done | bytes 131104 | tf_op jit(solution)/shard_map/ppermute | solution.py:27
  12.0 6.7 %collective-permute-start.2 = (bf16[768,256]{1,0:T(8,128)(2,1)S(1)}, bf16[768,256]{1,0:T(8,128)(2,1)S(1)}, u32[]{:S(2)}, u32[]{:S(2)}) collective-permute-start(bf16[768,256]{1,0:T(8,128)(2,1)S(1)} %pad_maximum_fusion.near_ref), channel_id=1, source_target_pairs={{0,4},{4,0},{1,5},{5,1},{2,6},{6,2},{3,7},{7,3},{8,12},{12,8},{9,1... | collective-permute-start | bytes 1179656 | tf_op jit(solution)/shard_map/ppermute | solution.py:41
  18.7 3.3 %collective-permute-start.3 = (bf16[256,256]{1,0:T(8,128)(2,1)S(1)}, bf16[256,256]{1,0:T(8,128)(2,1)S(1)}, u32[]{:S(2)}, u32[]{:S(2)}) collective-permute-start(bf16[256,256]{1,0:T(8,128)(2,1)S(1)} %constant_dynamic-slice_fusion), channel_id=1, source_target_pairs={{4,16},{12,24},{16,4},{20,32},{24,12},{28,40},{32,20},{36,48},{40,... | collective-permute-start | bytes 393224 | tf_op jit(solution)/shard_map/ppermute | solution.py:37
  22.0 0.5 broadcast.54
  22.6 1.3 %reduce.3 = s32[8,12]{1,0:T(8,128)S(1)} reduce(s32[8,1,12]{2,1,0:T(1,128)} %param.6, s32[]{:T(128)} %broadcast.54), dimensions={1}, to_apply=%param.6.reduce_sub_computation.3 | reduce | bytes 772 | tf_op args[1]
  23.9 0.1 squeeze.6
  24.0 3.2 %collective-permute-done.3.far_ref = bf16[256,256]{1,0:T(8,128)(2,1)S(1)} collective-permute-done((bf16[256,256]{1,0:T(8,128)(2,1)S(1)}, bf16[256,256]{1,0:T(8,128)(2,1)S(1)}, u32[]{:S(2)}, u32[]{:S(2)}) %collective-permute-start.3) | collective-permute-done | bytes 131104 | tf_op jit(solution)/shard_map/ppermute | solution.py:37
  27.2 0.0 collective-permute-done.2.other_ref
  27.2 0.0 copy-start.4
  27.2 1.9 %copy-done.4 = bf16[8,1,12,128,128]{4,3,2,1,0:T(8,128)(2,1)S(1)} copy-done((bf16[8,1,12,128,128]{4,3,2,1,0:T(8,128)(2,1)S(1)}, bf16[8,1,12,128,128]{4,3,2,1,0:T(8,128)(2,1)}, u32[]{:S(2)}) %copy-start.4) | copy-done | bytes 3145752
  29.1 3.0 %partial_aggregate.1 = bf16[4,256,256]{2,1,0:T(8,128)(2,1)S(1)} custom-call(s32[96]{0:T(128)S(1)} %fusion.4.slot_ref, bf16[8,12,128,128]{3,2,1,0:T(8,128)(2,1)S(1)} %bitcast.3, bf16[768,256]{1,0:T(8,128)(2,1)S(1)} %pad_maximum_fusion.near_ref, bf16[768,256]{1,0:T(8,128)(2,1)S(1)} %collective-permute-done.2.other_ref, ...), custom_call_target="tpu_custom_call" | custom-call | flops 1073741824 | bytes 5242880 | tf_op jit(solution)/shard_map/partial_aggregate/pallas_call | solution.py:101
  32.1 9.3 %all_to_all.25.parts_ref = bf16[4,256,256]{2,1,0:T(8,128)(2,1)S(1)} all-to-all(bf16[4,256,256]{2,1,0:T(8,128)(2,1)S(1)} %partial_aggregate.1), channel_id=1, replica_groups=mesh['x'=4,'z'=16,'core'=2,'rep'=4] {'rep'}, dimensions={0} | all-to-all | bytes 1048576 | tf_op jit(solution)/shard_map/all_to_all | solution.py:242
  41.4 0.0 copy-done.6
  41.4 0.0 copy-done.7
  41.4 1.3 %dense_layer.1 = (bf16[256,256]{1,0:T(8,128)(2,1)}, bf16[4,320,256]{2,1,0:T(8,128)(2,1)}) custom-call(bf16[4,256,256]{2,1,0:T(8,128)(2,1)S(1)} %all_to_all.25.parts_ref, bf16[256,256]{1,0:T(8,128)(2,1)S(1)} %copy-done.6, bf16[256,256]{1,0:T(8,128)(2,1)S(1)} %copy-done.7), custom_call_target="tpu_custom_call" | custom-call | flops 104857600 | bytes 2097152 | tf_op jit(solution)/shard_map/dense_layer/pallas_call | solution.py:152
  42.7 3.5 %all-to-all-start.1 = ((bf16[4,320,256]{2,1,0:T(8,128)(2,1)}), bf16[4,320,256]{2,1,0:T(8,128)(2,1)S(1)}, u32[]{:S(2)}, u32[]{:S(2)}) async-start(bf16[4,320,256]{2,1,0:T(8,128)(2,1)} %get-tuple-element.8), calls=%async_computation.1 | async-start | bytes 1310720 | tf_op jit(solution)/shard_map/all_to_all | solution.py:245
  46.2 0.0 copy-start.5
  46.2 1.9 %copy-done.5 = bf16[8,1,12,128,128]{4,3,2,1,0:T(8,128)(2,1)S(1)} copy-done((bf16[8,1,12,128,128]{4,3,2,1,0:T(8,128)(2,1)S(1)}, bf16[8,1,12,128,128]{4,3,2,1,0:T(8,128)(2,1)}, u32[]{:S(2)}) %copy-start.5) | copy-done | bytes 3145752
  48.1 4.1 %transposed_band.1.band_ref = bf16[1792,1024]{1,0:T(8,128)(2,1)S(1)} custom-call(s32[96]{0:T(128)S(1)} %fusion.4.slot_ref, bf16[8,12,128,128]{3,2,1,0:T(8,128)(2,1)S(1)} %bitcast.4), custom_call_target="tpu_custom_call" | custom-call | bytes 16777216 | tf_op jit(solution)/shard_map/transposed_band/pallas_call | solution.py:58
  52.2 0.0 copy-start.1
  52.2 1.8 %copy-done.1 = bf16[1792,1024]{1,0:T(8,128)(2,1)} copy-done((bf16[1792,1024]{1,0:T(8,128)(2,1)}, bf16[1792,1024]{1,0:T(8,128)(2,1)S(1)}, u32[]{:S(2)}) %copy-start.1) | copy-done | bytes 3670040
  54.0 0.0 all-to-all-done.1.back_ref
  54.0 0.6 convert_reduce_fusion
  54.7 11.9 %all-to-all-start.2 = ((f32[8,8,256]{2,1,0:T(8,128)}), f32[8,8,256]{2,1,0:T(8,128)S(1)}, u32[]{:S(2)}, u32[]{:S(2)}) async-start(f32[8,8,256]{2,1,0:T(8,128)} %bitcast.1), calls=%async_computation.2 | async-start | bytes 131072 | tf_op jit(solution)/shard_map/all_to_all | solution.py:249
  66.5 0.0 copy-start.2
  66.5 2.0 %copy-done.2 = bf16[1792,1024]{1,0:T(8,128)(2,1)S(1)} copy-done((bf16[1792,1024]{1,0:T(8,128)(2,1)S(1)}, bf16[1792,1024]{1,0:T(8,128)(2,1)}, u32[]{:S(2)}) %copy-start.2) | copy-done | bytes 3670040
  68.6 0.7 leaving_gradient.1
  69.3 1.9 %collective-permute-start.4 = (bf16[768,256]{1,0:T(8,128)(2,1)S(1)}, bf16[768,256]{1,0:T(8,128)(2,1)}, u32[]{:S(2)}, u32[]{:S(2)}) collective-permute-start(bf16[768,256]{1,0:T(8,128)(2,1)S(1)} %get-tuple-element.9), channel_id=1, source_target_pairs={{0,4},{4,0},{1,5},{5,1},{2,6},{6,2},{3,7},{7,3},{8,12},{12,8},{9,1... | collective-permute-start | bytes 1179656 | tf_op jit(solution)/shard_map/ppermute | solution.py:41
  71.2 0.2 all-to-all-done.2
  71.4 0.6 broadcast_in_dim.29
  72.0 12.9 %all-to-all-start.3 = ((bf16[16,8,256]{2,1,0:T(8,128)(2,1)}), bf16[16,8,256]{2,1,0:T(8,128)(2,1)S(1)}, u32[]{:S(2)}, u32[]{:S(2)}) async-start(bf16[16,8,256]{2,1,0:T(8,128)(2,1)} %broadcast_in_dim.29), calls=%async_computation.3 | async-start | bytes 131072 | tf_op jit(solution)/shard_map/all_to_all | solution.py:252
  85.0 5.4 %collective-permute-start.7 = (bf16[256,256]{1,0:T(8,128)(2,1)S(1)}, bf16[256,256]{1,0:T(8,128)(2,1)S(1)}, u32[]{:S(2)}, u32[]{:S(2)}) collective-permute-start(bf16[256,256]{1,0:T(8,128)(2,1)S(1)} %get-tuple-element.10), channel_id=1, source_target_pairs={{4,16},{12,24},{16,4},{20,32},{24,12},{28,40},{32,20},{36,48},{40,... | collective-permute-start | bytes 393224 | tf_op jit(solution)/shard_map/ppermute | solution.py:37
  90.4 0.0 copy-start.3
  90.4 2.0 %copy-done.3 = bf16[1792,1024]{1,0:T(8,128)(2,1)S(1)} copy-done((bf16[1792,1024]{1,0:T(8,128)(2,1)S(1)}, bf16[1792,1024]{1,0:T(8,128)(2,1)}, u32[]{:S(2)}) %copy-start.3) | copy-done | bytes 3670040
  92.4 0.6 staying_gradient.1
  93.0 3.6 %all-to-all-done.3 = bf16[16,8,256]{2,1,0:T(8,128)(2,1)S(1)} async-done(((bf16[16,8,256]{2,1,0:T(8,128)(2,1)}), bf16[16,8,256]{2,1,0:T(8,128)(2,1)S(1)}, u32[]{:S(2)}, u32[]{:S(2)}) %all-to-all-start.3) | async-done | bytes 65568 | tf_op jit(solution)/shard_map/all_to_all | solution.py:252
  96.6 0.0 collective-permute-done.4
  96.6 1.1 fusion.5
  97.7 1.3 %collective-permute-start.5 = (bf16[256,256]{1,0:T(8,128)(2,1)S(1)}, bf16[256,256]{1,0:T(8,128)(2,1)S(1)}, u32[]{:S(2)}, u32[]{:S(2)}) collective-permute-start(bf16[256,256]{1,0:T(8,128)(2,1)S(1)} %get-tuple-element.13), channel_id=1, source_target_pairs={{8,0},{12,4},{16,8},{20,12},{24,16},{28,20},{32,24},{36,28},{40,32... | collective-permute-start | bytes 393224 | tf_op jit(solution)/shard_map/ppermute | solution.py:27
  99.0 4.0 %collective-permute-start.6 = (bf16[256,256]{1,0:T(8,128)(2,1)S(1)}, bf16[256,256]{1,0:T(8,128)(2,1)S(1)}, u32[]{:S(2)}, u32[]{:S(2)}) collective-permute-start(bf16[256,256]{1,0:T(8,128)(2,1)S(1)} %get-tuple-element.14), channel_id=1, source_target_pairs={{0,8},{4,12},{8,16},{12,20},{16,24},{20,28},{24,32},{28,36},{32,40... | collective-permute-start | bytes 393224 | tf_op jit(solution)/shard_map/ppermute | solution.py:27
  103.0 0.7 broadcast_in_dim.30
  103.7 8.0 %all-to-all-start.4 = ((f32[32,8,256]{2,1,0:T(8,128)}), f32[32,8,256]{2,1,0:T(8,128)S(1)}, u32[]{:S(2)}, u32[]{:S(2)}) async-start(f32[32,8,256]{2,1,0:T(8,128)} %broadcast_in_dim.30), calls=%async_computation.4 | async-start | bytes 524288 | tf_op jit(solution)/shard_map/all_to_all | solution.py:256
  111.7 0.0 collective-permute-done.7
  111.7 0.0 collective-permute-done.5
  111.7 0.0 collective-permute-done.6
  111.8 0.8 fusion.1
  112.5 8.0 %all-to-all-done.4 = f32[32,8,256]{2,1,0:T(8,128)S(1)} async-done(((f32[32,8,256]{2,1,0:T(8,128)}), f32[32,8,256]{2,1,0:T(8,128)S(1)}, u32[]{:S(2)}, u32[]{:S(2)}) %all-to-all-start.4) | async-done | bytes 262176 | tf_op jit(solution)/shard_map/all_to_all | solution.py:256
  120.5 0.7 copy.9
  (7 shorter events, 0.1 us)
Async XLA Ops:
  0.6 1.0 copy-start
  0.6 40.8 %copy-start.6 = (bf16[256,256]{1,0:T(8,128)(2,1)S(1)}, bf16[256,256]{1,0:T(8,128)(2,1)}, u32[]{:S(2)}) copy-start(bf16[256,256]{1,0:T(8,128)(2,1)} %weight_ref.1) | copy-start | bytes 393220
  0.7 40.8 %copy-start.7 = (bf16[256,256]{1,0:T(8,128)(2,1)S(1)}, bf16[256,256]{1,0:T(8,128)(2,1)}, u32[]{:S(2)}) copy-start(bf16[256,256]{1,0:T(8,128)(2,1)} %cotangent_ref.1) | copy-start | bytes 393220
  1.7 6.3 %collective-permute-start = (bf16[256,256]{1,0:T(8,128)(2,1)S(1)}, bf16[256,256]{1,0:T(8,128)(2,1)S(1)}, u32[]{:S(2)}, u32[]{:S(2)}) collective-permute-start(bf16[256,256]{1,0:T(8,128)(2,1)S(1)} %constant_dynamic-slice_fusion), channel_id=1, source_target_pairs={{0,8},{4,12},{8,16},{12,20},{16,24},{20,28},{24,32},{28,36},{32,40... | collective-permute-start | bytes 393224 | tf_op jit(solution)/shard_map/ppermute | solution.py:27
  6.1 5.9 %collective-permute-start.1 = (bf16[256,256]{1,0:T(8,128)(2,1)S(1)}, bf16[256,256]{1,0:T(8,128)(2,1)S(1)}, u32[]{:S(2)}, u32[]{:S(2)}) collective-permute-start(bf16[256,256]{1,0:T(8,128)(2,1)S(1)} %constant_dynamic-slice_fusion), channel_id=1, source_target_pairs={{8,0},{12,4},{16,8},{20,12},{24,16},{28,20},{32,24},{36,28},{40,32... | collective-permute-start | bytes 393224 | tf_op jit(solution)/shard_map/ppermute | solution.py:27
  12.0 15.2 %collective-permute-start.2 = (bf16[768,256]{1,0:T(8,128)(2,1)S(1)}, bf16[768,256]{1,0:T(8,128)(2,1)S(1)}, u32[]{:S(2)}, u32[]{:S(2)}) collective-permute-start(bf16[768,256]{1,0:T(8,128)(2,1)S(1)} %pad_maximum_fusion.near_ref), channel_id=1, source_target_pairs={{0,4},{4,0},{1,5},{5,1},{2,6},{6,2},{3,7},{7,3},{8,12},{12,8},{9,1... | collective-permute-start | bytes 1179656 | tf_op jit(solution)/shard_map/ppermute | solution.py:41
  18.7 8.5 %collective-permute-start.3 = (bf16[256,256]{1,0:T(8,128)(2,1)S(1)}, bf16[256,256]{1,0:T(8,128)(2,1)S(1)}, u32[]{:S(2)}, u32[]{:S(2)}) collective-permute-start(bf16[256,256]{1,0:T(8,128)(2,1)S(1)} %constant_dynamic-slice_fusion), channel_id=1, source_target_pairs={{4,16},{12,24},{16,4},{20,32},{24,12},{28,40},{32,20},{36,48},{40,... | collective-permute-start | bytes 393224 | tf_op jit(solution)/shard_map/ppermute | solution.py:37
  27.2 1.9 %copy-start.4 = (bf16[8,1,12,128,128]{4,3,2,1,0:T(8,128)(2,1)S(1)}, bf16[8,1,12,128,128]{4,3,2,1,0:T(8,128)(2,1)}, u32[]{:S(2)}) copy-start(bf16[8,1,12,128,128]{4,3,2,1,0:T(8,128)(2,1)} %param.7) | copy-start | bytes 9437188
  42.7 11.3 %all-to-all-start.1 = ((bf16[4,320,256]{2,1,0:T(8,128)(2,1)}), bf16[4,320,256]{2,1,0:T(8,128)(2,1)S(1)}, u32[]{:S(2)}, u32[]{:S(2)}) async-start(bf16[4,320,256]{2,1,0:T(8,128)(2,1)} %get-tuple-element.8), calls=%async_computation.1 | async-start | bytes 1310720 | tf_op jit(solution)/shard_map/all_to_all | solution.py:245
  46.2 1.9 %copy-start.5 = (bf16[8,1,12,128,128]{4,3,2,1,0:T(8,128)(2,1)S(1)}, bf16[8,1,12,128,128]{4,3,2,1,0:T(8,128)(2,1)}, u32[]{:S(2)}) copy-start(bf16[8,1,12,128,128]{4,3,2,1,0:T(8,128)(2,1)} %param.7) | copy-start | bytes 9437188
  52.2 1.8 %copy-start.1 = (bf16[1792,1024]{1,0:T(8,128)(2,1)}, bf16[1792,1024]{1,0:T(8,128)(2,1)S(1)}, u32[]{:S(2)}) copy-start(bf16[1792,1024]{1,0:T(8,128)(2,1)S(1)} %transposed_band.1.band_ref) | copy-start | bytes 11010052
  54.7 16.7 %all-to-all-start.2 = ((f32[8,8,256]{2,1,0:T(8,128)}), f32[8,8,256]{2,1,0:T(8,128)S(1)}, u32[]{:S(2)}, u32[]{:S(2)}) async-start(f32[8,8,256]{2,1,0:T(8,128)} %bitcast.1), calls=%async_computation.2 | async-start | bytes 131072 | tf_op jit(solution)/shard_map/all_to_all | solution.py:249
  66.5 2.0 %copy-start.2 = (bf16[1792,1024]{1,0:T(8,128)(2,1)S(1)}, bf16[1792,1024]{1,0:T(8,128)(2,1)}, u32[]{:S(2)}) copy-start(bf16[1792,1024]{1,0:T(8,128)(2,1)} %copy-done.1) | copy-start | bytes 11010052
  69.3 27.3 %collective-permute-start.4 = (bf16[768,256]{1,0:T(8,128)(2,1)S(1)}, bf16[768,256]{1,0:T(8,128)(2,1)}, u32[]{:S(2)}, u32[]{:S(2)}) collective-permute-start(bf16[768,256]{1,0:T(8,128)(2,1)S(1)} %get-tuple-element.9), channel_id=1, source_target_pairs={{0,4},{4,0},{1,5},{5,1},{2,6},{6,2},{3,7},{7,3},{8,12},{12,8},{9,1... | collective-permute-start | bytes 1179656 | tf_op jit(solution)/shard_map/ppermute | solution.py:41
  72.0 24.5 %all-to-all-start.3 = ((bf16[16,8,256]{2,1,0:T(8,128)(2,1)}), bf16[16,8,256]{2,1,0:T(8,128)(2,1)S(1)}, u32[]{:S(2)}, u32[]{:S(2)}) async-start(bf16[16,8,256]{2,1,0:T(8,128)(2,1)} %broadcast_in_dim.29), calls=%async_computation.3 | async-start | bytes 131072 | tf_op jit(solution)/shard_map/all_to_all | solution.py:252
  85.0 26.8 %collective-permute-start.7 = (bf16[256,256]{1,0:T(8,128)(2,1)S(1)}, bf16[256,256]{1,0:T(8,128)(2,1)S(1)}, u32[]{:S(2)}, u32[]{:S(2)}) collective-permute-start(bf16[256,256]{1,0:T(8,128)(2,1)S(1)} %get-tuple-element.10), channel_id=1, source_target_pairs={{4,16},{12,24},{16,4},{20,32},{24,12},{28,40},{32,20},{36,48},{40,... | collective-permute-start | bytes 393224 | tf_op jit(solution)/shard_map/ppermute | solution.py:37
  90.4 2.0 %copy-start.3 = (bf16[1792,1024]{1,0:T(8,128)(2,1)S(1)}, bf16[1792,1024]{1,0:T(8,128)(2,1)}, u32[]{:S(2)}) copy-start(bf16[1792,1024]{1,0:T(8,128)(2,1)} %copy-done.1) | copy-start | bytes 11010052
  97.7 14.0 %collective-permute-start.5 = (bf16[256,256]{1,0:T(8,128)(2,1)S(1)}, bf16[256,256]{1,0:T(8,128)(2,1)S(1)}, u32[]{:S(2)}, u32[]{:S(2)}) collective-permute-start(bf16[256,256]{1,0:T(8,128)(2,1)S(1)} %get-tuple-element.13), channel_id=1, source_target_pairs={{8,0},{12,4},{16,8},{20,12},{24,16},{28,20},{32,24},{36,28},{40,32... | collective-permute-start | bytes 393224 | tf_op jit(solution)/shard_map/ppermute | solution.py:27
  99.0 12.8 %collective-permute-start.6 = (bf16[256,256]{1,0:T(8,128)(2,1)S(1)}, bf16[256,256]{1,0:T(8,128)(2,1)S(1)}, u32[]{:S(2)}, u32[]{:S(2)}) collective-permute-start(bf16[256,256]{1,0:T(8,128)(2,1)S(1)} %get-tuple-element.14), channel_id=1, source_target_pairs={{0,8},{4,12},{8,16},{12,20},{16,24},{20,28},{24,32},{28,36},{32,40... | collective-permute-start | bytes 393224 | tf_op jit(solution)/shard_map/ppermute | solution.py:27
  103.7 16.8 %all-to-all-start.4 = ((f32[32,8,256]{2,1,0:T(8,128)}), f32[32,8,256]{2,1,0:T(8,128)S(1)}, u32[]{:S(2)}, u32[]{:S(2)}) async-start(f32[32,8,256]{2,1,0:T(8,128)} %broadcast_in_dim.30), calls=%async_computation.4 | async-start | bytes 524288 | tf_op jit(solution)/shard_map/all_to_all | solution.py:256

commit v2 on v1

v2 whole, which is shorter than its diff:
```python
import jax
import jax.numpy as jnp
from jax import lax
from jax.experimental import pallas as pl
from jax.experimental.pallas import tpu as pltpu
from jax.sharding import Mesh
from jax.sharding import PartitionSpec as P

HALF = 3
SECTIONS = 2 * HALF + 1
CORES = 2
X_CHIPS = 4
ROW = ("x", "z", "core")
PLANE = ("x", "core", "rep")
BF16 = jnp.bfloat16
F32 = jnp.float32
PIECE_OF = ((6, 1, 4, 0, 3, 2, 5), (4, 1, 3, 0, 5, 2, 6))
PIECE_CODE = tuple(sum(p << (4 * d) for d, p in enumerate(row)) for row in PIECE_OF)


def cost(us):
    return pl.CostEstimate(flops=0, transcendentals=0, bytes_accessed=int(us * 3.6e6))


def params(mib):
    return pltpu.CompilerParams(vmem_limit_bytes=mib << 20)


def chip_shift(x, by):
    devices = lax.axis_size(ROW)
    by = by * CORES
    return lax.ppermute(x, ROW, [(i, i + by) for i in range(devices) if 0 <= i + by < devices])


def far_shift(x):
    devices = lax.axis_size(ROW)
    pairs = []
    for i in range(devices):
        to = i + HALF if i % CORES else i - HALF
        if 0 <= to < devices:
            pairs.append((i, to))
    return lax.ppermute(x, ROW, pairs)


def core_swap(x):
    return lax.ppermute(x, "core", [(0, 1), (1, 0)])


def rep_shift(x, by):
    devices = lax.axis_size("rep")
    return lax.ppermute(x, "rep", [(i, (i - by) % devices) for i in range(devices)])


def to_all(x, axes):
    return lax.all_to_all(x, axes, 0, 0, tiled=False)


def band_kernel(blocks_group, per_rep, cols_ref, vals_ref, out_ref, sum_ref):
    block = pl.program_id(0)
    slots, side = vals_ref.shape[1:3]
    group = lax.axis_index(ROW)
    first = lax.axis_index("rep") * per_rep
    code = jnp.where(lax.axis_index("core") == 0, PIECE_CODE[0], PIECE_CODE[1])
    sum_ref[...] = jnp.zeros_like(sum_ref)
    for s in range(slots):
        column = cols_ref[block, 0, s]
        source = lax.div(column, blocks_group)
        piece = lax.shift_right_logical(code, 4 * (source - group + HALF)) & 15
        at = piece * per_rep + column - source * blocks_group - first
        sum_ref[at] += vals_ref[0, s].astype(F32)
    for c in range(sum_ref.shape[0]):
        out_ref[:, c * side : (c + 1) * side] = sum_ref[c].astype(BF16)


def dense_band(cols, vals, blocks_group, per_rep):
    blocks, count, side, _ = vals.shape
    columns = SECTIONS * per_rep

    def kernel(*refs):
        band_kernel(blocks_group, per_rep, *refs)

    return pl.pallas_call(
        kernel,
        grid_spec=pltpu.PrefetchScalarGridSpec(
            num_scalar_prefetch=1,
            grid=(blocks,),
            in_specs=[pl.BlockSpec((1, count, side, side), lambda b, s: (b, 0, 0, 0))],
            out_specs=pl.BlockSpec((side, columns * side), lambda b, s: (b, 0)),
            scratch_shapes=[pltpu.VMEM((columns, side, side), F32)],
        ),
        out_shape=pltpu.HBM((blocks * side, columns * side), BF16),
        compiler_params=params(8),
        cost_estimate=cost(3),
        name="dense_band",
    )(cols, pltpu.with_memory_space_constraint(vals, pltpu.HBM))


def transpose_kernel(band_ref, out_ref):
    out_ref[...] = band_ref[...].T


def transposed(band, side):
    rows, columns = band.shape
    return pl.pallas_call(
        transpose_kernel,
        grid=(rows // side,),
        in_specs=[pl.BlockSpec((side, columns), lambda b: (b, 0))],
        out_specs=pl.BlockSpec((columns, side), lambda b: (0, b)),
        out_shape=pltpu.HBM((columns, rows), BF16),
        compiler_params=params(8),
        cost_estimate=cost(3),
        name="transposed_band",
    )(pltpu.with_memory_space_constraint(band, pltpu.HBM))


def aggregate_kernel(band_ref, near_ref, other_ref, far_ref, out_ref):
    rows, hidden = out_ref.shape[1:]
    total = jnp.zeros((rows, hidden), F32)
    at = 0
    for ref in (near_ref, other_ref, far_ref):
        total = total + jnp.dot(
            band_ref[:, at : at + ref.shape[0]], ref[...], preferred_element_type=F32
        )
        at += ref.shape[0]
    out_ref[0] = total.astype(BF16)


def partial_aggregate(band, near, other, far, reps):
    rows, hidden = band.shape[0] // reps, near.shape[1]

    def whole(x):
        return pl.BlockSpec(x.shape, lambda q: (0, 0))

    return pl.pallas_call(
        aggregate_kernel,
        grid=(reps,),
        in_specs=[pl.BlockSpec((rows, band.shape[1]), lambda q: (q, 0)), whole(near), whole(other), whole(far)],
        out_specs=pl.BlockSpec((1, rows, hidden), lambda q: (q, 0, 0)),
        out_shape=jax.ShapeDtypeStruct((reps, rows, hidden), BF16),
        compiler_params=params(12),
        cost_estimate=cost(1.5),
        name="partial_aggregate",
    )(pltpu.with_memory_space_constraint(band, pltpu.HBM), near, other, far)


def dense_kernel(parts_ref, weight_ref, cotangent_ref, out_ref, back_ref, local_ref):
    reps, rows, hidden = parts_ref.shape
    summed = parts_ref[0].astype(F32)
    for q in range(1, reps):
        summed = summed + parts_ref[q].astype(F32)
    aggregate = summed.astype(BF16)
    preact = jnp.dot(aggregate, weight_ref[...], preferred_element_type=F32)
    sigmoid_pre = 1.0 / (1.0 + jnp.exp(-preact))
    grad_pre = (
        cotangent_ref[...].astype(F32) * sigmoid_pre * (1.0 + preact * (1.0 - sigmoid_pre))
    ).astype(BF16)
    backward = lax.dot_general(
        grad_pre, weight_ref[...], (((1,), (1,)), ((), ())), preferred_element_type=F32
    ).astype(BF16)
    back_ref[...] = backward
    local_ref[...] = lax.dot_general(
        aggregate, grad_pre, (((0,), (0,)), ((), ())), preferred_element_type=F32
    )
    out_ref[...] = (preact * sigmoid_pre).astype(BF16)


def dense_layer(parts, weight, cotangent):
    reps, rows, hidden = parts.shape
    return pl.pallas_call(
        dense_kernel,
        out_shape=(
            jax.ShapeDtypeStruct((rows, hidden), BF16),
            jax.ShapeDtypeStruct((rows, hidden), BF16),
            jax.ShapeDtypeStruct((hidden, hidden), F32),
        ),
        compiler_params=params(8),
        cost_estimate=cost(1.3),
        name="dense_layer",
    )(parts, weight, cotangent)


def gradient_kernel(reps, band_ref, *refs):
    near_ref, other_ref, far_ref = refs[reps:]
    rows, hidden = far_ref.shape
    piece = pl.program_id(0)
    rep = lax.axis_index("rep")
    total = jnp.zeros((rows, hidden), F32)
    for k in range(reps):
        at = pl.multiple_of(lax.rem(rep + k, reps) * rows, rows)
        total = total + jnp.dot(
            band_ref[:, pl.ds(at, rows)], refs[k][...], preferred_element_type=F32
        )

    @pl.when(piece < HALF)
    def _():
        near_ref[pl.ds(pl.multiple_of(piece * rows, rows), rows), :] = total

    @pl.when(jnp.logical_and(piece >= HALF, piece < 2 * HALF))
    def _():
        at = pl.multiple_of((piece - HALF) * rows, rows)
        other_ref[pl.ds(at, rows), :] = total.astype(BF16)

    @pl.when(piece == 2 * HALF)
    def _():
        far_ref[...] = total.astype(BF16)


def window_gradient(band, back):
    reps = len(back)
    rows, hidden = back[0].shape

    def kernel(*refs):
        gradient_kernel(reps, *refs)

    return pl.pallas_call(
        kernel,
        grid=(SECTIONS,),
        in_specs=[pl.BlockSpec((rows, reps * rows), lambda p: (p, 0))]
        + [pl.BlockSpec((rows, hidden), lambda p: (0, 0))] * reps,
        out_specs=[
            pl.BlockSpec((HALF * rows, hidden), lambda p: (0, 0)),
            pl.BlockSpec((HALF * rows, hidden), lambda p: (0, 0)),
            pl.BlockSpec((rows, hidden), lambda p: (0, 0)),
        ],
        out_shape=(
            jax.ShapeDtypeStruct((HALF * rows, hidden), F32),
            jax.ShapeDtypeStruct((HALF * rows, hidden), BF16),
            jax.ShapeDtypeStruct((rows, hidden), BF16),
        ),
        compiler_params=params(16),
        cost_estimate=cost(1.5),
        name="window_gradient",
    )(pltpu.with_memory_space_constraint(band, pltpu.HBM), *back)


def chip_sum_kernel(near_ref, swapped_ref, own_ref, before_ref, after_ref):
    rows = own_ref.shape[0]
    for k, ref in enumerate((own_ref, before_ref, after_ref)):
        at = slice(k * rows, (k + 1) * rows)
        ref[...] = (near_ref[at, :] + swapped_ref[at, :].astype(F32)).astype(ref.dtype)


def chip_sum(near, swapped):
    rows, hidden = near.shape[0] // HALF, near.shape[1]
    return pl.pallas_call(
        chip_sum_kernel,
        out_shape=tuple(jax.ShapeDtypeStruct((rows, hidden), t) for t in (F32, BF16, BF16)),
        compiler_params=params(8),
        cost_estimate=cost(0.5),
        name="chip_sum",
    )(near, swapped)


def spread_kernel(scale, terms_ref, out_ref):
    total = terms_ref[0].astype(F32)
    for k in range(1, terms_ref.shape[0]):
        total = total + terms_ref[k].astype(F32)
    if scale is not None:
        total = total * scale
    total = total.astype(out_ref.dtype)
    for k in range(out_ref.shape[0]):
        out_ref[k] = total


def sum_and_spread(terms, copies, dtype, scale=None):
    def kernel(*refs):
        spread_kernel(scale, *refs)

    return pl.pallas_call(
        kernel,
        out_shape=jax.ShapeDtypeStruct((copies,) + terms.shape[1:], dtype),
        compiler_params=params(8),
        cost_estimate=cost(0.4),
        name="sum_and_spread",
    )(terms)


def on_device(features, block_cols, block_vals, weight, cotangent):
    reps = lax.axis_size("rep")
    rep = lax.axis_index("rep")
    group_rows, hidden = features.shape
    side = block_vals.shape[-1]
    blocks_group = group_rows // side
    per_rep = blocks_group // reps
    rows = per_rep * side

    own = lax.dynamic_slice_in_dim(features, rep * rows, rows, 0)
    before = chip_shift(own, 1)
    after = chip_shift(own, -1)
    far = far_shift(own)
    band = dense_band(block_cols, block_vals[:, 0], blocks_group, per_rep)
    before, after, far, band = lax.optimization_barrier((before, after, far, band))

    near = jnp.concatenate([own, before, after], axis=0)
    other = core_swap(near)
    partial_rows = partial_aggregate(band, near, other, far, reps)
    partial_rows, band = lax.optimization_barrier((partial_rows, band))
    parts = to_all(partial_rows, "rep")
    turned = transposed(band, side)
    parts, turned = lax.optimization_barrier((parts, turned))

    output_rows, backward, local = dense_layer(parts, weight, cotangent)
    back = [backward] + [rep_shift(backward, k) for k in range(1, reps)]

    line = lax.axis_size("z")
    plane = lax.axis_size(PLANE)
    node_count = group_rows * lax.axis_size(ROW)
    terms = to_all(local.reshape(plane, -1, hidden), PLANE)

    spread = sum_and_spread(terms, line, BF16)
    terms = to_all(spread, "z")
    turned, _ = lax.optimization_barrier((turned, spread))
    near_grad, other_grad, far_grad = window_gradient(turned, back)
    swapped = core_swap(other_grad)
    from_far = far_shift(far_grad)
    own_grad, before_grad, after_grad = chip_sum(near_grad, swapped)
    terms, _, _ = lax.optimization_barrier((terms, before_grad, after_grad))
    from_after = chip_shift(before_grad, -1)
    from_before = chip_shift(after_grad, 1)
    terms = to_all(sum_and_spread(terms, plane, F32, node_count ** (-0.5)), PLANE)
    grad_weight = terms.reshape(hidden, hidden)
    grad_features = own_grad + from_after.astype(F32) + from_before.astype(F32) + from_far.astype(F32)
    return output_rows, grad_weight, grad_features


def solution(mesh):
    devices = mesh.devices
    split = Mesh(devices.reshape(X_CHIPS, -1, CORES, devices.shape[1]), ROW + ("rep",))
    everywhere = ROW + ("rep",)
    return jax.shard_map(
        on_device,
        mesh=split,
        in_specs=(
            P(ROW, None),
            P(ROW, "rep", None),
            P(ROW, "rep", None, None, None),
            P(),
            P(everywhere, None),
        ),
        out_specs=(P(everywhere, None), P(), P(everywhere, None)),
        check_vma=False,
    )
```

time: 122 us -> 119 us (0.975)
  Pallas kernels: 9.65 us -> 27.3 us
  local copies, waits for them, and re-layouts: 13.3 us -> 2.44 us
  blocking collectives: 9.33 us -> 0 us
  starting transfers between devices: 64.5 us -> 70.7 us
  waiting for transfers between devices: 19.5 us -> 15.6 us
  other arithmetic: 3.93 us -> 0.79 us
    pallas_call x4 -> x7, Pallas kernels: 8.38 us -> 26.1 us  [the longest x1 7.54 us: dense_band(): pl.pallas_call(kernel, grid_spec=pltpu.PrefetchScalarGridSpec(num_scalar_...]
    ppermute x0 -> x3, starting transfers between devices: none -> 10.7 us  [rep_shift(): lax.ppermute(x, 'rep', [(i, (i - by) % devices) for i in range(devices)])]
    unnamed x18 -> x9, local copies, waits for them, and re-layouts: 11.9 us -> 2.43 us
    all_to_all x1 -> x0, blocking collectives: 9.33 us -> none  [on_device(): parts = lax.all_to_all(partial_rows, 'rep', 0, 0, tiled=False)]
    all_to_all x4, starting transfers between devices: 36.3 us -> 31.4 us  [to_all(): return lax.all_to_all(x, axes, 0, 0, tiled=False)]
    ppermute x4, waiting for transfers between devices: 4.6 us -> 0.01 us  [chip_shift(): lax.ppermute(x, ROW, [(i, i + by) for i in range(devices) if 0 <= i + by...]
    ppermute x2, waiting for transfers between devices: 3.18 us -> 0.01 us  [far_shift(): return lax.ppermute(x, ROW, pairs)]
    ppermute x0 -> x3, waiting for transfers between devices: none -> 2.53 us  [rep_shift(): lax.ppermute(x, 'rep', [(i, (i - by) % devices) for i in range(devices)])]
  transfers between devices with their start and end apart: 12 -> 15, of which waited for: 6 -> 5; matrix products, arithmetic and copies ran while one was open for 4% -> 1% of each run, Pallas kernels for 4% -> 14%
where the time goes in v2:
time: 119 us; the launch traced here: 118 us
  starting transfers between devices  70.7 us (59%)
  Pallas kernels  27.3 us (23%)
  waiting for transfers between devices  15.6 us (13%)
  local copies, waits for them, and re-layouts  2.44 us (2%)
    all_to_all x4, starting transfers between devices, to_all(): return lax.all_to_all(x, axes, 0, 0, tiled=False)  31.4 us
    all_to_all x4, waiting for transfers between devices, to_all(): return lax.all_to_all(x, axes, 0, 0, tiled=False)  11.8 us
    ppermute x2, starting transfers between devices, far_shift(): return lax.ppermute(x, ROW, pairs)  10.9 us
    ppermute x4, starting transfers between devices, chip_shift(): lax.ppermute(x, ROW, [(i, i + by) for i in range(devices) if 0 <= i + by...  10.8 us
    ppermute x3, starting transfers between devices, rep_shift(): lax.ppermute(x, 'rep', [(i, (i - by) % devices) for i in range(devices)])  10.7 us
    pallas_call x1, Pallas kernels, dense_band(): pl.pallas_call(kernel, grid_spec=pltpu.PrefetchScalarGridSpec(num_scalar_...  7.54 us
    pallas_call x1, Pallas kernels, transposed(): pl.pallas_call(transpose_kernel, grid=(rows // side,), in_specs=[pl.Block...  7.05 us
    ppermute x2, starting transfers between devices, core_swap(): return lax.ppermute(x, 'core', [(0, 1), (1, 0)])  6.95 us
  transfers between devices with their start and end apart: 15, of which 5 were waited for; matrix products, arithmetic and copies ran while one was open for 1% of the time, Pallas kernels for 14%

profile of v2, /device:TPU:1, one launch (start us, length us, event | category | flops | bytes accessed | tf_op | source)
XLA Modules:
  0.0 117.7 jit_solution(9310514292779872148)
XLA Ops:
  0.6 0.0 copy-start
  0.6 1.0 copy-done
  1.7 6.3 %collective-permute-start.2 = (bf16[256,256]{1,0:T(8,128)(2,1)S(1)}, bf16[256,256]{1,0:T(8,128)(2,1)S(1)}, u32[]{:S(2)}, u32[]{:S(2)}) collective-permute-start(bf16[256,256]{1,0:T(8,128)(2,1)S(1)} %constant_dynamic-slice_fusion), channel_id=1, source_target_pairs={{4,16},{12,24},{16,4},{20,32},{24,12},{28,40},{32,20},{36,48},{40,... | collective-permute-start | bytes 393224 | tf_op jit(solution)/shard_map/ppermute | solution.py:42
  8.0 1.3 %collective-permute-start.1 = (bf16[256,256]{1,0:T(8,128)(2,1)S(1)}, bf16[256,256]{1,0:T(8,128)(2,1)S(1)}, u32[]{:S(2)}, u32[]{:S(2)}) collective-permute-start(bf16[256,256]{1,0:T(8,128)(2,1)S(1)} %constant_dynamic-slice_fusion), channel_id=1, source_target_pairs={{8,0},{12,4},{16,8},{20,12},{24,16},{28,20},{32,24},{36,28},{40,32... | collective-permute-start | bytes 393224 | tf_op jit(solution)/shard_map/ppermute | solution.py:32
  9.3 4.2 %collective-permute-start = (bf16[256,256]{1,0:T(8,128)(2,1)S(1)}, bf16[256,256]{1,0:T(8,128)(2,1)S(1)}, u32[]{:S(2)}, u32[]{:S(2)}) collective-permute-start(bf16[256,256]{1,0:T(8,128)(2,1)S(1)} %constant_dynamic-slice_fusion), channel_id=1, source_target_pairs={{0,8},{4,12},{8,16},{12,20},{16,24},{20,28},{24,32},{28,36},{32,40... | collective-permute-start | bytes 393224 | tf_op jit(solution)/shard_map/ppermute | solution.py:32
  13.5 0.0 copy-start.3
  13.5 0.7 copy-done.3
  14.2 7.5 %dense_band.1.band_ref = bf16[1024,1792]{1,0:T(8,128)(2,1)} custom-call(s32[8,1,12]{2,1,0:T(1,128)S(1)} %copy-done.3, bf16[8,12,128,128]{3,2,1,0:T(8,128)(2,1)} %bitcast.3), custom_call_target="tpu_custom_call" | custom-call | bytes 10800000 | tf_op jit(solution)/shard_map/dense_band/pallas_call | solution.py:82
  21.7 0.0 collective-permute-done.2.far_ref
  21.7 0.0 collective-permute-done.1
  21.7 0.0 collective-permute-done
  21.8 3.5 %collective-permute-start.3 = (bf16[768,256]{1,0:T(8,128)(2,1)S(1)}, bf16[768,256]{1,0:T(8,128)(2,1)S(1)}, u32[]{:S(2)}, u32[]{:S(2)}) collective-permute-start(bf16[768,256]{1,0:T(8,128)(2,1)S(1)} %pad_maximum_fusion.near_ref), channel_id=1, source_target_pairs={{0,4},{4,0},{1,5},{5,1},{2,6},{6,2},{3,7},{7,3},{8,12},{12,8},{9,1... | collective-permute-start | bytes 1179656 | tf_op jit(solution)/shard_map/ppermute | solution.py:46
  25.3 1.3 %collective-permute-done.3.other_ref = bf16[768,256]{1,0:T(8,128)(2,1)S(1)} collective-permute-done((bf16[768,256]{1,0:T(8,128)(2,1)S(1)}, bf16[768,256]{1,0:T(8,128)(2,1)S(1)}, u32[]{:S(2)}, u32[]{:S(2)}) %collective-permute-start.3) | collective-permute-done | bytes 393248 | tf_op jit(solution)/shard_map/ppermute | solution.py:46
  26.6 4.5 %partial_aggregate.1 = bf16[4,256,256]{2,1,0:T(8,128)(2,1)} custom-call(bf16[1024,1792]{1,0:T(8,128)(2,1)} %dense_band.1.band_ref, bf16[768,256]{1,0:T(8,128)(2,1)S(1)} %pad_maximum_fusion.near_ref, bf16[768,256]{1,0:T(8,128)(2,1)S(1)} %collective-permute-done.3.other_ref, bf16[256,256]{1,0:T(8,128)(2,1)S(1)} %collective-permute-done.2.far_ref), custom_call_target="tpu_custom_call" | custom-call | bytes 5400000 | tf_op jit(solution)/shard_map/partial_aggregate/pallas_call | solution.py:134
  31.2 3.5 %all-to-all-start = ((bf16[4,256,256]{2,1,0:T(8,128)(2,1)}), bf16[4,256,256]{2,1,0:T(8,128)(2,1)S(1)}, u32[]{:S(2)}, u32[]{:S(2)}) async-start(bf16[4,256,256]{2,1,0:T(8,128)(2,1)} %partial_aggregate.1), calls=%async_computation | async-start | bytes 1048576 | tf_op jit(solution)/shard_map/all_to_all | solution.py:55
  34.6 0.0 copy-start.1
  34.7 0.0 copy-start.2
  34.7 7.0 %transposed_band.1.refs_0_ = bf16[1792,1024]{1,0:T(8,128)(2,1)} custom-call(bf16[1024,1792]{1,0:T(8,128)(2,1)} %dense_band.1.band_ref), custom_call_target="tpu_custom_call" | custom-call | bytes 10800000 | tf_op jit(solution)/shard_map/transposed_band/pallas_call | solution.py:104
  41.7 2.1 %all-to-all-done.parts_ref = bf16[4,256,256]{2,1,0:T(8,128)(2,1)S(1)} async-done(((bf16[4,256,256]{2,1,0:T(8,128)(2,1)}), bf16[4,256,256]{2,1,0:T(8,128)(2,1)S(1)}, u32[]{:S(2)}, u32[]{:S(2)}) %all-to-all-start) | async-done | bytes 524320 | tf_op jit(solution)/shard_map/all_to_all | solution.py:55
  43.8 0.0 copy-done.1
  43.8 0.0 copy-done.2
  43.8 1.1 dense_layer.1
  45.0 12.2 %all-to-all-start.1 = ((f32[32,8,256]{2,1,0:T(8,128)}), f32[32,8,256]{2,1,0:T(8,128)S(1)}, u32[]{:S(2)}, u32[]{:S(2)}) async-start(f32[32,8,256]{2,1,0:T(8,128)} %bitcast.1), calls=%async_computation.1 | async-start | bytes 524288 | tf_op jit(solution)/shard_map/all_to_all | solution.py:55
  57.2 3.3 %collective-permute-start.6 = (bf16[256,256]{1,0:T(8,128)(2,1)S(1)}, bf16[256,256]{1,0:T(8,128)(2,1)S(1)}, u32[]{:S(2)}, u32[]{:S(2)}) collective-permute-start(bf16[256,256]{1,0:T(8,128)(2,1)S(1)} %get-tuple-element.33.refs_1_), channel_id=1, source_target_pairs={{0,1},{1,2},{2,3},{3,0},{4,5},{5,6},{6,7},{7,4},{8,9},{9,10},{10,1... | collective-permute-start | bytes 393224 | tf_op jit(solution)/shard_map/ppermute | solution.py:51
  60.5 4.3 %collective-permute-start.5 = (bf16[256,256]{1,0:T(8,128)(2,1)S(1)}, bf16[256,256]{1,0:T(8,128)(2,1)S(1)}, u32[]{:S(2)}, u32[]{:S(2)}) collective-permute-start(bf16[256,256]{1,0:T(8,128)(2,1)S(1)} %get-tuple-element.33.refs_1_), channel_id=1, source_target_pairs={{0,2},{1,3},{2,0},{3,1},{4,6},{5,7},{6,4},{7,5},{8,10},{9,11},{10,... | collective-permute-start | bytes 393224 | tf_op jit(solution)/shard_map/ppermute | solution.py:51
  64.8 3.1 %collective-permute-start.4 = (bf16[256,256]{1,0:T(8,128)(2,1)S(1)}, bf16[256,256]{1,0:T(8,128)(2,1)S(1)}, u32[]{:S(2)}, u32[]{:S(2)}) collective-permute-start(bf16[256,256]{1,0:T(8,128)(2,1)S(1)} %get-tuple-element.33.refs_1_), channel_id=1, source_target_pairs={{0,3},{1,0},{2,1},{3,2},{4,7},{5,4},{6,5},{7,6},{8,11},{9,8},{10,9... | collective-permute-start | bytes 393224 | tf_op jit(solution)/shard_map/ppermute | solution.py:51
  67.9 0.0 all-to-all-done.1.refs_0_
  68.0 0.7 sum_and_spread.2
  68.6 0.0 collective-permute-done.6.refs_4_
  68.6 2.5 %collective-permute-done.5.refs_3_ = bf16[256,256]{1,0:T(8,128)(2,1)S(1)} collective-permute-done((bf16[256,256]{1,0:T(8,128)(2,1)S(1)}, bf16[256,256]{1,0:T(8,128)(2,1)S(1)}, u32[]{:S(2)}, u32[]{:S(2)}) %collective-permute-start.5) | collective-permute-done | bytes 131104 | tf_op jit(solution)/shard_map/ppermute | solution.py:51
  71.1 0.0 collective-permute-done.4.refs_2_
  71.2 5.5 %window_gradient.1 = (f32[768,256]{1,0:T(8,128)S(1)}, bf16[768,256]{1,0:T(8,128)(2,1)S(1)}, bf16[256,256]{1,0:T(8,128)(2,1)S(1)}) custom-call(bf16[1792,1024]{1,0:T(8,128)(2,1)} %transposed_band.1.refs_0_, bf16[256,256]{1,0:T(8,128)(2,1)S(1)} %get-tuple-element.33.refs_1_, bf16[256,256]{1,0:T(8,128)(2,1)S(1)} %collective-permute-done.4.refs_2_, ...), custom_call_target="tpu_custom_call" | custom-call | bytes 5400000 | tf_op jit(solution)/shard_map/window_gradient/pallas_call | solution.py:215
  76.7 3.4 %collective-permute-start.7 = (bf16[768,256]{1,0:T(8,128)(2,1)S(1)}, bf16[768,256]{1,0:T(8,128)(2,1)S(1)}, u32[]{:S(2)}, u32[]{:S(2)}) collective-permute-start(bf16[768,256]{1,0:T(8,128)(2,1)S(1)} %get-tuple-element.35), channel_id=1, source_target_pairs={{0,4},{4,0},{1,5},{5,1},{2,6},{6,2},{3,7},{7,3},{8,12},{12,8},{9,1... | collective-permute-start | bytes 1179656 | tf_op jit(solution)/shard_map/ppermute | solution.py:46
  80.1 7.2 %all-to-all-start.2 = ((bf16[16,8,256]{2,1,0:T(8,128)(2,1)}), bf16[16,8,256]{2,1,0:T(8,128)(2,1)S(1)}, u32[]{:S(2)}, u32[]{:S(2)}) async-start(bf16[16,8,256]{2,1,0:T(8,128)(2,1)} %sum_and_spread.2), calls=%async_computation.2 | async-start | bytes 131072 | tf_op jit(solution)/shard_map/all_to_all | solution.py:55
  87.3 4.6 %collective-permute-start.10 = (bf16[256,256]{1,0:T(8,128)(2,1)S(1)}, bf16[256,256]{1,0:T(8,128)(2,1)S(1)}, u32[]{:S(2)}, u32[]{:S(2)}) collective-permute-start(bf16[256,256]{1,0:T(8,128)(2,1)S(1)} %get-tuple-element.40), channel_id=1, source_target_pairs={{4,16},{12,24},{16,4},{20,32},{24,12},{28,40},{32,20},{36,48},{40,... | collective-permute-start | bytes 393224 | tf_op jit(solution)/shard_map/ppermute | solution.py:42
  91.9 0.0 collective-permute-done.7.swapped_ref
  92.0 0.1 chip_sum.1
  92.0 1.3 %collective-permute-start.8 = (bf16[256,256]{1,0:T(8,128)(2,1)S(1)}, bf16[256,256]{1,0:T(8,128)(2,1)S(1)}, u32[]{:S(2)}, u32[]{:S(2)}) collective-permute-start(bf16[256,256]{1,0:T(8,128)(2,1)S(1)} %get-tuple-element.36), channel_id=1, source_target_pairs={{8,0},{12,4},{16,8},{20,12},{24,16},{28,20},{32,24},{36,28},{40,32... | collective-permute-start | bytes 393224 | tf_op jit(solution)/shard_map/ppermute | solution.py:32
  93.3 4.0 %collective-permute-start.9 = (bf16[256,256]{1,0:T(8,128)(2,1)S(1)}, bf16[256,256]{1,0:T(8,128)(2,1)S(1)}, u32[]{:S(2)}, u32[]{:S(2)}) collective-permute-start(bf16[256,256]{1,0:T(8,128)(2,1)S(1)} %get-tuple-element.37), channel_id=1, source_target_pairs={{0,8},{4,12},{8,16},{12,20},{16,24},{20,28},{24,32},{28,36},{32,40... | collective-permute-start | bytes 393224 | tf_op jit(solution)/shard_map/ppermute | solution.py:32
  97.3 1.6 %all-to-all-done.2.refs_0_ = bf16[16,8,256]{2,1,0:T(8,128)(2,1)S(1)} async-done(((bf16[16,8,256]{2,1,0:T(8,128)(2,1)}), bf16[16,8,256]{2,1,0:T(8,128)(2,1)S(1)}, u32[]{:S(2)}, u32[]{:S(2)}) %all-to-all-start.2) | async-done | bytes 65568 | tf_op jit(solution)/shard_map/all_to_all | solution.py:55
  99.0 0.7 sum_and_spread.3
  99.7 8.5 %all-to-all-start.3 = ((f32[32,8,256]{2,1,0:T(8,128)}), f32[32,8,256]{2,1,0:T(8,128)S(1)}, u32[]{:S(2)}, u32[]{:S(2)}) async-start(f32[32,8,256]{2,1,0:T(8,128)} %sum_and_spread.3), calls=%async_computation.3 | async-start | bytes 524288 | tf_op jit(solution)/shard_map/all_to_all | solution.py:55
  108.2 0.0 collective-permute-done.10
  108.2 0.0 collective-permute-done.8
  108.3 0.0 collective-permute-done.9
  108.3 0.8 convert_add_fusion
  109.0 8.0 %all-to-all-done.3 = f32[32,8,256]{2,1,0:T(8,128)S(1)} async-done(((f32[32,8,256]{2,1,0:T(8,128)}), f32[32,8,256]{2,1,0:T(8,128)S(1)}, u32[]{:S(2)}, u32[]{:S(2)}) %all-to-all-start.3) | async-done | bytes 262176 | tf_op jit(solution)/shard_map/all_to_all | solution.py:55
  117.0 0.7 copy.9
  (2 shorter events, 0.0 us)
Async XLA Ops:
  0.6 1.0 copy-start
  1.7 20.0 %collective-permute-start.2 = (bf16[256,256]{1,0:T(8,128)(2,1)S(1)}, bf16[256,256]{1,0:T(8,128)(2,1)S(1)}, u32[]{:S(2)}, u32[]{:S(2)}) collective-permute-start(bf16[256,256]{1,0:T(8,128)(2,1)S(1)} %constant_dynamic-slice_fusion), channel_id=1, source_target_pairs={{4,16},{12,24},{16,4},{20,32},{24,12},{28,40},{32,20},{36,48},{40,... | collective-permute-start | bytes 393224 | tf_op jit(solution)/shard_map/ppermute | solution.py:42
  8.0 13.7 %collective-permute-start.1 = (bf16[256,256]{1,0:T(8,128)(2,1)S(1)}, bf16[256,256]{1,0:T(8,128)(2,1)S(1)}, u32[]{:S(2)}, u32[]{:S(2)}) collective-permute-start(bf16[256,256]{1,0:T(8,128)(2,1)S(1)} %constant_dynamic-slice_fusion), channel_id=1, source_target_pairs={{8,0},{12,4},{16,8},{20,12},{24,16},{28,20},{32,24},{36,28},{40,32... | collective-permute-start | bytes 393224 | tf_op jit(solution)/shard_map/ppermute | solution.py:32
  9.3 12.4 %collective-permute-start = (bf16[256,256]{1,0:T(8,128)(2,1)S(1)}, bf16[256,256]{1,0:T(8,128)(2,1)S(1)}, u32[]{:S(2)}, u32[]{:S(2)}) collective-permute-start(bf16[256,256]{1,0:T(8,128)(2,1)S(1)} %constant_dynamic-slice_fusion), channel_id=1, source_target_pairs={{0,8},{4,12},{8,16},{12,20},{16,24},{20,28},{24,32},{28,36},{32,40... | collective-permute-start | bytes 393224 | tf_op jit(solution)/shard_map/ppermute | solution.py:32
  13.5 0.7 copy-start.3
  21.8 4.9 %collective-permute-start.3 = (bf16[768,256]{1,0:T(8,128)(2,1)S(1)}, bf16[768,256]{1,0:T(8,128)(2,1)S(1)}, u32[]{:S(2)}, u32[]{:S(2)}) collective-permute-start(bf16[768,256]{1,0:T(8,128)(2,1)S(1)} %pad_maximum_fusion.near_ref), channel_id=1, source_target_pairs={{0,4},{4,0},{1,5},{5,1},{2,6},{6,2},{3,7},{7,3},{8,12},{12,8},{9,1... | collective-permute-start | bytes 1179656 | tf_op jit(solution)/shard_map/ppermute | solution.py:46
  31.2 12.7 %all-to-all-start = ((bf16[4,256,256]{2,1,0:T(8,128)(2,1)}), bf16[4,256,256]{2,1,0:T(8,128)(2,1)S(1)}, u32[]{:S(2)}, u32[]{:S(2)}) async-start(bf16[4,256,256]{2,1,0:T(8,128)(2,1)} %partial_aggregate.1), calls=%async_computation | async-start | bytes 1048576 | tf_op jit(solution)/shard_map/all_to_all | solution.py:55
  34.6 9.2 %copy-start.1 = (bf16[256,256]{1,0:T(8,128)(2,1)S(1)}, bf16[256,256]{1,0:T(8,128)(2,1)}, u32[]{:S(2)}) copy-start(bf16[256,256]{1,0:T(8,128)(2,1)} %weight_ref.1) | copy-start | bytes 393220
  34.7 9.2 %copy-start.2 = (bf16[256,256]{1,0:T(8,128)(2,1)S(1)}, bf16[256,256]{1,0:T(8,128)(2,1)}, u32[]{:S(2)}) copy-start(bf16[256,256]{1,0:T(8,128)(2,1)} %cotangent_ref.1) | copy-start | bytes 393220
  45.0 23.0 %all-to-all-start.1 = ((f32[32,8,256]{2,1,0:T(8,128)}), f32[32,8,256]{2,1,0:T(8,128)S(1)}, u32[]{:S(2)}, u32[]{:S(2)}) async-start(f32[32,8,256]{2,1,0:T(8,128)} %bitcast.1), calls=%async_computation.1 | async-start | bytes 524288 | tf_op jit(solution)/shard_map/all_to_all | solution.py:55
  57.2 11.4 %collective-permute-start.6 = (bf16[256,256]{1,0:T(8,128)(2,1)S(1)}, bf16[256,256]{1,0:T(8,128)(2,1)S(1)}, u32[]{:S(2)}, u32[]{:S(2)}) collective-permute-start(bf16[256,256]{1,0:T(8,128)(2,1)S(1)} %get-tuple-element.33.refs_1_), channel_id=1, source_target_pairs={{0,1},{1,2},{2,3},{3,0},{4,5},{5,6},{6,7},{7,4},{8,9},{9,10},{10,1... | collective-permute-start | bytes 393224 | tf_op jit(solution)/shard_map/ppermute | solution.py:51
  60.5 10.6 %collective-permute-start.5 = (bf16[256,256]{1,0:T(8,128)(2,1)S(1)}, bf16[256,256]{1,0:T(8,128)(2,1)S(1)}, u32[]{:S(2)}, u32[]{:S(2)}) collective-permute-start(bf16[256,256]{1,0:T(8,128)(2,1)S(1)} %get-tuple-element.33.refs_1_), channel_id=1, source_target_pairs={{0,2},{1,3},{2,0},{3,1},{4,6},{5,7},{6,4},{7,5},{8,10},{9,11},{10,... | collective-permute-start | bytes 393224 | tf_op jit(solution)/shard_map/ppermute | solution.py:51
  64.8 6.3 %collective-permute-start.4 = (bf16[256,256]{1,0:T(8,128)(2,1)S(1)}, bf16[256,256]{1,0:T(8,128)(2,1)S(1)}, u32[]{:S(2)}, u32[]{:S(2)}) collective-permute-start(bf16[256,256]{1,0:T(8,128)(2,1)S(1)} %get-tuple-element.33.refs_1_), channel_id=1, source_target_pairs={{0,3},{1,0},{2,1},{3,2},{4,7},{5,4},{6,5},{7,6},{8,11},{9,8},{10,9... | collective-permute-start | bytes 393224 | tf_op jit(solution)/shard_map/ppermute | solution.py:51
  76.7 15.3 %collective-permute-start.7 = (bf16[768,256]{1,0:T(8,128)(2,1)S(1)}, bf16[768,256]{1,0:T(8,128)(2,1)S(1)}, u32[]{:S(2)}, u32[]{:S(2)}) collective-permute-start(bf16[768,256]{1,0:T(8,128)(2,1)S(1)} %get-tuple-element.35), channel_id=1, source_target_pairs={{0,4},{4,0},{1,5},{5,1},{2,6},{6,2},{3,7},{7,3},{8,12},{12,8},{9,1... | collective-permute-start | bytes 1179656 | tf_op jit(solution)/shard_map/ppermute | solution.py:46
  80.1 18.9 %all-to-all-start.2 = ((bf16[16,8,256]{2,1,0:T(8,128)(2,1)}), bf16[16,8,256]{2,1,0:T(8,128)(2,1)S(1)}, u32[]{:S(2)}, u32[]{:S(2)}) async-start(bf16[16,8,256]{2,1,0:T(8,128)(2,1)} %sum_and_spread.2), calls=%async_computation.2 | async-start | bytes 131072 | tf_op jit(solution)/shard_map/all_to_all | solution.py:55
  87.3 20.9 %collective-permute-start.10 = (bf16[256,256]{1,0:T(8,128)(2,1)S(1)}, bf16[256,256]{1,0:T(8,128)(2,1)S(1)}, u32[]{:S(2)}, u32[]{:S(2)}) collective-permute-start(bf16[256,256]{1,0:T(8,128)(2,1)S(1)} %get-tuple-element.40), channel_id=1, source_target_pairs={{4,16},{12,24},{16,4},{20,32},{24,12},{28,40},{32,20},{36,48},{40,... | collective-permute-start | bytes 393224 | tf_op jit(solution)/shard_map/ppermute | solution.py:42
  92.0 16.2 %collective-permute-start.8 = (bf16[256,256]{1,0:T(8,128)(2,1)S(1)}, bf16[256,256]{1,0:T(8,128)(2,1)S(1)}, u32[]{:S(2)}, u32[]{:S(2)}) collective-permute-start(bf16[256,256]{1,0:T(8,128)(2,1)S(1)} %get-tuple-element.36), channel_id=1, source_target_pairs={{8,0},{12,4},{16,8},{20,12},{24,16},{28,20},{32,24},{36,28},{40,32... | collective-permute-start | bytes 393224 | tf_op jit(solution)/shard_map/ppermute | solution.py:32
  93.3 14.9 %collective-permute-start.9 = (bf16[256,256]{1,0:T(8,128)(2,1)S(1)}, bf16[256,256]{1,0:T(8,128)(2,1)S(1)}, u32[]{:S(2)}, u32[]{:S(2)}) collective-permute-start(bf16[256,256]{1,0:T(8,128)(2,1)S(1)} %get-tuple-element.37), channel_id=1, source_target_pairs={{0,8},{4,12},{8,16},{12,20},{16,24},{20,28},{24,32},{28,36},{32,40... | collective-permute-start | bytes 393224 | tf_op jit(solution)/shard_map/ppermute | solution.py:32
  99.7 17.3 %all-to-all-start.3 = ((f32[32,8,256]{2,1,0:T(8,128)}), f32[32,8,256]{2,1,0:T(8,128)S(1)}, u32[]{:S(2)}, u32[]{:S(2)}) async-start(f32[32,8,256]{2,1,0:T(8,128)} %sum_and_spread.3), calls=%async_computation.3 | async-start | bytes 524288 | tf_op jit(solution)/shard_map/all_to_all | solution.py:55

commit v3 on v2

v3 whole, which is shorter than its diff:
```python
import jax
import jax.numpy as jnp
from jax import lax
from jax.experimental import pallas as pl
from jax.experimental.pallas import tpu as pltpu
from jax.sharding import Mesh
from jax.sharding import PartitionSpec as P

HALF = 3
SECTIONS = 2 * HALF + 1
CORES = 2
X_CHIPS = 4
ROW = ("x", "z", "core")
PLANE = ("x", "core", "rep")
BF16 = jnp.bfloat16
F32 = jnp.float32
PIECE_OF = ((6, 1, 4, 0, 3, 2, 5), (4, 1, 3, 0, 5, 2, 6))
PIECE_CODE = tuple(sum(p << (4 * d) for d, p in enumerate(row)) for row in PIECE_OF)


GRADIENT_US = 2.0
CHIP_SUM_US = 0.5


def cost(us):
    return pl.CostEstimate(flops=0, transcendentals=0, bytes_accessed=int(us * 3.6e6))


def params(mib):
    return pltpu.CompilerParams(vmem_limit_bytes=mib << 20)


def chip_shift(x, by):
    devices = lax.axis_size(ROW)
    by = by * CORES
    return lax.ppermute(x, ROW, [(i, i + by) for i in range(devices) if 0 <= i + by < devices])


def far_shift(x):
    devices = lax.axis_size(ROW)
    pairs = []
    for i in range(devices):
        to = i + HALF if i % CORES else i - HALF
        if 0 <= to < devices:
            pairs.append((i, to))
    return lax.ppermute(x, ROW, pairs)


def core_swap(x):
    return lax.ppermute(x, "core", [(0, 1), (1, 0)])


def rep_shift(x, by):
    devices = lax.axis_size("rep")
    return lax.ppermute(x, "rep", [(i, (i - by) % devices) for i in range(devices)])


def to_all(x, axes):
    return lax.all_to_all(x, axes, 0, 0, tiled=False)


def band_kernel(blocks_group, per_rep, cols_ref, vals_ref, out_ref, kept_ref, held, sums, arrived, left):
    blocks, slots, side = held.shape[:3]
    columns = sums.shape[0]
    group = lax.axis_index(ROW)
    first = lax.axis_index("rep") * per_rep
    code = jnp.where(lax.axis_index("core") == 0, PIECE_CODE[0], PIECE_CODE[1])

    def fetch(block):
        return pltpu.make_async_copy(vals_ref.at[block], held.at[block], arrived.at[block])

    def rows_of(block):
        return pl.ds(pl.multiple_of(block * side, side), side)

    def keep(block):
        at = rows_of(block)
        return pltpu.make_async_copy(out_ref.at[:, at, :], kept_ref.at[:, at, :], left.at[block])

    for block in range(blocks):
        fetch(block).start()

    def step(block, carry):
        fetch(block).wait()
        sums[...] = jnp.zeros_like(sums)
        for s in range(slots):
            column = cols_ref[block, 0, s]
            source = lax.div(column, blocks_group)
            piece = lax.shift_right_logical(code, 4 * (source - group + HALF)) & 15
            at = piece * per_rep + column - source * blocks_group - first
            sums[at] += held[block, s].astype(F32)
        for c in range(columns):
            lanes = slice(c % per_rep * side, (c % per_rep + 1) * side)
            out_ref[c // per_rep, rows_of(block), lanes] = sums[c].astype(BF16)
        keep(block).start()
        return carry

    lax.fori_loop(0, blocks, step, 0)
    for block in range(blocks):
        keep(block).wait()


def dense_band(cols, vals, blocks_group, per_rep):
    blocks, count, side, _ = vals.shape
    columns = SECTIONS * per_rep
    shape = (SECTIONS, blocks * side, per_rep * side)

    def kernel(*refs):
        band_kernel(blocks_group, per_rep, *refs)

    return pl.pallas_call(
        kernel,
        in_specs=[pl.BlockSpec(memory_space=pltpu.SMEM), pl.BlockSpec(memory_space=pltpu.HBM)],
        out_specs=[pl.BlockSpec(memory_space=pltpu.VMEM), pl.BlockSpec(memory_space=pltpu.HBM)],
        out_shape=[jax.ShapeDtypeStruct(shape, BF16), pltpu.HBM(shape, BF16)],
        scratch_shapes=[
            pltpu.VMEM(vals.shape, BF16),
            pltpu.VMEM((columns, side, side), F32),
            pltpu.SemaphoreType.DMA((blocks,)),
            pltpu.SemaphoreType.DMA((blocks,)),
        ],
        compiler_params=params(16),
        cost_estimate=cost(4),
        name="dense_band",
    )(pltpu.with_memory_space_constraint(cols, pltpu.HBM), pltpu.with_memory_space_constraint(vals, pltpu.HBM))


def aggregate_kernel(band_ref, near_ref, other_ref, far_ref, out_ref):
    reps, rows, hidden = out_ref.shape
    for q in range(reps):
        total = jnp.zeros((rows, hidden), F32)
        piece = 0
        for ref in (near_ref, other_ref, far_ref):
            for k in range(ref.shape[0] // rows):
                total = total + jnp.dot(
                    band_ref[piece, q * rows : (q + 1) * rows, :],
                    ref[k * rows : (k + 1) * rows, :],
                    preferred_element_type=F32,
                )
                piece += 1
        out_ref[q] = total.astype(BF16)


def partial_aggregate(band, near, other, far, reps):
    rows, hidden = band.shape[1] // reps, near.shape[1]
    return pl.pallas_call(
        aggregate_kernel,
        out_shape=jax.ShapeDtypeStruct((reps, rows, hidden), BF16),
        compiler_params=params(12),
        cost_estimate=cost(1.5),
        name="partial_aggregate",
    )(band, near, other, far)


def dense_kernel(parts_ref, weight_ref, cotangent_ref, out_ref, back_ref, local_ref):
    reps, rows, hidden = parts_ref.shape
    summed = parts_ref[0].astype(F32)
    for q in range(1, reps):
        summed = summed + parts_ref[q].astype(F32)
    aggregate = summed.astype(BF16)
    preact = jnp.dot(aggregate, weight_ref[...], preferred_element_type=F32)
    sigmoid_pre = 1.0 / (1.0 + jnp.exp(-preact))
    grad_pre = (
        cotangent_ref[...].astype(F32) * sigmoid_pre * (1.0 + preact * (1.0 - sigmoid_pre))
    ).astype(BF16)
    back_ref[...] = lax.dot_general(
        weight_ref[...], grad_pre, (((1,), (1,)), ((), ())), preferred_element_type=F32
    ).astype(BF16)
    local_ref[...] = lax.dot_general(
        aggregate, grad_pre, (((0,), (0,)), ((), ())), preferred_element_type=F32
    )
    out_ref[...] = (preact * sigmoid_pre).astype(BF16)


def dense_layer(parts, weight, cotangent):
    reps, rows, hidden = parts.shape
    return pl.pallas_call(
        dense_kernel,
        out_shape=(
            jax.ShapeDtypeStruct((rows, hidden), BF16),
            jax.ShapeDtypeStruct((hidden, rows), BF16),
            jax.ShapeDtypeStruct((hidden, hidden), F32),
        ),
        compiler_params=params(8),
        cost_estimate=cost(1.3),
        name="dense_layer",
    )(parts, weight, cotangent)


def gradient_kernel(reps, band_ref, *refs):
    near_ref, other_ref, far_ref, held, arrived = refs[reps:]
    hidden, rows = far_ref.shape
    rep = lax.axis_index("rep")

    def fetch(piece):
        return pltpu.make_async_copy(band_ref.at[piece], held.at[piece], arrived.at[piece])

    order = [*range(HALF, 2 * HALF + 1), *range(HALF)]
    for piece in order:
        fetch(piece).start()
    for piece in order:
        fetch(piece).wait()
        total = jnp.zeros((hidden, rows), F32)
        for k in range(reps):
            at = pl.multiple_of(lax.rem(rep + k, reps) * rows, rows)
            total = total + jnp.dot(
                refs[k][...], held[piece, pl.ds(at, rows), :], preferred_element_type=F32
            )
        if piece < HALF:
            near_ref[piece * hidden : (piece + 1) * hidden, :] = total
        elif piece < 2 * HALF:
            other_ref[(piece - HALF) * hidden : (piece - HALF + 1) * hidden, :] = total.astype(BF16)
        else:
            far_ref[...] = total.astype(BF16)


def window_gradient(band, back):
    reps = len(back)
    hidden, rows = back[0].shape

    def kernel(*refs):
        gradient_kernel(reps, *refs)

    return pl.pallas_call(
        kernel,
        in_specs=[pl.BlockSpec(memory_space=pltpu.HBM)] + [pl.BlockSpec(memory_space=pltpu.VMEM)] * reps,
        out_shape=(
            jax.ShapeDtypeStruct((HALF * hidden, rows), F32),
            jax.ShapeDtypeStruct((HALF * hidden, rows), BF16),
            jax.ShapeDtypeStruct((hidden, rows), BF16),
        ),
        scratch_shapes=[pltpu.VMEM(band.shape, BF16), pltpu.SemaphoreType.DMA((SECTIONS,))],
        compiler_params=params(12),
        cost_estimate=cost(GRADIENT_US),
        name="window_gradient",
    )(pltpu.with_memory_space_constraint(band, pltpu.HBM), *back)


def chip_sum_kernel(near_ref, swapped_ref, own_ref, before_ref, after_ref):
    rows = own_ref.shape[0]
    for k, ref in enumerate((own_ref, before_ref, after_ref)):
        at = slice(k * rows, (k + 1) * rows)
        ref[...] = (near_ref[at, :] + swapped_ref[at, :].astype(F32)).astype(ref.dtype)


def chip_sum(near, swapped):
    rows, hidden = near.shape[0] // HALF, near.shape[1]
    return pl.pallas_call(
        chip_sum_kernel,
        out_shape=tuple(jax.ShapeDtypeStruct((rows, hidden), t) for t in (F32, BF16, BF16)),
        compiler_params=params(8),
        cost_estimate=cost(CHIP_SUM_US),
        name="chip_sum",
    )(near, swapped)


def total_kernel(own_ref, after_ref, before_ref, far_ref, out_ref):
    total = own_ref[...]
    for ref in (after_ref, before_ref, far_ref):
        total = total + ref[...].astype(F32)
    out_ref[...] = total.T


def total_gradient(own, after, before, far):
    hidden, rows = own.shape
    return pl.pallas_call(
        total_kernel,
        out_shape=jax.ShapeDtypeStruct((rows, hidden), F32),
        compiler_params=params(8),
        cost_estimate=cost(0.6),
        name="total_gradient",
    )(own, after, before, far)


def spread_kernel(scale, terms_ref, out_ref):
    total = terms_ref[0].astype(F32)
    for k in range(1, terms_ref.shape[0]):
        total = total + terms_ref[k].astype(F32)
    if scale is not None:
        total = total * scale
    total = total.astype(out_ref.dtype)
    for k in range(out_ref.shape[0]):
        out_ref[k] = total


def sum_and_spread(terms, copies, dtype, scale=None):
    def kernel(*refs):
        spread_kernel(scale, *refs)

    return pl.pallas_call(
        kernel,
        out_shape=jax.ShapeDtypeStruct((copies,) + terms.shape[1:], dtype),
        compiler_params=params(8),
        cost_estimate=cost(0.4),
        name="sum_and_spread",
    )(terms)


def on_device(features, block_cols, block_vals, weight, cotangent):
    reps = lax.axis_size("rep")
    rep = lax.axis_index("rep")
    group_rows, hidden = features.shape
    side = block_vals.shape[-1]
    blocks_group = group_rows // side
    per_rep = blocks_group // reps
    rows = per_rep * side

    own = lax.dynamic_slice_in_dim(features, rep * rows, rows, 0)
    before = chip_shift(own, 1)
    after = chip_shift(own, -1)
    far = far_shift(own)
    band, kept = dense_band(block_cols, block_vals[:, 0], blocks_group, per_rep)
    before, after, far, band = lax.optimization_barrier((before, after, far, band))

    near = jnp.concatenate([own, before, after], axis=0)
    other = core_swap(near)
    parts = to_all(partial_aggregate(band, near, other, far, reps), "rep")

    output_rows, backward, local = dense_layer(parts, weight, cotangent)
    line = lax.axis_size("z")
    plane = lax.axis_size(PLANE)
    node_count = group_rows * lax.axis_size(ROW)
    terms = to_all(local.reshape(plane, -1, hidden), PLANE)
    back = [backward] + [rep_shift(backward, k) for k in range(1, reps)]

    spread = sum_and_spread(terms, line, BF16)
    terms = to_all(spread, "z")
    kept, _ = lax.optimization_barrier((kept, spread))
    near_grad, other_grad, far_grad = window_gradient(kept, back)
    swapped = core_swap(other_grad)
    from_far = far_shift(far_grad)
    own_grad, before_grad, after_grad = chip_sum(near_grad, swapped)
    from_after = chip_shift(before_grad, -1)
    from_before = chip_shift(after_grad, 1)
    terms, from_far, from_after, from_before = lax.optimization_barrier((terms, from_far, from_after, from_before))
    terms = to_all(sum_and_spread(terms, plane, BF16, node_count ** (-0.5)), PLANE)
    grad_weight = terms.reshape(hidden, hidden).astype(F32)
    grad_features = total_gradient(own_grad, from_after, from_before, from_far)
    return output_rows, grad_weight, grad_features


def solution(mesh):
    devices = mesh.devices
    split = Mesh(devices.reshape(X_CHIPS, -1, CORES, devices.shape[1]), ROW + ("rep",))
    everywhere = ROW + ("rep",)
    return jax.shard_map(
        on_device,
        mesh=split,
        in_specs=(
            P(ROW, None),
            P(ROW, "rep", None),
            P(ROW, "rep", None, None, None),
            P(),
            P(everywhere, None),
        ),
        out_specs=(P(everywhere, None), P(), P(everywhere, None)),
        check_vma=False,
    )
```

time: 119 us -> 114 us (0.958)
  Pallas kernels: 27.3 us -> 13 us
  blocking collectives: 0 us -> 11.9 us
  waiting for transfers between devices: 15.6 us -> 12.5 us
  starting transfers between devices: 70.7 us -> 73 us
  local copies, waits for them, and re-layouts: 2.44 us -> 1.06 us
    pallas_call x4, Pallas kernels: 24.6 us -> 10.3 us  [the longest x1 4.45 us: dense_band(): pl.pallas_call(kernel, in_specs=[pl.BlockSpec(memory_space=pltpu.SMEM), p...]
    all_to_all x0 -> x1, blocking collectives: none -> 11.9 us  [to_all(): return lax.all_to_all(x, axes, 0, 0, tiled=False)]
    all_to_all x4 -> x3, waiting for transfers between devices: 11.8 us -> 8.31 us  [to_all(): return lax.all_to_all(x, axes, 0, 0, tiled=False)]
    all_to_all x4 -> x3, starting transfers between devices: 31.4 us -> 33.6 us  [to_all(): return lax.all_to_all(x, axes, 0, 0, tiled=False)]
    unnamed x9 -> x6, local copies, waits for them, and re-layouts: 2.43 us -> 1.05 us
  transfers between devices with their start and end apart: 15 -> 14, of which waited for: 5 -> 5; matrix products, arithmetic and copies ran while one was open for 1% -> 0% of each run, Pallas kernels for 14% -> 5%
where the time goes in v3:
time: 114 us; the launch traced here: 113 us
  starting transfers between devices  73 us (64%)
  Pallas kernels  13 us (11%)
  waiting for transfers between devices  12.5 us (11%)
  blocking collectives  11.9 us (10%)
    all_to_all x3, starting transfers between devices, to_all(): return lax.all_to_all(x, axes, 0, 0, tiled=False)  33.6 us
    all_to_all x1, blocking collectives, to_all(): return lax.all_to_all(x, axes, 0, 0, tiled=False)  11.9 us
    ppermute x2, starting transfers between devices, far_shift(): return lax.ppermute(x, ROW, pairs)  10.9 us
    ppermute x4, starting transfers between devices, chip_shift(): lax.ppermute(x, ROW, [(i, i + by) for i in range(devices) if 0 <= i + by...  10.8 us
    ppermute x3, starting transfers between devices, rep_shift(): lax.ppermute(x, 'rep', [(i, (i - by) % devices) for i in range(devices)])  10.7 us
    all_to_all x3, waiting for transfers between devices, to_all(): return lax.all_to_all(x, axes, 0, 0, tiled=False)  8.31 us
    ppermute x2, starting transfers between devices, core_swap(): return lax.ppermute(x, 'core', [(0, 1), (1, 0)])  7.08 us
    pallas_call x1, Pallas kernels, dense_band(): pl.pallas_call(kernel, in_specs=[pl.BlockSpec(memory_space=pltpu.SMEM), p...  4.45 us
  transfers between devices with their start and end apart: 14, of which 5 were waited for; matrix products, arithmetic and copies ran while one was open for 0% of the time, Pallas kernels for 5%

profile of v3, /device:TPU:1, one launch (start us, length us, event | category | flops | bytes accessed | tf_op | source)
XLA Modules:
  0.0 113.1 jit_solution(1594645845967798737)
XLA Ops:
  0.6 0.0 copy-start
  0.6 1.0 copy-done
  1.7 6.3 %collective-permute-start.2 = (bf16[256,256]{1,0:T(8,128)(2,1)S(1)}, bf16[256,256]{1,0:T(8,128)(2,1)S(1)}, u32[]{:S(2)}, u32[]{:S(2)}) collective-permute-start(bf16[256,256]{1,0:T(8,128)(2,1)S(1)} %constant_dynamic-slice_fusion), channel_id=1, source_target_pairs={{4,16},{12,24},{16,4},{20,32},{24,12},{28,40},{32,20},{36,48},{40,... | collective-permute-start | bytes 393224 | tf_op jit(solution)/shard_map/ppermute | solution.py:46
  8.0 1.3 %collective-permute-start.1 = (bf16[256,256]{1,0:T(8,128)(2,1)S(1)}, bf16[256,256]{1,0:T(8,128)(2,1)S(1)}, u32[]{:S(2)}, u32[]{:S(2)}) collective-permute-start(bf16[256,256]{1,0:T(8,128)(2,1)S(1)} %constant_dynamic-slice_fusion), channel_id=1, source_target_pairs={{8,0},{12,4},{16,8},{20,12},{24,16},{28,20},{32,24},{36,28},{40,32... | collective-permute-start | bytes 393224 | tf_op jit(solution)/shard_map/ppermute | solution.py:36
  9.3 4.2 %collective-permute-start = (bf16[256,256]{1,0:T(8,128)(2,1)S(1)}, bf16[256,256]{1,0:T(8,128)(2,1)S(1)}, u32[]{:S(2)}, u32[]{:S(2)}) collective-permute-start(bf16[256,256]{1,0:T(8,128)(2,1)S(1)} %constant_dynamic-slice_fusion), channel_id=1, source_target_pairs={{0,8},{4,12},{8,16},{12,20},{16,24},{20,28},{24,32},{28,36},{32,40... | collective-permute-start | bytes 393224 | tf_op jit(solution)/shard_map/ppermute | solution.py:36
  13.5 4.5 %dense_band.1 = (bf16[7,1024,256]{2,1,0:T(8,128)(2,1)S(1)}, bf16[7,1024,256]{2,1,0:T(8,128)(2,1)}) custom-call(s32[8,1,12]{2,1,0:T(1,128)} %refs_0_.1, bf16[8,12,128,128]{3,2,1,0:T(8,128)(2,1)} %bitcast.5), custom_call_target="tpu_custom_call" | custom-call | bytes 14400000 | tf_op jit(solution)/shard_map/dense_band/pallas_call | solution.py:110
  17.9 0.0 copy-start.1
  17.9 0.0 copy-start.2
  18.0 0.0 collective-permute-done.2.far_ref
  18.0 0.0 collective-permute-done.1
  18.0 0.0 collective-permute-done
  18.0 3.7 %collective-permute-start.3 = (bf16[768,256]{1,0:T(8,128)(2,1)S(1)}, bf16[768,256]{1,0:T(8,128)(2,1)S(1)}, u32[]{:S(2)}, u32[]{:S(2)}) collective-permute-start(bf16[768,256]{1,0:T(8,128)(2,1)S(1)} %pad_maximum_fusion.near_ref), channel_id=1, source_target_pairs={{0,4},{4,0},{1,5},{5,1},{2,6},{6,2},{3,7},{7,3},{8,12},{12,8},{9,1... | collective-permute-start | bytes 1179656 | tf_op jit(solution)/shard_map/ppermute | solution.py:50
  21.7 1.3 %collective-permute-done.3.other_ref = bf16[768,256]{1,0:T(8,128)(2,1)S(1)} collective-permute-done((bf16[768,256]{1,0:T(8,128)(2,1)S(1)}, bf16[768,256]{1,0:T(8,128)(2,1)S(1)}, u32[]{:S(2)}, u32[]{:S(2)}) %collective-permute-start.3) | collective-permute-done | bytes 393248 | tf_op jit(solution)/shard_map/ppermute | solution.py:50
  23.0 1.1 partial_aggregate.1
  24.2 11.9 %all_to_all.20.parts_ref = bf16[4,256,256]{2,1,0:T(8,128)(2,1)S(1)} all-to-all(bf16[4,256,256]{2,1,0:T(8,128)(2,1)S(1)} %partial_aggregate.1), channel_id=1, replica_groups=mesh['x'=4,'z'=16,'core'=2,'rep'=4] {'rep'}, dimensions={0} | all-to-all | bytes 1048576 | tf_op jit(solution)/shard_map/all_to_all | solution.py:59
  36.0 0.0 copy-done.1
  36.0 0.0 copy-done.2
  36.0 1.2 %dense_layer.1 = (bf16[256,256]{1,0:T(8,128)(2,1)}, bf16[256,256]{1,0:T(8,128)(2,1)S(1)}, f32[256,256]{1,0:T(8,128)}) custom-call(bf16[4,256,256]{2,1,0:T(8,128)(2,1)S(1)} %all_to_all.20.parts_ref, bf16[256,256]{1,0:T(8,128)(2,1)S(1)} %copy-done.1, bf16[256,256]{1,0:T(8,128)(2,1)S(1)} %copy-done.2), custom_call_target="tpu_custom_call" | custom-call | bytes 4680000 | tf_op jit(solution)/shard_map/dense_layer/pallas_call | solution.py:176
  37.2 14.2 %all-to-all-start.1 = ((f32[32,8,256]{2,1,0:T(8,128)}), f32[32,8,256]{2,1,0:T(8,128)S(1)}, u32[]{:S(2)}, u32[]{:S(2)}) async-start(f32[32,8,256]{2,1,0:T(8,128)} %bitcast.1), calls=%async_computation.1 | async-start | bytes 524288 | tf_op jit(solution)/shard_map/all_to_all | solution.py:59
  51.5 3.3 %collective-permute-start.6 = (bf16[256,256]{1,0:T(8,128)(2,1)S(1)}, bf16[256,256]{1,0:T(8,128)(2,1)S(1)}, u32[]{:S(2)}, u32[]{:S(2)}) collective-permute-start(bf16[256,256]{1,0:T(8,128)(2,1)S(1)} %get-tuple-element.32.refs_1_), channel_id=1, source_target_pairs={{0,1},{1,2},{2,3},{3,0},{4,5},{5,6},{6,7},{7,4},{8,9},{9,10},{10,1... | collective-permute-start | bytes 393224 | tf_op jit(solution)/shard_map/ppermute | solution.py:55
  54.8 4.3 %collective-permute-start.5 = (bf16[256,256]{1,0:T(8,128)(2,1)S(1)}, bf16[256,256]{1,0:T(8,128)(2,1)S(1)}, u32[]{:S(2)}, u32[]{:S(2)}) collective-permute-start(bf16[256,256]{1,0:T(8,128)(2,1)S(1)} %get-tuple-element.32.refs_1_), channel_id=1, source_target_pairs={{0,2},{1,3},{2,0},{3,1},{4,6},{5,7},{6,4},{7,5},{8,10},{9,11},{10,... | collective-permute-start | bytes 393224 | tf_op jit(solution)/shard_map/ppermute | solution.py:55
  59.1 3.1 %collective-permute-start.4 = (bf16[256,256]{1,0:T(8,128)(2,1)S(1)}, bf16[256,256]{1,0:T(8,128)(2,1)S(1)}, u32[]{:S(2)}, u32[]{:S(2)}) collective-permute-start(bf16[256,256]{1,0:T(8,128)(2,1)S(1)} %get-tuple-element.32.refs_1_), channel_id=1, source_target_pairs={{0,3},{1,0},{2,1},{3,2},{4,7},{5,4},{6,5},{7,6},{8,11},{9,8},{10,9... | collective-permute-start | bytes 393224 | tf_op jit(solution)/shard_map/ppermute | solution.py:55
  62.2 0.0 all-to-all-done.1.refs_0_
  62.2 0.7 sum_and_spread.2
  62.9 0.0 collective-permute-done.6.refs_4_
  62.9 2.5 %collective-permute-done.5.refs_3_ = bf16[256,256]{1,0:T(8,128)(2,1)S(1)} collective-permute-done((bf16[256,256]{1,0:T(8,128)(2,1)S(1)}, bf16[256,256]{1,0:T(8,128)(2,1)S(1)}, u32[]{:S(2)}, u32[]{:S(2)}) %collective-permute-start.5) | collective-permute-done | bytes 131104 | tf_op jit(solution)/shard_map/ppermute | solution.py:55
  65.4 0.0 collective-permute-done.4.refs_2_
  65.4 3.9 %window_gradient.1 = (f32[768,256]{1,0:T(8,128)S(1)}, bf16[768,256]{1,0:T(8,128)(2,1)S(1)}, bf16[256,256]{1,0:T(8,128)(2,1)S(1)}) custom-call(bf16[7,1024,256]{2,1,0:T(8,128)(2,1)} %get-tuple-element.31.refs_0_, bf16[256,256]{1,0:T(8,128)(2,1)S(1)} %get-tuple-element.32.refs_1_, bf16[256,256]{1,0:T(8,128)(2,1)S(1)} %collective-permute-done.4.refs_2_, ...), custom_call_target="tpu_custom_call" | custom-call | bytes 7200000 | tf_op jit(solution)/shard_map/window_gradient/pallas_call | solution.py:223
  69.3 3.4 %collective-permute-start.8 = (bf16[768,256]{1,0:T(8,128)(2,1)S(1)}, bf16[768,256]{1,0:T(8,128)(2,1)S(1)}, u32[]{:S(2)}, u32[]{:S(2)}) collective-permute-start(bf16[768,256]{1,0:T(8,128)(2,1)S(1)} %get-tuple-element.35), channel_id=1, source_target_pairs={{0,4},{4,0},{1,5},{5,1},{2,6},{6,2},{3,7},{7,3},{8,12},{12,8},{9,1... | collective-permute-start | bytes 1179656 | tf_op jit(solution)/shard_map/ppermute | solution.py:50
  72.7 5.9 %all-to-all-start.2 = ((bf16[16,8,256]{2,1,0:T(8,128)(2,1)}), bf16[16,8,256]{2,1,0:T(8,128)(2,1)S(1)}, u32[]{:S(2)}, u32[]{:S(2)}) async-start(bf16[16,8,256]{2,1,0:T(8,128)(2,1)} %sum_and_spread.2), calls=%async_computation.2 | async-start | bytes 131072 | tf_op jit(solution)/shard_map/all_to_all | solution.py:59
  78.6 4.6 %collective-permute-start.7 = (bf16[256,256]{1,0:T(8,128)(2,1)S(1)}, bf16[256,256]{1,0:T(8,128)(2,1)S(1)}, u32[]{:S(2)}, u32[]{:S(2)}) collective-permute-start(bf16[256,256]{1,0:T(8,128)(2,1)S(1)} %get-tuple-element.33), channel_id=1, source_target_pairs={{4,16},{12,24},{16,4},{20,32},{24,12},{28,40},{32,20},{36,48},{40,... | collective-permute-start | bytes 393224 | tf_op jit(solution)/shard_map/ppermute | solution.py:46
  83.3 0.0 collective-permute-done.8.swapped_ref
  83.3 0.1 chip_sum.1
  83.3 1.3 %collective-permute-start.9 = (bf16[256,256]{1,0:T(8,128)(2,1)S(1)}, bf16[256,256]{1,0:T(8,128)(2,1)S(1)}, u32[]{:S(2)}, u32[]{:S(2)}) collective-permute-start(bf16[256,256]{1,0:T(8,128)(2,1)S(1)} %get-tuple-element.36), channel_id=1, source_target_pairs={{8,0},{12,4},{16,8},{20,12},{24,16},{28,20},{32,24},{36,28},{40,32... | collective-permute-start | bytes 393224 | tf_op jit(solution)/shard_map/ppermute | solution.py:36
  84.6 4.0 %collective-permute-start.10 = (bf16[256,256]{1,0:T(8,128)(2,1)S(1)}, bf16[256,256]{1,0:T(8,128)(2,1)S(1)}, u32[]{:S(2)}, u32[]{:S(2)}) collective-permute-start(bf16[256,256]{1,0:T(8,128)(2,1)S(1)} %get-tuple-element.37), channel_id=1, source_target_pairs={{0,8},{4,12},{8,16},{12,20},{16,24},{20,28},{24,32},{28,36},{32,40... | collective-permute-start | bytes 393224 | tf_op jit(solution)/shard_map/ppermute | solution.py:36
  88.6 0.0 collective-permute-done.7.far_ref
  88.7 1.6 %all-to-all-done.2.refs_0_ = bf16[16,8,256]{2,1,0:T(8,128)(2,1)S(1)} async-done(((bf16[16,8,256]{2,1,0:T(8,128)(2,1)}), bf16[16,8,256]{2,1,0:T(8,128)(2,1)S(1)}, u32[]{:S(2)}, u32[]{:S(2)}) %all-to-all-start.2) | async-done | bytes 65568 | tf_op jit(solution)/shard_map/all_to_all | solution.py:59
  90.3 0.0 collective-permute-done.9.after_ref
  90.3 0.3 collective-permute-done.10.before_ref
  90.6 0.7 sum_and_spread.3
  91.2 13.5 %all-to-all-start.3 = ((bf16[32,8,256]{2,1,0:T(8,128)(2,1)}), bf16[32,8,256]{2,1,0:T(8,128)(2,1)S(1)}, u32[]{:S(2)}, u32[]{:S(2)}) async-start(bf16[32,8,256]{2,1,0:T(8,128)(2,1)} %sum_and_spread.3), calls=%async_computation.3 | async-start | bytes 262144 | tf_op jit(solution)/shard_map/all_to_all | solution.py:59
  104.8 0.8 total_gradient.1
  105.6 6.7 %all-to-all-done.3 = bf16[32,8,256]{2,1,0:T(8,128)(2,1)S(1)} async-done(((bf16[32,8,256]{2,1,0:T(8,128)(2,1)}), bf16[32,8,256]{2,1,0:T(8,128)(2,1)S(1)}, u32[]{:S(2)}, u32[]{:S(2)}) %all-to-all-start.3) | async-done | bytes 131104 | tf_op jit(solution)/shard_map/all_to_all | solution.py:59
  112.3 0.7 bitcast_convert_fusion
  (2 shorter events, 0.0 us)
Async XLA Ops:
  0.6 1.0 copy-start
  1.7 16.3 %collective-permute-start.2 = (bf16[256,256]{1,0:T(8,128)(2,1)S(1)}, bf16[256,256]{1,0:T(8,128)(2,1)S(1)}, u32[]{:S(2)}, u32[]{:S(2)}) collective-permute-start(bf16[256,256]{1,0:T(8,128)(2,1)S(1)} %constant_dynamic-slice_fusion), channel_id=1, source_target_pairs={{4,16},{12,24},{16,4},{20,32},{24,12},{28,40},{32,20},{36,48},{40,... | collective-permute-start | bytes 393224 | tf_op jit(solution)/shard_map/ppermute | solution.py:46
  8.0 10.0 %collective-permute-start.1 = (bf16[256,256]{1,0:T(8,128)(2,1)S(1)}, bf16[256,256]{1,0:T(8,128)(2,1)S(1)}, u32[]{:S(2)}, u32[]{:S(2)}) collective-permute-start(bf16[256,256]{1,0:T(8,128)(2,1)S(1)} %constant_dynamic-slice_fusion), channel_id=1, source_target_pairs={{8,0},{12,4},{16,8},{20,12},{24,16},{28,20},{32,24},{36,28},{40,32... | collective-permute-start | bytes 393224 | tf_op jit(solution)/shard_map/ppermute | solution.py:36
  9.3 8.7 %collective-permute-start = (bf16[256,256]{1,0:T(8,128)(2,1)S(1)}, bf16[256,256]{1,0:T(8,128)(2,1)S(1)}, u32[]{:S(2)}, u32[]{:S(2)}) collective-permute-start(bf16[256,256]{1,0:T(8,128)(2,1)S(1)} %constant_dynamic-slice_fusion), channel_id=1, source_target_pairs={{0,8},{4,12},{8,16},{12,20},{16,24},{20,28},{24,32},{28,36},{32,40... | collective-permute-start | bytes 393224 | tf_op jit(solution)/shard_map/ppermute | solution.py:36
  17.9 18.1 %copy-start.1 = (bf16[256,256]{1,0:T(8,128)(2,1)S(1)}, bf16[256,256]{1,0:T(8,128)(2,1)}, u32[]{:S(2)}) copy-start(bf16[256,256]{1,0:T(8,128)(2,1)} %weight_ref.1) | copy-start | bytes 393220
  17.9 18.1 %copy-start.2 = (bf16[256,256]{1,0:T(8,128)(2,1)S(1)}, bf16[256,256]{1,0:T(8,128)(2,1)}, u32[]{:S(2)}) copy-start(bf16[256,256]{1,0:T(8,128)(2,1)} %cotangent_ref.1) | copy-start | bytes 393220
  18.0 5.0 %collective-permute-start.3 = (bf16[768,256]{1,0:T(8,128)(2,1)S(1)}, bf16[768,256]{1,0:T(8,128)(2,1)S(1)}, u32[]{:S(2)}, u32[]{:S(2)}) collective-permute-start(bf16[768,256]{1,0:T(8,128)(2,1)S(1)} %pad_maximum_fusion.near_ref), channel_id=1, source_target_pairs={{0,4},{4,0},{1,5},{5,1},{2,6},{6,2},{3,7},{7,3},{8,12},{12,8},{9,1... | collective-permute-start | bytes 1179656 | tf_op jit(solution)/shard_map/ppermute | solution.py:50
  37.2 24.9 %all-to-all-start.1 = ((f32[32,8,256]{2,1,0:T(8,128)}), f32[32,8,256]{2,1,0:T(8,128)S(1)}, u32[]{:S(2)}, u32[]{:S(2)}) async-start(f32[32,8,256]{2,1,0:T(8,128)} %bitcast.1), calls=%async_computation.1 | async-start | bytes 524288 | tf_op jit(solution)/shard_map/all_to_all | solution.py:59
  51.5 11.4 %collective-permute-start.6 = (bf16[256,256]{1,0:T(8,128)(2,1)S(1)}, bf16[256,256]{1,0:T(8,128)(2,1)S(1)}, u32[]{:S(2)}, u32[]{:S(2)}) collective-permute-start(bf16[256,256]{1,0:T(8,128)(2,1)S(1)} %get-tuple-element.32.refs_1_), channel_id=1, source_target_pairs={{0,1},{1,2},{2,3},{3,0},{4,5},{5,6},{6,7},{7,4},{8,9},{9,10},{10,1... | collective-permute-start | bytes 393224 | tf_op jit(solution)/shard_map/ppermute | solution.py:55
  54.8 10.6 %collective-permute-start.5 = (bf16[256,256]{1,0:T(8,128)(2,1)S(1)}, bf16[256,256]{1,0:T(8,128)(2,1)S(1)}, u32[]{:S(2)}, u32[]{:S(2)}) collective-permute-start(bf16[256,256]{1,0:T(8,128)(2,1)S(1)} %get-tuple-element.32.refs_1_), channel_id=1, source_target_pairs={{0,2},{1,3},{2,0},{3,1},{4,6},{5,7},{6,4},{7,5},{8,10},{9,11},{10,... | collective-permute-start | bytes 393224 | tf_op jit(solution)/shard_map/ppermute | solution.py:55
  59.1 6.3 %collective-permute-start.4 = (bf16[256,256]{1,0:T(8,128)(2,1)S(1)}, bf16[256,256]{1,0:T(8,128)(2,1)S(1)}, u32[]{:S(2)}, u32[]{:S(2)}) collective-permute-start(bf16[256,256]{1,0:T(8,128)(2,1)S(1)} %get-tuple-element.32.refs_1_), channel_id=1, source_target_pairs={{0,3},{1,0},{2,1},{3,2},{4,7},{5,4},{6,5},{7,6},{8,11},{9,8},{10,9... | collective-permute-start | bytes 393224 | tf_op jit(solution)/shard_map/ppermute | solution.py:55
  69.3 13.9 %collective-permute-start.8 = (bf16[768,256]{1,0:T(8,128)(2,1)S(1)}, bf16[768,256]{1,0:T(8,128)(2,1)S(1)}, u32[]{:S(2)}, u32[]{:S(2)}) collective-permute-start(bf16[768,256]{1,0:T(8,128)(2,1)S(1)} %get-tuple-element.35), channel_id=1, source_target_pairs={{0,4},{4,0},{1,5},{5,1},{2,6},{6,2},{3,7},{7,3},{8,12},{12,8},{9,1... | collective-permute-start | bytes 1179656 | tf_op jit(solution)/shard_map/ppermute | solution.py:50
  72.7 17.5 %all-to-all-start.2 = ((bf16[16,8,256]{2,1,0:T(8,128)(2,1)}), bf16[16,8,256]{2,1,0:T(8,128)(2,1)S(1)}, u32[]{:S(2)}, u32[]{:S(2)}) async-start(bf16[16,8,256]{2,1,0:T(8,128)(2,1)} %sum_and_spread.2), calls=%async_computation.2 | async-start | bytes 131072 | tf_op jit(solution)/shard_map/all_to_all | solution.py:59
  78.6 10.1 %collective-permute-start.7 = (bf16[256,256]{1,0:T(8,128)(2,1)S(1)}, bf16[256,256]{1,0:T(8,128)(2,1)S(1)}, u32[]{:S(2)}, u32[]{:S(2)}) collective-permute-start(bf16[256,256]{1,0:T(8,128)(2,1)S(1)} %get-tuple-element.33), channel_id=1, source_target_pairs={{4,16},{12,24},{16,4},{20,32},{24,12},{28,40},{32,20},{36,48},{40,... | collective-permute-start | bytes 393224 | tf_op jit(solution)/shard_map/ppermute | solution.py:46
  83.3 6.9 %collective-permute-start.9 = (bf16[256,256]{1,0:T(8,128)(2,1)S(1)}, bf16[256,256]{1,0:T(8,128)(2,1)S(1)}, u32[]{:S(2)}, u32[]{:S(2)}) collective-permute-start(bf16[256,256]{1,0:T(8,128)(2,1)S(1)} %get-tuple-element.36), channel_id=1, source_target_pairs={{8,0},{12,4},{16,8},{20,12},{24,16},{28,20},{32,24},{36,28},{40,32... | collective-permute-start | bytes 393224 | tf_op jit(solution)/shard_map/ppermute | solution.py:36
  84.6 5.9 %collective-permute-start.10 = (bf16[256,256]{1,0:T(8,128)(2,1)S(1)}, bf16[256,256]{1,0:T(8,128)(2,1)S(1)}, u32[]{:S(2)}, u32[]{:S(2)}) collective-permute-start(bf16[256,256]{1,0:T(8,128)(2,1)S(1)} %get-tuple-element.37), channel_id=1, source_target_pairs={{0,8},{4,12},{8,16},{12,20},{16,24},{20,28},{24,32},{28,36},{32,40... | collective-permute-start | bytes 393224 | tf_op jit(solution)/shard_map/ppermute | solution.py:36
  91.2 21.1 %all-to-all-start.3 = ((bf16[32,8,256]{2,1,0:T(8,128)(2,1)}), bf16[32,8,256]{2,1,0:T(8,128)(2,1)S(1)}, u32[]{:S(2)}, u32[]{:S(2)}) async-start(bf16[32,8,256]{2,1,0:T(8,128)(2,1)} %sum_and_spread.3), calls=%async_computation.3 | async-start | bytes 262144 | tf_op jit(solution)/shard_map/all_to_all | solution.py:59

commit v4 on v3

--- a/solution.py
+++ b/solution.py
@@ -59,6 +59,27 @@
     return lax.all_to_all(x, axes, 0, 0, tiled=False)
 
 
+def quarter_kernel(features_ref, out_ref, arrived):
+    rows = out_ref.shape[0]
+    at = pl.multiple_of(lax.axis_index("rep") * rows, rows)
+    fetch = pltpu.make_async_copy(features_ref.at[pl.ds(at, rows), :], out_ref, arrived)
+    fetch.start()
+    fetch.wait()
+
+
+def own_quarter(features, rows):
+    return pl.pallas_call(
+        quarter_kernel,
+        in_specs=[pl.BlockSpec(memory_space=pltpu.HBM)],
+        out_specs=pl.BlockSpec(memory_space=pltpu.VMEM),
+        out_shape=jax.ShapeDtypeStruct((rows, features.shape[1]), features.dtype),
+        scratch_shapes=[pltpu.SemaphoreType.DMA(())],
+        compiler_params=params(4),
+        cost_estimate=cost(0.5),
+        name="own_quarter",
+    )(pltpu.with_memory_space_constraint(features, pltpu.HBM))
+
+
 def band_kernel(blocks_group, per_rep, cols_ref, vals_ref, out_ref, kept_ref, held, sums, arrived, left):
     blocks, slots, side = held.shape[:3]
     columns = sums.shape[0]
@@ -77,7 +98,7 @@
         return pltpu.make_async_copy(out_ref.at[:, at, :], kept_ref.at[:, at, :], left.at[block])
 
     for block in range(blocks):
-        fetch(block).start()
+        fetch(block).start(priority=block % 2)
 
     def step(block, carry):
         fetch(block).wait()
@@ -195,8 +216,8 @@
         return pltpu.make_async_copy(band_ref.at[piece], held.at[piece], arrived.at[piece])
 
     order = [*range(HALF, 2 * HALF + 1), *range(HALF)]
-    for piece in order:
-        fetch(piece).start()
+    for turn, piece in enumerate(order):
+        fetch(piece).start(priority=turn % 2)
     for piece in order:
         fetch(piece).wait()
         total = jnp.zeros((hidden, rows), F32)
@@ -297,14 +318,13 @@
 
 def on_device(features, block_cols, block_vals, weight, cotangent):
     reps = lax.axis_size("rep")
-    rep = lax.axis_index("rep")
     group_rows, hidden = features.shape
     side = block_vals.shape[-1]
     blocks_group = group_rows // side
     per_rep = blocks_group // reps
     rows = per_rep * side
 
-    own = lax.dynamic_slice_in_dim(features, rep * rows, rows, 0)
+    own = own_quarter(features, rows)
     before = chip_shift(own, 1)
     after = chip_shift(own, -1)
     far = far_shift(own)
@@ -319,19 +339,19 @@
     line = lax.axis_size("z")
     plane = lax.axis_size(PLANE)
     node_count = group_rows * lax.axis_size(ROW)
+    back = [backward] + [rep_shift(backward, k) for k in range(1, reps)]
+    local, back[1] = lax.optimization_barrier((local, back[1]))
     terms = to_all(local.reshape(plane, -1, hidden), PLANE)
-    back = [backward] + [rep_shift(backward, k) for k in range(1, reps)]
 
     spread = sum_and_spread(terms, line, BF16)
     terms = to_all(spread, "z")
-    kept, _ = lax.optimization_barrier((kept, spread))
     near_grad, other_grad, far_grad = window_gradient(kept, back)
     swapped = core_swap(other_grad)
     from_far = far_shift(far_grad)
     own_grad, before_grad, after_grad = chip_sum(near_grad, swapped)
     from_after = chip_shift(before_grad, -1)
     from_before = chip_shift(after_grad, 1)
-    terms, from_far, from_after, from_before = lax.optimization_barrier((terms, from_far, from_after, from_before))
+    terms, from_far, _, _ = lax.optimization_barrier((terms, from_far, before_grad, after_grad))
     terms = to_all(sum_and_spread(terms, plane, BF16, node_count ** (-0.5)), PLANE)
     grad_weight = terms.reshape(hidden, hidden).astype(F32)
     grad_features = total_gradient(own_grad, from_after, from_before, from_far)

time: 114 us -> 105 us (0.921)
  starting transfers between devices: 73 us -> 64.8 us
  Pallas kernels: 13 us -> 14.5 us
    all_to_all x3, starting transfers between devices: 33.6 us -> 29 us  [to_all(): return lax.all_to_all(x, axes, 0, 0, tiled=False)]
    ppermute x3, starting transfers between devices: 10.7 us -> 7.8 us  [rep_shift(): lax.ppermute(x, 'rep', [(i, (i - by) % devices) for i in range(devices)])]
    ppermute x3, waiting for transfers between devices: 2.53 us -> 0.01 us  [rep_shift(): lax.ppermute(x, 'rep', [(i, (i - by) % devices) for i in range(devices)])]
    all_to_all x3, waiting for transfers between devices: 8.31 us -> 10.2 us  [to_all(): return lax.all_to_all(x, axes, 0, 0, tiled=False)]
    ppermute x2, starting transfers between devices: 7.08 us -> 5.81 us  [core_swap(): return lax.ppermute(x, 'core', [(0, 1), (1, 0)])]
  transfers between devices with their start and end apart: 14 -> 14, of which waited for: 5 -> 4; matrix products, arithmetic and copies ran while one was open for 0% -> 0% of each run, Pallas kernels for 5% -> 11%
where the time goes in v4:
time: 105 us; the launch traced here: 104 us
  starting transfers between devices  64.8 us (62%)
  Pallas kernels  14.5 us (14%)
  blocking collectives  11.9 us (11%)
  waiting for transfers between devices  11.5 us (11%)
    all_to_all x3, starting transfers between devices, to_all(): return lax.all_to_all(x, axes, 0, 0, tiled=False)  29 us
    all_to_all x1, blocking collectives, to_all(): return lax.all_to_all(x, axes, 0, 0, tiled=False)  11.9 us
    ppermute x2, starting transfers between devices, far_shift(): return lax.ppermute(x, ROW, pairs)  11.5 us
    ppermute x4, starting transfers between devices, chip_shift(): lax.ppermute(x, ROW, [(i, i + by) for i in range(devices) if 0 <= i + by...  10.8 us
    all_to_all x3, waiting for transfers between devices, to_all(): return lax.all_to_all(x, axes, 0, 0, tiled=False)  10.2 us
    ppermute x3, starting transfers between devices, rep_shift(): lax.ppermute(x, 'rep', [(i, (i - by) % devices) for i in range(devices)])  7.8 us
    ppermute x2, starting transfers between devices, core_swap(): return lax.ppermute(x, 'core', [(0, 1), (1, 0)])  5.81 us
    pallas_call x1, Pallas kernels, dense_band(): pl.pallas_call(kernel, in_specs=[pl.BlockSpec(memory_space=pltpu.SMEM), p...  4.72 us
  transfers between devices with their start and end apart: 14, of which 4 were waited for; matrix products, arithmetic and copies ran while one was open for 0% of the time, Pallas kernels for 11%

profile of v4, /device:TPU:1, one launch (start us, length us, event | category | flops | bytes accessed | tf_op | source)
XLA Modules:
  0.0 104.4 jit_solution(5620540254981549777)
XLA Ops:
  0.6 0.9 own_quarter.1
  1.6 6.3 %collective-permute-start.2 = (bf16[256,256]{1,0:T(8,128)(2,1)S(1)}, bf16[256,256]{1,0:T(8,128)(2,1)S(1)}, u32[]{:S(2)}, u32[]{:S(2)}) collective-permute-start(bf16[256,256]{1,0:T(8,128)(2,1)S(1)} %own_quarter.1), channel_id=1, source_target_pairs={{4,16},{12,24},{16,4},{20,32},{24,12},{28,40},{32,20},{36,48},{40,... | collective-permute-start | bytes 393224 | tf_op jit(solution)/shard_map/ppermute | solution.py:46
  7.9 1.3 %collective-permute-start.1 = (bf16[256,256]{1,0:T(8,128)(2,1)S(1)}, bf16[256,256]{1,0:T(8,128)(2,1)S(1)}, u32[]{:S(2)}, u32[]{:S(2)}) collective-permute-start(bf16[256,256]{1,0:T(8,128)(2,1)S(1)} %own_quarter.1), channel_id=1, source_target_pairs={{8,0},{12,4},{16,8},{20,12},{24,16},{28,20},{32,24},{36,28},{40,32... | collective-permute-start | bytes 393224 | tf_op jit(solution)/shard_map/ppermute | solution.py:36
  9.2 4.2 %collective-permute-start = (bf16[256,256]{1,0:T(8,128)(2,1)S(1)}, bf16[256,256]{1,0:T(8,128)(2,1)S(1)}, u32[]{:S(2)}, u32[]{:S(2)}) collective-permute-start(bf16[256,256]{1,0:T(8,128)(2,1)S(1)} %own_quarter.1), channel_id=1, source_target_pairs={{0,8},{4,12},{8,16},{12,20},{16,24},{20,28},{24,32},{28,36},{32,40... | collective-permute-start | bytes 393224 | tf_op jit(solution)/shard_map/ppermute | solution.py:36
  13.3 4.7 %dense_band.1 = (bf16[7,1024,256]{2,1,0:T(8,128)(2,1)S(1)}, bf16[7,1024,256]{2,1,0:T(8,128)(2,1)}) custom-call(s32[8,1,12]{2,1,0:T(1,128)} %refs_0_.1, bf16[8,12,128,128]{3,2,1,0:T(8,128)(2,1)} %bitcast.5), custom_call_target="tpu_custom_call" | custom-call | bytes 14400000 | tf_op jit(solution)/shard_map/dense_band/pallas_call | solution.py:131
  18.1 0.0 copy-start
  18.1 0.0 copy-start.1
  18.1 0.0 collective-permute-done.2.far_ref
  18.1 0.0 collective-permute-done.1
  18.1 0.0 collective-permute-done
  18.2 3.7 %collective-permute-start.3 = (bf16[768,256]{1,0:T(8,128)(2,1)S(1)}, bf16[768,256]{1,0:T(8,128)(2,1)S(1)}, u32[]{:S(2)}, u32[]{:S(2)}) collective-permute-start(bf16[768,256]{1,0:T(8,128)(2,1)S(1)} %pad_maximum_fusion.near_ref), channel_id=1, source_target_pairs={{0,4},{4,0},{1,5},{5,1},{2,6},{6,2},{3,7},{7,3},{8,12},{12,8},{9,1... | collective-permute-start | bytes 1179656 | tf_op jit(solution)/shard_map/ppermute | solution.py:50
  21.8 1.3 %collective-permute-done.3.other_ref = bf16[768,256]{1,0:T(8,128)(2,1)S(1)} collective-permute-done((bf16[768,256]{1,0:T(8,128)(2,1)S(1)}, bf16[768,256]{1,0:T(8,128)(2,1)S(1)}, u32[]{:S(2)}, u32[]{:S(2)}) %collective-permute-start.3) | collective-permute-done | bytes 393248 | tf_op jit(solution)/shard_map/ppermute | solution.py:50
  23.2 1.1 %partial_aggregate.1 = bf16[4,256,256]{2,1,0:T(8,128)(2,1)S(1)} custom-call(bf16[7,1024,256]{2,1,0:T(8,128)(2,1)S(1)} %get-tuple-element.23.band_ref, bf16[768,256]{1,0:T(8,128)(2,1)S(1)} %pad_maximum_fusion.near_ref, bf16[768,256]{1,0:T(8,128)(2,1)S(1)} %collective-permute-done.3.other_ref, bf16[256,256]{1,0:T(8,128)(2,1)S(1)} %collective-permute-done.2.far_ref), custom_call_target="tpu_custom_call" | custom-call | bytes 5400000 | tf_op jit(solution)/shard_map/partial_aggregate/pallas_call | solution.py:166
  24.3 11.9 %all_to_all.20.parts_ref = bf16[4,256,256]{2,1,0:T(8,128)(2,1)S(1)} all-to-all(bf16[4,256,256]{2,1,0:T(8,128)(2,1)S(1)} %partial_aggregate.1), channel_id=1, replica_groups=mesh['x'=4,'z'=16,'core'=2,'rep'=4] {'rep'}, dimensions={0} | all-to-all | bytes 1048576 | tf_op jit(solution)/shard_map/all_to_all | solution.py:59
  36.2 0.0 copy-done
  36.2 0.0 copy-done.1
  36.2 1.2 %dense_layer.1 = (bf16[256,256]{1,0:T(8,128)(2,1)}, bf16[256,256]{1,0:T(8,128)(2,1)S(1)}, f32[256,256]{1,0:T(8,128)}) custom-call(bf16[4,256,256]{2,1,0:T(8,128)(2,1)S(1)} %all_to_all.20.parts_ref, bf16[256,256]{1,0:T(8,128)(2,1)S(1)} %copy-done, bf16[256,256]{1,0:T(8,128)(2,1)S(1)} %copy-done.1), custom_call_target="tpu_custom_call" | custom-call | bytes 4680000 | tf_op jit(solution)/shard_map/dense_layer/pallas_call | solution.py:197
  37.4 2.8 %collective-permute-start.4 = (bf16[256,256]{1,0:T(8,128)(2,1)S(1)}, bf16[256,256]{1,0:T(8,128)(2,1)S(1)}, u32[]{:S(2)}, u32[]{:S(2)}) collective-permute-start(bf16[256,256]{1,0:T(8,128)(2,1)S(1)} %get-tuple-element.29.refs_1_), channel_id=1, source_target_pairs={{0,3},{1,0},{2,1},{3,2},{4,7},{5,4},{6,5},{7,6},{8,11},{9,8},{10,9... | collective-permute-start | bytes 393224 | tf_op jit(solution)/shard_map/ppermute | solution.py:55
  40.2 2.5 %collective-permute-start.6 = (bf16[256,256]{1,0:T(8,128)(2,1)S(1)}, bf16[256,256]{1,0:T(8,128)(2,1)S(1)}, u32[]{:S(2)}, u32[]{:S(2)}) collective-permute-start(bf16[256,256]{1,0:T(8,128)(2,1)S(1)} %get-tuple-element.29.refs_1_), channel_id=1, source_target_pairs={{0,1},{1,2},{2,3},{3,0},{4,5},{5,6},{6,7},{7,4},{8,9},{9,10},{10,1... | collective-permute-start | bytes 393224 | tf_op jit(solution)/shard_map/ppermute | solution.py:55
  42.7 2.5 %collective-permute-start.5 = (bf16[256,256]{1,0:T(8,128)(2,1)S(1)}, bf16[256,256]{1,0:T(8,128)(2,1)S(1)}, u32[]{:S(2)}, u32[]{:S(2)}) collective-permute-start(bf16[256,256]{1,0:T(8,128)(2,1)S(1)} %get-tuple-element.29.refs_1_), channel_id=1, source_target_pairs={{0,2},{1,3},{2,0},{3,1},{4,6},{5,7},{6,4},{7,5},{8,10},{9,11},{10,... | collective-permute-start | bytes 393224 | tf_op jit(solution)/shard_map/ppermute | solution.py:55
  45.2 0.0 collective-permute-done.4.refs_2_
  45.2 16.3 %all-to-all-start.1 = ((f32[32,8,256]{2,1,0:T(8,128)}), f32[32,8,256]{2,1,0:T(8,128)S(1)}, u32[]{:S(2)}, u32[]{:S(2)}) async-start(f32[32,8,256]{2,1,0:T(8,128)} %bitcast.1), calls=%async_computation.1 | async-start | bytes 524288 | tf_op jit(solution)/shard_map/all_to_all | solution.py:59
  61.5 0.0 collective-permute-done.6.refs_4_
  61.5 0.0 collective-permute-done.5.refs_3_
  61.5 4.3 %window_gradient.1 = (f32[768,256]{1,0:T(8,128)S(1)}, bf16[768,256]{1,0:T(8,128)(2,1)S(1)}, bf16[256,256]{1,0:T(8,128)(2,1)S(1)}) custom-call(bf16[7,1024,256]{2,1,0:T(8,128)(2,1)} %get-tuple-element.31.refs_0_, bf16[256,256]{1,0:T(8,128)(2,1)S(1)} %get-tuple-element.29.refs_1_, bf16[256,256]{1,0:T(8,128)(2,1)S(1)} %collective-permute-done.4.refs_2_, ...), custom_call_target="tpu_custom_call" | custom-call | bytes 7200000 | tf_op jit(solution)/shard_map/window_gradient/pallas_call | solution.py:244
  65.8 2.1 %collective-permute-start.8 = (bf16[768,256]{1,0:T(8,128)(2,1)S(1)}, bf16[768,256]{1,0:T(8,128)(2,1)S(1)}, u32[]{:S(2)}, u32[]{:S(2)}) collective-permute-start(bf16[768,256]{1,0:T(8,128)(2,1)S(1)} %get-tuple-element.35), channel_id=1, source_target_pairs={{0,4},{4,0},{1,5},{5,1},{2,6},{6,2},{3,7},{7,3},{8,12},{12,8},{9,1... | collective-permute-start | bytes 1179656 | tf_op jit(solution)/shard_map/ppermute | solution.py:50
  67.9 2.4 %all-to-all-done.1.refs_0_ = f32[32,8,256]{2,1,0:T(8,128)S(1)} async-done(((f32[32,8,256]{2,1,0:T(8,128)}), f32[32,8,256]{2,1,0:T(8,128)S(1)}, u32[]{:S(2)}, u32[]{:S(2)}) %all-to-all-start.1) | async-done | bytes 262176 | tf_op jit(solution)/shard_map/all_to_all | solution.py:59
  70.3 0.7 sum_and_spread.2
  71.0 6.1 %all-to-all-start.2 = ((bf16[16,8,256]{2,1,0:T(8,128)(2,1)}), bf16[16,8,256]{2,1,0:T(8,128)(2,1)S(1)}, u32[]{:S(2)}, u32[]{:S(2)}) async-start(bf16[16,8,256]{2,1,0:T(8,128)(2,1)} %sum_and_spread.2), calls=%async_computation.2 | async-start | bytes 131072 | tf_op jit(solution)/shard_map/all_to_all | solution.py:59
  77.0 5.2 %collective-permute-start.7 = (bf16[256,256]{1,0:T(8,128)(2,1)S(1)}, bf16[256,256]{1,0:T(8,128)(2,1)S(1)}, u32[]{:S(2)}, u32[]{:S(2)}) collective-permute-start(bf16[256,256]{1,0:T(8,128)(2,1)S(1)} %get-tuple-element.33), channel_id=1, source_target_pairs={{4,16},{12,24},{16,4},{20,32},{24,12},{28,40},{32,20},{36,48},{40,... | collective-permute-start | bytes 393224 | tf_op jit(solution)/shard_map/ppermute | solution.py:46
  82.2 0.0 collective-permute-done.8.swapped_ref
  82.2 0.1 chip_sum.1
  82.3 1.3 %collective-permute-start.9 = (bf16[256,256]{1,0:T(8,128)(2,1)S(1)}, bf16[256,256]{1,0:T(8,128)(2,1)S(1)}, u32[]{:S(2)}, u32[]{:S(2)}) collective-permute-start(bf16[256,256]{1,0:T(8,128)(2,1)S(1)} %get-tuple-element.36), channel_id=1, source_target_pairs={{8,0},{12,4},{16,8},{20,12},{24,16},{28,20},{32,24},{36,28},{40,32... | collective-permute-start | bytes 393224 | tf_op jit(solution)/shard_map/ppermute | solution.py:36
  83.6 4.0 %collective-permute-start.10 = (bf16[256,256]{1,0:T(8,128)(2,1)S(1)}, bf16[256,256]{1,0:T(8,128)(2,1)S(1)}, u32[]{:S(2)}, u32[]{:S(2)}) collective-permute-start(bf16[256,256]{1,0:T(8,128)(2,1)S(1)} %get-tuple-element.37), channel_id=1, source_target_pairs={{0,8},{4,12},{8,16},{12,20},{16,24},{20,28},{24,32},{28,36},{32,40... | collective-permute-start | bytes 393224 | tf_op jit(solution)/shard_map/ppermute | solution.py:36
  87.6 0.0 collective-permute-done.7.far_ref
  87.6 1.1 %all-to-all-done.2.refs_0_ = bf16[16,8,256]{2,1,0:T(8,128)(2,1)S(1)} async-done(((bf16[16,8,256]{2,1,0:T(8,128)(2,1)}), bf16[16,8,256]{2,1,0:T(8,128)(2,1)S(1)}, u32[]{:S(2)}, u32[]{:S(2)}) %all-to-all-start.2) | async-done | bytes 65568 | tf_op jit(solution)/shard_map/all_to_all | solution.py:59
  88.7 0.7 sum_and_spread.3
  89.4 6.7 %all-to-all-start.3 = ((bf16[32,8,256]{2,1,0:T(8,128)(2,1)}), bf16[32,8,256]{2,1,0:T(8,128)(2,1)S(1)}, u32[]{:S(2)}, u32[]{:S(2)}) async-start(bf16[32,8,256]{2,1,0:T(8,128)(2,1)} %sum_and_spread.3), calls=%async_computation.3 | async-start | bytes 262144 | tf_op jit(solution)/shard_map/all_to_all | solution.py:59
  96.1 0.0 collective-permute-done.9.after_ref
  96.1 0.0 collective-permute-done.10.before_ref
  96.1 0.8 total_gradient.1
  96.9 6.7 %all-to-all-done.3 = bf16[32,8,256]{2,1,0:T(8,128)(2,1)S(1)} async-done(((bf16[32,8,256]{2,1,0:T(8,128)(2,1)}), bf16[32,8,256]{2,1,0:T(8,128)(2,1)S(1)}, u32[]{:S(2)}, u32[]{:S(2)}) %all-to-all-start.3) | async-done | bytes 131104 | tf_op jit(solution)/shard_map/all_to_all | solution.py:59
  103.6 0.7 bitcast_convert_fusion
  (1 shorter events, 0.0 us)
Async XLA Ops:
  1.6 16.5 %collective-permute-start.2 = (bf16[256,256]{1,0:T(8,128)(2,1)S(1)}, bf16[256,256]{1,0:T(8,128)(2,1)S(1)}, u32[]{:S(2)}, u32[]{:S(2)}) collective-permute-start(bf16[256,256]{1,0:T(8,128)(2,1)S(1)} %own_quarter.1), channel_id=1, source_target_pairs={{4,16},{12,24},{16,4},{20,32},{24,12},{28,40},{32,20},{36,48},{40,... | collective-permute-start | bytes 393224 | tf_op jit(solution)/shard_map/ppermute | solution.py:46
  7.9 10.3 %collective-permute-start.1 = (bf16[256,256]{1,0:T(8,128)(2,1)S(1)}, bf16[256,256]{1,0:T(8,128)(2,1)S(1)}, u32[]{:S(2)}, u32[]{:S(2)}) collective-permute-start(bf16[256,256]{1,0:T(8,128)(2,1)S(1)} %own_quarter.1), channel_id=1, source_target_pairs={{8,0},{12,4},{16,8},{20,12},{24,16},{28,20},{32,24},{36,28},{40,32... | collective-permute-start | bytes 393224 | tf_op jit(solution)/shard_map/ppermute | solution.py:36
  9.2 9.0 %collective-permute-start = (bf16[256,256]{1,0:T(8,128)(2,1)S(1)}, bf16[256,256]{1,0:T(8,128)(2,1)S(1)}, u32[]{:S(2)}, u32[]{:S(2)}) collective-permute-start(bf16[256,256]{1,0:T(8,128)(2,1)S(1)} %own_quarter.1), channel_id=1, source_target_pairs={{0,8},{4,12},{8,16},{12,20},{16,24},{20,28},{24,32},{28,36},{32,40... | collective-permute-start | bytes 393224 | tf_op jit(solution)/shard_map/ppermute | solution.py:36
  18.1 18.1 %copy-start = (bf16[256,256]{1,0:T(8,128)(2,1)S(1)}, bf16[256,256]{1,0:T(8,128)(2,1)}, u32[]{:S(2)}) copy-start(bf16[256,256]{1,0:T(8,128)(2,1)} %weight_ref.1) | copy-start | bytes 393220
  18.1 18.1 %copy-start.1 = (bf16[256,256]{1,0:T(8,128)(2,1)S(1)}, bf16[256,256]{1,0:T(8,128)(2,1)}, u32[]{:S(2)}) copy-start(bf16[256,256]{1,0:T(8,128)(2,1)} %cotangent_ref.1) | copy-start | bytes 393220
  18.2 5.0 %collective-permute-start.3 = (bf16[768,256]{1,0:T(8,128)(2,1)S(1)}, bf16[768,256]{1,0:T(8,128)(2,1)S(1)}, u32[]{:S(2)}, u32[]{:S(2)}) collective-permute-start(bf16[768,256]{1,0:T(8,128)(2,1)S(1)} %pad_maximum_fusion.near_ref), channel_id=1, source_target_pairs={{0,4},{4,0},{1,5},{5,1},{2,6},{6,2},{3,7},{7,3},{8,12},{12,8},{9,1... | collective-permute-start | bytes 1179656 | tf_op jit(solution)/shard_map/ppermute | solution.py:50
  37.4 7.8 %collective-permute-start.4 = (bf16[256,256]{1,0:T(8,128)(2,1)S(1)}, bf16[256,256]{1,0:T(8,128)(2,1)S(1)}, u32[]{:S(2)}, u32[]{:S(2)}) collective-permute-start(bf16[256,256]{1,0:T(8,128)(2,1)S(1)} %get-tuple-element.29.refs_1_), channel_id=1, source_target_pairs={{0,3},{1,0},{2,1},{3,2},{4,7},{5,4},{6,5},{7,6},{8,11},{9,8},{10,9... | collective-permute-start | bytes 393224 | tf_op jit(solution)/shard_map/ppermute | solution.py:55
  40.2 21.3 %collective-permute-start.6 = (bf16[256,256]{1,0:T(8,128)(2,1)S(1)}, bf16[256,256]{1,0:T(8,128)(2,1)S(1)}, u32[]{:S(2)}, u32[]{:S(2)}) collective-permute-start(bf16[256,256]{1,0:T(8,128)(2,1)S(1)} %get-tuple-element.29.refs_1_), channel_id=1, source_target_pairs={{0,1},{1,2},{2,3},{3,0},{4,5},{5,6},{6,7},{7,4},{8,9},{9,10},{10,1... | collective-permute-start | bytes 393224 | tf_op jit(solution)/shard_map/ppermute | solution.py:55
  42.7 18.8 %collective-permute-start.5 = (bf16[256,256]{1,0:T(8,128)(2,1)S(1)}, bf16[256,256]{1,0:T(8,128)(2,1)S(1)}, u32[]{:S(2)}, u32[]{:S(2)}) collective-permute-start(bf16[256,256]{1,0:T(8,128)(2,1)S(1)} %get-tuple-element.29.refs_1_), channel_id=1, source_target_pairs={{0,2},{1,3},{2,0},{3,1},{4,6},{5,7},{6,4},{7,5},{8,10},{9,11},{10,... | collective-permute-start | bytes 393224 | tf_op jit(solution)/shard_map/ppermute | solution.py:55
  45.2 25.1 %all-to-all-start.1 = ((f32[32,8,256]{2,1,0:T(8,128)}), f32[32,8,256]{2,1,0:T(8,128)S(1)}, u32[]{:S(2)}, u32[]{:S(2)}) async-start(f32[32,8,256]{2,1,0:T(8,128)} %bitcast.1), calls=%async_computation.1 | async-start | bytes 524288 | tf_op jit(solution)/shard_map/all_to_all | solution.py:59
  65.8 16.5 %collective-permute-start.8 = (bf16[768,256]{1,0:T(8,128)(2,1)S(1)}, bf16[768,256]{1,0:T(8,128)(2,1)S(1)}, u32[]{:S(2)}, u32[]{:S(2)}) collective-permute-start(bf16[768,256]{1,0:T(8,128)(2,1)S(1)} %get-tuple-element.35), channel_id=1, source_target_pairs={{0,4},{4,0},{1,5},{5,1},{2,6},{6,2},{3,7},{7,3},{8,12},{12,8},{9,1... | collective-permute-start | bytes 1179656 | tf_op jit(solution)/shard_map/ppermute | solution.py:50
  71.0 17.8 %all-to-all-start.2 = ((bf16[16,8,256]{2,1,0:T(8,128)(2,1)}), bf16[16,8,256]{2,1,0:T(8,128)(2,1)S(1)}, u32[]{:S(2)}, u32[]{:S(2)}) async-start(bf16[16,8,256]{2,1,0:T(8,128)(2,1)} %sum_and_spread.2), calls=%async_computation.2 | async-start | bytes 131072 | tf_op jit(solution)/shard_map/all_to_all | solution.py:59
  77.0 10.6 %collective-permute-start.7 = (bf16[256,256]{1,0:T(8,128)(2,1)S(1)}, bf16[256,256]{1,0:T(8,128)(2,1)S(1)}, u32[]{:S(2)}, u32[]{:S(2)}) collective-permute-start(bf16[256,256]{1,0:T(8,128)(2,1)S(1)} %get-tuple-element.33), channel_id=1, source_target_pairs={{4,16},{12,24},{16,4},{20,32},{24,12},{28,40},{32,20},{36,48},{40,... | collective-permute-start | bytes 393224 | tf_op jit(solution)/shard_map/ppermute | solution.py:46
  82.3 13.7 %collective-permute-start.9 = (bf16[256,256]{1,0:T(8,128)(2,1)S(1)}, bf16[256,256]{1,0:T(8,128)(2,1)S(1)}, u32[]{:S(2)}, u32[]{:S(2)}) collective-permute-start(bf16[256,256]{1,0:T(8,128)(2,1)S(1)} %get-tuple-element.36), channel_id=1, source_target_pairs={{8,0},{12,4},{16,8},{20,12},{24,16},{28,20},{32,24},{36,28},{40,32... | collective-permute-start | bytes 393224 | tf_op jit(solution)/shard_map/ppermute | solution.py:36
  83.6 12.5 %collective-permute-start.10 = (bf16[256,256]{1,0:T(8,128)(2,1)S(1)}, bf16[256,256]{1,0:T(8,128)(2,1)S(1)}, u32[]{:S(2)}, u32[]{:S(2)}) collective-permute-start(bf16[256,256]{1,0:T(8,128)(2,1)S(1)} %get-tuple-element.37), channel_id=1, source_target_pairs={{0,8},{4,12},{8,16},{12,20},{16,24},{20,28},{24,32},{28,36},{32,40... | collective-permute-start | bytes 393224 | tf_op jit(solution)/shard_map/ppermute | solution.py:36
  89.4 14.2 %all-to-all-start.3 = ((bf16[32,8,256]{2,1,0:T(8,128)(2,1)}), bf16[32,8,256]{2,1,0:T(8,128)(2,1)S(1)}, u32[]{:S(2)}, u32[]{:S(2)}) async-start(bf16[32,8,256]{2,1,0:T(8,128)(2,1)} %sum_and_spread.3), calls=%async_computation.3 | async-start | bytes 262144 | tf_op jit(solution)/shard_map/all_to_all | solution.py:59

commit v5 on v4

--- a/solution.py
+++ b/solution.py
@@ -80,7 +80,8 @@
     )(pltpu.with_memory_space_constraint(features, pltpu.HBM))
 
 
-def band_kernel(blocks_group, per_rep, cols_ref, vals_ref, out_ref, kept_ref, held, sums, arrived, left):
+def band_kernel(blocks_group, per_rep, start, cols_ref, vals_ref, *refs):
+    out_ref, held, sums, arrived = refs[-4:]
     blocks, slots, side = held.shape[:3]
     columns = sums.shape[0]
     group = lax.axis_index(ROW)
@@ -88,23 +89,19 @@
     code = jnp.where(lax.axis_index("core") == 0, PIECE_CODE[0], PIECE_CODE[1])
 
     def fetch(block):
-        return pltpu.make_async_copy(vals_ref.at[block], held.at[block], arrived.at[block])
+        return pltpu.make_async_copy(vals_ref.at[start + block], held.at[block], arrived.at[block])
 
     def rows_of(block):
-        return pl.ds(pl.multiple_of(block * side, side), side)
-
-    def keep(block):
-        at = rows_of(block)
-        return pltpu.make_async_copy(out_ref.at[:, at, :], kept_ref.at[:, at, :], left.at[block])
+        return pl.ds(pl.multiple_of((start + block) * side, side), side)
 
     for block in range(blocks):
-        fetch(block).start(priority=block % 2)
+        fetch(block).start()
 
     def step(block, carry):
         fetch(block).wait()
         sums[...] = jnp.zeros_like(sums)
         for s in range(slots):
-            column = cols_ref[block, 0, s]
+            column = cols_ref[start + block, 0, s]
             source = lax.div(column, blocks_group)
             piece = lax.shift_right_logical(code, 4 * (source - group + HALF)) & 15
             at = piece * per_rep + column - source * blocks_group - first
@@ -112,37 +109,39 @@
         for c in range(columns):
             lanes = slice(c % per_rep * side, (c % per_rep + 1) * side)
             out_ref[c // per_rep, rows_of(block), lanes] = sums[c].astype(BF16)
-        keep(block).start()
         return carry
 
     lax.fori_loop(0, blocks, step, 0)
-    for block in range(blocks):
-        keep(block).wait()
-
-
-def dense_band(cols, vals, blocks_group, per_rep):
+
+
+def dense_band(cols, vals, blocks_group, per_rep, start, stop, band=None):
     blocks, count, side, _ = vals.shape
     columns = SECTIONS * per_rep
-    shape = (SECTIONS, blocks * side, per_rep * side)
+    built = stop - start
 
     def kernel(*refs):
-        band_kernel(blocks_group, per_rep, *refs)
-
+        band_kernel(blocks_group, per_rep, start, *refs)
+
+    args = [pltpu.with_memory_space_constraint(cols, pltpu.HBM), pltpu.with_memory_space_constraint(vals, pltpu.HBM)]
+    specs = [pl.BlockSpec(memory_space=pltpu.SMEM), pl.BlockSpec(memory_space=pltpu.HBM)]
+    if band is not None:
+        args.append(band)
+        specs.append(pl.BlockSpec(memory_space=pltpu.VMEM))
     return pl.pallas_call(
         kernel,
-        in_specs=[pl.BlockSpec(memory_space=pltpu.SMEM), pl.BlockSpec(memory_space=pltpu.HBM)],
-        out_specs=[pl.BlockSpec(memory_space=pltpu.VMEM), pl.BlockSpec(memory_space=pltpu.HBM)],
-        out_shape=[jax.ShapeDtypeStruct(shape, BF16), pltpu.HBM(shape, BF16)],
+        in_specs=specs,
+        out_specs=pl.BlockSpec(memory_space=pltpu.VMEM),
+        out_shape=jax.ShapeDtypeStruct((SECTIONS, blocks * side, per_rep * side), BF16),
+        input_output_aliases={} if band is None else {2: 0},
         scratch_shapes=[
-            pltpu.VMEM(vals.shape, BF16),
+            pltpu.VMEM((built, count, side, side), BF16),
             pltpu.VMEM((columns, side, side), F32),
-            pltpu.SemaphoreType.DMA((blocks,)),
-            pltpu.SemaphoreType.DMA((blocks,)),
+            pltpu.SemaphoreType.DMA((built,)),
         ],
         compiler_params=params(16),
-        cost_estimate=cost(4),
+        cost_estimate=cost(2),
         name="dense_band",
-    )(pltpu.with_memory_space_constraint(cols, pltpu.HBM), pltpu.with_memory_space_constraint(vals, pltpu.HBM))
+    )(*args)
 
 
 def aggregate_kernel(band_ref, near_ref, other_ref, far_ref, out_ref):
@@ -172,8 +171,9 @@
     )(band, near, other, far)
 
 
-def dense_kernel(parts_ref, weight_ref, cotangent_ref, out_ref, back_ref, local_ref):
+def dense_kernel(parts_ref, weight_ref, cotangent_ref, out_ref, back_ref, quarter_ref, *refs):
     reps, rows, hidden = parts_ref.shape
+    *send_refs, local_ref = refs
     summed = parts_ref[0].astype(F32)
     for q in range(1, reps):
         summed = summed + parts_ref[q].astype(F32)
@@ -183,58 +183,74 @@
     grad_pre = (
         cotangent_ref[...].astype(F32) * sigmoid_pre * (1.0 + preact * (1.0 - sigmoid_pre))
     ).astype(BF16)
-    back_ref[...] = lax.dot_general(
+    backward = lax.dot_general(
         weight_ref[...], grad_pre, (((1,), (1,)), ((), ())), preferred_element_type=F32
     ).astype(BF16)
+    back_ref[...] = backward
     local_ref[...] = lax.dot_general(
         aggregate, grad_pre, (((0,), (0,)), ((), ())), preferred_element_type=F32
     )
+    plane = X_CHIPS * CORES
+    piece = hidden // (plane * reps)
+    rep = lax.axis_index("rep")
+    for k in range(reps):
+        of_rep = []
+        for i in range(plane):
+            at = pl.multiple_of((i * reps + lax.rem(rep + reps - k, reps)) * piece, piece)
+            of_rep.append(local_ref[pl.ds(at, piece), :])
+        quarter = jnp.concatenate(of_rep, axis=0)
+        if k == 0:
+            quarter_ref[...] = quarter
+        else:
+            send_refs[k - 1][:hidden, :] = backward
+            send_refs[k - 1][hidden:, :] = quarter.astype(BF16)
     out_ref[...] = (preact * sigmoid_pre).astype(BF16)
 
 
 def dense_layer(parts, weight, cotangent):
     reps, rows, hidden = parts.shape
+    quarter = hidden // reps
     return pl.pallas_call(
         dense_kernel,
-        out_shape=(
+        out_shape=[
             jax.ShapeDtypeStruct((rows, hidden), BF16),
             jax.ShapeDtypeStruct((hidden, rows), BF16),
-            jax.ShapeDtypeStruct((hidden, hidden), F32),
-        ),
+            jax.ShapeDtypeStruct((quarter, hidden), F32),
+        ]
+        + [jax.ShapeDtypeStruct((hidden + quarter, rows), BF16)] * (reps - 1),
+        scratch_shapes=[pltpu.VMEM((hidden, hidden), F32)],
         compiler_params=params(8),
         cost_estimate=cost(1.3),
         name="dense_layer",
     )(parts, weight, cotangent)
 
 
-def gradient_kernel(reps, band_ref, *refs):
-    near_ref, other_ref, far_ref, held, arrived = refs[reps:]
+def gradient_kernel(reps, band_ref, quarter_ref, *refs):
+    near_ref, other_ref, far_ref, sum_ref = refs[reps:]
     hidden, rows = far_ref.shape
     rep = lax.axis_index("rep")
 
-    def fetch(piece):
-        return pltpu.make_async_copy(band_ref.at[piece], held.at[piece], arrived.at[piece])
-
-    order = [*range(HALF, 2 * HALF + 1), *range(HALF)]
-    for turn, piece in enumerate(order):
-        fetch(piece).start(priority=turn % 2)
-    for piece in order:
-        fetch(piece).wait()
+    def product(piece):
         total = jnp.zeros((hidden, rows), F32)
         for k in range(reps):
             at = pl.multiple_of(lax.rem(rep + k, reps) * rows, rows)
             total = total + jnp.dot(
-                refs[k][...], held[piece, pl.ds(at, rows), :], preferred_element_type=F32
+                refs[k][:hidden, :], band_ref[piece, pl.ds(at, rows), :], preferred_element_type=F32
             )
-        if piece < HALF:
-            near_ref[piece * hidden : (piece + 1) * hidden, :] = total
-        elif piece < 2 * HALF:
-            other_ref[(piece - HALF) * hidden : (piece - HALF + 1) * hidden, :] = total.astype(BF16)
-        else:
-            far_ref[...] = total.astype(BF16)
-
-
-def window_gradient(band, back):
+        return total
+
+    total = quarter_ref[...]
+    for k in range(1, reps):
+        total = total + refs[k][hidden:, :].astype(F32)
+    sum_ref[...] = total
+    for k in range(HALF):
+        at = slice(k * hidden, (k + 1) * hidden)
+        other_ref[at, :] = product(HALF + k).astype(BF16)
+        near_ref[at, :] = product(k)
+    far_ref[...] = product(2 * HALF).astype(BF16)
+
+
+def window_gradient(band, quarter, back):
     reps = len(back)
     hidden, rows = back[0].shape
 
@@ -243,17 +259,16 @@
 
     return pl.pallas_call(
         kernel,
-        in_specs=[pl.BlockSpec(memory_space=pltpu.HBM)] + [pl.BlockSpec(memory_space=pltpu.VMEM)] * reps,
         out_shape=(
             jax.ShapeDtypeStruct((HALF * hidden, rows), F32),
             jax.ShapeDtypeStruct((HALF * hidden, rows), BF16),
             jax.ShapeDtypeStruct((hidden, rows), BF16),
+            jax.ShapeDtypeStruct(quarter.shape, F32),
         ),
-        scratch_shapes=[pltpu.VMEM(band.shape, BF16), pltpu.SemaphoreType.DMA((SECTIONS,))],
         compiler_params=params(12),
         cost_estimate=cost(GRADIENT_US),
         name="window_gradient",
-    )(pltpu.with_memory_space_constraint(band, pltpu.HBM), *back)
+    )(band, quarter, *back)
 
 
 def chip_sum_kernel(near_ref, swapped_ref, own_ref, before_ref, after_ref):
@@ -328,33 +343,35 @@
     before = chip_shift(own, 1)
     after = chip_shift(own, -1)
     far = far_shift(own)
-    band, kept = dense_band(block_cols, block_vals[:, 0], blocks_group, per_rep)
+    vals = block_vals[:, 0]
+    half = blocks_group // 2
+    band = dense_band(block_cols, vals, blocks_group, per_rep, 0, half)
     before, after, far, band = lax.optimization_barrier((before, after, far, band))
 
     near = jnp.concatenate([own, before, after], axis=0)
+    near, band = lax.optimization_barrier((near, band))
     other = core_swap(near)
+    band = dense_band(block_cols, vals, blocks_group, per_rep, half, blocks_group, band)
     parts = to_all(partial_aggregate(band, near, other, far, reps), "rep")
 
-    output_rows, backward, local = dense_layer(parts, weight, cotangent)
+    output_rows, backward, quarter, *sends = dense_layer(parts, weight, cotangent)
+    back = [backward] + [rep_shift(send, k + 1) for k, send in enumerate(sends)]
     line = lax.axis_size("z")
-    plane = lax.axis_size(PLANE)
+    plane = lax.axis_size(("x", "core"))
     node_count = group_rows * lax.axis_size(ROW)
-    back = [backward] + [rep_shift(backward, k) for k in range(1, reps)]
-    local, back[1] = lax.optimization_barrier((local, back[1]))
-    terms = to_all(local.reshape(plane, -1, hidden), PLANE)
-
-    spread = sum_and_spread(terms, line, BF16)
-    terms = to_all(spread, "z")
-    near_grad, other_grad, far_grad = window_gradient(kept, back)
+    near_grad, other_grad, far_grad, quarter = window_gradient(band, quarter, back)
+    terms = to_all(quarter.reshape(plane, -1, hidden), ("x", "core"))
     swapped = core_swap(other_grad)
     from_far = far_shift(far_grad)
+    terms = to_all(sum_and_spread(terms, line, BF16), "z")
     own_grad, before_grad, after_grad = chip_sum(near_grad, swapped)
     from_after = chip_shift(before_grad, -1)
     from_before = chip_shift(after_grad, 1)
     terms, from_far, _, _ = lax.optimization_barrier((terms, from_far, before_grad, after_grad))
-    terms = to_all(sum_and_spread(terms, plane, BF16, node_count ** (-0.5)), PLANE)
+    terms = to_all(sum_and_spread(terms, plane * reps, BF16, node_count ** (-0.5)), PLANE)
+    grad_features = total_gradient(own_grad, from_after, from_before, from_far)
+    terms, grad_features = lax.optimization_barrier((terms, grad_features))
     grad_weight = terms.reshape(hidden, hidden).astype(F32)
-    grad_features = total_gradient(own_grad, from_after, from_before, from_far)
     return output_rows, grad_weight, grad_features
 
 

time: 105 us -> 108 us (1.029)
  blocking collectives: 11.9 us -> 30.2 us
  starting transfers between devices: 64.8 us -> 49.4 us
  waiting for transfers between devices: 11.5 us -> 14.4 us
  Pallas kernels: 14.5 us -> 11.8 us
    all_to_all x1 -> x2, blocking collectives: 11.9 us -> 30.2 us  [to_all(): return lax.all_to_all(x, axes, 0, 0, tiled=False)]
    all_to_all x3 -> x2, starting transfers between devices: 29 us -> 11.3 us  [to_all(): return lax.all_to_all(x, axes, 0, 0, tiled=False)]
    ppermute x3, waiting for transfers between devices: 0.01 us -> 6.81 us  [rep_shift(): lax.ppermute(x, 'rep', [(i, (i - by) % devices) for i in range(devices)])]
    pallas_call x3 -> x4, Pallas kernels: 10.2 us -> 7.5 us  [the longest x2 5.28 us: dense_band(): pl.pallas_call(kernel, in_specs=specs, out_specs=pl.BlockSpec(memory_spac...]
    all_to_all x3 -> x2, waiting for transfers between devices: 10.2 us -> 7.59 us  [to_all(): return lax.all_to_all(x, axes, 0, 0, tiled=False)]
    ppermute x2, starting transfers between devices: 5.81 us -> 7.93 us  [core_swap(): return lax.ppermute(x, 'core', [(0, 1), (1, 0)])]
    ppermute x2, waiting for transfers between devices: 1.33 us -> 0.01 us  [core_swap(): return lax.ppermute(x, 'core', [(0, 1), (1, 0)])]
  transfers between devices with their start and end apart: 14 -> 13, of which waited for: 4 -> 4; matrix products, arithmetic and copies ran while one was open for 0% -> 0% of each run, Pallas kernels for 11% -> 7%
where the time goes in v5:
time: 108 us; the launch traced here: 107 us
  starting transfers between devices  49.4 us (46%)
  blocking collectives  30.2 us (28%)
  waiting for transfers between devices  14.4 us (13%)
  Pallas kernels  11.8 us (11%)
    all_to_all x2, blocking collectives, to_all(): return lax.all_to_all(x, axes, 0, 0, tiled=False)  30.2 us
    ppermute x2, starting transfers between devices, far_shift(): return lax.ppermute(x, ROW, pairs)  11.7 us
    all_to_all x2, starting transfers between devices, to_all(): return lax.all_to_all(x, axes, 0, 0, tiled=False)  11.3 us
    ppermute x4, starting transfers between devices, chip_shift(): lax.ppermute(x, ROW, [(i, i + by) for i in range(devices) if 0 <= i + by...  10.8 us
    ppermute x2, starting transfers between devices, core_swap(): return lax.ppermute(x, 'core', [(0, 1), (1, 0)])  7.93 us
    ppermute x3, starting transfers between devices, rep_shift(): lax.ppermute(x, 'rep', [(i, (i - by) % devices) for i in range(devices)])  7.8 us
    all_to_all x2, waiting for transfers between devices, to_all(): return lax.all_to_all(x, axes, 0, 0, tiled=False)  7.59 us
    ppermute x3, waiting for transfers between devices, rep_shift(): lax.ppermute(x, 'rep', [(i, (i - by) % devices) for i in range(devices)])  6.81 us
  transfers between devices with their start and end apart: 13, of which 4 were waited for; matrix products, arithmetic and copies ran while one was open for 0% of the time, Pallas kernels for 7%

profile of v5, /device:TPU:1, one launch (start us, length us, event | category | flops | bytes accessed | tf_op | source)
XLA Modules:
  0.0 107.5 jit_solution(12941698053916590736)
XLA Ops:
  0.6 0.9 own_quarter.1
  1.6 6.3 %collective-permute-start.2 = (bf16[256,256]{1,0:T(8,128)(2,1)S(1)}, bf16[256,256]{1,0:T(8,128)(2,1)S(1)}, u32[]{:S(2)}, u32[]{:S(2)}) collective-permute-start(bf16[256,256]{1,0:T(8,128)(2,1)S(1)} %own_quarter.1), channel_id=1, source_target_pairs={{4,16},{12,24},{16,4},{20,32},{24,12},{28,40},{32,20},{36,48},{40,... | collective-permute-start | bytes 393224 | tf_op jit(solution)/shard_map/ppermute | solution.py:46
  7.9 1.3 %collective-permute-start.1 = (bf16[256,256]{1,0:T(8,128)(2,1)S(1)}, bf16[256,256]{1,0:T(8,128)(2,1)S(1)}, u32[]{:S(2)}, u32[]{:S(2)}) collective-permute-start(bf16[256,256]{1,0:T(8,128)(2,1)S(1)} %own_quarter.1), channel_id=1, source_target_pairs={{8,0},{12,4},{16,8},{20,12},{24,16},{28,20},{32,24},{36,28},{40,32... | collective-permute-start | bytes 393224 | tf_op jit(solution)/shard_map/ppermute | solution.py:36
  9.2 4.2 %collective-permute-start = (bf16[256,256]{1,0:T(8,128)(2,1)S(1)}, bf16[256,256]{1,0:T(8,128)(2,1)S(1)}, u32[]{:S(2)}, u32[]{:S(2)}) collective-permute-start(bf16[256,256]{1,0:T(8,128)(2,1)S(1)} %own_quarter.1), channel_id=1, source_target_pairs={{0,8},{4,12},{8,16},{12,20},{16,24},{20,28},{24,32},{28,36},{32,40... | collective-permute-start | bytes 393224 | tf_op jit(solution)/shard_map/ppermute | solution.py:36
  13.3 2.6 %dense_band.2.refs_2_ = bf16[7,1024,256]{2,1,0:T(8,128)(2,1)S(1)} custom-call(s32[8,1,12]{2,1,0:T(1,128)} %refs_0_.3, bf16[8,12,128,128]{3,2,1,0:T(8,128)(2,1)} %bitcast.6), custom_call_target="tpu_custom_call" | custom-call | bytes 7200000 | tf_op jit(solution)/shard_map/dense_band/pallas_call | solution.py:130
  16.0 0.0 collective-permute-done.2.far_ref
  16.0 0.0 collective-permute-done.1
  16.0 0.0 collective-permute-done
  16.1 4.2 %collective-permute-start.3 = (bf16[768,256]{1,0:T(8,128)(2,1)S(1)}, bf16[768,256]{1,0:T(8,128)(2,1)S(1)}, u32[]{:S(2)}, u32[]{:S(2)}) collective-permute-start(bf16[768,256]{1,0:T(8,128)(2,1)S(1)} %pad_maximum_fusion.near_ref), channel_id=1, source_target_pairs={{0,4},{4,0},{1,5},{5,1},{2,6},{6,2},{3,7},{7,3},{8,12},{12,8},{9,1... | collective-permute-start | bytes 1179656 | tf_op jit(solution)/shard_map/ppermute | solution.py:50
  20.3 2.6 %dense_band.3.band_ref.refs_0_ = bf16[7,1024,256]{2,1,0:T(8,128)(2,1)S(1)} custom-call(s32[8,1,12]{2,1,0:T(1,128)} %refs_0_.3, bf16[8,12,128,128]{3,2,1,0:T(8,128)(2,1)} %bitcast.7, bf16[7,1024,256]{2,1,0:T(8,128)(2,1)S(1)} %dense_band.2.refs_2_), custom_call_target="tpu_custom_call", output_to_operand_aliasing={{}: (2, {})} | custom-call | bytes 7200000 | tf_op jit(solution)/shard_map/dense_band/pallas_call | solution.py:130
  22.9 0.0 copy-start
  22.9 0.0 copy-start.1
  23.0 0.0 collective-permute-done.3.other_ref
  23.0 1.1 %partial_aggregate.1 = bf16[4,256,256]{2,1,0:T(8,128)(2,1)S(1)} custom-call(bf16[7,1024,256]{2,1,0:T(8,128)(2,1)S(1)} %dense_band.3.band_ref.refs_0_, bf16[768,256]{1,0:T(8,128)(2,1)S(1)} %pad_maximum_fusion.near_ref, bf16[768,256]{1,0:T(8,128)(2,1)S(1)} %collective-permute-done.3.other_ref, bf16[256,256]{1,0:T(8,128)(2,1)S(1)} %collective-permute-done.2.far_ref), custom_call_target="tpu_custom_call" | custom-call | bytes 5400000 | tf_op jit(solution)/shard_map/partial_aggregate/pallas_call | solution.py:165
  24.1 11.7 %all_to_all.20.parts_ref = bf16[4,256,256]{2,1,0:T(8,128)(2,1)S(1)} all-to-all(bf16[4,256,256]{2,1,0:T(8,128)(2,1)S(1)} %partial_aggregate.1), channel_id=1, replica_groups=mesh['x'=4,'z'=16,'core'=2,'rep'=4] {'rep'}, dimensions={0} | all-to-all | bytes 1048576 | tf_op jit(solution)/shard_map/all_to_all | solution.py:59
  35.8 0.0 copy-done
  35.8 0.0 copy-done.1
  35.8 1.1 %dense_layer.1 = (bf16[256,256]{1,0:T(8,128)(2,1)}, bf16[256,256]{1,0:T(8,128)(2,1)S(1)}, f32[64,256]{1,0:T(8,128)S(1)}, bf16[320,256]{1,0:T(8,128)(2,1)S(1)}, b...) custom-call(bf16[4,256,256]{2,1,0:T(8,128)(2,1)S(1)} %all_to_all.20.parts_ref, bf16[256,256]{1,0:T(8,128)(2,1)S(1)} %copy-done, ...), custom_call_target="tpu_custom_call" | custom-call | bytes 4680000 | tf_op jit(solution)/shard_map/dense_layer/pallas_call | solution.py:213
  36.9 2.8 %collective-permute-start.4 = (bf16[320,256]{1,0:T(8,128)(2,1)S(1)}, bf16[320,256]{1,0:T(8,128)(2,1)S(1)}, u32[]{:S(2)}, u32[]{:S(2)}) collective-permute-start(bf16[320,256]{1,0:T(8,128)(2,1)S(1)} %get-tuple-element.35), channel_id=1, source_target_pairs={{0,3},{1,0},{2,1},{3,2},{4,7},{5,4},{6,5},{7,6},{8,11},{9,8},{10,9... | collective-permute-start | bytes 491528 | tf_op jit(solution)/shard_map/ppermute | solution.py:55
  39.7 3.1 %collective-permute-start.5 = (bf16[320,256]{1,0:T(8,128)(2,1)S(1)}, bf16[320,256]{1,0:T(8,128)(2,1)S(1)}, u32[]{:S(2)}, u32[]{:S(2)}) collective-permute-start(bf16[320,256]{1,0:T(8,128)(2,1)S(1)} %get-tuple-element.36), channel_id=1, source_target_pairs={{0,2},{1,3},{2,0},{3,1},{4,6},{5,7},{6,4},{7,5},{8,10},{9,11},{10,... | collective-permute-start | bytes 491528 | tf_op jit(solution)/shard_map/ppermute | solution.py:55
  42.8 1.9 %collective-permute-start.6 = (bf16[320,256]{1,0:T(8,128)(2,1)S(1)}, bf16[320,256]{1,0:T(8,128)(2,1)S(1)}, u32[]{:S(2)}, u32[]{:S(2)}) collective-permute-start(bf16[320,256]{1,0:T(8,128)(2,1)S(1)} %get-tuple-element.37), channel_id=1, source_target_pairs={{0,1},{1,2},{2,3},{3,0},{4,5},{5,6},{6,7},{7,4},{8,9},{9,10},{10,1... | collective-permute-start | bytes 491528 | tf_op jit(solution)/shard_map/ppermute | solution.py:55
  44.7 0.0 collective-permute-done.4.refs_3_
  44.7 2.5 %collective-permute-done.5.refs_4_ = bf16[320,256]{1,0:T(8,128)(2,1)S(1)} collective-permute-done((bf16[320,256]{1,0:T(8,128)(2,1)S(1)}, bf16[320,256]{1,0:T(8,128)(2,1)S(1)}, u32[]{:S(2)}, u32[]{:S(2)}) %collective-permute-start.5) | collective-permute-done | bytes 163872 | tf_op jit(solution)/shard_map/ppermute | solution.py:55
  47.2 4.3 %collective-permute-done.6.refs_5_ = bf16[320,256]{1,0:T(8,128)(2,1)S(1)} collective-permute-done((bf16[320,256]{1,0:T(8,128)(2,1)S(1)}, bf16[320,256]{1,0:T(8,128)(2,1)S(1)}, u32[]{:S(2)}, u32[]{:S(2)}) %collective-permute-start.6) | collective-permute-done | bytes 163872 | tf_op jit(solution)/shard_map/ppermute | solution.py:55
  51.5 1.1 %window_gradient.1 = (f32[768,256]{1,0:T(8,128)S(1)}, bf16[768,256]{1,0:T(8,128)(2,1)S(1)}, bf16[256,256]{1,0:T(8,128)(2,1)S(1)}, f32[64,256]{1,0:T(8,128)S(1)}) custom-call(bf16[7,1024,256]{2,1,0:T(8,128)(2,1)S(1)} %dense_band.3.band_ref.refs_0_, f32[64,256]{1,0:T(8,128)S(1)} %get-tuple-element.33.refs_1_, bf16[256,256]{1,0:T(8,128)(2,1)S(1)} %get-tuple-element.34.refs_2_, ...), custom_call_target="tpu_custom_call" | custom-call | bytes 7200000 | tf_op jit(solution)/shard_map/window_gradient/pallas_call | solution.py:260
  52.7 3.7 %collective-permute-start.8 = (bf16[768,256]{1,0:T(8,128)(2,1)S(1)}, bf16[768,256]{1,0:T(8,128)(2,1)S(1)}, u32[]{:S(2)}, u32[]{:S(2)}) collective-permute-start(bf16[768,256]{1,0:T(8,128)(2,1)S(1)} %get-tuple-element.41), channel_id=1, source_target_pairs={{0,4},{4,0},{1,5},{5,1},{2,6},{6,2},{3,7},{7,3},{8,12},{12,8},{9,1... | collective-permute-start | bytes 1179656 | tf_op jit(solution)/shard_map/ppermute | solution.py:50
  56.4 18.6 %all_to_all.21.refs_0_ = f32[8,8,256]{2,1,0:T(8,128)S(1)} all-to-all(f32[8,8,256]{2,1,0:T(8,128)S(1)} %bitcast.5), channel_id=1, replica_groups=mesh['x'=4,'z'=16,'core'=2,'rep'=4] {'x','core'}, dimensions={0} | all-to-all | bytes 131072 | tf_op jit(solution)/shard_map/all_to_all | solution.py:59
  74.9 0.6 sum_and_spread.2
  75.6 5.5 %all-to-all-start.2 = ((bf16[16,8,256]{2,1,0:T(8,128)(2,1)}), bf16[16,8,256]{2,1,0:T(8,128)(2,1)S(1)}, u32[]{:S(2)}, u32[]{:S(2)}) async-start(bf16[16,8,256]{2,1,0:T(8,128)(2,1)} %sum_and_spread.2), calls=%async_computation.2 | async-start | bytes 131072 | tf_op jit(solution)/shard_map/all_to_all | solution.py:59
  81.1 5.4 %collective-permute-start.7 = (bf16[256,256]{1,0:T(8,128)(2,1)S(1)}, bf16[256,256]{1,0:T(8,128)(2,1)S(1)}, u32[]{:S(2)}, u32[]{:S(2)}) collective-permute-start(bf16[256,256]{1,0:T(8,128)(2,1)S(1)} %get-tuple-element.39), channel_id=1, source_target_pairs={{4,16},{12,24},{16,4},{20,32},{24,12},{28,40},{32,20},{36,48},{40,... | collective-permute-start | bytes 393224 | tf_op jit(solution)/shard_map/ppermute | solution.py:46
  86.5 0.0 collective-permute-done.8.swapped_ref
  86.5 0.1 chip_sum.1
  86.6 1.3 %collective-permute-start.9 = (bf16[256,256]{1,0:T(8,128)(2,1)S(1)}, bf16[256,256]{1,0:T(8,128)(2,1)S(1)}, u32[]{:S(2)}, u32[]{:S(2)}) collective-permute-start(bf16[256,256]{1,0:T(8,128)(2,1)S(1)} %get-tuple-element.42), channel_id=1, source_target_pairs={{8,0},{12,4},{16,8},{20,12},{24,16},{28,20},{32,24},{36,28},{40,32... | collective-permute-start | bytes 393224 | tf_op jit(solution)/shard_map/ppermute | solution.py:36
  87.9 4.0 %collective-permute-start.10 = (bf16[256,256]{1,0:T(8,128)(2,1)S(1)}, bf16[256,256]{1,0:T(8,128)(2,1)S(1)}, u32[]{:S(2)}, u32[]{:S(2)}) collective-permute-start(bf16[256,256]{1,0:T(8,128)(2,1)S(1)} %get-tuple-element.43), channel_id=1, source_target_pairs={{0,8},{4,12},{8,16},{12,20},{16,24},{20,28},{24,32},{28,36},{32,40... | collective-permute-start | bytes 393224 | tf_op jit(solution)/shard_map/ppermute | solution.py:36
  91.9 0.0 collective-permute-done.7.far_ref
  91.9 0.8 all-to-all-done.2.refs_0_
  92.7 0.7 sum_and_spread.3
  93.3 5.8 %all-to-all-start.3 = ((bf16[32,8,256]{2,1,0:T(8,128)(2,1)}), bf16[32,8,256]{2,1,0:T(8,128)(2,1)S(1)}, u32[]{:S(2)}, u32[]{:S(2)}) async-start(bf16[32,8,256]{2,1,0:T(8,128)(2,1)} %sum_and_spread.3), calls=%async_computation.3 | async-start | bytes 262144 | tf_op jit(solution)/shard_map/all_to_all | solution.py:59
  99.1 0.0 collective-permute-done.9.after_ref
  99.1 0.0 collective-permute-done.10.before_ref
  99.1 0.8 total_gradient.1
  100.0 6.8 %all-to-all-done.3 = bf16[32,8,256]{2,1,0:T(8,128)(2,1)S(1)} async-done(((bf16[32,8,256]{2,1,0:T(8,128)(2,1)}), bf16[32,8,256]{2,1,0:T(8,128)(2,1)S(1)}, u32[]{:S(2)}, u32[]{:S(2)}) %all-to-all-start.3) | async-done | bytes 131104 | tf_op jit(solution)/shard_map/all_to_all | solution.py:59
  106.8 0.7 bitcast_convert_fusion
  (1 shorter events, 0.0 us)
Async XLA Ops:
  1.6 14.4 %collective-permute-start.2 = (bf16[256,256]{1,0:T(8,128)(2,1)S(1)}, bf16[256,256]{1,0:T(8,128)(2,1)S(1)}, u32[]{:S(2)}, u32[]{:S(2)}) collective-permute-start(bf16[256,256]{1,0:T(8,128)(2,1)S(1)} %own_quarter.1), channel_id=1, source_target_pairs={{4,16},{12,24},{16,4},{20,32},{24,12},{28,40},{32,20},{36,48},{40,... | collective-permute-start | bytes 393224 | tf_op jit(solution)/shard_map/ppermute | solution.py:46
  7.9 8.1 %collective-permute-start.1 = (bf16[256,256]{1,0:T(8,128)(2,1)S(1)}, bf16[256,256]{1,0:T(8,128)(2,1)S(1)}, u32[]{:S(2)}, u32[]{:S(2)}) collective-permute-start(bf16[256,256]{1,0:T(8,128)(2,1)S(1)} %own_quarter.1), channel_id=1, source_target_pairs={{8,0},{12,4},{16,8},{20,12},{24,16},{28,20},{32,24},{36,28},{40,32... | collective-permute-start | bytes 393224 | tf_op jit(solution)/shard_map/ppermute | solution.py:36
  9.2 6.9 %collective-permute-start = (bf16[256,256]{1,0:T(8,128)(2,1)S(1)}, bf16[256,256]{1,0:T(8,128)(2,1)S(1)}, u32[]{:S(2)}, u32[]{:S(2)}) collective-permute-start(bf16[256,256]{1,0:T(8,128)(2,1)S(1)} %own_quarter.1), channel_id=1, source_target_pairs={{0,8},{4,12},{8,16},{12,20},{16,24},{20,28},{24,32},{28,36},{32,40... | collective-permute-start | bytes 393224 | tf_op jit(solution)/shard_map/ppermute | solution.py:36
  16.1 6.9 %collective-permute-start.3 = (bf16[768,256]{1,0:T(8,128)(2,1)S(1)}, bf16[768,256]{1,0:T(8,128)(2,1)S(1)}, u32[]{:S(2)}, u32[]{:S(2)}) collective-permute-start(bf16[768,256]{1,0:T(8,128)(2,1)S(1)} %pad_maximum_fusion.near_ref), channel_id=1, source_target_pairs={{0,4},{4,0},{1,5},{5,1},{2,6},{6,2},{3,7},{7,3},{8,12},{12,8},{9,1... | collective-permute-start | bytes 1179656 | tf_op jit(solution)/shard_map/ppermute | solution.py:50
  22.9 12.8 %copy-start = (bf16[256,256]{1,0:T(8,128)(2,1)S(1)}, bf16[256,256]{1,0:T(8,128)(2,1)}, u32[]{:S(2)}) copy-start(bf16[256,256]{1,0:T(8,128)(2,1)} %weight_ref.1) | copy-start | bytes 393220
  22.9 12.8 %copy-start.1 = (bf16[256,256]{1,0:T(8,128)(2,1)S(1)}, bf16[256,256]{1,0:T(8,128)(2,1)}, u32[]{:S(2)}) copy-start(bf16[256,256]{1,0:T(8,128)(2,1)} %cotangent_ref.1) | copy-start | bytes 393220
  36.9 7.8 %collective-permute-start.4 = (bf16[320,256]{1,0:T(8,128)(2,1)S(1)}, bf16[320,256]{1,0:T(8,128)(2,1)S(1)}, u32[]{:S(2)}, u32[]{:S(2)}) collective-permute-start(bf16[320,256]{1,0:T(8,128)(2,1)S(1)} %get-tuple-element.35), channel_id=1, source_target_pairs={{0,3},{1,0},{2,1},{3,2},{4,7},{5,4},{6,5},{7,6},{8,11},{9,8},{10,9... | collective-permute-start | bytes 491528 | tf_op jit(solution)/shard_map/ppermute | solution.py:55
  39.7 7.6 %collective-permute-start.5 = (bf16[320,256]{1,0:T(8,128)(2,1)S(1)}, bf16[320,256]{1,0:T(8,128)(2,1)S(1)}, u32[]{:S(2)}, u32[]{:S(2)}) collective-permute-start(bf16[320,256]{1,0:T(8,128)(2,1)S(1)} %get-tuple-element.36), channel_id=1, source_target_pairs={{0,2},{1,3},{2,0},{3,1},{4,6},{5,7},{6,4},{7,5},{8,10},{9,11},{10,... | collective-permute-start | bytes 491528 | tf_op jit(solution)/shard_map/ppermute | solution.py:55
  42.8 8.7 %collective-permute-start.6 = (bf16[320,256]{1,0:T(8,128)(2,1)S(1)}, bf16[320,256]{1,0:T(8,128)(2,1)S(1)}, u32[]{:S(2)}, u32[]{:S(2)}) collective-permute-start(bf16[320,256]{1,0:T(8,128)(2,1)S(1)} %get-tuple-element.37), channel_id=1, source_target_pairs={{0,1},{1,2},{2,3},{3,0},{4,5},{5,6},{6,7},{7,4},{8,9},{9,10},{10,1... | collective-permute-start | bytes 491528 | tf_op jit(solution)/shard_map/ppermute | solution.py:55
  52.7 33.8 %collective-permute-start.8 = (bf16[768,256]{1,0:T(8,128)(2,1)S(1)}, bf16[768,256]{1,0:T(8,128)(2,1)S(1)}, u32[]{:S(2)}, u32[]{:S(2)}) collective-permute-start(bf16[768,256]{1,0:T(8,128)(2,1)S(1)} %get-tuple-element.41), channel_id=1, source_target_pairs={{0,4},{4,0},{1,5},{5,1},{2,6},{6,2},{3,7},{7,3},{8,12},{12,8},{9,1... | collective-permute-start | bytes 1179656 | tf_op jit(solution)/shard_map/ppermute | solution.py:50
  75.6 17.1 %all-to-all-start.2 = ((bf16[16,8,256]{2,1,0:T(8,128)(2,1)}), bf16[16,8,256]{2,1,0:T(8,128)(2,1)S(1)}, u32[]{:S(2)}, u32[]{:S(2)}) async-start(bf16[16,8,256]{2,1,0:T(8,128)(2,1)} %sum_and_spread.2), calls=%async_computation.2 | async-start | bytes 131072 | tf_op jit(solution)/shard_map/all_to_all | solution.py:59
  81.1 10.8 %collective-permute-start.7 = (bf16[256,256]{1,0:T(8,128)(2,1)S(1)}, bf16[256,256]{1,0:T(8,128)(2,1)S(1)}, u32[]{:S(2)}, u32[]{:S(2)}) collective-permute-start(bf16[256,256]{1,0:T(8,128)(2,1)S(1)} %get-tuple-element.39), channel_id=1, source_target_pairs={{4,16},{12,24},{16,4},{20,32},{24,12},{28,40},{32,20},{36,48},{40,... | collective-permute-start | bytes 393224 | tf_op jit(solution)/shard_map/ppermute | solution.py:46
  86.6 12.5 %collective-permute-start.9 = (bf16[256,256]{1,0:T(8,128)(2,1)S(1)}, bf16[256,256]{1,0:T(8,128)(2,1)S(1)}, u32[]{:S(2)}, u32[]{:S(2)}) collective-permute-start(bf16[256,256]{1,0:T(8,128)(2,1)S(1)} %get-tuple-element.42), channel_id=1, source_target_pairs={{8,0},{12,4},{16,8},{20,12},{24,16},{28,20},{32,24},{36,28},{40,32... | collective-permute-start | bytes 393224 | tf_op jit(solution)/shard_map/ppermute | solution.py:36
  87.9 11.3 %collective-permute-start.10 = (bf16[256,256]{1,0:T(8,128)(2,1)S(1)}, bf16[256,256]{1,0:T(8,128)(2,1)S(1)}, u32[]{:S(2)}, u32[]{:S(2)}) collective-permute-start(bf16[256,256]{1,0:T(8,128)(2,1)S(1)} %get-tuple-element.43), channel_id=1, source_target_pairs={{0,8},{4,12},{8,16},{12,20},{16,24},{20,28},{24,32},{28,36},{32,40... | collective-permute-start | bytes 393224 | tf_op jit(solution)/shard_map/ppermute | solution.py:36
  93.3 13.4 %all-to-all-start.3 = ((bf16[32,8,256]{2,1,0:T(8,128)(2,1)}), bf16[32,8,256]{2,1,0:T(8,128)(2,1)S(1)}, u32[]{:S(2)}, u32[]{:S(2)}) async-start(bf16[32,8,256]{2,1,0:T(8,128)(2,1)} %sum_and_spread.3), calls=%async_computation.3 | async-start | bytes 262144 | tf_op jit(solution)/shard_map/all_to_all | solution.py:59

commit v6 on v4

--- a/solution.py
+++ b/solution.py
@@ -80,7 +80,7 @@
     )(pltpu.with_memory_space_constraint(features, pltpu.HBM))
 
 
-def band_kernel(blocks_group, per_rep, cols_ref, vals_ref, out_ref, kept_ref, held, sums, arrived, left):
+def band_kernel(blocks_group, per_rep, cols_ref, vals_ref, out_ref, held, sums, arrived):
     blocks, slots, side = held.shape[:3]
     columns = sums.shape[0]
     group = lax.axis_index(ROW)
@@ -93,12 +93,8 @@
     def rows_of(block):
         return pl.ds(pl.multiple_of(block * side, side), side)
 
-    def keep(block):
-        at = rows_of(block)
-        return pltpu.make_async_copy(out_ref.at[:, at, :], kept_ref.at[:, at, :], left.at[block])
-
     for block in range(blocks):
-        fetch(block).start(priority=block % 2)
+        fetch(block).start()
 
     def step(block, carry):
         fetch(block).wait()
@@ -112,12 +108,9 @@
         for c in range(columns):
             lanes = slice(c % per_rep * side, (c % per_rep + 1) * side)
             out_ref[c // per_rep, rows_of(block), lanes] = sums[c].astype(BF16)
-        keep(block).start()
         return carry
 
     lax.fori_loop(0, blocks, step, 0)
-    for block in range(blocks):
-        keep(block).wait()
 
 
 def dense_band(cols, vals, blocks_group, per_rep):
@@ -131,12 +124,11 @@
     return pl.pallas_call(
         kernel,
         in_specs=[pl.BlockSpec(memory_space=pltpu.SMEM), pl.BlockSpec(memory_space=pltpu.HBM)],
-        out_specs=[pl.BlockSpec(memory_space=pltpu.VMEM), pl.BlockSpec(memory_space=pltpu.HBM)],
-        out_shape=[jax.ShapeDtypeStruct(shape, BF16), pltpu.HBM(shape, BF16)],
+        out_specs=pl.BlockSpec(memory_space=pltpu.VMEM),
+        out_shape=jax.ShapeDtypeStruct(shape, BF16),
         scratch_shapes=[
             pltpu.VMEM(vals.shape, BF16),
             pltpu.VMEM((columns, side, side), F32),
-            pltpu.SemaphoreType.DMA((blocks,)),
             pltpu.SemaphoreType.DMA((blocks,)),
         ],
         compiler_params=params(16),
@@ -216,8 +208,8 @@
         return pltpu.make_async_copy(band_ref.at[piece], held.at[piece], arrived.at[piece])
 
     order = [*range(HALF, 2 * HALF + 1), *range(HALF)]
-    for turn, piece in enumerate(order):
-        fetch(piece).start(priority=turn % 2)
+    for piece in order:
+        fetch(piece).start()
     for piece in order:
         fetch(piece).wait()
         total = jnp.zeros((hidden, rows), F32)
@@ -328,7 +320,7 @@
     before = chip_shift(own, 1)
     after = chip_shift(own, -1)
     far = far_shift(own)
-    band, kept = dense_band(block_cols, block_vals[:, 0], blocks_group, per_rep)
+    band = dense_band(block_cols, block_vals[:, 0], blocks_group, per_rep)
     before, after, far, band = lax.optimization_barrier((before, after, far, band))
 
     near = jnp.concatenate([own, before, after], axis=0)
@@ -345,7 +337,7 @@
 
     spread = sum_and_spread(terms, line, BF16)
     terms = to_all(spread, "z")
-    near_grad, other_grad, far_grad = window_gradient(kept, back)
+    near_grad, other_grad, far_grad = window_gradient(band, back)
     swapped = core_swap(other_grad)
     from_far = far_shift(far_grad)
     own_grad, before_grad, after_grad = chip_sum(near_grad, swapped)
@@ -353,8 +345,9 @@
     from_before = chip_shift(after_grad, 1)
     terms, from_far, _, _ = lax.optimization_barrier((terms, from_far, before_grad, after_grad))
     terms = to_all(sum_and_spread(terms, plane, BF16, node_count ** (-0.5)), PLANE)
+    grad_features = total_gradient(own_grad, from_after, from_before, from_far)
+    terms, grad_features = lax.optimization_barrier((terms, grad_features))
     grad_weight = terms.reshape(hidden, hidden).astype(F32)
-    grad_features = total_gradient(own_grad, from_after, from_before, from_far)
     return output_rows, grad_weight, grad_features
 
 

time: 105 us -> 107 us (1.019)
  starting transfers between devices: 64.8 us -> 66.5 us
  Pallas kernels: 14.5 us -> 13 us
  blocking collectives: 11.9 us -> 13 us
    all_to_all x3, starting transfers between devices: 29 us -> 31.4 us  [to_all(): return lax.all_to_all(x, axes, 0, 0, tiled=False)]
    pallas_call x1, Pallas kernels: 4.72 us -> 3.56 us  [dense_band(): pl.pallas_call(kernel, in_specs=[pl.BlockSpec(memory_space=pltpu.SMEM), p...]
    all_to_all x1, blocking collectives: 11.9 us -> 13 us  [to_all(): return lax.all_to_all(x, axes, 0, 0, tiled=False)]
    ppermute x2, starting transfers between devices: 5.81 us -> 4.71 us  [core_swap(): return lax.ppermute(x, 'core', [(0, 1), (1, 0)])]
  transfers between devices with their start and end apart: 14 -> 14, of which waited for: 4 -> 4; matrix products, arithmetic and copies ran while one was open for 0% -> 0% of each run, Pallas kernels for 11% -> 9%
where the time goes in v6:
time: 107 us; the launch traced here: 106 us
  starting transfers between devices  66.5 us (62%)
  Pallas kernels  13 us (12%)
  blocking collectives  13 us (12%)
  waiting for transfers between devices  11.8 us (11%)
    all_to_all x3, starting transfers between devices, to_all(): return lax.all_to_all(x, axes, 0, 0, tiled=False)  31.4 us
    all_to_all x1, blocking collectives, to_all(): return lax.all_to_all(x, axes, 0, 0, tiled=False)  13 us
    ppermute x2, starting transfers between devices, far_shift(): return lax.ppermute(x, ROW, pairs)  11.6 us
    ppermute x4, starting transfers between devices, chip_shift(): lax.ppermute(x, ROW, [(i, i + by) for i in range(devices) if 0 <= i + by...  11 us
    all_to_all x3, waiting for transfers between devices, to_all(): return lax.all_to_all(x, axes, 0, 0, tiled=False)  10.5 us
    ppermute x3, starting transfers between devices, rep_shift(): lax.ppermute(x, 'rep', [(i, (i - by) % devices) for i in range(devices)])  7.8 us
    ppermute x2, starting transfers between devices, core_swap(): return lax.ppermute(x, 'core', [(0, 1), (1, 0)])  4.71 us
    pallas_call x1, Pallas kernels, window_gradient(): pl.pallas_call(kernel, in_specs=[pl.BlockSpec(memory_space=pltpu.HBM)] +...  3.93 us
  transfers between devices with their start and end apart: 14, of which 4 were waited for; matrix products, arithmetic and copies ran while one was open for 0% of the time, Pallas kernels for 9%

profile of v6, /device:TPU:1, one launch (start us, length us, event | category | flops | bytes accessed | tf_op | source)
XLA Modules:
  0.0 106.0 jit_solution(4447329014347625652)
XLA Ops:
  0.6 0.9 own_quarter.1
  1.6 4.4 %collective-permute-start = (bf16[256,256]{1,0:T(8,128)(2,1)S(1)}, bf16[256,256]{1,0:T(8,128)(2,1)S(1)}, u32[]{:S(2)}, u32[]{:S(2)}) collective-permute-start(bf16[256,256]{1,0:T(8,128)(2,1)S(1)} %own_quarter.1), channel_id=1, source_target_pairs={{0,8},{4,12},{8,16},{12,20},{16,24},{20,28},{24,32},{28,36},{32,40... | collective-permute-start | bytes 393224 | tf_op jit(solution)/shard_map/ppermute | solution.py:36
  5.9 1.3 %collective-permute-start.1 = (bf16[256,256]{1,0:T(8,128)(2,1)S(1)}, bf16[256,256]{1,0:T(8,128)(2,1)S(1)}, u32[]{:S(2)}, u32[]{:S(2)}) collective-permute-start(bf16[256,256]{1,0:T(8,128)(2,1)S(1)} %own_quarter.1), channel_id=1, source_target_pairs={{8,0},{12,4},{16,8},{20,12},{24,16},{28,20},{32,24},{36,28},{40,32... | collective-permute-start | bytes 393224 | tf_op jit(solution)/shard_map/ppermute | solution.py:36
  7.2 6.5 %collective-permute-start.2 = (bf16[256,256]{1,0:T(8,128)(2,1)S(1)}, bf16[256,256]{1,0:T(8,128)(2,1)S(1)}, u32[]{:S(2)}, u32[]{:S(2)}) collective-permute-start(bf16[256,256]{1,0:T(8,128)(2,1)S(1)} %own_quarter.1), channel_id=1, source_target_pairs={{4,16},{12,24},{16,4},{20,32},{24,12},{28,40},{32,20},{36,48},{40,... | collective-permute-start | bytes 393224 | tf_op jit(solution)/shard_map/ppermute | solution.py:46
  13.7 3.6 %dense_band.1.band_ref.refs_0_ = bf16[7,1024,256]{2,1,0:T(8,128)(2,1)S(1)} custom-call(s32[8,1,12]{2,1,0:T(1,128)} %refs_0_.1, bf16[8,12,128,128]{3,2,1,0:T(8,128)(2,1)} %bitcast.5), custom_call_target="tpu_custom_call" | custom-call | bytes 14400000 | tf_op jit(solution)/shard_map/dense_band/pallas_call | solution.py:124
  17.3 0.0 copy-start
  17.3 0.0 copy-start.1
  17.3 0.0 copy-start.2
  17.3 0.0 collective-permute-done
  17.3 0.0 collective-permute-done.1
  17.3 0.0 collective-permute-done.2.far_ref
  17.4 2.6 %collective-permute-start.3 = (bf16[768,256]{1,0:T(8,128)(2,1)S(1)}, bf16[768,256]{1,0:T(8,128)(2,1)S(1)}, u32[]{:S(2)}, u32[]{:S(2)}) collective-permute-start(bf16[768,256]{1,0:T(8,128)(2,1)S(1)} %pad_maximum_fusion.near_ref), channel_id=1, source_target_pairs={{0,4},{4,0},{1,5},{5,1},{2,6},{6,2},{3,7},{7,3},{8,12},{12,8},{9,1... | collective-permute-start | bytes 1179656 | tf_op jit(solution)/shard_map/ppermute | solution.py:50
  20.0 1.3 %collective-permute-done.3.other_ref = bf16[768,256]{1,0:T(8,128)(2,1)S(1)} collective-permute-done((bf16[768,256]{1,0:T(8,128)(2,1)S(1)}, bf16[768,256]{1,0:T(8,128)(2,1)S(1)}, u32[]{:S(2)}, u32[]{:S(2)}) %collective-permute-start.3) | collective-permute-done | bytes 393248 | tf_op jit(solution)/shard_map/ppermute | solution.py:50
  21.3 1.1 %partial_aggregate.1 = bf16[4,256,256]{2,1,0:T(8,128)(2,1)S(1)} custom-call(bf16[7,1024,256]{2,1,0:T(8,128)(2,1)S(1)} %dense_band.1.band_ref.refs_0_, bf16[768,256]{1,0:T(8,128)(2,1)S(1)} %pad_maximum_fusion.near_ref, bf16[768,256]{1,0:T(8,128)(2,1)S(1)} %collective-permute-done.3.other_ref, bf16[256,256]{1,0:T(8,128)(2,1)S(1)} %collective-permute-done.2.far_ref), custom_call_target="tpu_custom_call" | custom-call | bytes 5400000 | tf_op jit(solution)/shard_map/partial_aggregate/pallas_call | solution.py:158
  22.4 13.0 %all_to_all.20.parts_ref = bf16[4,256,256]{2,1,0:T(8,128)(2,1)S(1)} all-to-all(bf16[4,256,256]{2,1,0:T(8,128)(2,1)S(1)} %partial_aggregate.1), channel_id=1, replica_groups=mesh['x'=4,'z'=16,'core'=2,'rep'=4] {'rep'}, dimensions={0} | all-to-all | bytes 1048576 | tf_op jit(solution)/shard_map/all_to_all | solution.py:59
  35.4 0.0 copy-done.1
  35.4 0.0 copy-done.2
  35.4 1.2 %dense_layer.1 = (bf16[256,256]{1,0:T(8,128)(2,1)}, bf16[256,256]{1,0:T(8,128)(2,1)S(1)}, f32[256,256]{1,0:T(8,128)}) custom-call(bf16[4,256,256]{2,1,0:T(8,128)(2,1)S(1)} %all_to_all.20.parts_ref, bf16[256,256]{1,0:T(8,128)(2,1)S(1)} %copy-done.1, bf16[256,256]{1,0:T(8,128)(2,1)S(1)} %copy-done.2), custom_call_target="tpu_custom_call" | custom-call | bytes 4680000 | tf_op jit(solution)/shard_map/dense_layer/pallas_call | solution.py:189
  36.6 0.0 copy-done
  36.6 2.8 %collective-permute-start.4 = (bf16[256,256]{1,0:T(8,128)(2,1)S(1)}, bf16[256,256]{1,0:T(8,128)(2,1)S(1)}, u32[]{:S(2)}, u32[]{:S(2)}) collective-permute-start(bf16[256,256]{1,0:T(8,128)(2,1)S(1)} %get-tuple-element.28.refs_1_), channel_id=1, source_target_pairs={{0,3},{1,0},{2,1},{3,2},{4,7},{5,4},{6,5},{7,6},{8,11},{9,8},{10,9... | collective-permute-start | bytes 393224 | tf_op jit(solution)/shard_map/ppermute | solution.py:55
  39.4 3.1 %collective-permute-start.5 = (bf16[256,256]{1,0:T(8,128)(2,1)S(1)}, bf16[256,256]{1,0:T(8,128)(2,1)S(1)}, u32[]{:S(2)}, u32[]{:S(2)}) collective-permute-start(bf16[256,256]{1,0:T(8,128)(2,1)S(1)} %get-tuple-element.28.refs_1_), channel_id=1, source_target_pairs={{0,2},{1,3},{2,0},{3,1},{4,6},{5,7},{6,4},{7,5},{8,10},{9,11},{10,... | collective-permute-start | bytes 393224 | tf_op jit(solution)/shard_map/ppermute | solution.py:55
  42.5 1.9 %collective-permute-start.6 = (bf16[256,256]{1,0:T(8,128)(2,1)S(1)}, bf16[256,256]{1,0:T(8,128)(2,1)S(1)}, u32[]{:S(2)}, u32[]{:S(2)}) collective-permute-start(bf16[256,256]{1,0:T(8,128)(2,1)S(1)} %get-tuple-element.28.refs_1_), channel_id=1, source_target_pairs={{0,1},{1,2},{2,3},{3,0},{4,5},{5,6},{6,7},{7,4},{8,9},{9,10},{10,1... | collective-permute-start | bytes 393224 | tf_op jit(solution)/shard_map/ppermute | solution.py:55
  44.4 0.0 collective-permute-done.4.refs_2_
  44.4 18.0 %all-to-all-start.1 = ((f32[32,8,256]{2,1,0:T(8,128)}), f32[32,8,256]{2,1,0:T(8,128)S(1)}, u32[]{:S(2)}, u32[]{:S(2)}) async-start(f32[32,8,256]{2,1,0:T(8,128)} %bitcast.1), calls=%async_computation.1 | async-start | bytes 524288 | tf_op jit(solution)/shard_map/all_to_all | solution.py:59
  62.4 0.0 collective-permute-done.5.refs_3_
  62.4 0.0 collective-permute-done.6.refs_4_
  62.4 3.9 %window_gradient.1 = (f32[768,256]{1,0:T(8,128)S(1)}, bf16[768,256]{1,0:T(8,128)(2,1)S(1)}, bf16[256,256]{1,0:T(8,128)(2,1)S(1)}) custom-call(bf16[7,1024,256]{2,1,0:T(8,128)(2,1)} %copy-done, bf16[256,256]{1,0:T(8,128)(2,1)S(1)} %get-tuple-element.28.refs_1_, bf16[256,256]{1,0:T(8,128)(2,1)S(1)} %collective-permute-done.4.refs_2_, ...), custom_call_target="tpu_custom_call" | custom-call | bytes 7200000 | tf_op jit(solution)/shard_map/window_gradient/pallas_call | solution.py:236
  66.4 2.1 %collective-permute-start.8 = (bf16[768,256]{1,0:T(8,128)(2,1)S(1)}, bf16[768,256]{1,0:T(8,128)(2,1)S(1)}, u32[]{:S(2)}, u32[]{:S(2)}) collective-permute-start(bf16[768,256]{1,0:T(8,128)(2,1)S(1)} %get-tuple-element.33), channel_id=1, source_target_pairs={{0,4},{4,0},{1,5},{5,1},{2,6},{6,2},{3,7},{7,3},{8,12},{12,8},{9,1... | collective-permute-start | bytes 1179656 | tf_op jit(solution)/shard_map/ppermute | solution.py:50
  68.5 2.7 %all-to-all-done.1.refs_0_ = f32[32,8,256]{2,1,0:T(8,128)S(1)} async-done(((f32[32,8,256]{2,1,0:T(8,128)}), f32[32,8,256]{2,1,0:T(8,128)S(1)}, u32[]{:S(2)}, u32[]{:S(2)}) %all-to-all-start.1) | async-done | bytes 262176 | tf_op jit(solution)/shard_map/all_to_all | solution.py:59
  71.2 0.7 sum_and_spread.2
  71.9 7.1 %all-to-all-start.2 = ((bf16[16,8,256]{2,1,0:T(8,128)(2,1)}), bf16[16,8,256]{2,1,0:T(8,128)(2,1)S(1)}, u32[]{:S(2)}, u32[]{:S(2)}) async-start(bf16[16,8,256]{2,1,0:T(8,128)(2,1)} %sum_and_spread.2), calls=%async_computation.2 | async-start | bytes 131072 | tf_op jit(solution)/shard_map/all_to_all | solution.py:59
  79.0 5.2 %collective-permute-start.7 = (bf16[256,256]{1,0:T(8,128)(2,1)S(1)}, bf16[256,256]{1,0:T(8,128)(2,1)S(1)}, u32[]{:S(2)}, u32[]{:S(2)}) collective-permute-start(bf16[256,256]{1,0:T(8,128)(2,1)S(1)} %get-tuple-element.31), channel_id=1, source_target_pairs={{4,16},{12,24},{16,4},{20,32},{24,12},{28,40},{32,20},{36,48},{40,... | collective-permute-start | bytes 393224 | tf_op jit(solution)/shard_map/ppermute | solution.py:46
  84.2 0.0 collective-permute-done.8.swapped_ref
  84.2 0.1 chip_sum.1
  84.2 1.3 %collective-permute-start.9 = (bf16[256,256]{1,0:T(8,128)(2,1)S(1)}, bf16[256,256]{1,0:T(8,128)(2,1)S(1)}, u32[]{:S(2)}, u32[]{:S(2)}) collective-permute-start(bf16[256,256]{1,0:T(8,128)(2,1)S(1)} %get-tuple-element.34), channel_id=1, source_target_pairs={{8,0},{12,4},{16,8},{20,12},{24,16},{28,20},{32,24},{36,28},{40,32... | collective-permute-start | bytes 393224 | tf_op jit(solution)/shard_map/ppermute | solution.py:36
  85.5 4.0 %collective-permute-start.10 = (bf16[256,256]{1,0:T(8,128)(2,1)S(1)}, bf16[256,256]{1,0:T(8,128)(2,1)S(1)}, u32[]{:S(2)}, u32[]{:S(2)}) collective-permute-start(bf16[256,256]{1,0:T(8,128)(2,1)S(1)} %get-tuple-element.35), channel_id=1, source_target_pairs={{0,8},{4,12},{8,16},{12,20},{16,24},{20,28},{24,32},{28,36},{32,40... | collective-permute-start | bytes 393224 | tf_op jit(solution)/shard_map/ppermute | solution.py:36
  89.5 0.0 collective-permute-done.7.far_ref
  89.6 1.1 %all-to-all-done.2.refs_0_ = bf16[16,8,256]{2,1,0:T(8,128)(2,1)S(1)} async-done(((bf16[16,8,256]{2,1,0:T(8,128)(2,1)}), bf16[16,8,256]{2,1,0:T(8,128)(2,1)S(1)}, u32[]{:S(2)}, u32[]{:S(2)}) %all-to-all-start.2) | async-done | bytes 65568 | tf_op jit(solution)/shard_map/all_to_all | solution.py:59
  90.6 0.7 sum_and_spread.3
  91.3 6.4 %all-to-all-start.3 = ((bf16[32,8,256]{2,1,0:T(8,128)(2,1)}), bf16[32,8,256]{2,1,0:T(8,128)(2,1)S(1)}, u32[]{:S(2)}, u32[]{:S(2)}) async-start(bf16[32,8,256]{2,1,0:T(8,128)(2,1)} %sum_and_spread.3), calls=%async_computation.3 | async-start | bytes 262144 | tf_op jit(solution)/shard_map/all_to_all | solution.py:59
  97.7 0.0 collective-permute-done.9.after_ref
  97.7 0.0 collective-permute-done.10.before_ref
  97.7 0.8 total_gradient.1
  98.6 6.7 %all-to-all-done.3 = bf16[32,8,256]{2,1,0:T(8,128)(2,1)S(1)} async-done(((bf16[32,8,256]{2,1,0:T(8,128)(2,1)}), bf16[32,8,256]{2,1,0:T(8,128)(2,1)S(1)}, u32[]{:S(2)}, u32[]{:S(2)}) %all-to-all-start.3) | async-done | bytes 131104 | tf_op jit(solution)/shard_map/all_to_all | solution.py:59
  105.3 0.7 bitcast_convert_fusion
  (1 shorter events, 0.0 us)
Async XLA Ops:
  1.6 15.8 %collective-permute-start = (bf16[256,256]{1,0:T(8,128)(2,1)S(1)}, bf16[256,256]{1,0:T(8,128)(2,1)S(1)}, u32[]{:S(2)}, u32[]{:S(2)}) collective-permute-start(bf16[256,256]{1,0:T(8,128)(2,1)S(1)} %own_quarter.1), channel_id=1, source_target_pairs={{0,8},{4,12},{8,16},{12,20},{16,24},{20,28},{24,32},{28,36},{32,40... | collective-permute-start | bytes 393224 | tf_op jit(solution)/shard_map/ppermute | solution.py:36
  5.9 11.4 %collective-permute-start.1 = (bf16[256,256]{1,0:T(8,128)(2,1)S(1)}, bf16[256,256]{1,0:T(8,128)(2,1)S(1)}, u32[]{:S(2)}, u32[]{:S(2)}) collective-permute-start(bf16[256,256]{1,0:T(8,128)(2,1)S(1)} %own_quarter.1), channel_id=1, source_target_pairs={{8,0},{12,4},{16,8},{20,12},{24,16},{28,20},{32,24},{36,28},{40,32... | collective-permute-start | bytes 393224 | tf_op jit(solution)/shard_map/ppermute | solution.py:36
  7.2 10.1 %collective-permute-start.2 = (bf16[256,256]{1,0:T(8,128)(2,1)S(1)}, bf16[256,256]{1,0:T(8,128)(2,1)S(1)}, u32[]{:S(2)}, u32[]{:S(2)}) collective-permute-start(bf16[256,256]{1,0:T(8,128)(2,1)S(1)} %own_quarter.1), channel_id=1, source_target_pairs={{4,16},{12,24},{16,4},{20,32},{24,12},{28,40},{32,20},{36,48},{40,... | collective-permute-start | bytes 393224 | tf_op jit(solution)/shard_map/ppermute | solution.py:46
  17.3 19.3 %copy-start = (bf16[7,1024,256]{2,1,0:T(8,128)(2,1)}, bf16[7,1024,256]{2,1,0:T(8,128)(2,1)S(1)}, u32[]{:S(2)}) copy-start(bf16[7,1024,256]{2,1,0:T(8,128)(2,1)S(1)} %dense_band.1.band_ref.refs_0_) | copy-start | bytes 11010052
  17.3 18.1 %copy-start.1 = (bf16[256,256]{1,0:T(8,128)(2,1)S(1)}, bf16[256,256]{1,0:T(8,128)(2,1)}, u32[]{:S(2)}) copy-start(bf16[256,256]{1,0:T(8,128)(2,1)} %weight_ref.1) | copy-start | bytes 393220
  17.3 18.1 %copy-start.2 = (bf16[256,256]{1,0:T(8,128)(2,1)S(1)}, bf16[256,256]{1,0:T(8,128)(2,1)}, u32[]{:S(2)}) copy-start(bf16[256,256]{1,0:T(8,128)(2,1)} %cotangent_ref.1) | copy-start | bytes 393220
  17.4 3.9 %collective-permute-start.3 = (bf16[768,256]{1,0:T(8,128)(2,1)S(1)}, bf16[768,256]{1,0:T(8,128)(2,1)S(1)}, u32[]{:S(2)}, u32[]{:S(2)}) collective-permute-start(bf16[768,256]{1,0:T(8,128)(2,1)S(1)} %pad_maximum_fusion.near_ref), channel_id=1, source_target_pairs={{0,4},{4,0},{1,5},{5,1},{2,6},{6,2},{3,7},{7,3},{8,12},{12,8},{9,1... | collective-permute-start | bytes 1179656 | tf_op jit(solution)/shard_map/ppermute | solution.py:50
  36.6 7.8 %collective-permute-start.4 = (bf16[256,256]{1,0:T(8,128)(2,1)S(1)}, bf16[256,256]{1,0:T(8,128)(2,1)S(1)}, u32[]{:S(2)}, u32[]{:S(2)}) collective-permute-start(bf16[256,256]{1,0:T(8,128)(2,1)S(1)} %get-tuple-element.28.refs_1_), channel_id=1, source_target_pairs={{0,3},{1,0},{2,1},{3,2},{4,7},{5,4},{6,5},{7,6},{8,11},{9,8},{10,9... | collective-permute-start | bytes 393224 | tf_op jit(solution)/shard_map/ppermute | solution.py:55
  39.4 23.0 %collective-permute-start.5 = (bf16[256,256]{1,0:T(8,128)(2,1)S(1)}, bf16[256,256]{1,0:T(8,128)(2,1)S(1)}, u32[]{:S(2)}, u32[]{:S(2)}) collective-permute-start(bf16[256,256]{1,0:T(8,128)(2,1)S(1)} %get-tuple-element.28.refs_1_), channel_id=1, source_target_pairs={{0,2},{1,3},{2,0},{3,1},{4,6},{5,7},{6,4},{7,5},{8,10},{9,11},{10,... | collective-permute-start | bytes 393224 | tf_op jit(solution)/shard_map/ppermute | solution.py:55
  42.5 19.9 %collective-permute-start.6 = (bf16[256,256]{1,0:T(8,128)(2,1)S(1)}, bf16[256,256]{1,0:T(8,128)(2,1)S(1)}, u32[]{:S(2)}, u32[]{:S(2)}) collective-permute-start(bf16[256,256]{1,0:T(8,128)(2,1)S(1)} %get-tuple-element.28.refs_1_), channel_id=1, source_target_pairs={{0,1},{1,2},{2,3},{3,0},{4,5},{5,6},{6,7},{7,4},{8,9},{9,10},{10,1... | collective-permute-start | bytes 393224 | tf_op jit(solution)/shard_map/ppermute | solution.py:55
  44.4 26.8 %all-to-all-start.1 = ((f32[32,8,256]{2,1,0:T(8,128)}), f32[32,8,256]{2,1,0:T(8,128)S(1)}, u32[]{:S(2)}, u32[]{:S(2)}) async-start(f32[32,8,256]{2,1,0:T(8,128)} %bitcast.1), calls=%async_computation.1 | async-start | bytes 524288 | tf_op jit(solution)/shard_map/all_to_all | solution.py:59
  66.4 17.8 %collective-permute-start.8 = (bf16[768,256]{1,0:T(8,128)(2,1)S(1)}, bf16[768,256]{1,0:T(8,128)(2,1)S(1)}, u32[]{:S(2)}, u32[]{:S(2)}) collective-permute-start(bf16[768,256]{1,0:T(8,128)(2,1)S(1)} %get-tuple-element.33), channel_id=1, source_target_pairs={{0,4},{4,0},{1,5},{5,1},{2,6},{6,2},{3,7},{7,3},{8,12},{12,8},{9,1... | collective-permute-start | bytes 1179656 | tf_op jit(solution)/shard_map/ppermute | solution.py:50
  71.9 18.8 %all-to-all-start.2 = ((bf16[16,8,256]{2,1,0:T(8,128)(2,1)}), bf16[16,8,256]{2,1,0:T(8,128)(2,1)S(1)}, u32[]{:S(2)}, u32[]{:S(2)}) async-start(bf16[16,8,256]{2,1,0:T(8,128)(2,1)} %sum_and_spread.2), calls=%async_computation.2 | async-start | bytes 131072 | tf_op jit(solution)/shard_map/all_to_all | solution.py:59
  79.0 10.6 %collective-permute-start.7 = (bf16[256,256]{1,0:T(8,128)(2,1)S(1)}, bf16[256,256]{1,0:T(8,128)(2,1)S(1)}, u32[]{:S(2)}, u32[]{:S(2)}) collective-permute-start(bf16[256,256]{1,0:T(8,128)(2,1)S(1)} %get-tuple-element.31), channel_id=1, source_target_pairs={{4,16},{12,24},{16,4},{20,32},{24,12},{28,40},{32,20},{36,48},{40,... | collective-permute-start | bytes 393224 | tf_op jit(solution)/shard_map/ppermute | solution.py:46
  84.2 13.5 %collective-permute-start.9 = (bf16[256,256]{1,0:T(8,128)(2,1)S(1)}, bf16[256,256]{1,0:T(8,128)(2,1)S(1)}, u32[]{:S(2)}, u32[]{:S(2)}) collective-permute-start(bf16[256,256]{1,0:T(8,128)(2,1)S(1)} %get-tuple-element.34), channel_id=1, source_target_pairs={{8,0},{12,4},{16,8},{20,12},{24,16},{28,20},{32,24},{36,28},{40,32... | collective-permute-start | bytes 393224 | tf_op jit(solution)/shard_map/ppermute | solution.py:36
  85.5 12.2 %collective-permute-start.10 = (bf16[256,256]{1,0:T(8,128)(2,1)S(1)}, bf16[256,256]{1,0:T(8,128)(2,1)S(1)}, u32[]{:S(2)}, u32[]{:S(2)}) collective-permute-start(bf16[256,256]{1,0:T(8,128)(2,1)S(1)} %get-tuple-element.35), channel_id=1, source_target_pairs={{0,8},{4,12},{8,16},{12,20},{16,24},{20,28},{24,32},{28,36},{32,40... | collective-permute-start | bytes 393224 | tf_op jit(solution)/shard_map/ppermute | solution.py:36
  91.3 14.0 %all-to-all-start.3 = ((bf16[32,8,256]{2,1,0:T(8,128)(2,1)}), bf16[32,8,256]{2,1,0:T(8,128)(2,1)S(1)}, u32[]{:S(2)}, u32[]{:S(2)}) async-start(bf16[32,8,256]{2,1,0:T(8,128)(2,1)} %sum_and_spread.3), calls=%async_computation.3 | async-start | bytes 262144 | tf_op jit(solution)/shard_map/all_to_all | solution.py:59

commit v7 on v6

--- a/solution.py
+++ b/solution.py
@@ -321,7 +321,7 @@
     after = chip_shift(own, -1)
     far = far_shift(own)
     band = dense_band(block_cols, block_vals[:, 0], blocks_group, per_rep)
-    before, after, far, band = lax.optimization_barrier((before, after, far, band))
+    far, after, before, band = lax.optimization_barrier((far, after, before, band))
 
     near = jnp.concatenate([own, before, after], axis=0)
     other = core_swap(near)

time: 107 us -> 105 us (0.981)
  blocking collectives: 13 us -> 11.9 us
    ppermute x2, starting transfers between devices: 4.71 us -> 5.82 us  [core_swap(): return lax.ppermute(x, 'core', [(0, 1), (1, 0)])]
    all_to_all x1, blocking collectives: 13 us -> 11.9 us  [to_all(): return lax.all_to_all(x, axes, 0, 0, tiled=False)]
    all_to_all x3, starting transfers between devices: 31.4 us -> 30.3 us  [to_all(): return lax.all_to_all(x, axes, 0, 0, tiled=False)]
where the time goes in v7:
time: 105 us
  starting transfers between devices  66.2 us (63%)
  Pallas kernels  13 us (12%)
  blocking collectives  11.9 us (11%)
  waiting for transfers between devices  11.8 us (11%)
    all_to_all x3, starting transfers between devices, to_all(): return lax.all_to_all(x, axes, 0, 0, tiled=False)  30.3 us
    all_to_all x1, blocking collectives, to_all(): return lax.all_to_all(x, axes, 0, 0, tiled=False)  11.9 us
    ppermute x2, starting transfers between devices, far_shift(): return lax.ppermute(x, ROW, pairs)  11.5 us
    ppermute x4, starting transfers between devices, chip_shift(): lax.ppermute(x, ROW, [(i, i + by) for i in range(devices) if 0 <= i + by...  10.8 us
    all_to_all x3, waiting for transfers between devices, to_all(): return lax.all_to_all(x, axes, 0, 0, tiled=False)  10.5 us
    ppermute x3, starting transfers between devices, rep_shift(): lax.ppermute(x, 'rep', [(i, (i - by) % devices) for i in range(devices)])  7.8 us
    ppermute x2, starting transfers between devices, core_swap(): return lax.ppermute(x, 'core', [(0, 1), (1, 0)])  5.82 us
    pallas_call x1, Pallas kernels, window_gradient(): pl.pallas_call(kernel, in_specs=[pl.BlockSpec(memory_space=pltpu.HBM)] +...  3.93 us
  transfers between devices with their start and end apart: 14, of which 4 were waited for; matrix products, arithmetic and copies ran while one was open for 0% of the time, Pallas kernels for 9%

profile of v7, /device:TPU:1, one launch (start us, length us, event | category | flops | bytes accessed | tf_op | source)
XLA Modules:
  0.0 104.6 jit_solution(11172878841163275879)
XLA Ops:
  0.6 0.9 own_quarter.1
  1.6 6.3 %collective-permute-start = (bf16[256,256]{1,0:T(8,128)(2,1)S(1)}, bf16[256,256]{1,0:T(8,128)(2,1)S(1)}, u32[]{:S(2)}, u32[]{:S(2)}) collective-permute-start(bf16[256,256]{1,0:T(8,128)(2,1)S(1)} %own_quarter.1), channel_id=1, source_target_pairs={{4,16},{12,24},{16,4},{20,32},{24,12},{28,40},{32,20},{36,48},{40,... | collective-permute-start | bytes 393224 | tf_op jit(solution)/shard_map/ppermute | solution.py:46
  7.9 1.3 %collective-permute-start.1 = (bf16[256,256]{1,0:T(8,128)(2,1)S(1)}, bf16[256,256]{1,0:T(8,128)(2,1)S(1)}, u32[]{:S(2)}, u32[]{:S(2)}) collective-permute-start(bf16[256,256]{1,0:T(8,128)(2,1)S(1)} %own_quarter.1), channel_id=1, source_target_pairs={{8,0},{12,4},{16,8},{20,12},{24,16},{28,20},{32,24},{36,28},{40,32... | collective-permute-start | bytes 393224 | tf_op jit(solution)/shard_map/ppermute | solution.py:36
  9.2 4.2 %collective-permute-start.2 = (bf16[256,256]{1,0:T(8,128)(2,1)S(1)}, bf16[256,256]{1,0:T(8,128)(2,1)S(1)}, u32[]{:S(2)}, u32[]{:S(2)}) collective-permute-start(bf16[256,256]{1,0:T(8,128)(2,1)S(1)} %own_quarter.1), channel_id=1, source_target_pairs={{0,8},{4,12},{8,16},{12,20},{16,24},{20,28},{24,32},{28,36},{32,40... | collective-permute-start | bytes 393224 | tf_op jit(solution)/shard_map/ppermute | solution.py:36
  13.3 3.6 %dense_band.1.band_ref.refs_0_ = bf16[7,1024,256]{2,1,0:T(8,128)(2,1)S(1)} custom-call(s32[8,1,12]{2,1,0:T(1,128)} %refs_0_.1, bf16[8,12,128,128]{3,2,1,0:T(8,128)(2,1)} %bitcast.5), custom_call_target="tpu_custom_call" | custom-call | bytes 14400000 | tf_op jit(solution)/shard_map/dense_band/pallas_call | solution.py:124
  16.9 0.0 copy-start
  16.9 0.0 copy-start.1
  16.9 0.0 copy-start.2
  17.0 0.0 collective-permute-done.far_ref
  17.0 0.0 collective-permute-done.1
  17.0 0.0 collective-permute-done.2
  17.0 3.7 %collective-permute-start.3 = (bf16[768,256]{1,0:T(8,128)(2,1)S(1)}, bf16[768,256]{1,0:T(8,128)(2,1)S(1)}, u32[]{:S(2)}, u32[]{:S(2)}) collective-permute-start(bf16[768,256]{1,0:T(8,128)(2,1)S(1)} %pad_maximum_fusion.near_ref), channel_id=1, source_target_pairs={{0,4},{4,0},{1,5},{5,1},{2,6},{6,2},{3,7},{7,3},{8,12},{12,8},{9,1... | collective-permute-start | bytes 1179656 | tf_op jit(solution)/shard_map/ppermute | solution.py:50
  20.7 1.3 %collective-permute-done.3.other_ref = bf16[768,256]{1,0:T(8,128)(2,1)S(1)} collective-permute-done((bf16[768,256]{1,0:T(8,128)(2,1)S(1)}, bf16[768,256]{1,0:T(8,128)(2,1)S(1)}, u32[]{:S(2)}, u32[]{:S(2)}) %collective-permute-start.3) | collective-permute-done | bytes 393248 | tf_op jit(solution)/shard_map/ppermute | solution.py:50
  22.0 1.1 %partial_aggregate.1 = bf16[4,256,256]{2,1,0:T(8,128)(2,1)S(1)} custom-call(bf16[7,1024,256]{2,1,0:T(8,128)(2,1)S(1)} %dense_band.1.band_ref.refs_0_, bf16[768,256]{1,0:T(8,128)(2,1)S(1)} %pad_maximum_fusion.near_ref, bf16[768,256]{1,0:T(8,128)(2,1)S(1)} %collective-permute-done.3.other_ref, bf16[256,256]{1,0:T(8,128)(2,1)S(1)} %collective-permute-done.far_ref), custom_call_target="tpu_custom_call" | custom-call | bytes 5400000 | tf_op jit(solution)/shard_map/partial_aggregate/pallas_call | solution.py:158
  23.1 11.9 %all_to_all.20.parts_ref = bf16[4,256,256]{2,1,0:T(8,128)(2,1)S(1)} all-to-all(bf16[4,256,256]{2,1,0:T(8,128)(2,1)S(1)} %partial_aggregate.1), channel_id=1, replica_groups=mesh['x'=4,'z'=16,'core'=2,'rep'=4] {'rep'}, dimensions={0} | all-to-all | bytes 1048576 | tf_op jit(solution)/shard_map/all_to_all | solution.py:59
  35.0 0.0 copy-done.1
  35.0 0.0 copy-done.2
  35.0 1.2 %dense_layer.1 = (bf16[256,256]{1,0:T(8,128)(2,1)}, bf16[256,256]{1,0:T(8,128)(2,1)S(1)}, f32[256,256]{1,0:T(8,128)}) custom-call(bf16[4,256,256]{2,1,0:T(8,128)(2,1)S(1)} %all_to_all.20.parts_ref, bf16[256,256]{1,0:T(8,128)(2,1)S(1)} %copy-done.1, bf16[256,256]{1,0:T(8,128)(2,1)S(1)} %copy-done.2), custom_call_target="tpu_custom_call" | custom-call | bytes 4680000 | tf_op jit(solution)/shard_map/dense_layer/pallas_call | solution.py:189
  36.2 0.0 copy-done
  36.2 2.8 %collective-permute-start.4 = (bf16[256,256]{1,0:T(8,128)(2,1)S(1)}, bf16[256,256]{1,0:T(8,128)(2,1)S(1)}, u32[]{:S(2)}, u32[]{:S(2)}) collective-permute-start(bf16[256,256]{1,0:T(8,128)(2,1)S(1)} %get-tuple-element.28.refs_1_), channel_id=1, source_target_pairs={{0,3},{1,0},{2,1},{3,2},{4,7},{5,4},{6,5},{7,6},{8,11},{9,8},{10,9... | collective-permute-start | bytes 393224 | tf_op jit(solution)/shard_map/ppermute | solution.py:55
  39.0 3.1 %collective-permute-start.5 = (bf16[256,256]{1,0:T(8,128)(2,1)S(1)}, bf16[256,256]{1,0:T(8,128)(2,1)S(1)}, u32[]{:S(2)}, u32[]{:S(2)}) collective-permute-start(bf16[256,256]{1,0:T(8,128)(2,1)S(1)} %get-tuple-element.28.refs_1_), channel_id=1, source_target_pairs={{0,2},{1,3},{2,0},{3,1},{4,6},{5,7},{6,4},{7,5},{8,10},{9,11},{10,... | collective-permute-start | bytes 393224 | tf_op jit(solution)/shard_map/ppermute | solution.py:55
  42.1 1.9 %collective-permute-start.6 = (bf16[256,256]{1,0:T(8,128)(2,1)S(1)}, bf16[256,256]{1,0:T(8,128)(2,1)S(1)}, u32[]{:S(2)}, u32[]{:S(2)}) collective-permute-start(bf16[256,256]{1,0:T(8,128)(2,1)S(1)} %get-tuple-element.28.refs_1_), channel_id=1, source_target_pairs={{0,1},{1,2},{2,3},{3,0},{4,5},{5,6},{6,7},{7,4},{8,9},{9,10},{10,1... | collective-permute-start | bytes 393224 | tf_op jit(solution)/shard_map/ppermute | solution.py:55
  44.1 0.0 collective-permute-done.4.refs_2_
  44.1 18.0 %all-to-all-start.1 = ((f32[32,8,256]{2,1,0:T(8,128)}), f32[32,8,256]{2,1,0:T(8,128)S(1)}, u32[]{:S(2)}, u32[]{:S(2)}) async-start(f32[32,8,256]{2,1,0:T(8,128)} %bitcast.1), calls=%async_computation.1 | async-start | bytes 524288 | tf_op jit(solution)/shard_map/all_to_all | solution.py:59
  62.1 0.0 collective-permute-done.5.refs_3_
  62.1 0.0 collective-permute-done.6.refs_4_
  62.1 3.9 %window_gradient.1 = (f32[768,256]{1,0:T(8,128)S(1)}, bf16[768,256]{1,0:T(8,128)(2,1)S(1)}, bf16[256,256]{1,0:T(8,128)(2,1)S(1)}) custom-call(bf16[7,1024,256]{2,1,0:T(8,128)(2,1)} %copy-done, bf16[256,256]{1,0:T(8,128)(2,1)S(1)} %get-tuple-element.28.refs_1_, bf16[256,256]{1,0:T(8,128)(2,1)S(1)} %collective-permute-done.4.refs_2_, ...), custom_call_target="tpu_custom_call" | custom-call | bytes 7200000 | tf_op jit(solution)/shard_map/window_gradient/pallas_call | solution.py:236
  66.0 2.1 %collective-permute-start.8 = (bf16[768,256]{1,0:T(8,128)(2,1)S(1)}, bf16[768,256]{1,0:T(8,128)(2,1)S(1)}, u32[]{:S(2)}, u32[]{:S(2)}) collective-permute-start(bf16[768,256]{1,0:T(8,128)(2,1)S(1)} %get-tuple-element.33), channel_id=1, source_target_pairs={{0,4},{4,0},{1,5},{5,1},{2,6},{6,2},{3,7},{7,3},{8,12},{12,8},{9,1... | collective-permute-start | bytes 1179656 | tf_op jit(solution)/shard_map/ppermute | solution.py:50
  68.2 2.7 %all-to-all-done.1.refs_0_ = f32[32,8,256]{2,1,0:T(8,128)S(1)} async-done(((f32[32,8,256]{2,1,0:T(8,128)}), f32[32,8,256]{2,1,0:T(8,128)S(1)}, u32[]{:S(2)}, u32[]{:S(2)}) %all-to-all-start.1) | async-done | bytes 262176 | tf_op jit(solution)/shard_map/all_to_all | solution.py:59
  70.9 0.7 sum_and_spread.2
  71.6 5.9 %all-to-all-start.2 = ((bf16[16,8,256]{2,1,0:T(8,128)(2,1)}), bf16[16,8,256]{2,1,0:T(8,128)(2,1)S(1)}, u32[]{:S(2)}, u32[]{:S(2)}) async-start(bf16[16,8,256]{2,1,0:T(8,128)(2,1)} %sum_and_spread.2), calls=%async_computation.2 | async-start | bytes 131072 | tf_op jit(solution)/shard_map/all_to_all | solution.py:59
  77.4 5.2 %collective-permute-start.7 = (bf16[256,256]{1,0:T(8,128)(2,1)S(1)}, bf16[256,256]{1,0:T(8,128)(2,1)S(1)}, u32[]{:S(2)}, u32[]{:S(2)}) collective-permute-start(bf16[256,256]{1,0:T(8,128)(2,1)S(1)} %get-tuple-element.31), channel_id=1, source_target_pairs={{4,16},{12,24},{16,4},{20,32},{24,12},{28,40},{32,20},{36,48},{40,... | collective-permute-start | bytes 393224 | tf_op jit(solution)/shard_map/ppermute | solution.py:46
  82.6 0.0 collective-permute-done.8.swapped_ref
  82.6 0.1 chip_sum.1
  82.7 1.3 %collective-permute-start.9 = (bf16[256,256]{1,0:T(8,128)(2,1)S(1)}, bf16[256,256]{1,0:T(8,128)(2,1)S(1)}, u32[]{:S(2)}, u32[]{:S(2)}) collective-permute-start(bf16[256,256]{1,0:T(8,128)(2,1)S(1)} %get-tuple-element.34), channel_id=1, source_target_pairs={{8,0},{12,4},{16,8},{20,12},{24,16},{28,20},{32,24},{36,28},{40,32... | collective-permute-start | bytes 393224 | tf_op jit(solution)/shard_map/ppermute | solution.py:36
  84.0 4.0 %collective-permute-start.10 = (bf16[256,256]{1,0:T(8,128)(2,1)S(1)}, bf16[256,256]{1,0:T(8,128)(2,1)S(1)}, u32[]{:S(2)}, u32[]{:S(2)}) collective-permute-start(bf16[256,256]{1,0:T(8,128)(2,1)S(1)} %get-tuple-element.35), channel_id=1, source_target_pairs={{0,8},{4,12},{8,16},{12,20},{16,24},{20,28},{24,32},{28,36},{32,40... | collective-permute-start | bytes 393224 | tf_op jit(solution)/shard_map/ppermute | solution.py:36
  88.0 0.0 collective-permute-done.7.far_ref
  88.0 1.1 %all-to-all-done.2.refs_0_ = bf16[16,8,256]{2,1,0:T(8,128)(2,1)S(1)} async-done(((bf16[16,8,256]{2,1,0:T(8,128)(2,1)}), bf16[16,8,256]{2,1,0:T(8,128)(2,1)S(1)}, u32[]{:S(2)}, u32[]{:S(2)}) %all-to-all-start.2) | async-done | bytes 65568 | tf_op jit(solution)/shard_map/all_to_all | solution.py:59
  89.1 0.7 sum_and_spread.3
  89.8 6.4 %all-to-all-start.3 = ((bf16[32,8,256]{2,1,0:T(8,128)(2,1)}), bf16[32,8,256]{2,1,0:T(8,128)(2,1)S(1)}, u32[]{:S(2)}, u32[]{:S(2)}) async-start(bf16[32,8,256]{2,1,0:T(8,128)(2,1)} %sum_and_spread.3), calls=%async_computation.3 | async-start | bytes 262144 | tf_op jit(solution)/shard_map/all_to_all | solution.py:59
  96.3 0.0 collective-permute-done.9.after_ref
  96.3 0.0 collective-permute-done.10.before_ref
  96.3 0.8 total_gradient.1
  97.1 6.7 %all-to-all-done.3 = bf16[32,8,256]{2,1,0:T(8,128)(2,1)S(1)} async-done(((bf16[32,8,256]{2,1,0:T(8,128)(2,1)}), bf16[32,8,256]{2,1,0:T(8,128)(2,1)S(1)}, u32[]{:S(2)}, u32[]{:S(2)}) %all-to-all-start.3) | async-done | bytes 131104 | tf_op jit(solution)/shard_map/all_to_all | solution.py:59
  103.8 0.7 bitcast_convert_fusion
  (1 shorter events, 0.0 us)
Async XLA Ops:
  1.6 15.4 %collective-permute-start = (bf16[256,256]{1,0:T(8,128)(2,1)S(1)}, bf16[256,256]{1,0:T(8,128)(2,1)S(1)}, u32[]{:S(2)}, u32[]{:S(2)}) collective-permute-start(bf16[256,256]{1,0:T(8,128)(2,1)S(1)} %own_quarter.1), channel_id=1, source_target_pairs={{4,16},{12,24},{16,4},{20,32},{24,12},{28,40},{32,20},{36,48},{40,... | collective-permute-start | bytes 393224 | tf_op jit(solution)/shard_map/ppermute | solution.py:46
  7.9 9.1 %collective-permute-start.1 = (bf16[256,256]{1,0:T(8,128)(2,1)S(1)}, bf16[256,256]{1,0:T(8,128)(2,1)S(1)}, u32[]{:S(2)}, u32[]{:S(2)}) collective-permute-start(bf16[256,256]{1,0:T(8,128)(2,1)S(1)} %own_quarter.1), channel_id=1, source_target_pairs={{8,0},{12,4},{16,8},{20,12},{24,16},{28,20},{32,24},{36,28},{40,32... | collective-permute-start | bytes 393224 | tf_op jit(solution)/shard_map/ppermute | solution.py:36
  9.2 7.8 %collective-permute-start.2 = (bf16[256,256]{1,0:T(8,128)(2,1)S(1)}, bf16[256,256]{1,0:T(8,128)(2,1)S(1)}, u32[]{:S(2)}, u32[]{:S(2)}) collective-permute-start(bf16[256,256]{1,0:T(8,128)(2,1)S(1)} %own_quarter.1), channel_id=1, source_target_pairs={{0,8},{4,12},{8,16},{12,20},{16,24},{20,28},{24,32},{28,36},{32,40... | collective-permute-start | bytes 393224 | tf_op jit(solution)/shard_map/ppermute | solution.py:36
  16.9 19.3 %copy-start = (bf16[7,1024,256]{2,1,0:T(8,128)(2,1)}, bf16[7,1024,256]{2,1,0:T(8,128)(2,1)S(1)}, u32[]{:S(2)}) copy-start(bf16[7,1024,256]{2,1,0:T(8,128)(2,1)S(1)} %dense_band.1.band_ref.refs_0_) | copy-start | bytes 11010052
  16.9 18.1 %copy-start.1 = (bf16[256,256]{1,0:T(8,128)(2,1)S(1)}, bf16[256,256]{1,0:T(8,128)(2,1)}, u32[]{:S(2)}) copy-start(bf16[256,256]{1,0:T(8,128)(2,1)} %weight_ref.1) | copy-start | bytes 393220
  16.9 18.1 %copy-start.2 = (bf16[256,256]{1,0:T(8,128)(2,1)S(1)}, bf16[256,256]{1,0:T(8,128)(2,1)}, u32[]{:S(2)}) copy-start(bf16[256,256]{1,0:T(8,128)(2,1)} %cotangent_ref.1) | copy-start | bytes 393220
  17.0 5.0 %collective-permute-start.3 = (bf16[768,256]{1,0:T(8,128)(2,1)S(1)}, bf16[768,256]{1,0:T(8,128)(2,1)S(1)}, u32[]{:S(2)}, u32[]{:S(2)}) collective-permute-start(bf16[768,256]{1,0:T(8,128)(2,1)S(1)} %pad_maximum_fusion.near_ref), channel_id=1, source_target_pairs={{0,4},{4,0},{1,5},{5,1},{2,6},{6,2},{3,7},{7,3},{8,12},{12,8},{9,1... | collective-permute-start | bytes 1179656 | tf_op jit(solution)/shard_map/ppermute | solution.py:50
  36.2 7.8 %collective-permute-start.4 = (bf16[256,256]{1,0:T(8,128)(2,1)S(1)}, bf16[256,256]{1,0:T(8,128)(2,1)S(1)}, u32[]{:S(2)}, u32[]{:S(2)}) collective-permute-start(bf16[256,256]{1,0:T(8,128)(2,1)S(1)} %get-tuple-element.28.refs_1_), channel_id=1, source_target_pairs={{0,3},{1,0},{2,1},{3,2},{4,7},{5,4},{6,5},{7,6},{8,11},{9,8},{10,9... | collective-permute-start | bytes 393224 | tf_op jit(solution)/shard_map/ppermute | solution.py:55
  39.0 23.1 %collective-permute-start.5 = (bf16[256,256]{1,0:T(8,128)(2,1)S(1)}, bf16[256,256]{1,0:T(8,128)(2,1)S(1)}, u32[]{:S(2)}, u32[]{:S(2)}) collective-permute-start(bf16[256,256]{1,0:T(8,128)(2,1)S(1)} %get-tuple-element.28.refs_1_), channel_id=1, source_target_pairs={{0,2},{1,3},{2,0},{3,1},{4,6},{5,7},{6,4},{7,5},{8,10},{9,11},{10,... | collective-permute-start | bytes 393224 | tf_op jit(solution)/shard_map/ppermute | solution.py:55
  42.1 20.0 %collective-permute-start.6 = (bf16[256,256]{1,0:T(8,128)(2,1)S(1)}, bf16[256,256]{1,0:T(8,128)(2,1)S(1)}, u32[]{:S(2)}, u32[]{:S(2)}) collective-permute-start(bf16[256,256]{1,0:T(8,128)(2,1)S(1)} %get-tuple-element.28.refs_1_), channel_id=1, source_target_pairs={{0,1},{1,2},{2,3},{3,0},{4,5},{5,6},{6,7},{7,4},{8,9},{9,10},{10,1... | collective-permute-start | bytes 393224 | tf_op jit(solution)/shard_map/ppermute | solution.py:55
  44.1 26.8 %all-to-all-start.1 = ((f32[32,8,256]{2,1,0:T(8,128)}), f32[32,8,256]{2,1,0:T(8,128)S(1)}, u32[]{:S(2)}, u32[]{:S(2)}) async-start(f32[32,8,256]{2,1,0:T(8,128)} %bitcast.1), calls=%async_computation.1 | async-start | bytes 524288 | tf_op jit(solution)/shard_map/all_to_all | solution.py:59
  66.0 16.6 %collective-permute-start.8 = (bf16[768,256]{1,0:T(8,128)(2,1)S(1)}, bf16[768,256]{1,0:T(8,128)(2,1)S(1)}, u32[]{:S(2)}, u32[]{:S(2)}) collective-permute-start(bf16[768,256]{1,0:T(8,128)(2,1)S(1)} %get-tuple-element.33), channel_id=1, source_target_pairs={{0,4},{4,0},{1,5},{5,1},{2,6},{6,2},{3,7},{7,3},{8,12},{12,8},{9,1... | collective-permute-start | bytes 1179656 | tf_op jit(solution)/shard_map/ppermute | solution.py:50
  71.6 17.6 %all-to-all-start.2 = ((bf16[16,8,256]{2,1,0:T(8,128)(2,1)}), bf16[16,8,256]{2,1,0:T(8,128)(2,1)S(1)}, u32[]{:S(2)}, u32[]{:S(2)}) async-start(bf16[16,8,256]{2,1,0:T(8,128)(2,1)} %sum_and_spread.2), calls=%async_computation.2 | async-start | bytes 131072 | tf_op jit(solution)/shard_map/all_to_all | solution.py:59
  77.4 10.6 %collective-permute-start.7 = (bf16[256,256]{1,0:T(8,128)(2,1)S(1)}, bf16[256,256]{1,0:T(8,128)(2,1)S(1)}, u32[]{:S(2)}, u32[]{:S(2)}) collective-permute-start(bf16[256,256]{1,0:T(8,128)(2,1)S(1)} %get-tuple-element.31), channel_id=1, source_target_pairs={{4,16},{12,24},{16,4},{20,32},{24,12},{28,40},{32,20},{36,48},{40,... | collective-permute-start | bytes 393224 | tf_op jit(solution)/shard_map/ppermute | solution.py:46
  82.7 13.5 %collective-permute-start.9 = (bf16[256,256]{1,0:T(8,128)(2,1)S(1)}, bf16[256,256]{1,0:T(8,128)(2,1)S(1)}, u32[]{:S(2)}, u32[]{:S(2)}) collective-permute-start(bf16[256,256]{1,0:T(8,128)(2,1)S(1)} %get-tuple-element.34), channel_id=1, source_target_pairs={{8,0},{12,4},{16,8},{20,12},{24,16},{28,20},{32,24},{36,28},{40,32... | collective-permute-start | bytes 393224 | tf_op jit(solution)/shard_map/ppermute | solution.py:36
  84.0 12.2 %collective-permute-start.10 = (bf16[256,256]{1,0:T(8,128)(2,1)S(1)}, bf16[256,256]{1,0:T(8,128)(2,1)S(1)}, u32[]{:S(2)}, u32[]{:S(2)}) collective-permute-start(bf16[256,256]{1,0:T(8,128)(2,1)S(1)} %get-tuple-element.35), channel_id=1, source_target_pairs={{0,8},{4,12},{8,16},{12,20},{16,24},{20,28},{24,32},{28,36},{32,40... | collective-permute-start | bytes 393224 | tf_op jit(solution)/shard_map/ppermute | solution.py:36
  89.8 14.0 %all-to-all-start.3 = ((bf16[32,8,256]{2,1,0:T(8,128)(2,1)}), bf16[32,8,256]{2,1,0:T(8,128)(2,1)S(1)}, u32[]{:S(2)}, u32[]{:S(2)}) async-start(bf16[32,8,256]{2,1,0:T(8,128)(2,1)} %sum_and_spread.3), calls=%async_computation.3 | async-start | bytes 262144 | tf_op jit(solution)/shard_map/all_to_all | solution.py:59

commit v8 on v7

--- a/solution.py
+++ b/solution.py
@@ -332,21 +332,22 @@
     plane = lax.axis_size(PLANE)
     node_count = group_rows * lax.axis_size(ROW)
     back = [backward] + [rep_shift(backward, k) for k in range(1, reps)]
-    local, back[1] = lax.optimization_barrier((local, back[1]))
     terms = to_all(local.reshape(plane, -1, hidden), PLANE)
 
-    spread = sum_and_spread(terms, line, BF16)
+    spread = sum_and_spread(terms, line, F32)
     terms = to_all(spread, "z")
+    band, _ = lax.optimization_barrier((band, spread))
     near_grad, other_grad, far_grad = window_gradient(band, back)
     swapped = core_swap(other_grad)
     from_far = far_shift(far_grad)
     own_grad, before_grad, after_grad = chip_sum(near_grad, swapped)
     from_after = chip_shift(before_grad, -1)
+    terms, from_far, _ = lax.optimization_barrier((terms, from_far, before_grad))
+    spread = sum_and_spread(terms, plane, BF16, node_count ** (-0.5))
+    terms = to_all(spread, PLANE)
+    after_grad, _ = lax.optimization_barrier((after_grad, spread))
     from_before = chip_shift(after_grad, 1)
-    terms, from_far, _, _ = lax.optimization_barrier((terms, from_far, before_grad, after_grad))
-    terms = to_all(sum_and_spread(terms, plane, BF16, node_count ** (-0.5)), PLANE)
     grad_features = total_gradient(own_grad, from_after, from_before, from_far)
-    terms, grad_features = lax.optimization_barrier((terms, grad_features))
     grad_weight = terms.reshape(hidden, hidden).astype(F32)
     return output_rows, grad_weight, grad_features
 

time: 105 us -> 107 us (1.019)
  the two profiles are of different devices: /device:TPU:1 before, /device:TPU:6 now
where the time goes in v8:
time: 107 us
  starting transfers between devices  62.2 us (58%)
  waiting for transfers between devices  15.7 us (15%)
  blocking collectives  14 us (13%)
  Pallas kernels  13 us (12%)
    ppermute x4, starting transfers between devices, chip_shift(): lax.ppermute(x, ROW, [(i, i + by) for i in range(devices) if 0 <= i + by...  19.9 us
    all_to_all x3, starting transfers between devices, to_all(): return lax.all_to_all(x, axes, 0, 0, tiled=False)  17.6 us
    all_to_all x1, blocking collectives, to_all(): return lax.all_to_all(x, axes, 0, 0, tiled=False)  14 us
    ppermute x3, starting transfers between devices, rep_shift(): lax.ppermute(x, 'rep', [(i, (i - by) % devices) for i in range(devices)])  11.3 us
    ppermute x2, starting transfers between devices, far_shift(): return lax.ppermute(x, ROW, pairs)  9.54 us
    ppermute x2, waiting for transfers between devices, far_shift(): return lax.ppermute(x, ROW, pairs)  7.35 us
    ppermute x4, waiting for transfers between devices, chip_shift(): lax.ppermute(x, ROW, [(i, i + by) for i in range(devices) if 0 <= i + by...  6.62 us
    pallas_call x1, Pallas kernels, window_gradient(): pl.pallas_call(kernel, in_specs=[pl.BlockSpec(memory_space=pltpu.HBM)] +...  3.93 us
  transfers between devices with their start and end apart: 14, of which 5 were waited for; matrix products, arithmetic and copies ran while one was open for 1% of the time, Pallas kernels for 8%

profile of v8, /device:TPU:6, one launch (start us, length us, event | category | flops | bytes accessed | tf_op | source)
XLA Modules:
  0.0 106.6 jit_solution(7327015381440692824)
XLA Ops:
  0.6 0.9 own_quarter.1
  1.6 3.8 %collective-permute-start.2 = (bf16[256,256]{1,0:T(8,128)(2,1)S(1)}, bf16[256,256]{1,0:T(8,128)(2,1)S(1)}, u32[]{:S(2)}, u32[]{:S(2)}) collective-permute-start(bf16[256,256]{1,0:T(8,128)(2,1)S(1)} %own_quarter.1), channel_id=1, source_target_pairs={{0,8},{4,12},{8,16},{12,20},{16,24},{20,28},{24,32},{28,36},{32,40... | collective-permute-start | bytes 393224 | tf_op jit(solution)/shard_map/ppermute | solution.py:36
  5.4 9.8 %collective-permute-start.1 = (bf16[256,256]{1,0:T(8,128)(2,1)S(1)}, bf16[256,256]{1,0:T(8,128)(2,1)S(1)}, u32[]{:S(2)}, u32[]{:S(2)}) collective-permute-start(bf16[256,256]{1,0:T(8,128)(2,1)S(1)} %own_quarter.1), channel_id=1, source_target_pairs={{8,0},{12,4},{16,8},{20,12},{24,16},{28,20},{32,24},{36,28},{40,32... | collective-permute-start | bytes 393224 | tf_op jit(solution)/shard_map/ppermute | solution.py:36
  15.2 3.2 %collective-permute-start = (bf16[256,256]{1,0:T(8,128)(2,1)S(1)}, bf16[256,256]{1,0:T(8,128)(2,1)S(1)}, u32[]{:S(2)}, u32[]{:S(2)}) collective-permute-start(bf16[256,256]{1,0:T(8,128)(2,1)S(1)} %own_quarter.1), channel_id=1, source_target_pairs={{4,16},{12,24},{16,4},{20,32},{24,12},{28,40},{32,20},{36,48},{40,... | collective-permute-start | bytes 393224 | tf_op jit(solution)/shard_map/ppermute | solution.py:46
  18.4 3.6 %dense_band.1.band_ref.refs_0_ = bf16[7,1024,256]{2,1,0:T(8,128)(2,1)S(1)} custom-call(s32[8,1,12]{2,1,0:T(1,128)} %refs_0_.1, bf16[8,12,128,128]{3,2,1,0:T(8,128)(2,1)} %bitcast.5), custom_call_target="tpu_custom_call" | custom-call | bytes 14400000 | tf_op jit(solution)/shard_map/dense_band/pallas_call | solution.py:124
  22.0 0.0 copy-start
  22.0 0.0 copy-start.1
  22.0 0.0 copy-start.2
  22.0 0.0 collective-permute-done.2
  22.0 0.0 collective-permute-done.1
  22.0 3.3 %collective-permute-done.far_ref = bf16[256,256]{1,0:T(8,128)(2,1)S(1)} collective-permute-done((bf16[256,256]{1,0:T(8,128)(2,1)S(1)}, bf16[256,256]{1,0:T(8,128)(2,1)S(1)}, u32[]{:S(2)}, u32[]{:S(2)}) %collective-permute-start) | collective-permute-done | bytes 131104 | tf_op jit(solution)/shard_map/ppermute | solution.py:46
  25.3 1.9 %collective-permute-start.3 = (bf16[768,256]{1,0:T(8,128)(2,1)S(1)}, bf16[768,256]{1,0:T(8,128)(2,1)S(1)}, u32[]{:S(2)}, u32[]{:S(2)}) collective-permute-start(bf16[768,256]{1,0:T(8,128)(2,1)S(1)} %pad_maximum_fusion.near_ref), channel_id=1, source_target_pairs={{0,4},{4,0},{1,5},{5,1},{2,6},{6,2},{3,7},{7,3},{8,12},{12,8},{9,1... | collective-permute-start | bytes 1179656 | tf_op jit(solution)/shard_map/ppermute | solution.py:50
  27.3 1.7 %collective-permute-done.3.other_ref = bf16[768,256]{1,0:T(8,128)(2,1)S(1)} collective-permute-done((bf16[768,256]{1,0:T(8,128)(2,1)S(1)}, bf16[768,256]{1,0:T(8,128)(2,1)S(1)}, u32[]{:S(2)}, u32[]{:S(2)}) %collective-permute-start.3) | collective-permute-done | bytes 393248 | tf_op jit(solution)/shard_map/ppermute | solution.py:50
  29.0 1.1 %partial_aggregate.1 = bf16[4,256,256]{2,1,0:T(8,128)(2,1)S(1)} custom-call(bf16[7,1024,256]{2,1,0:T(8,128)(2,1)S(1)} %dense_band.1.band_ref.refs_0_, bf16[768,256]{1,0:T(8,128)(2,1)S(1)} %pad_maximum_fusion.near_ref, bf16[768,256]{1,0:T(8,128)(2,1)S(1)} %collective-permute-done.3.other_ref, bf16[256,256]{1,0:T(8,128)(2,1)S(1)} %collective-permute-done.far_ref), custom_call_target="tpu_custom_call" | custom-call | bytes 5400000 | tf_op jit(solution)/shard_map/partial_aggregate/pallas_call | solution.py:158
  30.1 14.0 %all_to_all.20.parts_ref = bf16[4,256,256]{2,1,0:T(8,128)(2,1)S(1)} all-to-all(bf16[4,256,256]{2,1,0:T(8,128)(2,1)S(1)} %partial_aggregate.1), channel_id=1, replica_groups=mesh['x'=4,'z'=16,'core'=2,'rep'=4] {'rep'}, dimensions={0} | all-to-all | bytes 1048576 | tf_op jit(solution)/shard_map/all_to_all | solution.py:59
  44.1 0.0 copy-done.1
  44.1 0.0 copy-done.2
  44.1 1.2 %dense_layer.1 = (bf16[256,256]{1,0:T(8,128)(2,1)}, bf16[256,256]{1,0:T(8,128)(2,1)S(1)}, f32[256,256]{1,0:T(8,128)}) custom-call(bf16[4,256,256]{2,1,0:T(8,128)(2,1)S(1)} %all_to_all.20.parts_ref, bf16[256,256]{1,0:T(8,128)(2,1)S(1)} %copy-done.1, bf16[256,256]{1,0:T(8,128)(2,1)S(1)} %copy-done.2), custom_call_target="tpu_custom_call" | custom-call | bytes 4680000 | tf_op jit(solution)/shard_map/dense_layer/pallas_call | solution.py:189
  45.3 0.0 copy-done
  45.3 5.3 %all-to-all-start.1 = ((f32[32,8,256]{2,1,0:T(8,128)}), f32[32,8,256]{2,1,0:T(8,128)S(1)}, u32[]{:S(2)}, u32[]{:S(2)}) async-start(f32[32,8,256]{2,1,0:T(8,128)} %bitcast.1), calls=%async_computation.1 | async-start | bytes 524288 | tf_op jit(solution)/shard_map/all_to_all | solution.py:59
  50.7 3.4 %collective-permute-start.6 = (bf16[256,256]{1,0:T(8,128)(2,1)S(1)}, bf16[256,256]{1,0:T(8,128)(2,1)S(1)}, u32[]{:S(2)}, u32[]{:S(2)}) collective-permute-start(bf16[256,256]{1,0:T(8,128)(2,1)S(1)} %get-tuple-element.27.refs_1_), channel_id=1, source_target_pairs={{0,1},{1,2},{2,3},{3,0},{4,5},{5,6},{6,7},{7,4},{8,9},{9,10},{10,1... | collective-permute-start | bytes 393224 | tf_op jit(solution)/shard_map/ppermute | solution.py:55
  54.0 4.6 %collective-permute-start.5 = (bf16[256,256]{1,0:T(8,128)(2,1)S(1)}, bf16[256,256]{1,0:T(8,128)(2,1)S(1)}, u32[]{:S(2)}, u32[]{:S(2)}) collective-permute-start(bf16[256,256]{1,0:T(8,128)(2,1)S(1)} %get-tuple-element.27.refs_1_), channel_id=1, source_target_pairs={{0,2},{1,3},{2,0},{3,1},{4,6},{5,7},{6,4},{7,5},{8,10},{9,11},{10,... | collective-permute-start | bytes 393224 | tf_op jit(solution)/shard_map/ppermute | solution.py:55
  58.7 3.4 %collective-permute-start.4 = (bf16[256,256]{1,0:T(8,128)(2,1)S(1)}, bf16[256,256]{1,0:T(8,128)(2,1)S(1)}, u32[]{:S(2)}, u32[]{:S(2)}) collective-permute-start(bf16[256,256]{1,0:T(8,128)(2,1)S(1)} %get-tuple-element.27.refs_1_), channel_id=1, source_target_pairs={{0,3},{1,0},{2,1},{3,2},{4,7},{5,4},{6,5},{7,6},{8,11},{9,8},{10,9... | collective-permute-start | bytes 393224 | tf_op jit(solution)/shard_map/ppermute | solution.py:55
  62.0 0.0 all-to-all-done.1.refs_0_
  62.0 0.7 sum_and_spread.2
  62.7 7.4 %all-to-all-start.2 = ((f32[16,8,256]{2,1,0:T(8,128)}), f32[16,8,256]{2,1,0:T(8,128)S(1)}, u32[]{:S(2)}, u32[]{:S(2)}) async-start(f32[16,8,256]{2,1,0:T(8,128)} %sum_and_spread.2), calls=%async_computation.2 | async-start | bytes 262144 | tf_op jit(solution)/shard_map/all_to_all | solution.py:59
  70.1 0.0 collective-permute-done.6.refs_4_
  70.1 0.0 collective-permute-done.5.refs_3_
  70.1 0.0 collective-permute-done.4.refs_2_
  70.1 3.9 %window_gradient.1 = (f32[768,256]{1,0:T(8,128)S(1)}, bf16[768,256]{1,0:T(8,128)(2,1)S(1)}, bf16[256,256]{1,0:T(8,128)(2,1)S(1)}) custom-call(bf16[7,1024,256]{2,1,0:T(8,128)(2,1)} %copy-done, bf16[256,256]{1,0:T(8,128)(2,1)S(1)} %get-tuple-element.27.refs_1_, bf16[256,256]{1,0:T(8,128)(2,1)S(1)} %collective-permute-done.4.refs_2_, ...), custom_call_target="tpu_custom_call" | custom-call | bytes 7200000 | tf_op jit(solution)/shard_map/window_gradient/pallas_call | solution.py:236
  74.1 1.9 %collective-permute-start.8 = (bf16[768,256]{1,0:T(8,128)(2,1)S(1)}, bf16[768,256]{1,0:T(8,128)(2,1)S(1)}, u32[]{:S(2)}, u32[]{:S(2)}) collective-permute-start(bf16[768,256]{1,0:T(8,128)(2,1)S(1)} %get-tuple-element.30), channel_id=1, source_target_pairs={{0,4},{4,0},{1,5},{5,1},{2,6},{6,2},{3,7},{7,3},{8,12},{12,8},{9,1... | collective-permute-start | bytes 1179656 | tf_op jit(solution)/shard_map/ppermute | solution.py:50
  76.0 6.3 %collective-permute-start.7 = (bf16[256,256]{1,0:T(8,128)(2,1)S(1)}, bf16[256,256]{1,0:T(8,128)(2,1)S(1)}, u32[]{:S(2)}, u32[]{:S(2)}) collective-permute-start(bf16[256,256]{1,0:T(8,128)(2,1)S(1)} %get-tuple-element.28), channel_id=1, source_target_pairs={{4,16},{12,24},{16,4},{20,32},{24,12},{28,40},{32,20},{36,48},{40,... | collective-permute-start | bytes 393224 | tf_op jit(solution)/shard_map/ppermute | solution.py:46
  82.3 0.0 collective-permute-done.8.swapped_ref
  82.3 0.1 chip_sum.1
  82.4 4.1 %collective-permute-done.7.far_ref = bf16[256,256]{1,0:T(8,128)(2,1)S(1)} collective-permute-done((bf16[256,256]{1,0:T(8,128)(2,1)S(1)}, bf16[256,256]{1,0:T(8,128)(2,1)S(1)}, u32[]{:S(2)}, u32[]{:S(2)}) %collective-permute-start.7) | collective-permute-done | bytes 131104 | tf_op jit(solution)/shard_map/ppermute | solution.py:46
  86.5 0.0 all-to-all-done.2.refs_0_
  86.5 0.7 sum_and_spread.3
  87.1 4.9 %all-to-all-start.3 = ((bf16[32,8,256]{2,1,0:T(8,128)(2,1)}), bf16[32,8,256]{2,1,0:T(8,128)(2,1)S(1)}, u32[]{:S(2)}, u32[]{:S(2)}) async-start(bf16[32,8,256]{2,1,0:T(8,128)(2,1)} %sum_and_spread.3), calls=%async_computation.3 | async-start | bytes 262144 | tf_op jit(solution)/shard_map/all_to_all | solution.py:59
  92.1 4.4 %collective-permute-start.9 = (bf16[256,256]{1,0:T(8,128)(2,1)S(1)}, bf16[256,256]{1,0:T(8,128)(2,1)S(1)}, u32[]{:S(2)}, u32[]{:S(2)}) collective-permute-start(bf16[256,256]{1,0:T(8,128)(2,1)S(1)} %get-tuple-element.31), channel_id=1, source_target_pairs={{8,0},{12,4},{16,8},{20,12},{24,16},{28,20},{32,24},{36,28},{40,32... | collective-permute-start | bytes 393224 | tf_op jit(solution)/shard_map/ppermute | solution.py:36
  96.5 1.9 %collective-permute-start.10 = (bf16[256,256]{1,0:T(8,128)(2,1)S(1)}, bf16[256,256]{1,0:T(8,128)(2,1)S(1)}, u32[]{:S(2)}, u32[]{:S(2)}) collective-permute-start(bf16[256,256]{1,0:T(8,128)(2,1)S(1)} %get-tuple-element.35), channel_id=1, source_target_pairs={{0,8},{4,12},{8,16},{12,20},{16,24},{20,28},{24,32},{28,36},{32,40... | collective-permute-start | bytes 393224 | tf_op jit(solution)/shard_map/ppermute | solution.py:36
  98.4 0.0 all-to-all-done.3
  98.4 0.7 bitcast_convert_fusion
  99.1 0.5 collective-permute-done.9.after_ref
  99.7 6.1 %collective-permute-done.10.before_ref = bf16[256,256]{1,0:T(8,128)(2,1)S(1)} collective-permute-done((bf16[256,256]{1,0:T(8,128)(2,1)S(1)}, bf16[256,256]{1,0:T(8,128)(2,1)S(1)}, u32[]{:S(2)}, u32[]{:S(2)}) %collective-permute-start.10) | collective-permute-done | bytes 131104 | tf_op jit(solution)/shard_map/ppermute | solution.py:36
  105.7 0.8 total_gradient.1
  (1 shorter events, 0.0 us)
Async XLA Ops:
  1.6 20.5 %collective-permute-start.2 = (bf16[256,256]{1,0:T(8,128)(2,1)S(1)}, bf16[256,256]{1,0:T(8,128)(2,1)S(1)}, u32[]{:S(2)}, u32[]{:S(2)}) collective-permute-start(bf16[256,256]{1,0:T(8,128)(2,1)S(1)} %own_quarter.1), channel_id=1, source_target_pairs={{0,8},{4,12},{8,16},{12,20},{16,24},{20,28},{24,32},{28,36},{32,40... | collective-permute-start | bytes 393224 | tf_op jit(solution)/shard_map/ppermute | solution.py:36
  5.4 16.6 %collective-permute-start.1 = (bf16[256,256]{1,0:T(8,128)(2,1)S(1)}, bf16[256,256]{1,0:T(8,128)(2,1)S(1)}, u32[]{:S(2)}, u32[]{:S(2)}) collective-permute-start(bf16[256,256]{1,0:T(8,128)(2,1)S(1)} %own_quarter.1), channel_id=1, source_target_pairs={{8,0},{12,4},{16,8},{20,12},{24,16},{28,20},{32,24},{36,28},{40,32... | collective-permute-start | bytes 393224 | tf_op jit(solution)/shard_map/ppermute | solution.py:36
  15.2 10.2 %collective-permute-start = (bf16[256,256]{1,0:T(8,128)(2,1)S(1)}, bf16[256,256]{1,0:T(8,128)(2,1)S(1)}, u32[]{:S(2)}, u32[]{:S(2)}) collective-permute-start(bf16[256,256]{1,0:T(8,128)(2,1)S(1)} %own_quarter.1), channel_id=1, source_target_pairs={{4,16},{12,24},{16,4},{20,32},{24,12},{28,40},{32,20},{36,48},{40,... | collective-permute-start | bytes 393224 | tf_op jit(solution)/shard_map/ppermute | solution.py:46
  22.0 23.3 %copy-start = (bf16[7,1024,256]{2,1,0:T(8,128)(2,1)}, bf16[7,1024,256]{2,1,0:T(8,128)(2,1)S(1)}, u32[]{:S(2)}) copy-start(bf16[7,1024,256]{2,1,0:T(8,128)(2,1)S(1)} %dense_band.1.band_ref.refs_0_) | copy-start | bytes 11010052
  22.0 22.1 %copy-start.1 = (bf16[256,256]{1,0:T(8,128)(2,1)S(1)}, bf16[256,256]{1,0:T(8,128)(2,1)}, u32[]{:S(2)}) copy-start(bf16[256,256]{1,0:T(8,128)(2,1)} %weight_ref.1) | copy-start | bytes 393220
  22.0 22.1 %copy-start.2 = (bf16[256,256]{1,0:T(8,128)(2,1)S(1)}, bf16[256,256]{1,0:T(8,128)(2,1)}, u32[]{:S(2)}) copy-start(bf16[256,256]{1,0:T(8,128)(2,1)} %cotangent_ref.1) | copy-start | bytes 393220
  25.3 3.6 %collective-permute-start.3 = (bf16[768,256]{1,0:T(8,128)(2,1)S(1)}, bf16[768,256]{1,0:T(8,128)(2,1)S(1)}, u32[]{:S(2)}, u32[]{:S(2)}) collective-permute-start(bf16[768,256]{1,0:T(8,128)(2,1)S(1)} %pad_maximum_fusion.near_ref), channel_id=1, source_target_pairs={{0,4},{4,0},{1,5},{5,1},{2,6},{6,2},{3,7},{7,3},{8,12},{12,8},{9,1... | collective-permute-start | bytes 1179656 | tf_op jit(solution)/shard_map/ppermute | solution.py:50
  45.3 16.7 %all-to-all-start.1 = ((f32[32,8,256]{2,1,0:T(8,128)}), f32[32,8,256]{2,1,0:T(8,128)S(1)}, u32[]{:S(2)}, u32[]{:S(2)}) async-start(f32[32,8,256]{2,1,0:T(8,128)} %bitcast.1), calls=%async_computation.1 | async-start | bytes 524288 | tf_op jit(solution)/shard_map/all_to_all | solution.py:59
  50.7 19.4 %collective-permute-start.6 = (bf16[256,256]{1,0:T(8,128)(2,1)S(1)}, bf16[256,256]{1,0:T(8,128)(2,1)S(1)}, u32[]{:S(2)}, u32[]{:S(2)}) collective-permute-start(bf16[256,256]{1,0:T(8,128)(2,1)S(1)} %get-tuple-element.27.refs_1_), channel_id=1, source_target_pairs={{0,1},{1,2},{2,3},{3,0},{4,5},{5,6},{6,7},{7,4},{8,9},{9,10},{10,1... | collective-permute-start | bytes 393224 | tf_op jit(solution)/shard_map/ppermute | solution.py:55
  54.0 16.1 %collective-permute-start.5 = (bf16[256,256]{1,0:T(8,128)(2,1)S(1)}, bf16[256,256]{1,0:T(8,128)(2,1)S(1)}, u32[]{:S(2)}, u32[]{:S(2)}) collective-permute-start(bf16[256,256]{1,0:T(8,128)(2,1)S(1)} %get-tuple-element.27.refs_1_), channel_id=1, source_target_pairs={{0,2},{1,3},{2,0},{3,1},{4,6},{5,7},{6,4},{7,5},{8,10},{9,11},{10,... | collective-permute-start | bytes 393224 | tf_op jit(solution)/shard_map/ppermute | solution.py:55
  58.7 11.5 %collective-permute-start.4 = (bf16[256,256]{1,0:T(8,128)(2,1)S(1)}, bf16[256,256]{1,0:T(8,128)(2,1)S(1)}, u32[]{:S(2)}, u32[]{:S(2)}) collective-permute-start(bf16[256,256]{1,0:T(8,128)(2,1)S(1)} %get-tuple-element.27.refs_1_), channel_id=1, source_target_pairs={{0,3},{1,0},{2,1},{3,2},{4,7},{5,4},{6,5},{7,6},{8,11},{9,8},{10,9... | collective-permute-start | bytes 393224 | tf_op jit(solution)/shard_map/ppermute | solution.py:55
  62.7 23.7 %all-to-all-start.2 = ((f32[16,8,256]{2,1,0:T(8,128)}), f32[16,8,256]{2,1,0:T(8,128)S(1)}, u32[]{:S(2)}, u32[]{:S(2)}) async-start(f32[16,8,256]{2,1,0:T(8,128)} %sum_and_spread.2), calls=%async_computation.2 | async-start | bytes 262144 | tf_op jit(solution)/shard_map/all_to_all | solution.py:59
  74.1 8.2 %collective-permute-start.8 = (bf16[768,256]{1,0:T(8,128)(2,1)S(1)}, bf16[768,256]{1,0:T(8,128)(2,1)S(1)}, u32[]{:S(2)}, u32[]{:S(2)}) collective-permute-start(bf16[768,256]{1,0:T(8,128)(2,1)S(1)} %get-tuple-element.30), channel_id=1, source_target_pairs={{0,4},{4,0},{1,5},{5,1},{2,6},{6,2},{3,7},{7,3},{8,12},{12,8},{9,1... | collective-permute-start | bytes 1179656 | tf_op jit(solution)/shard_map/ppermute | solution.py:50
  76.0 10.5 %collective-permute-start.7 = (bf16[256,256]{1,0:T(8,128)(2,1)S(1)}, bf16[256,256]{1,0:T(8,128)(2,1)S(1)}, u32[]{:S(2)}, u32[]{:S(2)}) collective-permute-start(bf16[256,256]{1,0:T(8,128)(2,1)S(1)} %get-tuple-element.28), channel_id=1, source_target_pairs={{4,16},{12,24},{16,4},{20,32},{24,12},{28,40},{32,20},{36,48},{40,... | collective-permute-start | bytes 393224 | tf_op jit(solution)/shard_map/ppermute | solution.py:46
  87.1 11.2 %all-to-all-start.3 = ((bf16[32,8,256]{2,1,0:T(8,128)(2,1)}), bf16[32,8,256]{2,1,0:T(8,128)(2,1)S(1)}, u32[]{:S(2)}, u32[]{:S(2)}) async-start(bf16[32,8,256]{2,1,0:T(8,128)(2,1)} %sum_and_spread.3), calls=%async_computation.3 | async-start | bytes 262144 | tf_op jit(solution)/shard_map/all_to_all | solution.py:59
  92.1 7.6 %collective-permute-start.9 = (bf16[256,256]{1,0:T(8,128)(2,1)S(1)}, bf16[256,256]{1,0:T(8,128)(2,1)S(1)}, u32[]{:S(2)}, u32[]{:S(2)}) collective-permute-start(bf16[256,256]{1,0:T(8,128)(2,1)S(1)} %get-tuple-element.31), channel_id=1, source_target_pairs={{8,0},{12,4},{16,8},{20,12},{24,16},{28,20},{32,24},{36,28},{40,32... | collective-permute-start | bytes 393224 | tf_op jit(solution)/shard_map/ppermute | solution.py:36
  96.5 9.3 %collective-permute-start.10 = (bf16[256,256]{1,0:T(8,128)(2,1)S(1)}, bf16[256,256]{1,0:T(8,128)(2,1)S(1)}, u32[]{:S(2)}, u32[]{:S(2)}) collective-permute-start(bf16[256,256]{1,0:T(8,128)(2,1)S(1)} %get-tuple-element.35), channel_id=1, source_target_pairs={{0,8},{4,12},{8,16},{12,20},{16,24},{20,28},{24,32},{28,36},{32,40... | collective-permute-start | bytes 393224 | tf_op jit(solution)/shard_map/ppermute | solution.py:36

commit v9 on v8

--- a/solution.py
+++ b/solution.py
@@ -342,12 +342,13 @@
     from_far = far_shift(far_grad)
     own_grad, before_grad, after_grad = chip_sum(near_grad, swapped)
     from_after = chip_shift(before_grad, -1)
-    terms, from_far, _ = lax.optimization_barrier((terms, from_far, before_grad))
+    terms, _ = lax.optimization_barrier((terms, before_grad))
     spread = sum_and_spread(terms, plane, BF16, node_count ** (-0.5))
     terms = to_all(spread, PLANE)
     after_grad, _ = lax.optimization_barrier((after_grad, spread))
     from_before = chip_shift(after_grad, 1)
     grad_features = total_gradient(own_grad, from_after, from_before, from_far)
+    terms, from_far, from_after = lax.optimization_barrier((terms, from_far, from_after))
     grad_weight = terms.reshape(hidden, hidden).astype(F32)
     return output_rows, grad_weight, grad_features
 

time: 107 us -> 102 us (0.953)
  the two profiles are of different devices: /device:TPU:6 before, /device:TPU:1 now
where the time goes in v9:
time: 102 us; the launch traced here: 101 us
  starting transfers between devices  66.9 us (66%)
  Pallas kernels  13 us (13%)
  blocking collectives  13 us (13%)
  waiting for transfers between devices  6.71 us (7%)
    all_to_all x3, starting transfers between devices, to_all(): return lax.all_to_all(x, axes, 0, 0, tiled=False)  30.3 us
    all_to_all x1, blocking collectives, to_all(): return lax.all_to_all(x, axes, 0, 0, tiled=False)  13 us
    ppermute x2, starting transfers between devices, far_shift(): return lax.ppermute(x, ROW, pairs)  10.8 us
    ppermute x3, starting transfers between devices, rep_shift(): lax.ppermute(x, 'rep', [(i, (i - by) % devices) for i in range(devices)])  10.7 us
    ppermute x4, starting transfers between devices, chip_shift(): lax.ppermute(x, ROW, [(i, i + by) for i in range(devices) if 0 <= i + by...  9.16 us
    ppermute x2, starting transfers between devices, core_swap(): return lax.ppermute(x, 'core', [(0, 1), (1, 0)])  5.95 us
    all_to_all x3, waiting for transfers between devices, to_all(): return lax.all_to_all(x, axes, 0, 0, tiled=False)  5.36 us
    pallas_call x1, Pallas kernels, window_gradient(): pl.pallas_call(kernel, in_specs=[pl.BlockSpec(memory_space=pltpu.HBM)] +...  3.93 us
  transfers between devices with their start and end apart: 14, of which 2 were waited for; matrix products, arithmetic and copies ran while one was open for 1% of the time, Pallas kernels for 9%

profile of v9, /device:TPU:1, one launch (start us, length us, event | category | flops | bytes accessed | tf_op | source)
XLA Modules:
  0.0 101.3 jit_solution(10210762270223268318)
XLA Ops:
  0.6 0.9 own_quarter.1
  1.6 4.4 %collective-permute-start.2 = (bf16[256,256]{1,0:T(8,128)(2,1)S(1)}, bf16[256,256]{1,0:T(8,128)(2,1)S(1)}, u32[]{:S(2)}, u32[]{:S(2)}) collective-permute-start(bf16[256,256]{1,0:T(8,128)(2,1)S(1)} %own_quarter.1), channel_id=1, source_target_pairs={{0,8},{4,12},{8,16},{12,20},{16,24},{20,28},{24,32},{28,36},{32,40... | collective-permute-start | bytes 393224 | tf_op jit(solution)/shard_map/ppermute | solution.py:36
  5.9 1.3 %collective-permute-start.1 = (bf16[256,256]{1,0:T(8,128)(2,1)S(1)}, bf16[256,256]{1,0:T(8,128)(2,1)S(1)}, u32[]{:S(2)}, u32[]{:S(2)}) collective-permute-start(bf16[256,256]{1,0:T(8,128)(2,1)S(1)} %own_quarter.1), channel_id=1, source_target_pairs={{8,0},{12,4},{16,8},{20,12},{24,16},{28,20},{32,24},{36,28},{40,32... | collective-permute-start | bytes 393224 | tf_op jit(solution)/shard_map/ppermute | solution.py:36
  7.2 6.5 %collective-permute-start = (bf16[256,256]{1,0:T(8,128)(2,1)S(1)}, bf16[256,256]{1,0:T(8,128)(2,1)S(1)}, u32[]{:S(2)}, u32[]{:S(2)}) collective-permute-start(bf16[256,256]{1,0:T(8,128)(2,1)S(1)} %own_quarter.1), channel_id=1, source_target_pairs={{4,16},{12,24},{16,4},{20,32},{24,12},{28,40},{32,20},{36,48},{40,... | collective-permute-start | bytes 393224 | tf_op jit(solution)/shard_map/ppermute | solution.py:46
  13.7 3.6 %dense_band.1.band_ref.refs_0_ = bf16[7,1024,256]{2,1,0:T(8,128)(2,1)S(1)} custom-call(s32[8,1,12]{2,1,0:T(1,128)} %refs_0_.1, bf16[8,12,128,128]{3,2,1,0:T(8,128)(2,1)} %bitcast.5), custom_call_target="tpu_custom_call" | custom-call | bytes 14400000 | tf_op jit(solution)/shard_map/dense_band/pallas_call | solution.py:124
  17.3 0.0 copy-start
  17.3 0.0 copy-start.1
  17.3 0.0 copy-start.2
  17.3 0.0 collective-permute-done.2
  17.3 0.0 collective-permute-done.1
  17.3 0.0 collective-permute-done.far_ref
  17.4 2.6 %collective-permute-start.3 = (bf16[768,256]{1,0:T(8,128)(2,1)S(1)}, bf16[768,256]{1,0:T(8,128)(2,1)S(1)}, u32[]{:S(2)}, u32[]{:S(2)}) collective-permute-start(bf16[768,256]{1,0:T(8,128)(2,1)S(1)} %pad_maximum_fusion.near_ref), channel_id=1, source_target_pairs={{0,4},{4,0},{1,5},{5,1},{2,6},{6,2},{3,7},{7,3},{8,12},{12,8},{9,1... | collective-permute-start | bytes 1179656 | tf_op jit(solution)/shard_map/ppermute | solution.py:50
  20.0 1.3 %collective-permute-done.3.other_ref = bf16[768,256]{1,0:T(8,128)(2,1)S(1)} collective-permute-done((bf16[768,256]{1,0:T(8,128)(2,1)S(1)}, bf16[768,256]{1,0:T(8,128)(2,1)S(1)}, u32[]{:S(2)}, u32[]{:S(2)}) %collective-permute-start.3) | collective-permute-done | bytes 393248 | tf_op jit(solution)/shard_map/ppermute | solution.py:50
  21.3 1.1 %partial_aggregate.1 = bf16[4,256,256]{2,1,0:T(8,128)(2,1)S(1)} custom-call(bf16[7,1024,256]{2,1,0:T(8,128)(2,1)S(1)} %dense_band.1.band_ref.refs_0_, bf16[768,256]{1,0:T(8,128)(2,1)S(1)} %pad_maximum_fusion.near_ref, bf16[768,256]{1,0:T(8,128)(2,1)S(1)} %collective-permute-done.3.other_ref, bf16[256,256]{1,0:T(8,128)(2,1)S(1)} %collective-permute-done.far_ref), custom_call_target="tpu_custom_call" | custom-call | bytes 5400000 | tf_op jit(solution)/shard_map/partial_aggregate/pallas_call | solution.py:158
  22.4 13.0 %all_to_all.20.parts_ref = bf16[4,256,256]{2,1,0:T(8,128)(2,1)S(1)} all-to-all(bf16[4,256,256]{2,1,0:T(8,128)(2,1)S(1)} %partial_aggregate.1), channel_id=1, replica_groups=mesh['x'=4,'z'=16,'core'=2,'rep'=4] {'rep'}, dimensions={0} | all-to-all | bytes 1048576 | tf_op jit(solution)/shard_map/all_to_all | solution.py:59
  35.4 0.0 copy-done.1
  35.4 0.0 copy-done.2
  35.4 1.2 %dense_layer.1 = (bf16[256,256]{1,0:T(8,128)(2,1)}, bf16[256,256]{1,0:T(8,128)(2,1)S(1)}, f32[256,256]{1,0:T(8,128)}) custom-call(bf16[4,256,256]{2,1,0:T(8,128)(2,1)S(1)} %all_to_all.20.parts_ref, bf16[256,256]{1,0:T(8,128)(2,1)S(1)} %copy-done.1, bf16[256,256]{1,0:T(8,128)(2,1)S(1)} %copy-done.2), custom_call_target="tpu_custom_call" | custom-call | bytes 4680000 | tf_op jit(solution)/shard_map/dense_layer/pallas_call | solution.py:189
  36.6 0.0 copy-done
  36.6 15.0 %all-to-all-start.1 = ((f32[32,8,256]{2,1,0:T(8,128)}), f32[32,8,256]{2,1,0:T(8,128)S(1)}, u32[]{:S(2)}, u32[]{:S(2)}) async-start(f32[32,8,256]{2,1,0:T(8,128)} %bitcast.1), calls=%async_computation.1 | async-start | bytes 524288 | tf_op jit(solution)/shard_map/all_to_all | solution.py:59
  51.6 3.3 %collective-permute-start.6 = (bf16[256,256]{1,0:T(8,128)(2,1)S(1)}, bf16[256,256]{1,0:T(8,128)(2,1)S(1)}, u32[]{:S(2)}, u32[]{:S(2)}) collective-permute-start(bf16[256,256]{1,0:T(8,128)(2,1)S(1)} %get-tuple-element.27.refs_1_), channel_id=1, source_target_pairs={{0,1},{1,2},{2,3},{3,0},{4,5},{5,6},{6,7},{7,4},{8,9},{9,10},{10,1... | collective-permute-start | bytes 393224 | tf_op jit(solution)/shard_map/ppermute | solution.py:55
  54.9 4.3 %collective-permute-start.5 = (bf16[256,256]{1,0:T(8,128)(2,1)S(1)}, bf16[256,256]{1,0:T(8,128)(2,1)S(1)}, u32[]{:S(2)}, u32[]{:S(2)}) collective-permute-start(bf16[256,256]{1,0:T(8,128)(2,1)S(1)} %get-tuple-element.27.refs_1_), channel_id=1, source_target_pairs={{0,2},{1,3},{2,0},{3,1},{4,6},{5,7},{6,4},{7,5},{8,10},{9,11},{10,... | collective-permute-start | bytes 393224 | tf_op jit(solution)/shard_map/ppermute | solution.py:55
  59.3 3.1 %collective-permute-start.4 = (bf16[256,256]{1,0:T(8,128)(2,1)S(1)}, bf16[256,256]{1,0:T(8,128)(2,1)S(1)}, u32[]{:S(2)}, u32[]{:S(2)}) collective-permute-start(bf16[256,256]{1,0:T(8,128)(2,1)S(1)} %get-tuple-element.27.refs_1_), channel_id=1, source_target_pairs={{0,3},{1,0},{2,1},{3,2},{4,7},{5,4},{6,5},{7,6},{8,11},{9,8},{10,9... | collective-permute-start | bytes 393224 | tf_op jit(solution)/shard_map/ppermute | solution.py:55
  62.4 0.0 all-to-all-done.1.refs_0_
  62.4 0.7 sum_and_spread.2
  63.1 7.1 %all-to-all-start.2 = ((f32[16,8,256]{2,1,0:T(8,128)}), f32[16,8,256]{2,1,0:T(8,128)S(1)}, u32[]{:S(2)}, u32[]{:S(2)}) async-start(f32[16,8,256]{2,1,0:T(8,128)} %sum_and_spread.2), calls=%async_computation.2 | async-start | bytes 262144 | tf_op jit(solution)/shard_map/all_to_all | solution.py:59
  70.1 0.0 collective-permute-done.6.refs_4_
  70.2 0.0 collective-permute-done.5.refs_3_
  70.2 0.0 collective-permute-done.4.refs_2_
  70.2 3.9 %window_gradient.1 = (f32[768,256]{1,0:T(8,128)S(1)}, bf16[768,256]{1,0:T(8,128)(2,1)S(1)}, bf16[256,256]{1,0:T(8,128)(2,1)S(1)}) custom-call(bf16[7,1024,256]{2,1,0:T(8,128)(2,1)} %copy-done, bf16[256,256]{1,0:T(8,128)(2,1)S(1)} %get-tuple-element.27.refs_1_, bf16[256,256]{1,0:T(8,128)(2,1)S(1)} %collective-permute-done.4.refs_2_, ...), custom_call_target="tpu_custom_call" | custom-call | bytes 7200000 | tf_op jit(solution)/shard_map/window_gradient/pallas_call | solution.py:236
  74.1 3.4 %collective-permute-start.7 = (bf16[768,256]{1,0:T(8,128)(2,1)S(1)}, bf16[768,256]{1,0:T(8,128)(2,1)S(1)}, u32[]{:S(2)}, u32[]{:S(2)}) collective-permute-start(bf16[768,256]{1,0:T(8,128)(2,1)S(1)} %get-tuple-element.29), channel_id=1, source_target_pairs={{0,4},{4,0},{1,5},{5,1},{2,6},{6,2},{3,7},{7,3},{8,12},{12,8},{9,1... | collective-permute-start | bytes 1179656 | tf_op jit(solution)/shard_map/ppermute | solution.py:50
  77.5 4.3 %collective-permute-start.8 = (bf16[256,256]{1,0:T(8,128)(2,1)S(1)}, bf16[256,256]{1,0:T(8,128)(2,1)S(1)}, u32[]{:S(2)}, u32[]{:S(2)}) collective-permute-start(bf16[256,256]{1,0:T(8,128)(2,1)S(1)} %get-tuple-element.32), channel_id=1, source_target_pairs={{4,16},{12,24},{16,4},{20,32},{24,12},{28,40},{32,20},{36,48},{40,... | collective-permute-start | bytes 393224 | tf_op jit(solution)/shard_map/ppermute | solution.py:46
  81.9 0.0 collective-permute-done.7.swapped_ref
  81.9 0.1 chip_sum.1
  82.0 1.3 %collective-permute-start.9 = (bf16[256,256]{1,0:T(8,128)(2,1)S(1)}, bf16[256,256]{1,0:T(8,128)(2,1)S(1)}, u32[]{:S(2)}, u32[]{:S(2)}) collective-permute-start(bf16[256,256]{1,0:T(8,128)(2,1)S(1)} %get-tuple-element.30), channel_id=1, source_target_pairs={{8,0},{12,4},{16,8},{20,12},{24,16},{28,20},{32,24},{36,28},{40,32... | collective-permute-start | bytes 393224 | tf_op jit(solution)/shard_map/ppermute | solution.py:36
  83.3 0.0 all-to-all-done.2.refs_0_
  83.3 0.7 sum_and_spread.3
  83.9 8.2 %all-to-all-start.3 = ((bf16[32,8,256]{2,1,0:T(8,128)(2,1)}), bf16[32,8,256]{2,1,0:T(8,128)(2,1)S(1)}, u32[]{:S(2)}, u32[]{:S(2)}) async-start(bf16[32,8,256]{2,1,0:T(8,128)(2,1)} %sum_and_spread.3), calls=%async_computation.3 | async-start | bytes 262144 | tf_op jit(solution)/shard_map/all_to_all | solution.py:59
  92.2 2.2 %collective-permute-start.10 = (bf16[256,256]{1,0:T(8,128)(2,1)S(1)}, bf16[256,256]{1,0:T(8,128)(2,1)S(1)}, u32[]{:S(2)}, u32[]{:S(2)}) collective-permute-start(bf16[256,256]{1,0:T(8,128)(2,1)S(1)} %get-tuple-element.36), channel_id=1, source_target_pairs={{0,8},{4,12},{8,16},{12,20},{16,24},{20,28},{24,32},{28,36},{32,40... | collective-permute-start | bytes 393224 | tf_op jit(solution)/shard_map/ppermute | solution.py:36
  94.4 0.0 collective-permute-done.8.far_ref
  94.4 0.0 collective-permute-done.9.after_ref
  94.4 5.4 %all-to-all-done.3 = bf16[32,8,256]{2,1,0:T(8,128)(2,1)S(1)} async-done(((bf16[32,8,256]{2,1,0:T(8,128)(2,1)}), bf16[32,8,256]{2,1,0:T(8,128)(2,1)S(1)}, u32[]{:S(2)}, u32[]{:S(2)}) %all-to-all-start.3) | async-done | bytes 131104 | tf_op jit(solution)/shard_map/all_to_all | solution.py:59
  99.7 0.7 bitcast_convert_fusion
  100.5 0.0 collective-permute-done.10.before_ref
  100.5 0.8 total_gradient.1
  (1 shorter events, 0.0 us)
Async XLA Ops:
  1.6 15.8 %collective-permute-start.2 = (bf16[256,256]{1,0:T(8,128)(2,1)S(1)}, bf16[256,256]{1,0:T(8,128)(2,1)S(1)}, u32[]{:S(2)}, u32[]{:S(2)}) collective-permute-start(bf16[256,256]{1,0:T(8,128)(2,1)S(1)} %own_quarter.1), channel_id=1, source_target_pairs={{0,8},{4,12},{8,16},{12,20},{16,24},{20,28},{24,32},{28,36},{32,40... | collective-permute-start | bytes 393224 | tf_op jit(solution)/shard_map/ppermute | solution.py:36
  5.9 11.4 %collective-permute-start.1 = (bf16[256,256]{1,0:T(8,128)(2,1)S(1)}, bf16[256,256]{1,0:T(8,128)(2,1)S(1)}, u32[]{:S(2)}, u32[]{:S(2)}) collective-permute-start(bf16[256,256]{1,0:T(8,128)(2,1)S(1)} %own_quarter.1), channel_id=1, source_target_pairs={{8,0},{12,4},{16,8},{20,12},{24,16},{28,20},{32,24},{36,28},{40,32... | collective-permute-start | bytes 393224 | tf_op jit(solution)/shard_map/ppermute | solution.py:36
  7.2 10.1 %collective-permute-start = (bf16[256,256]{1,0:T(8,128)(2,1)S(1)}, bf16[256,256]{1,0:T(8,128)(2,1)S(1)}, u32[]{:S(2)}, u32[]{:S(2)}) collective-permute-start(bf16[256,256]{1,0:T(8,128)(2,1)S(1)} %own_quarter.1), channel_id=1, source_target_pairs={{4,16},{12,24},{16,4},{20,32},{24,12},{28,40},{32,20},{36,48},{40,... | collective-permute-start | bytes 393224 | tf_op jit(solution)/shard_map/ppermute | solution.py:46
  17.3 19.3 %copy-start = (bf16[7,1024,256]{2,1,0:T(8,128)(2,1)}, bf16[7,1024,256]{2,1,0:T(8,128)(2,1)S(1)}, u32[]{:S(2)}) copy-start(bf16[7,1024,256]{2,1,0:T(8,128)(2,1)S(1)} %dense_band.1.band_ref.refs_0_) | copy-start | bytes 11010052
  17.3 18.1 %copy-start.1 = (bf16[256,256]{1,0:T(8,128)(2,1)S(1)}, bf16[256,256]{1,0:T(8,128)(2,1)}, u32[]{:S(2)}) copy-start(bf16[256,256]{1,0:T(8,128)(2,1)} %weight_ref.1) | copy-start | bytes 393220
  17.3 18.1 %copy-start.2 = (bf16[256,256]{1,0:T(8,128)(2,1)S(1)}, bf16[256,256]{1,0:T(8,128)(2,1)}, u32[]{:S(2)}) copy-start(bf16[256,256]{1,0:T(8,128)(2,1)} %cotangent_ref.1) | copy-start | bytes 393220
  17.4 3.9 %collective-permute-start.3 = (bf16[768,256]{1,0:T(8,128)(2,1)S(1)}, bf16[768,256]{1,0:T(8,128)(2,1)S(1)}, u32[]{:S(2)}, u32[]{:S(2)}) collective-permute-start(bf16[768,256]{1,0:T(8,128)(2,1)S(1)} %pad_maximum_fusion.near_ref), channel_id=1, source_target_pairs={{0,4},{4,0},{1,5},{5,1},{2,6},{6,2},{3,7},{7,3},{8,12},{12,8},{9,1... | collective-permute-start | bytes 1179656 | tf_op jit(solution)/shard_map/ppermute | solution.py:50
  36.6 25.8 %all-to-all-start.1 = ((f32[32,8,256]{2,1,0:T(8,128)}), f32[32,8,256]{2,1,0:T(8,128)S(1)}, u32[]{:S(2)}, u32[]{:S(2)}) async-start(f32[32,8,256]{2,1,0:T(8,128)} %bitcast.1), calls=%async_computation.1 | async-start | bytes 524288 | tf_op jit(solution)/shard_map/all_to_all | solution.py:59
  51.6 18.5 %collective-permute-start.6 = (bf16[256,256]{1,0:T(8,128)(2,1)S(1)}, bf16[256,256]{1,0:T(8,128)(2,1)S(1)}, u32[]{:S(2)}, u32[]{:S(2)}) collective-permute-start(bf16[256,256]{1,0:T(8,128)(2,1)S(1)} %get-tuple-element.27.refs_1_), channel_id=1, source_target_pairs={{0,1},{1,2},{2,3},{3,0},{4,5},{5,6},{6,7},{7,4},{8,9},{9,10},{10,1... | collective-permute-start | bytes 393224 | tf_op jit(solution)/shard_map/ppermute | solution.py:55
  54.9 15.2 %collective-permute-start.5 = (bf16[256,256]{1,0:T(8,128)(2,1)S(1)}, bf16[256,256]{1,0:T(8,128)(2,1)S(1)}, u32[]{:S(2)}, u32[]{:S(2)}) collective-permute-start(bf16[256,256]{1,0:T(8,128)(2,1)S(1)} %get-tuple-element.27.refs_1_), channel_id=1, source_target_pairs={{0,2},{1,3},{2,0},{3,1},{4,6},{5,7},{6,4},{7,5},{8,10},{9,11},{10,... | collective-permute-start | bytes 393224 | tf_op jit(solution)/shard_map/ppermute | solution.py:55
  59.3 10.9 %collective-permute-start.4 = (bf16[256,256]{1,0:T(8,128)(2,1)S(1)}, bf16[256,256]{1,0:T(8,128)(2,1)S(1)}, u32[]{:S(2)}, u32[]{:S(2)}) collective-permute-start(bf16[256,256]{1,0:T(8,128)(2,1)S(1)} %get-tuple-element.27.refs_1_), channel_id=1, source_target_pairs={{0,3},{1,0},{2,1},{3,2},{4,7},{5,4},{6,5},{7,6},{8,11},{9,8},{10,9... | collective-permute-start | bytes 393224 | tf_op jit(solution)/shard_map/ppermute | solution.py:55
  63.1 20.2 %all-to-all-start.2 = ((f32[16,8,256]{2,1,0:T(8,128)}), f32[16,8,256]{2,1,0:T(8,128)S(1)}, u32[]{:S(2)}, u32[]{:S(2)}) async-start(f32[16,8,256]{2,1,0:T(8,128)} %sum_and_spread.2), calls=%async_computation.2 | async-start | bytes 262144 | tf_op jit(solution)/shard_map/all_to_all | solution.py:59
  74.1 7.8 %collective-permute-start.7 = (bf16[768,256]{1,0:T(8,128)(2,1)S(1)}, bf16[768,256]{1,0:T(8,128)(2,1)S(1)}, u32[]{:S(2)}, u32[]{:S(2)}) collective-permute-start(bf16[768,256]{1,0:T(8,128)(2,1)S(1)} %get-tuple-element.29), channel_id=1, source_target_pairs={{0,4},{4,0},{1,5},{5,1},{2,6},{6,2},{3,7},{7,3},{8,12},{12,8},{9,1... | collective-permute-start | bytes 1179656 | tf_op jit(solution)/shard_map/ppermute | solution.py:50
  77.5 16.9 %collective-permute-start.8 = (bf16[256,256]{1,0:T(8,128)(2,1)S(1)}, bf16[256,256]{1,0:T(8,128)(2,1)S(1)}, u32[]{:S(2)}, u32[]{:S(2)}) collective-permute-start(bf16[256,256]{1,0:T(8,128)(2,1)S(1)} %get-tuple-element.32), channel_id=1, source_target_pairs={{4,16},{12,24},{16,4},{20,32},{24,12},{28,40},{32,20},{36,48},{40,... | collective-permute-start | bytes 393224 | tf_op jit(solution)/shard_map/ppermute | solution.py:46
  82.0 12.4 %collective-permute-start.9 = (bf16[256,256]{1,0:T(8,128)(2,1)S(1)}, bf16[256,256]{1,0:T(8,128)(2,1)S(1)}, u32[]{:S(2)}, u32[]{:S(2)}) collective-permute-start(bf16[256,256]{1,0:T(8,128)(2,1)S(1)} %get-tuple-element.30), channel_id=1, source_target_pairs={{8,0},{12,4},{16,8},{20,12},{24,16},{28,20},{32,24},{36,28},{40,32... | collective-permute-start | bytes 393224 | tf_op jit(solution)/shard_map/ppermute | solution.py:36
  83.9 15.8 %all-to-all-start.3 = ((bf16[32,8,256]{2,1,0:T(8,128)(2,1)}), bf16[32,8,256]{2,1,0:T(8,128)(2,1)S(1)}, u32[]{:S(2)}, u32[]{:S(2)}) async-start(bf16[32,8,256]{2,1,0:T(8,128)(2,1)} %sum_and_spread.3), calls=%async_computation.3 | async-start | bytes 262144 | tf_op jit(solution)/shard_map/all_to_all | solution.py:59
  92.2 8.3 %collective-permute-start.10 = (bf16[256,256]{1,0:T(8,128)(2,1)S(1)}, bf16[256,256]{1,0:T(8,128)(2,1)S(1)}, u32[]{:S(2)}, u32[]{:S(2)}) collective-permute-start(bf16[256,256]{1,0:T(8,128)(2,1)S(1)} %get-tuple-element.36), channel_id=1, source_target_pairs={{0,8},{4,12},{8,16},{12,20},{16,24},{20,28},{24,32},{28,36},{32,40... | collective-permute-start | bytes 393224 | tf_op jit(solution)/shard_map/ppermute | solution.py:36

commit v10 on v9

--- a/solution.py
+++ b/solution.py
@@ -321,7 +321,7 @@
     after = chip_shift(own, -1)
     far = far_shift(own)
     band = dense_band(block_cols, block_vals[:, 0], blocks_group, per_rep)
-    far, after, before, band = lax.optimization_barrier((far, after, before, band))
+    before, after, far, band = lax.optimization_barrier((before, after, far, band))
 
     near = jnp.concatenate([own, before, after], axis=0)
     other = core_swap(near)

time: 102 us -> 101 us (level)
  blocking collectives: 13 us -> 11.9 us
    all_to_all x3, starting transfers between devices: 30.3 us -> 29.2 us  [to_all(): return lax.all_to_all(x, axes, 0, 0, tiled=False)]
    ppermute x2, starting transfers between devices: 5.95 us -> 7.06 us  [core_swap(): return lax.ppermute(x, 'core', [(0, 1), (1, 0)])]
    all_to_all x1, blocking collectives: 13 us -> 11.9 us  [to_all(): return lax.all_to_all(x, axes, 0, 0, tiled=False)]
where the time goes in v10:
time: 101 us; the launch traced here: 99.8 us
  starting transfers between devices  66.5 us (66%)
  Pallas kernels  13 us (13%)
  blocking collectives  11.9 us (12%)
  waiting for transfers between devices  6.71 us (7%)
    all_to_all x3, starting transfers between devices, to_all(): return lax.all_to_all(x, axes, 0, 0, tiled=False)  29.2 us
    all_to_all x1, blocking collectives, to_all(): return lax.all_to_all(x, axes, 0, 0, tiled=False)  11.9 us
    ppermute x3, starting transfers between devices, rep_shift(): lax.ppermute(x, 'rep', [(i, (i - by) % devices) for i in range(devices)])  10.7 us
    ppermute x2, starting transfers between devices, far_shift(): return lax.ppermute(x, ROW, pairs)  10.6 us
    ppermute x4, starting transfers between devices, chip_shift(): lax.ppermute(x, ROW, [(i, i + by) for i in range(devices) if 0 <= i + by...  8.96 us
    ppermute x2, starting transfers between devices, core_swap(): return lax.ppermute(x, 'core', [(0, 1), (1, 0)])  7.06 us
    all_to_all x3, waiting for transfers between devices, to_all(): return lax.all_to_all(x, axes, 0, 0, tiled=False)  5.35 us
    pallas_call x1, Pallas kernels, window_gradient(): pl.pallas_call(kernel, in_specs=[pl.BlockSpec(memory_space=pltpu.HBM)] +...  3.93 us
  transfers between devices with their start and end apart: 14, of which 2 were waited for; matrix products, arithmetic and copies ran while one was open for 1% of the time, Pallas kernels for 9%

profile of v10, /device:TPU:1, one launch (start us, length us, event | category | flops | bytes accessed | tf_op | source)
XLA Modules:
  0.0 99.8 jit_solution(15441325514666259226)
XLA Ops:
  0.6 0.9 own_quarter.1
  1.6 6.3 %collective-permute-start.2 = (bf16[256,256]{1,0:T(8,128)(2,1)S(1)}, bf16[256,256]{1,0:T(8,128)(2,1)S(1)}, u32[]{:S(2)}, u32[]{:S(2)}) collective-permute-start(bf16[256,256]{1,0:T(8,128)(2,1)S(1)} %own_quarter.1), channel_id=1, source_target_pairs={{4,16},{12,24},{16,4},{20,32},{24,12},{28,40},{32,20},{36,48},{40,... | collective-permute-start | bytes 393224 | tf_op jit(solution)/shard_map/ppermute | solution.py:46
  7.9 1.3 %collective-permute-start.1 = (bf16[256,256]{1,0:T(8,128)(2,1)S(1)}, bf16[256,256]{1,0:T(8,128)(2,1)S(1)}, u32[]{:S(2)}, u32[]{:S(2)}) collective-permute-start(bf16[256,256]{1,0:T(8,128)(2,1)S(1)} %own_quarter.1), channel_id=1, source_target_pairs={{8,0},{12,4},{16,8},{20,12},{24,16},{28,20},{32,24},{36,28},{40,32... | collective-permute-start | bytes 393224 | tf_op jit(solution)/shard_map/ppermute | solution.py:36
  9.2 4.2 %collective-permute-start = (bf16[256,256]{1,0:T(8,128)(2,1)S(1)}, bf16[256,256]{1,0:T(8,128)(2,1)S(1)}, u32[]{:S(2)}, u32[]{:S(2)}) collective-permute-start(bf16[256,256]{1,0:T(8,128)(2,1)S(1)} %own_quarter.1), channel_id=1, source_target_pairs={{0,8},{4,12},{8,16},{12,20},{16,24},{20,28},{24,32},{28,36},{32,40... | collective-permute-start | bytes 393224 | tf_op jit(solution)/shard_map/ppermute | solution.py:36
  13.3 3.6 %dense_band.1.band_ref.refs_0_ = bf16[7,1024,256]{2,1,0:T(8,128)(2,1)S(1)} custom-call(s32[8,1,12]{2,1,0:T(1,128)} %refs_0_.1, bf16[8,12,128,128]{3,2,1,0:T(8,128)(2,1)} %bitcast.5), custom_call_target="tpu_custom_call" | custom-call | bytes 14400000 | tf_op jit(solution)/shard_map/dense_band/pallas_call | solution.py:124
  16.9 0.0 copy-start
  16.9 0.0 copy-start.1
  16.9 0.0 copy-start.2
  16.9 0.0 collective-permute-done.2.far_ref
  17.0 0.0 collective-permute-done.1
  17.0 0.0 collective-permute-done
  17.0 3.7 %collective-permute-start.3 = (bf16[768,256]{1,0:T(8,128)(2,1)S(1)}, bf16[768,256]{1,0:T(8,128)(2,1)S(1)}, u32[]{:S(2)}, u32[]{:S(2)}) collective-permute-start(bf16[768,256]{1,0:T(8,128)(2,1)S(1)} %pad_maximum_fusion.near_ref), channel_id=1, source_target_pairs={{0,4},{4,0},{1,5},{5,1},{2,6},{6,2},{3,7},{7,3},{8,12},{12,8},{9,1... | collective-permute-start | bytes 1179656 | tf_op jit(solution)/shard_map/ppermute | solution.py:50
  20.7 1.3 %collective-permute-done.3.other_ref = bf16[768,256]{1,0:T(8,128)(2,1)S(1)} collective-permute-done((bf16[768,256]{1,0:T(8,128)(2,1)S(1)}, bf16[768,256]{1,0:T(8,128)(2,1)S(1)}, u32[]{:S(2)}, u32[]{:S(2)}) %collective-permute-start.3) | collective-permute-done | bytes 393248 | tf_op jit(solution)/shard_map/ppermute | solution.py:50
  22.0 1.1 %partial_aggregate.1 = bf16[4,256,256]{2,1,0:T(8,128)(2,1)S(1)} custom-call(bf16[7,1024,256]{2,1,0:T(8,128)(2,1)S(1)} %dense_band.1.band_ref.refs_0_, bf16[768,256]{1,0:T(8,128)(2,1)S(1)} %pad_maximum_fusion.near_ref, bf16[768,256]{1,0:T(8,128)(2,1)S(1)} %collective-permute-done.3.other_ref, bf16[256,256]{1,0:T(8,128)(2,1)S(1)} %collective-permute-done.2.far_ref), custom_call_target="tpu_custom_call" | custom-call | bytes 5400000 | tf_op jit(solution)/shard_map/partial_aggregate/pallas_call | solution.py:158
  23.1 11.9 %all_to_all.20.parts_ref = bf16[4,256,256]{2,1,0:T(8,128)(2,1)S(1)} all-to-all(bf16[4,256,256]{2,1,0:T(8,128)(2,1)S(1)} %partial_aggregate.1), channel_id=1, replica_groups=mesh['x'=4,'z'=16,'core'=2,'rep'=4] {'rep'}, dimensions={0} | all-to-all | bytes 1048576 | tf_op jit(solution)/shard_map/all_to_all | solution.py:59
  35.0 0.0 copy-done.1
  35.0 0.0 copy-done.2
  35.0 1.2 %dense_layer.1 = (bf16[256,256]{1,0:T(8,128)(2,1)}, bf16[256,256]{1,0:T(8,128)(2,1)S(1)}, f32[256,256]{1,0:T(8,128)}) custom-call(bf16[4,256,256]{2,1,0:T(8,128)(2,1)S(1)} %all_to_all.20.parts_ref, bf16[256,256]{1,0:T(8,128)(2,1)S(1)} %copy-done.1, bf16[256,256]{1,0:T(8,128)(2,1)S(1)} %copy-done.2), custom_call_target="tpu_custom_call" | custom-call | bytes 4680000 | tf_op jit(solution)/shard_map/dense_layer/pallas_call | solution.py:189
  36.2 0.0 copy-done
  36.2 15.1 %all-to-all-start.1 = ((f32[32,8,256]{2,1,0:T(8,128)}), f32[32,8,256]{2,1,0:T(8,128)S(1)}, u32[]{:S(2)}, u32[]{:S(2)}) async-start(f32[32,8,256]{2,1,0:T(8,128)} %bitcast.1), calls=%async_computation.1 | async-start | bytes 524288 | tf_op jit(solution)/shard_map/all_to_all | solution.py:59
  51.3 3.3 %collective-permute-start.6 = (bf16[256,256]{1,0:T(8,128)(2,1)S(1)}, bf16[256,256]{1,0:T(8,128)(2,1)S(1)}, u32[]{:S(2)}, u32[]{:S(2)}) collective-permute-start(bf16[256,256]{1,0:T(8,128)(2,1)S(1)} %get-tuple-element.27.refs_1_), channel_id=1, source_target_pairs={{0,1},{1,2},{2,3},{3,0},{4,5},{5,6},{6,7},{7,4},{8,9},{9,10},{10,1... | collective-permute-start | bytes 393224 | tf_op jit(solution)/shard_map/ppermute | solution.py:55
  54.6 4.3 %collective-permute-start.5 = (bf16[256,256]{1,0:T(8,128)(2,1)S(1)}, bf16[256,256]{1,0:T(8,128)(2,1)S(1)}, u32[]{:S(2)}, u32[]{:S(2)}) collective-permute-start(bf16[256,256]{1,0:T(8,128)(2,1)S(1)} %get-tuple-element.27.refs_1_), channel_id=1, source_target_pairs={{0,2},{1,3},{2,0},{3,1},{4,6},{5,7},{6,4},{7,5},{8,10},{9,11},{10,... | collective-permute-start | bytes 393224 | tf_op jit(solution)/shard_map/ppermute | solution.py:55
  58.9 3.1 %collective-permute-start.4 = (bf16[256,256]{1,0:T(8,128)(2,1)S(1)}, bf16[256,256]{1,0:T(8,128)(2,1)S(1)}, u32[]{:S(2)}, u32[]{:S(2)}) collective-permute-start(bf16[256,256]{1,0:T(8,128)(2,1)S(1)} %get-tuple-element.27.refs_1_), channel_id=1, source_target_pairs={{0,3},{1,0},{2,1},{3,2},{4,7},{5,4},{6,5},{7,6},{8,11},{9,8},{10,9... | collective-permute-start | bytes 393224 | tf_op jit(solution)/shard_map/ppermute | solution.py:55
  62.0 0.0 all-to-all-done.1.refs_0_
  62.1 0.7 sum_and_spread.2
  62.8 5.9 %all-to-all-start.2 = ((f32[16,8,256]{2,1,0:T(8,128)}), f32[16,8,256]{2,1,0:T(8,128)S(1)}, u32[]{:S(2)}, u32[]{:S(2)}) async-start(f32[16,8,256]{2,1,0:T(8,128)} %sum_and_spread.2), calls=%async_computation.2 | async-start | bytes 262144 | tf_op jit(solution)/shard_map/all_to_all | solution.py:59
  68.6 0.0 collective-permute-done.6.refs_4_
  68.6 0.0 collective-permute-done.5.refs_3_
  68.7 0.0 collective-permute-done.4.refs_2_
  68.7 3.9 %window_gradient.1 = (f32[768,256]{1,0:T(8,128)S(1)}, bf16[768,256]{1,0:T(8,128)(2,1)S(1)}, bf16[256,256]{1,0:T(8,128)(2,1)S(1)}) custom-call(bf16[7,1024,256]{2,1,0:T(8,128)(2,1)} %copy-done, bf16[256,256]{1,0:T(8,128)(2,1)S(1)} %get-tuple-element.27.refs_1_, bf16[256,256]{1,0:T(8,128)(2,1)S(1)} %collective-permute-done.4.refs_2_, ...), custom_call_target="tpu_custom_call" | custom-call | bytes 7200000 | tf_op jit(solution)/shard_map/window_gradient/pallas_call | solution.py:236
  72.6 3.4 %collective-permute-start.7 = (bf16[768,256]{1,0:T(8,128)(2,1)S(1)}, bf16[768,256]{1,0:T(8,128)(2,1)S(1)}, u32[]{:S(2)}, u32[]{:S(2)}) collective-permute-start(bf16[768,256]{1,0:T(8,128)(2,1)S(1)} %get-tuple-element.29), channel_id=1, source_target_pairs={{0,4},{4,0},{1,5},{5,1},{2,6},{6,2},{3,7},{7,3},{8,12},{12,8},{9,1... | collective-permute-start | bytes 1179656 | tf_op jit(solution)/shard_map/ppermute | solution.py:50
  76.0 4.3 %collective-permute-start.8 = (bf16[256,256]{1,0:T(8,128)(2,1)S(1)}, bf16[256,256]{1,0:T(8,128)(2,1)S(1)}, u32[]{:S(2)}, u32[]{:S(2)}) collective-permute-start(bf16[256,256]{1,0:T(8,128)(2,1)S(1)} %get-tuple-element.32), channel_id=1, source_target_pairs={{4,16},{12,24},{16,4},{20,32},{24,12},{28,40},{32,20},{36,48},{40,... | collective-permute-start | bytes 393224 | tf_op jit(solution)/shard_map/ppermute | solution.py:46
  80.4 0.0 collective-permute-done.7.swapped_ref
  80.4 0.1 chip_sum.1
  80.4 1.3 %collective-permute-start.9 = (bf16[256,256]{1,0:T(8,128)(2,1)S(1)}, bf16[256,256]{1,0:T(8,128)(2,1)S(1)}, u32[]{:S(2)}, u32[]{:S(2)}) collective-permute-start(bf16[256,256]{1,0:T(8,128)(2,1)S(1)} %get-tuple-element.30), channel_id=1, source_target_pairs={{8,0},{12,4},{16,8},{20,12},{24,16},{28,20},{32,24},{36,28},{40,32... | collective-permute-start | bytes 393224 | tf_op jit(solution)/shard_map/ppermute | solution.py:36
  81.7 0.0 all-to-all-done.2.refs_0_
  81.8 0.7 sum_and_spread.3
  82.4 8.2 %all-to-all-start.3 = ((bf16[32,8,256]{2,1,0:T(8,128)(2,1)}), bf16[32,8,256]{2,1,0:T(8,128)(2,1)S(1)}, u32[]{:S(2)}, u32[]{:S(2)}) async-start(bf16[32,8,256]{2,1,0:T(8,128)(2,1)} %sum_and_spread.3), calls=%async_computation.3 | async-start | bytes 262144 | tf_op jit(solution)/shard_map/all_to_all | solution.py:59
  90.6 2.2 %collective-permute-start.10 = (bf16[256,256]{1,0:T(8,128)(2,1)S(1)}, bf16[256,256]{1,0:T(8,128)(2,1)S(1)}, u32[]{:S(2)}, u32[]{:S(2)}) collective-permute-start(bf16[256,256]{1,0:T(8,128)(2,1)S(1)} %get-tuple-element.36), channel_id=1, source_target_pairs={{0,8},{4,12},{8,16},{12,20},{16,24},{20,28},{24,32},{28,36},{32,40... | collective-permute-start | bytes 393224 | tf_op jit(solution)/shard_map/ppermute | solution.py:36
  92.9 0.0 collective-permute-done.8.far_ref
  92.9 0.0 collective-permute-done.9.after_ref
  92.9 5.3 %all-to-all-done.3 = bf16[32,8,256]{2,1,0:T(8,128)(2,1)S(1)} async-done(((bf16[32,8,256]{2,1,0:T(8,128)(2,1)}), bf16[32,8,256]{2,1,0:T(8,128)(2,1)S(1)}, u32[]{:S(2)}, u32[]{:S(2)}) %all-to-all-start.3) | async-done | bytes 131104 | tf_op jit(solution)/shard_map/all_to_all | solution.py:59
  98.2 0.7 bitcast_convert_fusion
  98.9 0.0 collective-permute-done.10.before_ref
  98.9 0.8 total_gradient.1
  (1 shorter events, 0.0 us)
Async XLA Ops:
  1.6 15.4 %collective-permute-start.2 = (bf16[256,256]{1,0:T(8,128)(2,1)S(1)}, bf16[256,256]{1,0:T(8,128)(2,1)S(1)}, u32[]{:S(2)}, u32[]{:S(2)}) collective-permute-start(bf16[256,256]{1,0:T(8,128)(2,1)S(1)} %own_quarter.1), channel_id=1, source_target_pairs={{4,16},{12,24},{16,4},{20,32},{24,12},{28,40},{32,20},{36,48},{40,... | collective-permute-start | bytes 393224 | tf_op jit(solution)/shard_map/ppermute | solution.py:46
  7.9 9.1 %collective-permute-start.1 = (bf16[256,256]{1,0:T(8,128)(2,1)S(1)}, bf16[256,256]{1,0:T(8,128)(2,1)S(1)}, u32[]{:S(2)}, u32[]{:S(2)}) collective-permute-start(bf16[256,256]{1,0:T(8,128)(2,1)S(1)} %own_quarter.1), channel_id=1, source_target_pairs={{8,0},{12,4},{16,8},{20,12},{24,16},{28,20},{32,24},{36,28},{40,32... | collective-permute-start | bytes 393224 | tf_op jit(solution)/shard_map/ppermute | solution.py:36
  9.2 7.8 %collective-permute-start = (bf16[256,256]{1,0:T(8,128)(2,1)S(1)}, bf16[256,256]{1,0:T(8,128)(2,1)S(1)}, u32[]{:S(2)}, u32[]{:S(2)}) collective-permute-start(bf16[256,256]{1,0:T(8,128)(2,1)S(1)} %own_quarter.1), channel_id=1, source_target_pairs={{0,8},{4,12},{8,16},{12,20},{16,24},{20,28},{24,32},{28,36},{32,40... | collective-permute-start | bytes 393224 | tf_op jit(solution)/shard_map/ppermute | solution.py:36
  16.9 19.3 %copy-start = (bf16[7,1024,256]{2,1,0:T(8,128)(2,1)}, bf16[7,1024,256]{2,1,0:T(8,128)(2,1)S(1)}, u32[]{:S(2)}) copy-start(bf16[7,1024,256]{2,1,0:T(8,128)(2,1)S(1)} %dense_band.1.band_ref.refs_0_) | copy-start | bytes 11010052
  16.9 18.1 %copy-start.1 = (bf16[256,256]{1,0:T(8,128)(2,1)S(1)}, bf16[256,256]{1,0:T(8,128)(2,1)}, u32[]{:S(2)}) copy-start(bf16[256,256]{1,0:T(8,128)(2,1)} %weight_ref.1) | copy-start | bytes 393220
  16.9 18.1 %copy-start.2 = (bf16[256,256]{1,0:T(8,128)(2,1)S(1)}, bf16[256,256]{1,0:T(8,128)(2,1)}, u32[]{:S(2)}) copy-start(bf16[256,256]{1,0:T(8,128)(2,1)} %cotangent_ref.1) | copy-start | bytes 393220
  17.0 5.0 %collective-permute-start.3 = (bf16[768,256]{1,0:T(8,128)(2,1)S(1)}, bf16[768,256]{1,0:T(8,128)(2,1)S(1)}, u32[]{:S(2)}, u32[]{:S(2)}) collective-permute-start(bf16[768,256]{1,0:T(8,128)(2,1)S(1)} %pad_maximum_fusion.near_ref), channel_id=1, source_target_pairs={{0,4},{4,0},{1,5},{5,1},{2,6},{6,2},{3,7},{7,3},{8,12},{12,8},{9,1... | collective-permute-start | bytes 1179656 | tf_op jit(solution)/shard_map/ppermute | solution.py:50
  36.2 25.8 %all-to-all-start.1 = ((f32[32,8,256]{2,1,0:T(8,128)}), f32[32,8,256]{2,1,0:T(8,128)S(1)}, u32[]{:S(2)}, u32[]{:S(2)}) async-start(f32[32,8,256]{2,1,0:T(8,128)} %bitcast.1), calls=%async_computation.1 | async-start | bytes 524288 | tf_op jit(solution)/shard_map/all_to_all | solution.py:59
  51.3 17.3 %collective-permute-start.6 = (bf16[256,256]{1,0:T(8,128)(2,1)S(1)}, bf16[256,256]{1,0:T(8,128)(2,1)S(1)}, u32[]{:S(2)}, u32[]{:S(2)}) collective-permute-start(bf16[256,256]{1,0:T(8,128)(2,1)S(1)} %get-tuple-element.27.refs_1_), channel_id=1, source_target_pairs={{0,1},{1,2},{2,3},{3,0},{4,5},{5,6},{6,7},{7,4},{8,9},{9,10},{10,1... | collective-permute-start | bytes 393224 | tf_op jit(solution)/shard_map/ppermute | solution.py:55
  54.6 14.0 %collective-permute-start.5 = (bf16[256,256]{1,0:T(8,128)(2,1)S(1)}, bf16[256,256]{1,0:T(8,128)(2,1)S(1)}, u32[]{:S(2)}, u32[]{:S(2)}) collective-permute-start(bf16[256,256]{1,0:T(8,128)(2,1)S(1)} %get-tuple-element.27.refs_1_), channel_id=1, source_target_pairs={{0,2},{1,3},{2,0},{3,1},{4,6},{5,7},{6,4},{7,5},{8,10},{9,11},{10,... | collective-permute-start | bytes 393224 | tf_op jit(solution)/shard_map/ppermute | solution.py:55
  58.9 9.7 %collective-permute-start.4 = (bf16[256,256]{1,0:T(8,128)(2,1)S(1)}, bf16[256,256]{1,0:T(8,128)(2,1)S(1)}, u32[]{:S(2)}, u32[]{:S(2)}) collective-permute-start(bf16[256,256]{1,0:T(8,128)(2,1)S(1)} %get-tuple-element.27.refs_1_), channel_id=1, source_target_pairs={{0,3},{1,0},{2,1},{3,2},{4,7},{5,4},{6,5},{7,6},{8,11},{9,8},{10,9... | collective-permute-start | bytes 393224 | tf_op jit(solution)/shard_map/ppermute | solution.py:55
  62.8 19.0 %all-to-all-start.2 = ((f32[16,8,256]{2,1,0:T(8,128)}), f32[16,8,256]{2,1,0:T(8,128)S(1)}, u32[]{:S(2)}, u32[]{:S(2)}) async-start(f32[16,8,256]{2,1,0:T(8,128)} %sum_and_spread.2), calls=%async_computation.2 | async-start | bytes 262144 | tf_op jit(solution)/shard_map/all_to_all | solution.py:59
  72.6 7.8 %collective-permute-start.7 = (bf16[768,256]{1,0:T(8,128)(2,1)S(1)}, bf16[768,256]{1,0:T(8,128)(2,1)S(1)}, u32[]{:S(2)}, u32[]{:S(2)}) collective-permute-start(bf16[768,256]{1,0:T(8,128)(2,1)S(1)} %get-tuple-element.29), channel_id=1, source_target_pairs={{0,4},{4,0},{1,5},{5,1},{2,6},{6,2},{3,7},{7,3},{8,12},{12,8},{9,1... | collective-permute-start | bytes 1179656 | tf_op jit(solution)/shard_map/ppermute | solution.py:50
  76.0 16.9 %collective-permute-start.8 = (bf16[256,256]{1,0:T(8,128)(2,1)S(1)}, bf16[256,256]{1,0:T(8,128)(2,1)S(1)}, u32[]{:S(2)}, u32[]{:S(2)}) collective-permute-start(bf16[256,256]{1,0:T(8,128)(2,1)S(1)} %get-tuple-element.32), channel_id=1, source_target_pairs={{4,16},{12,24},{16,4},{20,32},{24,12},{28,40},{32,20},{36,48},{40,... | collective-permute-start | bytes 393224 | tf_op jit(solution)/shard_map/ppermute | solution.py:46
  80.4 12.4 %collective-permute-start.9 = (bf16[256,256]{1,0:T(8,128)(2,1)S(1)}, bf16[256,256]{1,0:T(8,128)(2,1)S(1)}, u32[]{:S(2)}, u32[]{:S(2)}) collective-permute-start(bf16[256,256]{1,0:T(8,128)(2,1)S(1)} %get-tuple-element.30), channel_id=1, source_target_pairs={{8,0},{12,4},{16,8},{20,12},{24,16},{28,20},{32,24},{36,28},{40,32... | collective-permute-start | bytes 393224 | tf_op jit(solution)/shard_map/ppermute | solution.py:36
  82.4 15.8 %all-to-all-start.3 = ((bf16[32,8,256]{2,1,0:T(8,128)(2,1)}), bf16[32,8,256]{2,1,0:T(8,128)(2,1)S(1)}, u32[]{:S(2)}, u32[]{:S(2)}) async-start(bf16[32,8,256]{2,1,0:T(8,128)(2,1)} %sum_and_spread.3), calls=%async_computation.3 | async-start | bytes 262144 | tf_op jit(solution)/shard_map/all_to_all | solution.py:59
  90.6 8.3 %collective-permute-start.10 = (bf16[256,256]{1,0:T(8,128)(2,1)S(1)}, bf16[256,256]{1,0:T(8,128)(2,1)S(1)}, u32[]{:S(2)}, u32[]{:S(2)}) collective-permute-start(bf16[256,256]{1,0:T(8,128)(2,1)S(1)} %get-tuple-element.36), channel_id=1, source_target_pairs={{0,8},{4,12},{8,16},{12,20},{16,24},{20,28},{24,32},{28,36},{32,40... | collective-permute-start | bytes 393224 | tf_op jit(solution)/shard_map/ppermute | solution.py:36

commit v11 on v10

--- a/solution.py
+++ b/solution.py
@@ -178,20 +178,24 @@
     back_ref[...] = lax.dot_general(
         weight_ref[...], grad_pre, (((1,), (1,)), ((), ())), preferred_element_type=F32
     ).astype(BF16)
-    local_ref[...] = lax.dot_general(
+    local = lax.dot_general(
         aggregate, grad_pre, (((0,), (0,)), ((), ())), preferred_element_type=F32
     )
+    piece = local_ref.shape[1]
+    for k in range(local_ref.shape[0]):
+        local_ref[k] = local[k * piece : (k + 1) * piece].astype(BF16)
     out_ref[...] = (preact * sigmoid_pre).astype(BF16)
 
 
 def dense_layer(parts, weight, cotangent):
     reps, rows, hidden = parts.shape
+    plane = X_CHIPS * CORES * reps
     return pl.pallas_call(
         dense_kernel,
         out_shape=(
             jax.ShapeDtypeStruct((rows, hidden), BF16),
             jax.ShapeDtypeStruct((hidden, rows), BF16),
-            jax.ShapeDtypeStruct((hidden, hidden), F32),
+            jax.ShapeDtypeStruct((plane, hidden // plane, hidden), BF16),
         ),
         compiler_params=params(8),
         cost_estimate=cost(1.3),
@@ -204,14 +208,17 @@
     hidden, rows = far_ref.shape
     rep = lax.axis_index("rep")
 
-    def fetch(piece):
-        return pltpu.make_async_copy(band_ref.at[piece], held.at[piece], arrived.at[piece])
-
-    order = [*range(HALF, 2 * HALF + 1), *range(HALF)]
-    for piece in order:
-        fetch(piece).start()
-    for piece in order:
-        fetch(piece).wait()
+    groups = (slice(HALF, SECTIONS), slice(0, HALF))
+
+    def fetch(turn):
+        at = groups[turn]
+        return pltpu.make_async_copy(band_ref.at[at], held.at[at], arrived.at[turn])
+
+    for turn in range(len(groups)):
+        fetch(turn).start()
+    for piece in (*range(HALF, SECTIONS), *range(HALF)):
+        if piece in (HALF, 0):
+            fetch(0 if piece else 1).wait()
         total = jnp.zeros((hidden, rows), F32)
         for k in range(reps):
             at = pl.multiple_of(lax.rem(rep + k, reps) * rows, rows)
@@ -241,7 +248,7 @@
             jax.ShapeDtypeStruct((HALF * hidden, rows), BF16),
             jax.ShapeDtypeStruct((hidden, rows), BF16),
         ),
-        scratch_shapes=[pltpu.VMEM(band.shape, BF16), pltpu.SemaphoreType.DMA((SECTIONS,))],
+        scratch_shapes=[pltpu.VMEM(band.shape, BF16), pltpu.SemaphoreType.DMA((2,))],
         compiler_params=params(12),
         cost_estimate=cost(GRADIENT_US),
         name="window_gradient",
@@ -332,7 +339,7 @@
     plane = lax.axis_size(PLANE)
     node_count = group_rows * lax.axis_size(ROW)
     back = [backward] + [rep_shift(backward, k) for k in range(1, reps)]
-    terms = to_all(local.reshape(plane, -1, hidden), PLANE)
+    terms = to_all(local, PLANE)
 
     spread = sum_and_spread(terms, line, F32)
     terms = to_all(spread, "z")

time: 101 us -> 100 us (0.990)
  transfers between devices with their start and end apart: 14 -> 14, of which waited for: 2 -> 2; matrix products, arithmetic and copies ran while one was open for 1% -> 1% of each run, Pallas kernels for 9% -> 8%
where the time goes in v11:
time: 100 us; the launch traced here: 99 us
  starting transfers between devices  66.7 us (67%)
  Pallas kernels  12.2 us (12%)
  blocking collectives  11.9 us (12%)
  waiting for transfers between devices  6.48 us (6%)
    all_to_all x3, starting transfers between devices, to_all(): return lax.all_to_all(x, axes, 0, 0, tiled=False)  29.2 us
    all_to_all x1, blocking collectives, to_all(): return lax.all_to_all(x, axes, 0, 0, tiled=False)  11.9 us
    ppermute x3, starting transfers between devices, rep_shift(): lax.ppermute(x, 'rep', [(i, (i - by) % devices) for i in range(devices)])  10.7 us
    ppermute x2, starting transfers between devices, far_shift(): return lax.ppermute(x, ROW, pairs)  10.6 us
    ppermute x4, starting transfers between devices, chip_shift(): lax.ppermute(x, ROW, [(i, i + by) for i in range(devices) if 0 <= i + by...  9.19 us
    ppermute x2, starting transfers between devices, core_swap(): return lax.ppermute(x, 'core', [(0, 1), (1, 0)])  7.07 us
    all_to_all x3, waiting for transfers between devices, to_all(): return lax.all_to_all(x, axes, 0, 0, tiled=False)  5.12 us
    pallas_call x1, Pallas kernels, dense_band(): pl.pallas_call(kernel, in_specs=[pl.BlockSpec(memory_space=pltpu.SMEM), p...  3.56 us
  transfers between devices with their start and end apart: 14, of which 2 were waited for; matrix products, arithmetic and copies ran while one was open for 1% of the time, Pallas kernels for 8%

profile of v11, /device:TPU:1, one launch (start us, length us, event | category | flops | bytes accessed | tf_op | source)
XLA Modules:
  0.0 99.0 jit_solution(12723279955416540737)
XLA Ops:
  0.6 0.9 own_quarter.1
  1.6 6.3 %collective-permute-start.2 = (bf16[256,256]{1,0:T(8,128)(2,1)S(1)}, bf16[256,256]{1,0:T(8,128)(2,1)S(1)}, u32[]{:S(2)}, u32[]{:S(2)}) collective-permute-start(bf16[256,256]{1,0:T(8,128)(2,1)S(1)} %own_quarter.1), channel_id=1, source_target_pairs={{4,16},{12,24},{16,4},{20,32},{24,12},{28,40},{32,20},{36,48},{40,... | collective-permute-start | bytes 393224 | tf_op jit(solution)/shard_map/ppermute | solution.py:46
  7.9 1.3 %collective-permute-start.1 = (bf16[256,256]{1,0:T(8,128)(2,1)S(1)}, bf16[256,256]{1,0:T(8,128)(2,1)S(1)}, u32[]{:S(2)}, u32[]{:S(2)}) collective-permute-start(bf16[256,256]{1,0:T(8,128)(2,1)S(1)} %own_quarter.1), channel_id=1, source_target_pairs={{8,0},{12,4},{16,8},{20,12},{24,16},{28,20},{32,24},{36,28},{40,32... | collective-permute-start | bytes 393224 | tf_op jit(solution)/shard_map/ppermute | solution.py:36
  9.2 4.2 %collective-permute-start = (bf16[256,256]{1,0:T(8,128)(2,1)S(1)}, bf16[256,256]{1,0:T(8,128)(2,1)S(1)}, u32[]{:S(2)}, u32[]{:S(2)}) collective-permute-start(bf16[256,256]{1,0:T(8,128)(2,1)S(1)} %own_quarter.1), channel_id=1, source_target_pairs={{0,8},{4,12},{8,16},{12,20},{16,24},{20,28},{24,32},{28,36},{32,40... | collective-permute-start | bytes 393224 | tf_op jit(solution)/shard_map/ppermute | solution.py:36
  13.3 3.6 %dense_band.1.band_ref.refs_0_ = bf16[7,1024,256]{2,1,0:T(8,128)(2,1)S(1)} custom-call(s32[8,1,12]{2,1,0:T(1,128)} %refs_0_.1, bf16[8,12,128,128]{3,2,1,0:T(8,128)(2,1)} %bitcast.4), custom_call_target="tpu_custom_call" | custom-call | bytes 14400000 | tf_op jit(solution)/shard_map/dense_band/pallas_call | solution.py:124
  16.9 0.0 copy-start
  16.9 0.0 copy-start.1
  16.9 0.0 copy-start.2
  16.9 0.0 collective-permute-done.2.far_ref
  17.0 0.0 collective-permute-done.1
  17.0 0.0 collective-permute-done
  17.0 3.7 %collective-permute-start.3 = (bf16[768,256]{1,0:T(8,128)(2,1)S(1)}, bf16[768,256]{1,0:T(8,128)(2,1)S(1)}, u32[]{:S(2)}, u32[]{:S(2)}) collective-permute-start(bf16[768,256]{1,0:T(8,128)(2,1)S(1)} %pad_maximum_fusion.near_ref), channel_id=1, source_target_pairs={{0,4},{4,0},{1,5},{5,1},{2,6},{6,2},{3,7},{7,3},{8,12},{12,8},{9,1... | collective-permute-start | bytes 1179656 | tf_op jit(solution)/shard_map/ppermute | solution.py:50
  20.7 1.3 %collective-permute-done.3.other_ref = bf16[768,256]{1,0:T(8,128)(2,1)S(1)} collective-permute-done((bf16[768,256]{1,0:T(8,128)(2,1)S(1)}, bf16[768,256]{1,0:T(8,128)(2,1)S(1)}, u32[]{:S(2)}, u32[]{:S(2)}) %collective-permute-start.3) | collective-permute-done | bytes 393248 | tf_op jit(solution)/shard_map/ppermute | solution.py:50
  22.0 1.1 %partial_aggregate.1 = bf16[4,256,256]{2,1,0:T(8,128)(2,1)S(1)} custom-call(bf16[7,1024,256]{2,1,0:T(8,128)(2,1)S(1)} %dense_band.1.band_ref.refs_0_, bf16[768,256]{1,0:T(8,128)(2,1)S(1)} %pad_maximum_fusion.near_ref, bf16[768,256]{1,0:T(8,128)(2,1)S(1)} %collective-permute-done.3.other_ref, bf16[256,256]{1,0:T(8,128)(2,1)S(1)} %collective-permute-done.2.far_ref), custom_call_target="tpu_custom_call" | custom-call | bytes 5400000 | tf_op jit(solution)/shard_map/partial_aggregate/pallas_call | solution.py:158
  23.1 11.9 %all_to_all.20.parts_ref = bf16[4,256,256]{2,1,0:T(8,128)(2,1)S(1)} all-to-all(bf16[4,256,256]{2,1,0:T(8,128)(2,1)S(1)} %partial_aggregate.1), channel_id=1, replica_groups=mesh['x'=4,'z'=16,'core'=2,'rep'=4] {'rep'}, dimensions={0} | all-to-all | bytes 1048576 | tf_op jit(solution)/shard_map/all_to_all | solution.py:59
  35.0 0.0 copy-done.1
  35.0 0.0 copy-done.2
  35.0 1.2 %dense_layer.1 = (bf16[256,256]{1,0:T(8,128)(2,1)}, bf16[256,256]{1,0:T(8,128)(2,1)S(1)}, bf16[32,8,256]{2,1,0:T(8,128)(2,1)}) custom-call(bf16[4,256,256]{2,1,0:T(8,128)(2,1)S(1)} %all_to_all.20.parts_ref, bf16[256,256]{1,0:T(8,128)(2,1)S(1)} %copy-done.1, bf16[256,256]{1,0:T(8,128)(2,1)S(1)} %copy-done.2), custom_call_target="tpu_custom_call" | custom-call | bytes 4680000 | tf_op jit(solution)/shard_map/dense_layer/pallas_call | solution.py:193
  36.2 0.0 copy-done
  36.2 15.1 %all-to-all-start.1 = ((bf16[32,8,256]{2,1,0:T(8,128)(2,1)}), bf16[32,8,256]{2,1,0:T(8,128)(2,1)S(1)}, u32[]{:S(2)}, u32[]{:S(2)}) async-start(bf16[32,8,256]{2,1,0:T(8,128)(2,1)} %get-tuple-element.25), calls=%async_computation.1 | async-start | bytes 262144 | tf_op jit(solution)/shard_map/all_to_all | solution.py:59
  51.3 3.3 %collective-permute-start.6 = (bf16[256,256]{1,0:T(8,128)(2,1)S(1)}, bf16[256,256]{1,0:T(8,128)(2,1)S(1)}, u32[]{:S(2)}, u32[]{:S(2)}) collective-permute-start(bf16[256,256]{1,0:T(8,128)(2,1)S(1)} %get-tuple-element.27.refs_1_), channel_id=1, source_target_pairs={{0,1},{1,2},{2,3},{3,0},{4,5},{5,6},{6,7},{7,4},{8,9},{9,10},{10,1... | collective-permute-start | bytes 393224 | tf_op jit(solution)/shard_map/ppermute | solution.py:55
  54.6 4.3 %collective-permute-start.5 = (bf16[256,256]{1,0:T(8,128)(2,1)S(1)}, bf16[256,256]{1,0:T(8,128)(2,1)S(1)}, u32[]{:S(2)}, u32[]{:S(2)}) collective-permute-start(bf16[256,256]{1,0:T(8,128)(2,1)S(1)} %get-tuple-element.27.refs_1_), channel_id=1, source_target_pairs={{0,2},{1,3},{2,0},{3,1},{4,6},{5,7},{6,4},{7,5},{8,10},{9,11},{10,... | collective-permute-start | bytes 393224 | tf_op jit(solution)/shard_map/ppermute | solution.py:55
  58.9 3.1 %collective-permute-start.4 = (bf16[256,256]{1,0:T(8,128)(2,1)S(1)}, bf16[256,256]{1,0:T(8,128)(2,1)S(1)}, u32[]{:S(2)}, u32[]{:S(2)}) collective-permute-start(bf16[256,256]{1,0:T(8,128)(2,1)S(1)} %get-tuple-element.27.refs_1_), channel_id=1, source_target_pairs={{0,3},{1,0},{2,1},{3,2},{4,7},{5,4},{6,5},{7,6},{8,11},{9,8},{10,9... | collective-permute-start | bytes 393224 | tf_op jit(solution)/shard_map/ppermute | solution.py:55
  62.0 0.0 all-to-all-done.1.refs_0_
  62.0 0.7 sum_and_spread.2
  62.7 5.9 %all-to-all-start.2 = ((f32[16,8,256]{2,1,0:T(8,128)}), f32[16,8,256]{2,1,0:T(8,128)S(1)}, u32[]{:S(2)}, u32[]{:S(2)}) async-start(f32[16,8,256]{2,1,0:T(8,128)} %sum_and_spread.2), calls=%async_computation.2 | async-start | bytes 262144 | tf_op jit(solution)/shard_map/all_to_all | solution.py:59
  68.6 0.0 collective-permute-done.6.refs_4_
  68.6 0.0 collective-permute-done.5.refs_3_
  68.6 0.0 collective-permute-done.4.refs_2_
  68.6 3.2 %window_gradient.1 = (f32[768,256]{1,0:T(8,128)S(1)}, bf16[768,256]{1,0:T(8,128)(2,1)S(1)}, bf16[256,256]{1,0:T(8,128)(2,1)S(1)}) custom-call(bf16[7,1024,256]{2,1,0:T(8,128)(2,1)} %copy-done, bf16[256,256]{1,0:T(8,128)(2,1)S(1)} %get-tuple-element.27.refs_1_, bf16[256,256]{1,0:T(8,128)(2,1)S(1)} %collective-permute-done.4.refs_2_, ...), custom_call_target="tpu_custom_call" | custom-call | bytes 7200000 | tf_op jit(solution)/shard_map/window_gradient/pallas_call | solution.py:243
  71.8 3.4 %collective-permute-start.7 = (bf16[768,256]{1,0:T(8,128)(2,1)S(1)}, bf16[768,256]{1,0:T(8,128)(2,1)S(1)}, u32[]{:S(2)}, u32[]{:S(2)}) collective-permute-start(bf16[768,256]{1,0:T(8,128)(2,1)S(1)} %get-tuple-element.29), channel_id=1, source_target_pairs={{0,4},{4,0},{1,5},{5,1},{2,6},{6,2},{3,7},{7,3},{8,12},{12,8},{9,1... | collective-permute-start | bytes 1179656 | tf_op jit(solution)/shard_map/ppermute | solution.py:50
  75.2 4.3 %collective-permute-start.8 = (bf16[256,256]{1,0:T(8,128)(2,1)S(1)}, bf16[256,256]{1,0:T(8,128)(2,1)S(1)}, u32[]{:S(2)}, u32[]{:S(2)}) collective-permute-start(bf16[256,256]{1,0:T(8,128)(2,1)S(1)} %get-tuple-element.32), channel_id=1, source_target_pairs={{4,16},{12,24},{16,4},{20,32},{24,12},{28,40},{32,20},{36,48},{40,... | collective-permute-start | bytes 393224 | tf_op jit(solution)/shard_map/ppermute | solution.py:46
  79.5 0.0 collective-permute-done.7.swapped_ref
  79.5 0.1 chip_sum.1
  79.6 1.3 %collective-permute-start.9 = (bf16[256,256]{1,0:T(8,128)(2,1)S(1)}, bf16[256,256]{1,0:T(8,128)(2,1)S(1)}, u32[]{:S(2)}, u32[]{:S(2)}) collective-permute-start(bf16[256,256]{1,0:T(8,128)(2,1)S(1)} %get-tuple-element.30), channel_id=1, source_target_pairs={{8,0},{12,4},{16,8},{20,12},{24,16},{28,20},{32,24},{36,28},{40,32... | collective-permute-start | bytes 393224 | tf_op jit(solution)/shard_map/ppermute | solution.py:36
  80.9 0.0 all-to-all-done.2.refs_0_
  80.9 0.7 sum_and_spread.3
  81.6 8.2 %all-to-all-start.3 = ((bf16[32,8,256]{2,1,0:T(8,128)(2,1)}), bf16[32,8,256]{2,1,0:T(8,128)(2,1)S(1)}, u32[]{:S(2)}, u32[]{:S(2)}) async-start(bf16[32,8,256]{2,1,0:T(8,128)(2,1)} %sum_and_spread.3), calls=%async_computation.3 | async-start | bytes 262144 | tf_op jit(solution)/shard_map/all_to_all | solution.py:59
  89.8 2.4 %collective-permute-start.10 = (bf16[256,256]{1,0:T(8,128)(2,1)S(1)}, bf16[256,256]{1,0:T(8,128)(2,1)S(1)}, u32[]{:S(2)}, u32[]{:S(2)}) collective-permute-start(bf16[256,256]{1,0:T(8,128)(2,1)S(1)} %get-tuple-element.36), channel_id=1, source_target_pairs={{0,8},{4,12},{8,16},{12,20},{16,24},{20,28},{24,32},{28,36},{32,40... | collective-permute-start | bytes 393224 | tf_op jit(solution)/shard_map/ppermute | solution.py:36
  92.3 0.0 collective-permute-done.8.far_ref
  92.3 0.0 collective-permute-done.9.after_ref
  92.3 5.1 %all-to-all-done.3 = bf16[32,8,256]{2,1,0:T(8,128)(2,1)S(1)} async-done(((bf16[32,8,256]{2,1,0:T(8,128)(2,1)}), bf16[32,8,256]{2,1,0:T(8,128)(2,1)S(1)}, u32[]{:S(2)}, u32[]{:S(2)}) %all-to-all-start.3) | async-done | bytes 131104 | tf_op jit(solution)/shard_map/all_to_all | solution.py:59
  97.4 0.7 bitcast_convert_fusion
  98.1 0.0 collective-permute-done.10.before_ref
  98.1 0.8 total_gradient.1
  (1 shorter events, 0.0 us)
Async XLA Ops:
  1.6 15.4 %collective-permute-start.2 = (bf16[256,256]{1,0:T(8,128)(2,1)S(1)}, bf16[256,256]{1,0:T(8,128)(2,1)S(1)}, u32[]{:S(2)}, u32[]{:S(2)}) collective-permute-start(bf16[256,256]{1,0:T(8,128)(2,1)S(1)} %own_quarter.1), channel_id=1, source_target_pairs={{4,16},{12,24},{16,4},{20,32},{24,12},{28,40},{32,20},{36,48},{40,... | collective-permute-start | bytes 393224 | tf_op jit(solution)/shard_map/ppermute | solution.py:46
  7.9 9.1 %collective-permute-start.1 = (bf16[256,256]{1,0:T(8,128)(2,1)S(1)}, bf16[256,256]{1,0:T(8,128)(2,1)S(1)}, u32[]{:S(2)}, u32[]{:S(2)}) collective-permute-start(bf16[256,256]{1,0:T(8,128)(2,1)S(1)} %own_quarter.1), channel_id=1, source_target_pairs={{8,0},{12,4},{16,8},{20,12},{24,16},{28,20},{32,24},{36,28},{40,32... | collective-permute-start | bytes 393224 | tf_op jit(solution)/shard_map/ppermute | solution.py:36
  9.2 7.8 %collective-permute-start = (bf16[256,256]{1,0:T(8,128)(2,1)S(1)}, bf16[256,256]{1,0:T(8,128)(2,1)S(1)}, u32[]{:S(2)}, u32[]{:S(2)}) collective-permute-start(bf16[256,256]{1,0:T(8,128)(2,1)S(1)} %own_quarter.1), channel_id=1, source_target_pairs={{0,8},{4,12},{8,16},{12,20},{16,24},{20,28},{24,32},{28,36},{32,40... | collective-permute-start | bytes 393224 | tf_op jit(solution)/shard_map/ppermute | solution.py:36
  16.9 19.3 %copy-start = (bf16[7,1024,256]{2,1,0:T(8,128)(2,1)}, bf16[7,1024,256]{2,1,0:T(8,128)(2,1)S(1)}, u32[]{:S(2)}) copy-start(bf16[7,1024,256]{2,1,0:T(8,128)(2,1)S(1)} %dense_band.1.band_ref.refs_0_) | copy-start | bytes 11010052
  16.9 18.1 %copy-start.1 = (bf16[256,256]{1,0:T(8,128)(2,1)S(1)}, bf16[256,256]{1,0:T(8,128)(2,1)}, u32[]{:S(2)}) copy-start(bf16[256,256]{1,0:T(8,128)(2,1)} %weight_ref.1) | copy-start | bytes 393220
  16.9 18.1 %copy-start.2 = (bf16[256,256]{1,0:T(8,128)(2,1)S(1)}, bf16[256,256]{1,0:T(8,128)(2,1)}, u32[]{:S(2)}) copy-start(bf16[256,256]{1,0:T(8,128)(2,1)} %cotangent_ref.1) | copy-start | bytes 393220
  17.0 5.0 %collective-permute-start.3 = (bf16[768,256]{1,0:T(8,128)(2,1)S(1)}, bf16[768,256]{1,0:T(8,128)(2,1)S(1)}, u32[]{:S(2)}, u32[]{:S(2)}) collective-permute-start(bf16[768,256]{1,0:T(8,128)(2,1)S(1)} %pad_maximum_fusion.near_ref), channel_id=1, source_target_pairs={{0,4},{4,0},{1,5},{5,1},{2,6},{6,2},{3,7},{7,3},{8,12},{12,8},{9,1... | collective-permute-start | bytes 1179656 | tf_op jit(solution)/shard_map/ppermute | solution.py:50
  36.2 25.8 %all-to-all-start.1 = ((bf16[32,8,256]{2,1,0:T(8,128)(2,1)}), bf16[32,8,256]{2,1,0:T(8,128)(2,1)S(1)}, u32[]{:S(2)}, u32[]{:S(2)}) async-start(bf16[32,8,256]{2,1,0:T(8,128)(2,1)} %get-tuple-element.25), calls=%async_computation.1 | async-start | bytes 262144 | tf_op jit(solution)/shard_map/all_to_all | solution.py:59
  51.3 17.3 %collective-permute-start.6 = (bf16[256,256]{1,0:T(8,128)(2,1)S(1)}, bf16[256,256]{1,0:T(8,128)(2,1)S(1)}, u32[]{:S(2)}, u32[]{:S(2)}) collective-permute-start(bf16[256,256]{1,0:T(8,128)(2,1)S(1)} %get-tuple-element.27.refs_1_), channel_id=1, source_target_pairs={{0,1},{1,2},{2,3},{3,0},{4,5},{5,6},{6,7},{7,4},{8,9},{9,10},{10,1... | collective-permute-start | bytes 393224 | tf_op jit(solution)/shard_map/ppermute | solution.py:55
  54.6 14.0 %collective-permute-start.5 = (bf16[256,256]{1,0:T(8,128)(2,1)S(1)}, bf16[256,256]{1,0:T(8,128)(2,1)S(1)}, u32[]{:S(2)}, u32[]{:S(2)}) collective-permute-start(bf16[256,256]{1,0:T(8,128)(2,1)S(1)} %get-tuple-element.27.refs_1_), channel_id=1, source_target_pairs={{0,2},{1,3},{2,0},{3,1},{4,6},{5,7},{6,4},{7,5},{8,10},{9,11},{10,... | collective-permute-start | bytes 393224 | tf_op jit(solution)/shard_map/ppermute | solution.py:55
  58.9 9.7 %collective-permute-start.4 = (bf16[256,256]{1,0:T(8,128)(2,1)S(1)}, bf16[256,256]{1,0:T(8,128)(2,1)S(1)}, u32[]{:S(2)}, u32[]{:S(2)}) collective-permute-start(bf16[256,256]{1,0:T(8,128)(2,1)S(1)} %get-tuple-element.27.refs_1_), channel_id=1, source_target_pairs={{0,3},{1,0},{2,1},{3,2},{4,7},{5,4},{6,5},{7,6},{8,11},{9,8},{10,9... | collective-permute-start | bytes 393224 | tf_op jit(solution)/shard_map/ppermute | solution.py:55
  62.7 18.2 %all-to-all-start.2 = ((f32[16,8,256]{2,1,0:T(8,128)}), f32[16,8,256]{2,1,0:T(8,128)S(1)}, u32[]{:S(2)}, u32[]{:S(2)}) async-start(f32[16,8,256]{2,1,0:T(8,128)} %sum_and_spread.2), calls=%async_computation.2 | async-start | bytes 262144 | tf_op jit(solution)/shard_map/all_to_all | solution.py:59
  71.8 7.8 %collective-permute-start.7 = (bf16[768,256]{1,0:T(8,128)(2,1)S(1)}, bf16[768,256]{1,0:T(8,128)(2,1)S(1)}, u32[]{:S(2)}, u32[]{:S(2)}) collective-permute-start(bf16[768,256]{1,0:T(8,128)(2,1)S(1)} %get-tuple-element.29), channel_id=1, source_target_pairs={{0,4},{4,0},{1,5},{5,1},{2,6},{6,2},{3,7},{7,3},{8,12},{12,8},{9,1... | collective-permute-start | bytes 1179656 | tf_op jit(solution)/shard_map/ppermute | solution.py:50
  75.2 17.1 %collective-permute-start.8 = (bf16[256,256]{1,0:T(8,128)(2,1)S(1)}, bf16[256,256]{1,0:T(8,128)(2,1)S(1)}, u32[]{:S(2)}, u32[]{:S(2)}) collective-permute-start(bf16[256,256]{1,0:T(8,128)(2,1)S(1)} %get-tuple-element.32), channel_id=1, source_target_pairs={{4,16},{12,24},{16,4},{20,32},{24,12},{28,40},{32,20},{36,48},{40,... | collective-permute-start | bytes 393224 | tf_op jit(solution)/shard_map/ppermute | solution.py:46
  79.6 12.7 %collective-permute-start.9 = (bf16[256,256]{1,0:T(8,128)(2,1)S(1)}, bf16[256,256]{1,0:T(8,128)(2,1)S(1)}, u32[]{:S(2)}, u32[]{:S(2)}) collective-permute-start(bf16[256,256]{1,0:T(8,128)(2,1)S(1)} %get-tuple-element.30), channel_id=1, source_target_pairs={{8,0},{12,4},{16,8},{20,12},{24,16},{28,20},{32,24},{36,28},{40,32... | collective-permute-start | bytes 393224 | tf_op jit(solution)/shard_map/ppermute | solution.py:36
  81.6 15.8 %all-to-all-start.3 = ((bf16[32,8,256]{2,1,0:T(8,128)(2,1)}), bf16[32,8,256]{2,1,0:T(8,128)(2,1)S(1)}, u32[]{:S(2)}, u32[]{:S(2)}) async-start(bf16[32,8,256]{2,1,0:T(8,128)(2,1)} %sum_and_spread.3), calls=%async_computation.3 | async-start | bytes 262144 | tf_op jit(solution)/shard_map/all_to_all | solution.py:59
  89.8 8.3 %collective-permute-start.10 = (bf16[256,256]{1,0:T(8,128)(2,1)S(1)}, bf16[256,256]{1,0:T(8,128)(2,1)S(1)}, u32[]{:S(2)}, u32[]{:S(2)}) collective-permute-start(bf16[256,256]{1,0:T(8,128)(2,1)S(1)} %get-tuple-element.36), channel_id=1, source_target_pairs={{0,8},{4,12},{8,16},{12,20},{16,24},{20,28},{24,32},{28,36},{32,40... | collective-permute-start | bytes 393224 | tf_op jit(solution)/shard_map/ppermute | solution.py:36

commit v12 on v11

--- a/solution.py
+++ b/solution.py
@@ -203,7 +203,8 @@
     )(parts, weight, cotangent)
 
 
-def gradient_kernel(reps, band_ref, *refs):
+def gradient_kernel(steps, band_ref, *refs):
+    reps = len(steps)
     near_ref, other_ref, far_ref, held, arrived = refs[reps:]
     hidden, rows = far_ref.shape
     rep = lax.axis_index("rep")
@@ -220,10 +221,10 @@
         if piece in (HALF, 0):
             fetch(0 if piece else 1).wait()
         total = jnp.zeros((hidden, rows), F32)
-        for k in range(reps):
+        for ref, k in zip(refs, steps):
             at = pl.multiple_of(lax.rem(rep + k, reps) * rows, rows)
             total = total + jnp.dot(
-                refs[k][...], held[piece, pl.ds(at, rows), :], preferred_element_type=F32
+                ref[...], held[piece, pl.ds(at, rows), :], preferred_element_type=F32
             )
         if piece < HALF:
             near_ref[piece * hidden : (piece + 1) * hidden, :] = total
@@ -233,12 +234,12 @@
             far_ref[...] = total.astype(BF16)
 
 
-def window_gradient(band, back):
+def window_gradient(band, back, order):
     reps = len(back)
     hidden, rows = back[0].shape
 
     def kernel(*refs):
-        gradient_kernel(reps, *refs)
+        gradient_kernel(order, *refs)
 
     return pl.pallas_call(
         kernel,
@@ -338,13 +339,14 @@
     line = lax.axis_size("z")
     plane = lax.axis_size(PLANE)
     node_count = group_rows * lax.axis_size(ROW)
-    back = [backward] + [rep_shift(backward, k) for k in range(1, reps)]
+    order = [0, *range(2, reps, 2), *range(1, reps, 2)]
+    back = [rep_shift(backward, k) if k else backward for k in order]
     terms = to_all(local, PLANE)
 
     spread = sum_and_spread(terms, line, F32)
     terms = to_all(spread, "z")
     band, _ = lax.optimization_barrier((band, spread))
-    near_grad, other_grad, far_grad = window_gradient(band, back)
+    near_grad, other_grad, far_grad = window_gradient(band, back, order)
     swapped = core_swap(other_grad)
     from_far = far_shift(far_grad)
     own_grad, before_grad, after_grad = chip_sum(near_grad, swapped)

time: 100 us -> 101 us (1.010)
    all_to_all x3, starting transfers between devices: 29.2 us -> 30.4 us  [to_all(): return lax.all_to_all(x, axes, 0, 0, tiled=False)]
where the time goes in v12:
time: 101 us; the launch traced here: 99.6 us
  starting transfers between devices  67.3 us (67%)
  Pallas kernels  12.2 us (12%)
  blocking collectives  11.9 us (12%)
  waiting for transfers between devices  6.48 us (6%)
    all_to_all x3, starting transfers between devices, to_all(): return lax.all_to_all(x, axes, 0, 0, tiled=False)  30.4 us
    all_to_all x1, blocking collectives, to_all(): return lax.all_to_all(x, axes, 0, 0, tiled=False)  11.9 us
    ppermute x2, starting transfers between devices, far_shift(): return lax.ppermute(x, ROW, pairs)  10.6 us
    ppermute x3, starting transfers between devices, rep_shift(): lax.ppermute(x, 'rep', [(i, (i - by) % devices) for i in range(devices)])  10.1 us
    ppermute x4, starting transfers between devices, chip_shift(): lax.ppermute(x, ROW, [(i, i + by) for i in range(devices) if 0 <= i + by...  9.18 us
    ppermute x2, starting transfers between devices, core_swap(): return lax.ppermute(x, 'core', [(0, 1), (1, 0)])  7.06 us
    all_to_all x3, waiting for transfers between devices, to_all(): return lax.all_to_all(x, axes, 0, 0, tiled=False)  5.13 us
    pallas_call x1, Pallas kernels, dense_band(): pl.pallas_call(kernel, in_specs=[pl.BlockSpec(memory_space=pltpu.SMEM), p...  3.56 us
  transfers between devices with their start and end apart: 14, of which 2 were waited for; matrix products, arithmetic and copies ran while one was open for 1% of the time, Pallas kernels for 8%

profile of v12, /device:TPU:1, one launch (start us, length us, event | category | flops | bytes accessed | tf_op | source)
XLA Modules:
  0.0 99.6 jit_solution(4021867087026141049)
XLA Ops:
  0.6 0.9 own_quarter.1
  1.6 6.3 %collective-permute-start.2 = (bf16[256,256]{1,0:T(8,128)(2,1)S(1)}, bf16[256,256]{1,0:T(8,128)(2,1)S(1)}, u32[]{:S(2)}, u32[]{:S(2)}) collective-permute-start(bf16[256,256]{1,0:T(8,128)(2,1)S(1)} %own_quarter.1), channel_id=1, source_target_pairs={{4,16},{12,24},{16,4},{20,32},{24,12},{28,40},{32,20},{36,48},{40,... | collective-permute-start | bytes 393224 | tf_op jit(solution)/shard_map/ppermute | solution.py:46
  7.9 1.3 %collective-permute-start.1 = (bf16[256,256]{1,0:T(8,128)(2,1)S(1)}, bf16[256,256]{1,0:T(8,128)(2,1)S(1)}, u32[]{:S(2)}, u32[]{:S(2)}) collective-permute-start(bf16[256,256]{1,0:T(8,128)(2,1)S(1)} %own_quarter.1), channel_id=1, source_target_pairs={{8,0},{12,4},{16,8},{20,12},{24,16},{28,20},{32,24},{36,28},{40,32... | collective-permute-start | bytes 393224 | tf_op jit(solution)/shard_map/ppermute | solution.py:36
  9.2 4.2 %collective-permute-start = (bf16[256,256]{1,0:T(8,128)(2,1)S(1)}, bf16[256,256]{1,0:T(8,128)(2,1)S(1)}, u32[]{:S(2)}, u32[]{:S(2)}) collective-permute-start(bf16[256,256]{1,0:T(8,128)(2,1)S(1)} %own_quarter.1), channel_id=1, source_target_pairs={{0,8},{4,12},{8,16},{12,20},{16,24},{20,28},{24,32},{28,36},{32,40... | collective-permute-start | bytes 393224 | tf_op jit(solution)/shard_map/ppermute | solution.py:36
  13.3 3.6 %dense_band.1.band_ref.refs_0_ = bf16[7,1024,256]{2,1,0:T(8,128)(2,1)S(1)} custom-call(s32[8,1,12]{2,1,0:T(1,128)} %refs_0_.1, bf16[8,12,128,128]{3,2,1,0:T(8,128)(2,1)} %bitcast.4), custom_call_target="tpu_custom_call" | custom-call | bytes 14400000 | tf_op jit(solution)/shard_map/dense_band/pallas_call | solution.py:124
  16.9 0.0 copy-start
  16.9 0.0 copy-start.1
  16.9 0.0 copy-start.2
  16.9 0.0 collective-permute-done.2.far_ref
  17.0 0.0 collective-permute-done.1
  17.0 0.0 collective-permute-done
  17.0 3.7 %collective-permute-start.3 = (bf16[768,256]{1,0:T(8,128)(2,1)S(1)}, bf16[768,256]{1,0:T(8,128)(2,1)S(1)}, u32[]{:S(2)}, u32[]{:S(2)}) collective-permute-start(bf16[768,256]{1,0:T(8,128)(2,1)S(1)} %pad_maximum_fusion.near_ref), channel_id=1, source_target_pairs={{0,4},{4,0},{1,5},{5,1},{2,6},{6,2},{3,7},{7,3},{8,12},{12,8},{9,1... | collective-permute-start | bytes 1179656 | tf_op jit(solution)/shard_map/ppermute | solution.py:50
  20.7 1.3 %collective-permute-done.3.other_ref = bf16[768,256]{1,0:T(8,128)(2,1)S(1)} collective-permute-done((bf16[768,256]{1,0:T(8,128)(2,1)S(1)}, bf16[768,256]{1,0:T(8,128)(2,1)S(1)}, u32[]{:S(2)}, u32[]{:S(2)}) %collective-permute-start.3) | collective-permute-done | bytes 393248 | tf_op jit(solution)/shard_map/ppermute | solution.py:50
  22.0 1.1 %partial_aggregate.1 = bf16[4,256,256]{2,1,0:T(8,128)(2,1)S(1)} custom-call(bf16[7,1024,256]{2,1,0:T(8,128)(2,1)S(1)} %dense_band.1.band_ref.refs_0_, bf16[768,256]{1,0:T(8,128)(2,1)S(1)} %pad_maximum_fusion.near_ref, bf16[768,256]{1,0:T(8,128)(2,1)S(1)} %collective-permute-done.3.other_ref, bf16[256,256]{1,0:T(8,128)(2,1)S(1)} %collective-permute-done.2.far_ref), custom_call_target="tpu_custom_call" | custom-call | bytes 5400000 | tf_op jit(solution)/shard_map/partial_aggregate/pallas_call | solution.py:158
  23.1 11.9 %all_to_all.20.parts_ref = bf16[4,256,256]{2,1,0:T(8,128)(2,1)S(1)} all-to-all(bf16[4,256,256]{2,1,0:T(8,128)(2,1)S(1)} %partial_aggregate.1), channel_id=1, replica_groups=mesh['x'=4,'z'=16,'core'=2,'rep'=4] {'rep'}, dimensions={0} | all-to-all | bytes 1048576 | tf_op jit(solution)/shard_map/all_to_all | solution.py:59
  35.0 0.0 copy-done.1
  35.0 0.0 copy-done.2
  35.0 1.2 %dense_layer.1 = (bf16[256,256]{1,0:T(8,128)(2,1)}, bf16[256,256]{1,0:T(8,128)(2,1)S(1)}, bf16[32,8,256]{2,1,0:T(8,128)(2,1)}) custom-call(bf16[4,256,256]{2,1,0:T(8,128)(2,1)S(1)} %all_to_all.20.parts_ref, bf16[256,256]{1,0:T(8,128)(2,1)S(1)} %copy-done.1, bf16[256,256]{1,0:T(8,128)(2,1)S(1)} %copy-done.2), custom_call_target="tpu_custom_call" | custom-call | bytes 4680000 | tf_op jit(solution)/shard_map/dense_layer/pallas_call | solution.py:193
  36.2 0.0 copy-done
  36.2 15.1 %all-to-all-start.1 = ((bf16[32,8,256]{2,1,0:T(8,128)(2,1)}), bf16[32,8,256]{2,1,0:T(8,128)(2,1)S(1)}, u32[]{:S(2)}, u32[]{:S(2)}) async-start(bf16[32,8,256]{2,1,0:T(8,128)(2,1)} %get-tuple-element.25), calls=%async_computation.1 | async-start | bytes 262144 | tf_op jit(solution)/shard_map/all_to_all | solution.py:59
  51.3 3.3 %collective-permute-start.6 = (bf16[256,256]{1,0:T(8,128)(2,1)S(1)}, bf16[256,256]{1,0:T(8,128)(2,1)S(1)}, u32[]{:S(2)}, u32[]{:S(2)}) collective-permute-start(bf16[256,256]{1,0:T(8,128)(2,1)S(1)} %get-tuple-element.27.refs_1_), channel_id=1, source_target_pairs={{0,1},{1,2},{2,3},{3,0},{4,5},{5,6},{6,7},{7,4},{8,9},{9,10},{10,1... | collective-permute-start | bytes 393224 | tf_op jit(solution)/shard_map/ppermute | solution.py:55
  54.6 3.2 %collective-permute-start.5 = (bf16[256,256]{1,0:T(8,128)(2,1)S(1)}, bf16[256,256]{1,0:T(8,128)(2,1)S(1)}, u32[]{:S(2)}, u32[]{:S(2)}) collective-permute-start(bf16[256,256]{1,0:T(8,128)(2,1)S(1)} %get-tuple-element.27.refs_1_), channel_id=1, source_target_pairs={{0,3},{1,0},{2,1},{3,2},{4,7},{5,4},{6,5},{7,6},{8,11},{9,8},{10,9... | collective-permute-start | bytes 393224 | tf_op jit(solution)/shard_map/ppermute | solution.py:55
  57.8 3.6 %collective-permute-start.4 = (bf16[256,256]{1,0:T(8,128)(2,1)S(1)}, bf16[256,256]{1,0:T(8,128)(2,1)S(1)}, u32[]{:S(2)}, u32[]{:S(2)}) collective-permute-start(bf16[256,256]{1,0:T(8,128)(2,1)S(1)} %get-tuple-element.27.refs_1_), channel_id=1, source_target_pairs={{0,2},{1,3},{2,0},{3,1},{4,6},{5,7},{6,4},{7,5},{8,10},{9,11},{10,... | collective-permute-start | bytes 393224 | tf_op jit(solution)/shard_map/ppermute | solution.py:55
  61.4 0.0 all-to-all-done.1.refs_0_
  61.4 0.7 sum_and_spread.2
  62.1 5.9 %all-to-all-start.2 = ((f32[16,8,256]{2,1,0:T(8,128)}), f32[16,8,256]{2,1,0:T(8,128)S(1)}, u32[]{:S(2)}, u32[]{:S(2)}) async-start(f32[16,8,256]{2,1,0:T(8,128)} %sum_and_spread.2), calls=%async_computation.2 | async-start | bytes 262144 | tf_op jit(solution)/shard_map/all_to_all | solution.py:59
  68.0 0.0 collective-permute-done.6.refs_4_
  68.0 0.0 collective-permute-done.5.refs_3_
  68.0 0.0 collective-permute-done.4.refs_2_
  68.0 3.2 %window_gradient.1 = (f32[768,256]{1,0:T(8,128)S(1)}, bf16[768,256]{1,0:T(8,128)(2,1)S(1)}, bf16[256,256]{1,0:T(8,128)(2,1)S(1)}) custom-call(bf16[7,1024,256]{2,1,0:T(8,128)(2,1)} %copy-done, bf16[256,256]{1,0:T(8,128)(2,1)S(1)} %get-tuple-element.27.refs_1_, bf16[256,256]{1,0:T(8,128)(2,1)S(1)} %collective-permute-done.4.refs_2_, ...), custom_call_target="tpu_custom_call" | custom-call | bytes 7200000 | tf_op jit(solution)/shard_map/window_gradient/pallas_call | solution.py:244
  71.2 3.4 %collective-permute-start.7 = (bf16[768,256]{1,0:T(8,128)(2,1)S(1)}, bf16[768,256]{1,0:T(8,128)(2,1)S(1)}, u32[]{:S(2)}, u32[]{:S(2)}) collective-permute-start(bf16[768,256]{1,0:T(8,128)(2,1)S(1)} %get-tuple-element.29), channel_id=1, source_target_pairs={{0,4},{4,0},{1,5},{5,1},{2,6},{6,2},{3,7},{7,3},{8,12},{12,8},{9,1... | collective-permute-start | bytes 1179656 | tf_op jit(solution)/shard_map/ppermute | solution.py:50
  74.6 4.4 %collective-permute-start.8 = (bf16[256,256]{1,0:T(8,128)(2,1)S(1)}, bf16[256,256]{1,0:T(8,128)(2,1)S(1)}, u32[]{:S(2)}, u32[]{:S(2)}) collective-permute-start(bf16[256,256]{1,0:T(8,128)(2,1)S(1)} %get-tuple-element.32), channel_id=1, source_target_pairs={{4,16},{12,24},{16,4},{20,32},{24,12},{28,40},{32,20},{36,48},{40,... | collective-permute-start | bytes 393224 | tf_op jit(solution)/shard_map/ppermute | solution.py:46
  78.9 0.0 collective-permute-done.7.swapped_ref
  78.9 0.1 chip_sum.1
  79.0 1.3 %collective-permute-start.9 = (bf16[256,256]{1,0:T(8,128)(2,1)S(1)}, bf16[256,256]{1,0:T(8,128)(2,1)S(1)}, u32[]{:S(2)}, u32[]{:S(2)}) collective-permute-start(bf16[256,256]{1,0:T(8,128)(2,1)S(1)} %get-tuple-element.30), channel_id=1, source_target_pairs={{8,0},{12,4},{16,8},{20,12},{24,16},{28,20},{32,24},{36,28},{40,32... | collective-permute-start | bytes 393224 | tf_op jit(solution)/shard_map/ppermute | solution.py:36
  80.3 0.0 all-to-all-done.2.refs_0_
  80.3 0.7 sum_and_spread.3
  81.0 9.4 %all-to-all-start.3 = ((bf16[32,8,256]{2,1,0:T(8,128)(2,1)}), bf16[32,8,256]{2,1,0:T(8,128)(2,1)S(1)}, u32[]{:S(2)}, u32[]{:S(2)}) async-start(bf16[32,8,256]{2,1,0:T(8,128)(2,1)} %sum_and_spread.3), calls=%async_computation.3 | async-start | bytes 262144 | tf_op jit(solution)/shard_map/all_to_all | solution.py:59
  90.4 2.4 %collective-permute-start.10 = (bf16[256,256]{1,0:T(8,128)(2,1)S(1)}, bf16[256,256]{1,0:T(8,128)(2,1)S(1)}, u32[]{:S(2)}, u32[]{:S(2)}) collective-permute-start(bf16[256,256]{1,0:T(8,128)(2,1)S(1)} %get-tuple-element.36), channel_id=1, source_target_pairs={{0,8},{4,12},{8,16},{12,20},{16,24},{20,28},{24,32},{28,36},{32,40... | collective-permute-start | bytes 393224 | tf_op jit(solution)/shard_map/ppermute | solution.py:36
  92.9 0.0 collective-permute-done.8.far_ref
  92.9 0.0 collective-permute-done.9.after_ref
  92.9 5.1 %all-to-all-done.3 = bf16[32,8,256]{2,1,0:T(8,128)(2,1)S(1)} async-done(((bf16[32,8,256]{2,1,0:T(8,128)(2,1)}), bf16[32,8,256]{2,1,0:T(8,128)(2,1)S(1)}, u32[]{:S(2)}, u32[]{:S(2)}) %all-to-all-start.3) | async-done | bytes 131104 | tf_op jit(solution)/shard_map/all_to_all | solution.py:59
  98.0 0.7 bitcast_convert_fusion
  98.7 0.0 collective-permute-done.10.before_ref
  98.7 0.8 total_gradient.1
  (1 shorter events, 0.0 us)
Async XLA Ops:
  1.6 15.4 %collective-permute-start.2 = (bf16[256,256]{1,0:T(8,128)(2,1)S(1)}, bf16[256,256]{1,0:T(8,128)(2,1)S(1)}, u32[]{:S(2)}, u32[]{:S(2)}) collective-permute-start(bf16[256,256]{1,0:T(8,128)(2,1)S(1)} %own_quarter.1), channel_id=1, source_target_pairs={{4,16},{12,24},{16,4},{20,32},{24,12},{28,40},{32,20},{36,48},{40,... | collective-permute-start | bytes 393224 | tf_op jit(solution)/shard_map/ppermute | solution.py:46
  7.9 9.1 %collective-permute-start.1 = (bf16[256,256]{1,0:T(8,128)(2,1)S(1)}, bf16[256,256]{1,0:T(8,128)(2,1)S(1)}, u32[]{:S(2)}, u32[]{:S(2)}) collective-permute-start(bf16[256,256]{1,0:T(8,128)(2,1)S(1)} %own_quarter.1), channel_id=1, source_target_pairs={{8,0},{12,4},{16,8},{20,12},{24,16},{28,20},{32,24},{36,28},{40,32... | collective-permute-start | bytes 393224 | tf_op jit(solution)/shard_map/ppermute | solution.py:36
  9.2 7.8 %collective-permute-start = (bf16[256,256]{1,0:T(8,128)(2,1)S(1)}, bf16[256,256]{1,0:T(8,128)(2,1)S(1)}, u32[]{:S(2)}, u32[]{:S(2)}) collective-permute-start(bf16[256,256]{1,0:T(8,128)(2,1)S(1)} %own_quarter.1), channel_id=1, source_target_pairs={{0,8},{4,12},{8,16},{12,20},{16,24},{20,28},{24,32},{28,36},{32,40... | collective-permute-start | bytes 393224 | tf_op jit(solution)/shard_map/ppermute | solution.py:36
  16.9 19.3 %copy-start = (bf16[7,1024,256]{2,1,0:T(8,128)(2,1)}, bf16[7,1024,256]{2,1,0:T(8,128)(2,1)S(1)}, u32[]{:S(2)}) copy-start(bf16[7,1024,256]{2,1,0:T(8,128)(2,1)S(1)} %dense_band.1.band_ref.refs_0_) | copy-start | bytes 11010052
  16.9 18.1 %copy-start.1 = (bf16[256,256]{1,0:T(8,128)(2,1)S(1)}, bf16[256,256]{1,0:T(8,128)(2,1)}, u32[]{:S(2)}) copy-start(bf16[256,256]{1,0:T(8,128)(2,1)} %weight_ref.1) | copy-start | bytes 393220
  16.9 18.1 %copy-start.2 = (bf16[256,256]{1,0:T(8,128)(2,1)S(1)}, bf16[256,256]{1,0:T(8,128)(2,1)}, u32[]{:S(2)}) copy-start(bf16[256,256]{1,0:T(8,128)(2,1)} %cotangent_ref.1) | copy-start | bytes 393220
  17.0 5.0 %collective-permute-start.3 = (bf16[768,256]{1,0:T(8,128)(2,1)S(1)}, bf16[768,256]{1,0:T(8,128)(2,1)S(1)}, u32[]{:S(2)}, u32[]{:S(2)}) collective-permute-start(bf16[768,256]{1,0:T(8,128)(2,1)S(1)} %pad_maximum_fusion.near_ref), channel_id=1, source_target_pairs={{0,4},{4,0},{1,5},{5,1},{2,6},{6,2},{3,7},{7,3},{8,12},{12,8},{9,1... | collective-permute-start | bytes 1179656 | tf_op jit(solution)/shard_map/ppermute | solution.py:50
  36.2 25.2 %all-to-all-start.1 = ((bf16[32,8,256]{2,1,0:T(8,128)(2,1)}), bf16[32,8,256]{2,1,0:T(8,128)(2,1)S(1)}, u32[]{:S(2)}, u32[]{:S(2)}) async-start(bf16[32,8,256]{2,1,0:T(8,128)(2,1)} %get-tuple-element.25), calls=%async_computation.1 | async-start | bytes 262144 | tf_op jit(solution)/shard_map/all_to_all | solution.py:59
  51.3 16.7 %collective-permute-start.6 = (bf16[256,256]{1,0:T(8,128)(2,1)S(1)}, bf16[256,256]{1,0:T(8,128)(2,1)S(1)}, u32[]{:S(2)}, u32[]{:S(2)}) collective-permute-start(bf16[256,256]{1,0:T(8,128)(2,1)S(1)} %get-tuple-element.27.refs_1_), channel_id=1, source_target_pairs={{0,1},{1,2},{2,3},{3,0},{4,5},{5,6},{6,7},{7,4},{8,9},{9,10},{10,1... | collective-permute-start | bytes 393224 | tf_op jit(solution)/shard_map/ppermute | solution.py:55
  54.6 13.4 %collective-permute-start.5 = (bf16[256,256]{1,0:T(8,128)(2,1)S(1)}, bf16[256,256]{1,0:T(8,128)(2,1)S(1)}, u32[]{:S(2)}, u32[]{:S(2)}) collective-permute-start(bf16[256,256]{1,0:T(8,128)(2,1)S(1)} %get-tuple-element.27.refs_1_), channel_id=1, source_target_pairs={{0,3},{1,0},{2,1},{3,2},{4,7},{5,4},{6,5},{7,6},{8,11},{9,8},{10,9... | collective-permute-start | bytes 393224 | tf_op jit(solution)/shard_map/ppermute | solution.py:55
  57.8 10.2 %collective-permute-start.4 = (bf16[256,256]{1,0:T(8,128)(2,1)S(1)}, bf16[256,256]{1,0:T(8,128)(2,1)S(1)}, u32[]{:S(2)}, u32[]{:S(2)}) collective-permute-start(bf16[256,256]{1,0:T(8,128)(2,1)S(1)} %get-tuple-element.27.refs_1_), channel_id=1, source_target_pairs={{0,2},{1,3},{2,0},{3,1},{4,6},{5,7},{6,4},{7,5},{8,10},{9,11},{10,... | collective-permute-start | bytes 393224 | tf_op jit(solution)/shard_map/ppermute | solution.py:55
  62.1 18.2 %all-to-all-start.2 = ((f32[16,8,256]{2,1,0:T(8,128)}), f32[16,8,256]{2,1,0:T(8,128)S(1)}, u32[]{:S(2)}, u32[]{:S(2)}) async-start(f32[16,8,256]{2,1,0:T(8,128)} %sum_and_spread.2), calls=%async_computation.2 | async-start | bytes 262144 | tf_op jit(solution)/shard_map/all_to_all | solution.py:59
  71.2 7.8 %collective-permute-start.7 = (bf16[768,256]{1,0:T(8,128)(2,1)S(1)}, bf16[768,256]{1,0:T(8,128)(2,1)S(1)}, u32[]{:S(2)}, u32[]{:S(2)}) collective-permute-start(bf16[768,256]{1,0:T(8,128)(2,1)S(1)} %get-tuple-element.29), channel_id=1, source_target_pairs={{0,4},{4,0},{1,5},{5,1},{2,6},{6,2},{3,7},{7,3},{8,12},{12,8},{9,1... | collective-permute-start | bytes 1179656 | tf_op jit(solution)/shard_map/ppermute | solution.py:50
  74.6 18.3 %collective-permute-start.8 = (bf16[256,256]{1,0:T(8,128)(2,1)S(1)}, bf16[256,256]{1,0:T(8,128)(2,1)S(1)}, u32[]{:S(2)}, u32[]{:S(2)}) collective-permute-start(bf16[256,256]{1,0:T(8,128)(2,1)S(1)} %get-tuple-element.32), channel_id=1, source_target_pairs={{4,16},{12,24},{16,4},{20,32},{24,12},{28,40},{32,20},{36,48},{40,... | collective-permute-start | bytes 393224 | tf_op jit(solution)/shard_map/ppermute | solution.py:46
  79.0 13.9 %collective-permute-start.9 = (bf16[256,256]{1,0:T(8,128)(2,1)S(1)}, bf16[256,256]{1,0:T(8,128)(2,1)S(1)}, u32[]{:S(2)}, u32[]{:S(2)}) collective-permute-start(bf16[256,256]{1,0:T(8,128)(2,1)S(1)} %get-tuple-element.30), channel_id=1, source_target_pairs={{8,0},{12,4},{16,8},{20,12},{24,16},{28,20},{32,24},{36,28},{40,32... | collective-permute-start | bytes 393224 | tf_op jit(solution)/shard_map/ppermute | solution.py:36
  81.0 17.0 %all-to-all-start.3 = ((bf16[32,8,256]{2,1,0:T(8,128)(2,1)}), bf16[32,8,256]{2,1,0:T(8,128)(2,1)S(1)}, u32[]{:S(2)}, u32[]{:S(2)}) async-start(bf16[32,8,256]{2,1,0:T(8,128)(2,1)} %sum_and_spread.3), calls=%async_computation.3 | async-start | bytes 262144 | tf_op jit(solution)/shard_map/all_to_all | solution.py:59
  90.4 8.3 %collective-permute-start.10 = (bf16[256,256]{1,0:T(8,128)(2,1)S(1)}, bf16[256,256]{1,0:T(8,128)(2,1)S(1)}, u32[]{:S(2)}, u32[]{:S(2)}) collective-permute-start(bf16[256,256]{1,0:T(8,128)(2,1)S(1)} %get-tuple-element.36), channel_id=1, source_target_pairs={{0,8},{4,12},{8,16},{12,20},{16,24},{20,28},{24,32},{28,36},{32,40... | collective-permute-start | bytes 393224 | tf_op jit(solution)/shard_map/ppermute | solution.py:36

commit v13 on v11

--- a/solution.py
+++ b/solution.py
@@ -15,6 +15,7 @@
 BF16 = jnp.bfloat16
 F32 = jnp.float32
 PIECE_OF = ((6, 1, 4, 0, 3, 2, 5), (4, 1, 3, 0, 5, 2, 6))
+TOGETHER = 2
 PIECE_CODE = tuple(sum(p << (4 * d) for d, p in enumerate(row)) for row in PIECE_OF)
 
 
@@ -88,16 +89,20 @@
     code = jnp.where(lax.axis_index("core") == 0, PIECE_CODE[0], PIECE_CODE[1])
 
     def fetch(block):
-        return pltpu.make_async_copy(vals_ref.at[block], held.at[block], arrived.at[block])
+        at = pl.ds(block * TOGETHER, TOGETHER)
+        return pltpu.make_async_copy(vals_ref.at[at], held.at[at], arrived.at[block])
 
     def rows_of(block):
         return pl.ds(pl.multiple_of(block * side, side), side)
 
-    for block in range(blocks):
+    for block in range(blocks // TOGETHER):
         fetch(block).start()
 
     def step(block, carry):
-        fetch(block).wait()
+        @pl.when(lax.rem(block, TOGETHER) == 0)
+        def _():
+            fetch(lax.div(block, TOGETHER)).wait()
+
         sums[...] = jnp.zeros_like(sums)
         for s in range(slots):
             column = cols_ref[block, 0, s]
@@ -129,7 +134,7 @@
         scratch_shapes=[
             pltpu.VMEM(vals.shape, BF16),
             pltpu.VMEM((columns, side, side), F32),
-            pltpu.SemaphoreType.DMA((blocks,)),
+            pltpu.SemaphoreType.DMA((blocks // TOGETHER,)),
         ],
         compiler_params=params(16),
         cost_estimate=cost(4),

time: 100 us -> 100 us (level)
  no operation moved by 1% of the time
where the time goes in v13:
time: 100 us; the launch traced here: 99 us
  starting transfers between devices  66.6 us (67%)
  Pallas kernels  12.3 us (12%)
  blocking collectives  11.9 us (12%)
  waiting for transfers between devices  6.48 us (6%)
    all_to_all x3, starting transfers between devices, to_all(): return lax.all_to_all(x, axes, 0, 0, tiled=False)  29.1 us
    all_to_all x1, blocking collectives, to_all(): return lax.all_to_all(x, axes, 0, 0, tiled=False)  11.9 us
    ppermute x3, starting transfers between devices, rep_shift(): lax.ppermute(x, 'rep', [(i, (i - by) % devices) for i in range(devices)])  10.7 us
    ppermute x2, starting transfers between devices, far_shift(): return lax.ppermute(x, ROW, pairs)  10.6 us
    ppermute x4, starting transfers between devices, chip_shift(): lax.ppermute(x, ROW, [(i, i + by) for i in range(devices) if 0 <= i + by...  9.19 us
    ppermute x2, starting transfers between devices, core_swap(): return lax.ppermute(x, 'core', [(0, 1), (1, 0)])  7.07 us
    all_to_all x3, waiting for transfers between devices, to_all(): return lax.all_to_all(x, axes, 0, 0, tiled=False)  5.12 us
    pallas_call x1, Pallas kernels, dense_band(): pl.pallas_call(kernel, in_specs=[pl.BlockSpec(memory_space=pltpu.SMEM), p...  3.68 us
  transfers between devices with their start and end apart: 14, of which 2 were waited for; matrix products, arithmetic and copies ran while one was open for 1% of the time, Pallas kernels for 8%

profile of v13, /device:TPU:1, one launch (start us, length us, event | category | flops | bytes accessed | tf_op | source)
XLA Modules:
  0.0 99.0 jit_solution(3333587630770830681)
XLA Ops:
  0.6 0.9 own_quarter.1
  1.6 6.3 %collective-permute-start.2 = (bf16[256,256]{1,0:T(8,128)(2,1)S(1)}, bf16[256,256]{1,0:T(8,128)(2,1)S(1)}, u32[]{:S(2)}, u32[]{:S(2)}) collective-permute-start(bf16[256,256]{1,0:T(8,128)(2,1)S(1)} %own_quarter.1), channel_id=1, source_target_pairs={{4,16},{12,24},{16,4},{20,32},{24,12},{28,40},{32,20},{36,48},{40,... | collective-permute-start | bytes 393224 | tf_op jit(solution)/shard_map/ppermute | solution.py:47
  7.9 1.3 %collective-permute-start.1 = (bf16[256,256]{1,0:T(8,128)(2,1)S(1)}, bf16[256,256]{1,0:T(8,128)(2,1)S(1)}, u32[]{:S(2)}, u32[]{:S(2)}) collective-permute-start(bf16[256,256]{1,0:T(8,128)(2,1)S(1)} %own_quarter.1), channel_id=1, source_target_pairs={{8,0},{12,4},{16,8},{20,12},{24,16},{28,20},{32,24},{36,28},{40,32... | collective-permute-start | bytes 393224 | tf_op jit(solution)/shard_map/ppermute | solution.py:37
  9.2 4.2 %collective-permute-start = (bf16[256,256]{1,0:T(8,128)(2,1)S(1)}, bf16[256,256]{1,0:T(8,128)(2,1)S(1)}, u32[]{:S(2)}, u32[]{:S(2)}) collective-permute-start(bf16[256,256]{1,0:T(8,128)(2,1)S(1)} %own_quarter.1), channel_id=1, source_target_pairs={{0,8},{4,12},{8,16},{12,20},{16,24},{20,28},{24,32},{28,36},{32,40... | collective-permute-start | bytes 393224 | tf_op jit(solution)/shard_map/ppermute | solution.py:37
  13.3 3.7 %dense_band.1.band_ref.refs_0_ = bf16[7,1024,256]{2,1,0:T(8,128)(2,1)S(1)} custom-call(s32[8,1,12]{2,1,0:T(1,128)} %refs_0_.1, bf16[8,12,128,128]{3,2,1,0:T(8,128)(2,1)} %bitcast.4), custom_call_target="tpu_custom_call" | custom-call | bytes 14400000 | tf_op jit(solution)/shard_map/dense_band/pallas_call | solution.py:129
  17.0 0.0 copy-start
  17.0 0.0 copy-start.1
  17.1 0.0 copy-start.2
  17.1 0.0 collective-permute-done.2.far_ref
  17.1 0.0 collective-permute-done.1
  17.1 0.0 collective-permute-done
  17.1 3.7 %collective-permute-start.3 = (bf16[768,256]{1,0:T(8,128)(2,1)S(1)}, bf16[768,256]{1,0:T(8,128)(2,1)S(1)}, u32[]{:S(2)}, u32[]{:S(2)}) collective-permute-start(bf16[768,256]{1,0:T(8,128)(2,1)S(1)} %pad_maximum_fusion.near_ref), channel_id=1, source_target_pairs={{0,4},{4,0},{1,5},{5,1},{2,6},{6,2},{3,7},{7,3},{8,12},{12,8},{9,1... | collective-permute-start | bytes 1179656 | tf_op jit(solution)/shard_map/ppermute | solution.py:51
  20.8 1.3 %collective-permute-done.3.other_ref = bf16[768,256]{1,0:T(8,128)(2,1)S(1)} collective-permute-done((bf16[768,256]{1,0:T(8,128)(2,1)S(1)}, bf16[768,256]{1,0:T(8,128)(2,1)S(1)}, u32[]{:S(2)}, u32[]{:S(2)}) %collective-permute-start.3) | collective-permute-done | bytes 393248 | tf_op jit(solution)/shard_map/ppermute | solution.py:51
  22.1 1.1 %partial_aggregate.1 = bf16[4,256,256]{2,1,0:T(8,128)(2,1)S(1)} custom-call(bf16[7,1024,256]{2,1,0:T(8,128)(2,1)S(1)} %dense_band.1.band_ref.refs_0_, bf16[768,256]{1,0:T(8,128)(2,1)S(1)} %pad_maximum_fusion.near_ref, bf16[768,256]{1,0:T(8,128)(2,1)S(1)} %collective-permute-done.3.other_ref, bf16[256,256]{1,0:T(8,128)(2,1)S(1)} %collective-permute-done.2.far_ref), custom_call_target="tpu_custom_call" | custom-call | bytes 5400000 | tf_op jit(solution)/shard_map/partial_aggregate/pallas_call | solution.py:163
  23.3 11.9 %all_to_all.20.parts_ref = bf16[4,256,256]{2,1,0:T(8,128)(2,1)S(1)} all-to-all(bf16[4,256,256]{2,1,0:T(8,128)(2,1)S(1)} %partial_aggregate.1), channel_id=1, replica_groups=mesh['x'=4,'z'=16,'core'=2,'rep'=4] {'rep'}, dimensions={0} | all-to-all | bytes 1048576 | tf_op jit(solution)/shard_map/all_to_all | solution.py:60
  35.2 0.0 copy-done.1
  35.2 0.0 copy-done.2
  35.2 1.2 %dense_layer.1 = (bf16[256,256]{1,0:T(8,128)(2,1)}, bf16[256,256]{1,0:T(8,128)(2,1)S(1)}, bf16[32,8,256]{2,1,0:T(8,128)(2,1)}) custom-call(bf16[4,256,256]{2,1,0:T(8,128)(2,1)S(1)} %all_to_all.20.parts_ref, bf16[256,256]{1,0:T(8,128)(2,1)S(1)} %copy-done.1, bf16[256,256]{1,0:T(8,128)(2,1)S(1)} %copy-done.2), custom_call_target="tpu_custom_call" | custom-call | bytes 4680000 | tf_op jit(solution)/shard_map/dense_layer/pallas_call | solution.py:198
  36.3 0.0 copy-done
  36.3 15.0 %all-to-all-start.1 = ((bf16[32,8,256]{2,1,0:T(8,128)(2,1)}), bf16[32,8,256]{2,1,0:T(8,128)(2,1)S(1)}, u32[]{:S(2)}, u32[]{:S(2)}) async-start(bf16[32,8,256]{2,1,0:T(8,128)(2,1)} %get-tuple-element.25), calls=%async_computation.1 | async-start | bytes 262144 | tf_op jit(solution)/shard_map/all_to_all | solution.py:60
  51.3 3.3 %collective-permute-start.6 = (bf16[256,256]{1,0:T(8,128)(2,1)S(1)}, bf16[256,256]{1,0:T(8,128)(2,1)S(1)}, u32[]{:S(2)}, u32[]{:S(2)}) collective-permute-start(bf16[256,256]{1,0:T(8,128)(2,1)S(1)} %get-tuple-element.27.refs_1_), channel_id=1, source_target_pairs={{0,1},{1,2},{2,3},{3,0},{4,5},{5,6},{6,7},{7,4},{8,9},{9,10},{10,1... | collective-permute-start | bytes 393224 | tf_op jit(solution)/shard_map/ppermute | solution.py:56
  54.6 4.3 %collective-permute-start.5 = (bf16[256,256]{1,0:T(8,128)(2,1)S(1)}, bf16[256,256]{1,0:T(8,128)(2,1)S(1)}, u32[]{:S(2)}, u32[]{:S(2)}) collective-permute-start(bf16[256,256]{1,0:T(8,128)(2,1)S(1)} %get-tuple-element.27.refs_1_), channel_id=1, source_target_pairs={{0,2},{1,3},{2,0},{3,1},{4,6},{5,7},{6,4},{7,5},{8,10},{9,11},{10,... | collective-permute-start | bytes 393224 | tf_op jit(solution)/shard_map/ppermute | solution.py:56
  58.9 3.1 %collective-permute-start.4 = (bf16[256,256]{1,0:T(8,128)(2,1)S(1)}, bf16[256,256]{1,0:T(8,128)(2,1)S(1)}, u32[]{:S(2)}, u32[]{:S(2)}) collective-permute-start(bf16[256,256]{1,0:T(8,128)(2,1)S(1)} %get-tuple-element.27.refs_1_), channel_id=1, source_target_pairs={{0,3},{1,0},{2,1},{3,2},{4,7},{5,4},{6,5},{7,6},{8,11},{9,8},{10,9... | collective-permute-start | bytes 393224 | tf_op jit(solution)/shard_map/ppermute | solution.py:56
  62.0 0.0 all-to-all-done.1.refs_0_
  62.0 0.7 sum_and_spread.2
  62.7 5.9 %all-to-all-start.2 = ((f32[16,8,256]{2,1,0:T(8,128)}), f32[16,8,256]{2,1,0:T(8,128)S(1)}, u32[]{:S(2)}, u32[]{:S(2)}) async-start(f32[16,8,256]{2,1,0:T(8,128)} %sum_and_spread.2), calls=%async_computation.2 | async-start | bytes 262144 | tf_op jit(solution)/shard_map/all_to_all | solution.py:60
  68.6 0.0 collective-permute-done.6.refs_4_
  68.6 0.0 collective-permute-done.5.refs_3_
  68.6 0.0 collective-permute-done.4.refs_2_
  68.6 3.2 %window_gradient.1 = (f32[768,256]{1,0:T(8,128)S(1)}, bf16[768,256]{1,0:T(8,128)(2,1)S(1)}, bf16[256,256]{1,0:T(8,128)(2,1)S(1)}) custom-call(bf16[7,1024,256]{2,1,0:T(8,128)(2,1)} %copy-done, bf16[256,256]{1,0:T(8,128)(2,1)S(1)} %get-tuple-element.27.refs_1_, bf16[256,256]{1,0:T(8,128)(2,1)S(1)} %collective-permute-done.4.refs_2_, ...), custom_call_target="tpu_custom_call" | custom-call | bytes 7200000 | tf_op jit(solution)/shard_map/window_gradient/pallas_call | solution.py:248
  71.8 3.4 %collective-permute-start.7 = (bf16[768,256]{1,0:T(8,128)(2,1)S(1)}, bf16[768,256]{1,0:T(8,128)(2,1)S(1)}, u32[]{:S(2)}, u32[]{:S(2)}) collective-permute-start(bf16[768,256]{1,0:T(8,128)(2,1)S(1)} %get-tuple-element.29), channel_id=1, source_target_pairs={{0,4},{4,0},{1,5},{5,1},{2,6},{6,2},{3,7},{7,3},{8,12},{12,8},{9,1... | collective-permute-start | bytes 1179656 | tf_op jit(solution)/shard_map/ppermute | solution.py:51
  75.2 4.3 %collective-permute-start.8 = (bf16[256,256]{1,0:T(8,128)(2,1)S(1)}, bf16[256,256]{1,0:T(8,128)(2,1)S(1)}, u32[]{:S(2)}, u32[]{:S(2)}) collective-permute-start(bf16[256,256]{1,0:T(8,128)(2,1)S(1)} %get-tuple-element.32), channel_id=1, source_target_pairs={{4,16},{12,24},{16,4},{20,32},{24,12},{28,40},{32,20},{36,48},{40,... | collective-permute-start | bytes 393224 | tf_op jit(solution)/shard_map/ppermute | solution.py:47
  79.5 0.0 collective-permute-done.7.swapped_ref
  79.5 0.1 chip_sum.1
  79.6 1.3 %collective-permute-start.9 = (bf16[256,256]{1,0:T(8,128)(2,1)S(1)}, bf16[256,256]{1,0:T(8,128)(2,1)S(1)}, u32[]{:S(2)}, u32[]{:S(2)}) collective-permute-start(bf16[256,256]{1,0:T(8,128)(2,1)S(1)} %get-tuple-element.30), channel_id=1, source_target_pairs={{8,0},{12,4},{16,8},{20,12},{24,16},{28,20},{32,24},{36,28},{40,32... | collective-permute-start | bytes 393224 | tf_op jit(solution)/shard_map/ppermute | solution.py:37
  80.9 0.0 all-to-all-done.2.refs_0_
  80.9 0.7 sum_and_spread.3
  81.6 8.2 %all-to-all-start.3 = ((bf16[32,8,256]{2,1,0:T(8,128)(2,1)}), bf16[32,8,256]{2,1,0:T(8,128)(2,1)S(1)}, u32[]{:S(2)}, u32[]{:S(2)}) async-start(bf16[32,8,256]{2,1,0:T(8,128)(2,1)} %sum_and_spread.3), calls=%async_computation.3 | async-start | bytes 262144 | tf_op jit(solution)/shard_map/all_to_all | solution.py:60
  89.8 2.4 %collective-permute-start.10 = (bf16[256,256]{1,0:T(8,128)(2,1)S(1)}, bf16[256,256]{1,0:T(8,128)(2,1)S(1)}, u32[]{:S(2)}, u32[]{:S(2)}) collective-permute-start(bf16[256,256]{1,0:T(8,128)(2,1)S(1)} %get-tuple-element.36), channel_id=1, source_target_pairs={{0,8},{4,12},{8,16},{12,20},{16,24},{20,28},{24,32},{28,36},{32,40... | collective-permute-start | bytes 393224 | tf_op jit(solution)/shard_map/ppermute | solution.py:37
  92.3 0.0 collective-permute-done.8.far_ref
  92.3 0.0 collective-permute-done.9.after_ref
  92.3 5.1 %all-to-all-done.3 = bf16[32,8,256]{2,1,0:T(8,128)(2,1)S(1)} async-done(((bf16[32,8,256]{2,1,0:T(8,128)(2,1)}), bf16[32,8,256]{2,1,0:T(8,128)(2,1)S(1)}, u32[]{:S(2)}, u32[]{:S(2)}) %all-to-all-start.3) | async-done | bytes 131104 | tf_op jit(solution)/shard_map/all_to_all | solution.py:60
  97.4 0.7 bitcast_convert_fusion
  98.1 0.0 collective-permute-done.10.before_ref
  98.1 0.8 total_gradient.1
  (1 shorter events, 0.0 us)
Async XLA Ops:
  1.6 15.5 %collective-permute-start.2 = (bf16[256,256]{1,0:T(8,128)(2,1)S(1)}, bf16[256,256]{1,0:T(8,128)(2,1)S(1)}, u32[]{:S(2)}, u32[]{:S(2)}) collective-permute-start(bf16[256,256]{1,0:T(8,128)(2,1)S(1)} %own_quarter.1), channel_id=1, source_target_pairs={{4,16},{12,24},{16,4},{20,32},{24,12},{28,40},{32,20},{36,48},{40,... | collective-permute-start | bytes 393224 | tf_op jit(solution)/shard_map/ppermute | solution.py:47
  7.9 9.2 %collective-permute-start.1 = (bf16[256,256]{1,0:T(8,128)(2,1)S(1)}, bf16[256,256]{1,0:T(8,128)(2,1)S(1)}, u32[]{:S(2)}, u32[]{:S(2)}) collective-permute-start(bf16[256,256]{1,0:T(8,128)(2,1)S(1)} %own_quarter.1), channel_id=1, source_target_pairs={{8,0},{12,4},{16,8},{20,12},{24,16},{28,20},{32,24},{36,28},{40,32... | collective-permute-start | bytes 393224 | tf_op jit(solution)/shard_map/ppermute | solution.py:37
  9.2 7.9 %collective-permute-start = (bf16[256,256]{1,0:T(8,128)(2,1)S(1)}, bf16[256,256]{1,0:T(8,128)(2,1)S(1)}, u32[]{:S(2)}, u32[]{:S(2)}) collective-permute-start(bf16[256,256]{1,0:T(8,128)(2,1)S(1)} %own_quarter.1), channel_id=1, source_target_pairs={{0,8},{4,12},{8,16},{12,20},{16,24},{20,28},{24,32},{28,36},{32,40... | collective-permute-start | bytes 393224 | tf_op jit(solution)/shard_map/ppermute | solution.py:37
  17.0 19.3 %copy-start = (bf16[7,1024,256]{2,1,0:T(8,128)(2,1)}, bf16[7,1024,256]{2,1,0:T(8,128)(2,1)S(1)}, u32[]{:S(2)}) copy-start(bf16[7,1024,256]{2,1,0:T(8,128)(2,1)S(1)} %dense_band.1.band_ref.refs_0_) | copy-start | bytes 11010052
  17.0 18.1 %copy-start.1 = (bf16[256,256]{1,0:T(8,128)(2,1)S(1)}, bf16[256,256]{1,0:T(8,128)(2,1)}, u32[]{:S(2)}) copy-start(bf16[256,256]{1,0:T(8,128)(2,1)} %weight_ref.1) | copy-start | bytes 393220
  17.1 18.1 %copy-start.2 = (bf16[256,256]{1,0:T(8,128)(2,1)S(1)}, bf16[256,256]{1,0:T(8,128)(2,1)}, u32[]{:S(2)}) copy-start(bf16[256,256]{1,0:T(8,128)(2,1)} %cotangent_ref.1) | copy-start | bytes 393220
  17.1 5.0 %collective-permute-start.3 = (bf16[768,256]{1,0:T(8,128)(2,1)S(1)}, bf16[768,256]{1,0:T(8,128)(2,1)S(1)}, u32[]{:S(2)}, u32[]{:S(2)}) collective-permute-start(bf16[768,256]{1,0:T(8,128)(2,1)S(1)} %pad_maximum_fusion.near_ref), channel_id=1, source_target_pairs={{0,4},{4,0},{1,5},{5,1},{2,6},{6,2},{3,7},{7,3},{8,12},{12,8},{9,1... | collective-permute-start | bytes 1179656 | tf_op jit(solution)/shard_map/ppermute | solution.py:51
  36.3 25.7 %all-to-all-start.1 = ((bf16[32,8,256]{2,1,0:T(8,128)(2,1)}), bf16[32,8,256]{2,1,0:T(8,128)(2,1)S(1)}, u32[]{:S(2)}, u32[]{:S(2)}) async-start(bf16[32,8,256]{2,1,0:T(8,128)(2,1)} %get-tuple-element.25), calls=%async_computation.1 | async-start | bytes 262144 | tf_op jit(solution)/shard_map/all_to_all | solution.py:60
  51.3 17.3 %collective-permute-start.6 = (bf16[256,256]{1,0:T(8,128)(2,1)S(1)}, bf16[256,256]{1,0:T(8,128)(2,1)S(1)}, u32[]{:S(2)}, u32[]{:S(2)}) collective-permute-start(bf16[256,256]{1,0:T(8,128)(2,1)S(1)} %get-tuple-element.27.refs_1_), channel_id=1, source_target_pairs={{0,1},{1,2},{2,3},{3,0},{4,5},{5,6},{6,7},{7,4},{8,9},{9,10},{10,1... | collective-permute-start | bytes 393224 | tf_op jit(solution)/shard_map/ppermute | solution.py:56
  54.6 14.0 %collective-permute-start.5 = (bf16[256,256]{1,0:T(8,128)(2,1)S(1)}, bf16[256,256]{1,0:T(8,128)(2,1)S(1)}, u32[]{:S(2)}, u32[]{:S(2)}) collective-permute-start(bf16[256,256]{1,0:T(8,128)(2,1)S(1)} %get-tuple-element.27.refs_1_), channel_id=1, source_target_pairs={{0,2},{1,3},{2,0},{3,1},{4,6},{5,7},{6,4},{7,5},{8,10},{9,11},{10,... | collective-permute-start | bytes 393224 | tf_op jit(solution)/shard_map/ppermute | solution.py:56
  58.9 9.7 %collective-permute-start.4 = (bf16[256,256]{1,0:T(8,128)(2,1)S(1)}, bf16[256,256]{1,0:T(8,128)(2,1)S(1)}, u32[]{:S(2)}, u32[]{:S(2)}) collective-permute-start(bf16[256,256]{1,0:T(8,128)(2,1)S(1)} %get-tuple-element.27.refs_1_), channel_id=1, source_target_pairs={{0,3},{1,0},{2,1},{3,2},{4,7},{5,4},{6,5},{7,6},{8,11},{9,8},{10,9... | collective-permute-start | bytes 393224 | tf_op jit(solution)/shard_map/ppermute | solution.py:56
  62.7 18.2 %all-to-all-start.2 = ((f32[16,8,256]{2,1,0:T(8,128)}), f32[16,8,256]{2,1,0:T(8,128)S(1)}, u32[]{:S(2)}, u32[]{:S(2)}) async-start(f32[16,8,256]{2,1,0:T(8,128)} %sum_and_spread.2), calls=%async_computation.2 | async-start | bytes 262144 | tf_op jit(solution)/shard_map/all_to_all | solution.py:60
  71.8 7.8 %collective-permute-start.7 = (bf16[768,256]{1,0:T(8,128)(2,1)S(1)}, bf16[768,256]{1,0:T(8,128)(2,1)S(1)}, u32[]{:S(2)}, u32[]{:S(2)}) collective-permute-start(bf16[768,256]{1,0:T(8,128)(2,1)S(1)} %get-tuple-element.29), channel_id=1, source_target_pairs={{0,4},{4,0},{1,5},{5,1},{2,6},{6,2},{3,7},{7,3},{8,12},{12,8},{9,1... | collective-permute-start | bytes 1179656 | tf_op jit(solution)/shard_map/ppermute | solution.py:51
  75.2 17.1 %collective-permute-start.8 = (bf16[256,256]{1,0:T(8,128)(2,1)S(1)}, bf16[256,256]{1,0:T(8,128)(2,1)S(1)}, u32[]{:S(2)}, u32[]{:S(2)}) collective-permute-start(bf16[256,256]{1,0:T(8,128)(2,1)S(1)} %get-tuple-element.32), channel_id=1, source_target_pairs={{4,16},{12,24},{16,4},{20,32},{24,12},{28,40},{32,20},{36,48},{40,... | collective-permute-start | bytes 393224 | tf_op jit(solution)/shard_map/ppermute | solution.py:47
  79.6 12.7 %collective-permute-start.9 = (bf16[256,256]{1,0:T(8,128)(2,1)S(1)}, bf16[256,256]{1,0:T(8,128)(2,1)S(1)}, u32[]{:S(2)}, u32[]{:S(2)}) collective-permute-start(bf16[256,256]{1,0:T(8,128)(2,1)S(1)} %get-tuple-element.30), channel_id=1, source_target_pairs={{8,0},{12,4},{16,8},{20,12},{24,16},{28,20},{32,24},{36,28},{40,32... | collective-permute-start | bytes 393224 | tf_op jit(solution)/shard_map/ppermute | solution.py:37
  81.6 15.8 %all-to-all-start.3 = ((bf16[32,8,256]{2,1,0:T(8,128)(2,1)}), bf16[32,8,256]{2,1,0:T(8,128)(2,1)S(1)}, u32[]{:S(2)}, u32[]{:S(2)}) async-start(bf16[32,8,256]{2,1,0:T(8,128)(2,1)} %sum_and_spread.3), calls=%async_computation.3 | async-start | bytes 262144 | tf_op jit(solution)/shard_map/all_to_all | solution.py:60
  89.8 8.3 %collective-permute-start.10 = (bf16[256,256]{1,0:T(8,128)(2,1)S(1)}, bf16[256,256]{1,0:T(8,128)(2,1)S(1)}, u32[]{:S(2)}, u32[]{:S(2)}) collective-permute-start(bf16[256,256]{1,0:T(8,128)(2,1)S(1)} %get-tuple-element.36), channel_id=1, source_target_pairs={{0,8},{4,12},{8,16},{12,20},{16,24},{20,28},{24,32},{28,36},{32,40... | collective-permute-start | bytes 393224 | tf_op jit(solution)/shard_map/ppermute | solution.py:37
